TPU v7x, 32 devices: a whole 2x2x4 slice. The times are simulated.
32 devices in a mesh: groups: 2 (over y), gx: 4 (over x, core), vert: 4 (over z).
Axes of the slice: x: 2, y: 2, z: 4, core: 2. Of those that a mesh axis runs over, the one named last changes fastest.
Arguments:
- distribution: float32 [64, 16, 16, 2048], P(('groups', 'gx'), None, None, 'vert'), parts along dimension 0, may hold values from 0.05 to 2
- velocity_order: int32 [2048], P('vert'), may hold values from 0 to 2047, each once
- cell_codes: int32 [64, 16, 16], P(('groups', 'gx')), parts along dimension 0, may hold values from 0 to 2, as said below
- knudsen: float32 [2], P('groups'), parts along dimension 0, may hold values from 0.05 to 1
- inflow: float32 [8], P('groups'), parts along dimension 0, may hold values from 0.5 to 1.5
Outputs:
- evolved: float32 [64, 16, 16, 2048], P(('groups', 'gx'), None, None, 'vert'), parts along dimension 0
There are 2 independent parts, one for each index of `groups`. A program takes and returns all parts, laid end to end along the dimension named above; an argument that names none is the same for every part. Nothing has to cross between parts.
Inputs may be any that keep to these rules, and one draw needn't show every extreme that they name: `velocity_order`: names each of the 2048 velocity grid points once. `cell_codes`: 0 marks an open cell, 1 an inflow cell, 2 a wall cell.
All inputs are finite; a program needn't handle non-finite values.
Results may differ from a plain program's by a relative error of at most 0.0003.
Values sent between devices are 32-bit elements; how exact they have to be, the bound alone decides.
No kernel may reach another device: no remote copies, remote signals or barrier semaphores. Data moves between devices by JAX's collectives and lax.ppermute only.
A program may use at most 128 MiB of HBM per device.

v0:
```python
import functools

import jax
import jax.numpy as jnp
from jax import lax
from jax.experimental import pallas as pl
from jax.experimental.pallas import tpu as pltpu
from jax.sharding import PartitionSpec as P

VGX = 16
VGY = 16
VGZ = 8
STEPS = 3
LANES = 128
SUB = 8
FEATURES = 32
UNIT = 3.0 / 16.0
LOG2E = 1.4426950408889634
VMEM_LIMIT = 48 * 1024 * 1024
F32 = jnp.float32
BF16 = jnp.bfloat16


def minmod(lower, upper):
    return jnp.maximum(
        jnp.minimum(lower, upper), jnp.minimum(jnp.maximum(lower, upper), 0.0)
    )


def x_pass(load, rows, store, coef):
    first, last = rows[0], rows[-1]
    reach, lean = coef[0], coef[1]
    ahead = coef[2] > 0.0

    def one(y, carry):
        for t in range(2):
            cells = {n: load(n, y, t) for n in range(first - 2, last + 3)}
            steps = {n: cells[n + 1] - cells[n] for n in range(first - 2, last + 2)}
            faces = {
                n: cells[n] + lean * minmod(steps[n - 1], steps[n])
                for n in range(first - 1, last + 2)
            }
            for n in rows:
                source = jnp.where(ahead, faces[n - 1], faces[n + 1])
                store(n, y, t, cells[n] - reach * (faces[n] - source))
        return carry

    lax.fori_loop(0, 16, one, 0)


def yz_pass(load, update, coef):
    reach_y, lean_y, ahead_y = coef[3], coef[4], coef[5] > 0.0
    reach_z, lean_z, ahead_z = coef[6], coef[7], coef[8] > 0.0
    place = lax.broadcasted_iota(jnp.int32, (SUB, LANES), 0)
    top, bottom = place == SUB - 1, place == 0
    crossing = (ahead_z & bottom) | (jnp.logical_not(ahead_z) & top)
    count = 16
    cells = {}
    steps = {}
    faces = {}

    def cell(y, t):
        y %= count
        if (y, t) not in cells:
            cells[y, t] = load(y, t)
        return cells[y, t]

    def step(y, t):
        y %= count
        if (y, t) not in steps:
            steps[y, t] = cell(y + 1, t) - cell(y, t)
        return steps[y, t]

    def face(y, t):
        y %= count
        if (y, t) not in faces:
            faces[y, t] = cell(y, t) + lean_y * minmod(step(y - 1, t), step(y, t))
        return faces[y, t]

    def up(v):
        return pltpu.roll(v, SUB - 1, 0)

    def down(v):
        return pltpu.roll(v, 1, 0)

    for y in range(count):
        changes = [
            reach_y * (face(y, t) - jnp.where(ahead_y, face(y - 1, t), face(y + 1, t)))
            for t in range(2)
        ]
        low, high = cell(y, 0), cell(y, 1)
        up_low, up_high = up(low), up(high)
        step_low = jnp.where(top, up_high, up_low) - low
        step_high = jnp.where(top, up_low, up_high) - high
        down_low, down_high = down(step_low), down(step_high)
        face_low = low + lean_z * minmod(
            jnp.where(bottom, down_high, down_low), step_low
        )
        face_high = high + lean_z * minmod(
            jnp.where(bottom, down_low, down_high), step_high
        )
        turn_low = jnp.where(ahead_z, down(face_low), up(face_low))
        turn_high = jnp.where(ahead_z, down(face_high), up(face_high))
        changes[0] += reach_z * (face_low - jnp.where(crossing, turn_high, turn_low))
        changes[1] += reach_z * (face_high - jnp.where(crossing, turn_low, turn_high))
        for t in range(2):
            update(y, t, changes[t])


def row_moments(block, weights):
    flat = block.reshape(256, LANES)
    high = flat.astype(BF16)
    rest = (flat - high.astype(F32)).astype(BF16)
    contract = (((1,), (1,)), ((), ()))
    total = lax.dot_general(weights, high, contract, preferred_element_type=F32)
    total += lax.dot_general(weights, rest, contract, preferred_element_type=F32)
    return total[:SUB]


def write_moments(out, place, value):
    for m in range(4):
        out[m, pl.ds(place, 1), :] = value[m : m + 1]
    out[4, pl.ds(place, 1), :] = value[4:5] + value[5:6]


def three_parts(value):
    high = value.astype(BF16).astype(F32)
    rest = value - high
    middle = rest.astype(BF16).astype(F32)
    low = (rest - middle).astype(BF16).astype(F32)
    return high, middle, low


def spread_features(params, wide, tall, rows):
    alpha, beta_x, beta_y, beta_z, gamma, keep = params
    alpha = jnp.where(gamma == 0.0, -10000.0, alpha)
    zero = jnp.zeros_like(alpha)
    columns = []
    for value in (alpha, beta_x, beta_y, beta_z, gamma, gamma, keep):
        columns.extend(three_parts(value))
    columns.extend([zero] * (FEATURES - len(columns)))
    for k, value in enumerate(columns):
        for r in range(rows):
            wide[r, k : k + 1, :] = value[r : r + 1]
    for r in range(rows):
        tall[r] = wide[r].T.astype(BF16)


def relax_row(features, table, source):
    product = jnp.dot(features, table, preferred_element_type=F32)
    block = source.reshape(256, LANES)
    block = product[:, LANES:] * block + jnp.exp2(product[:, :LANES])
    return block.reshape(16, 2, SUB, LANES)


def param_kernel(total, count, *refs):
    parts = refs[:count]
    codes, knudsen, inflow, out, out_low, out_high = refs[count:]
    sums = [parts[0][m] for m in range(5)]
    for part in parts[1:]:
        sums = [s + part[m] for m, s in enumerate(sums)]
    density = sums[0] * (1.0 / total)
    scale = UNIT / sums[0]
    u_x, u_y, u_z = (sums[m] * scale for m in (1, 2, 3))
    heat = (UNIT * sums[4] * scale - (u_x * u_x + u_y * u_y + u_z * u_z)) * (1.0 / 3.0)
    rate = 0.5 * density / (density + knudsen[0])
    code = codes[...]
    flowing, wall = code == 1, code == 2
    closed = flowing | wall
    u_x = jnp.where(flowing, inflow[1], jnp.where(wall, 0.0, u_x))
    u_y = jnp.where(closed, 0.0, u_y)
    u_z = jnp.where(closed, 0.0, u_z)
    heat = jnp.where(flowing, inflow[2], jnp.where(wall, inflow[3], heat))
    amount = jnp.where(flowing, inflow[0], jnp.where(wall, density, rate * density))
    keep = jnp.where(closed, 0.0, 1.0 - rate)
    g = (-0.5 * LOG2E) / heat

    def line(u, n, unit):
        s = None
        for i in range(n):
            gap = (i + 0.5 - n / 2) * unit - u
            e = jnp.exp2(g * (gap * gap))
            s = e if s is None else s + e
        return s

    norm = line(u_x, VGX, 6.0 / VGX) * line(u_y, VGY, 6.0 / VGY)
    norm = norm * line(u_z, VGZ, 6.0 / VGZ) * (1.0 / total)
    alpha = (jnp.log(amount) - jnp.log(norm)) * LOG2E
    alpha = alpha + g * (u_x * u_x + u_y * u_y + u_z * u_z)
    lean = (-2.0 * UNIT) * g
    params = (alpha, lean * u_x, lean * u_y, lean * u_z, g * (UNIT * UNIT), keep)
    rows = code.shape[0]
    for k, value in enumerate(params):
        out[k] = value
        out_low[k] = value[:2]
        out_high[k] = value[rows - 2 :]


def inner_kernel(relax, rows, *refs):
    if relax:
        (m_low, m_mid, m_high, params, table, coef_ref, weights, state, out, sums,
         wide, tall, acc) = refs
    else:
        state, coef_ref, weights, out, sums, acc = refs
    chunk, chunks = pl.program_id(0), pl.num_programs(0)
    inner = rows - 4
    if relax:

        @pl.when(chunk == 0)
        def _():
            spread_features([params[k] for k in range(6)], wide, tall, rows)

        columns = table[0]
        for r in range(2):
            state[r] = relax_row(tall[r], columns, m_low[r])

        def middle(r, carry):
            state[r + 2] = relax_row(tall[r + 2], columns, m_mid[r])
            return carry

        lax.fori_loop(0, inner, middle, 0)
        for r in range(2):
            state[rows - 2 + r] = relax_row(tall[rows - 2 + r], columns, m_high[r])
    coef = [coef_ref[k] for k in range(9)]

    def store(n, y, t, v):
        out[n - 2, y, t] = v

    x_pass(lambda n, y, t: state[n, y, t], list(range(2, rows - 2)), store, coef)

    def one(r, carry):
        def update(y, t, v):
            out[r, y, t] = out[r, y, t] - v

        yz_pass(lambda y, t: state[r + 2, y, t], update, coef)
        part = row_moments(out[r], weights[...])

        @pl.when(chunk == 0)
        def _():
            acc[r] = part

        @pl.when(chunk > 0)
        def _():
            acc[r] = acc[r] + part

        return carry

    lax.fori_loop(0, inner, one, 0)

    @pl.when(chunk == chunks - 1)
    def _():
        for r in range(inner):
            write_moments(sums, r, acc[r])


def edge_kernel(relax, rows, *refs):
    if relax:
        (h_low, h_high, p_low, p_high, table, state, coef_ref, weights, inner_sums,
         out_low, out_high, sums, wide, tall, halo, acc) = refs
    else:
        (h_low, h_high, state, coef_ref, weights, inner_sums,
         out_low, out_high, sums, acc) = refs
    chunk, chunks = pl.program_id(0), pl.num_programs(0)
    if relax:

        @pl.when(chunk == 0)
        def _():
            spread_features([p_low[k] for k in range(6)], wide, tall.at[0], 2)
            spread_features([p_high[k] for k in range(6)], wide, tall.at[1], 2)

        columns = table[0]
        for r in range(2):
            halo[0, r] = relax_row(tall[0, r], columns, h_low[r])
            halo[1, r] = relax_row(tall[1, r], columns, h_high[r])
        low, high = halo.at[0], halo.at[1]
    else:
        low, high = h_low, h_high
    coef = [coef_ref[k] for k in range(9)]

    def load(n, y, t):
        if n < 0:
            return low[n + 2, y, t]
        if n >= rows:
            return high[n - rows, y, t]
        return state[n, y, t]

    for side, first, out in ((0, 0, out_low), (1, rows - 2, out_high)):

        def store(n, y, t, v, first=first, out=out):
            out[n - first, y, t] = v

        x_pass(load, [first, first + 1], store, coef)

        def one(r, carry, side=side, first=first, out=out):
            def update(y, t, v):
                out[r, y, t] = out[r, y, t] - v

            yz_pass(lambda y, t: state[r + first, y, t], update, coef)
            part = row_moments(out[r], weights[...])
            place = r + 2 * side

            @pl.when(chunk == 0)
            def _():
                acc[place] = part

            @pl.when(chunk > 0)
            def _():
                acc[place] = acc[place] + part

            return carry

        lax.fori_loop(0, 2, one, 0)

    @pl.when(chunk == chunks - 1)
    def _():
        for m in range(5):
            sums[m, 2 : rows - 2, :] = inner_sums[m]
        for r in range(2):
            write_moments(sums, r, acc[r])
            write_moments(sums, rows - 2 + r, acc[2 + r])


def final_kernel(rows, *refs):
    m_low, m_mid, m_high, params, table, out, wide, tall = refs

    @pl.when(pl.program_id(0) == 0)
    def _():
        spread_features([params[k] for k in range(6)], wide, tall, rows)

    columns = table[0]
    for r in range(2):
        out[r] = relax_row(tall[r], columns, m_low[r])
        out[rows - 2 + r] = relax_row(tall[rows - 2 + r], columns, m_high[r])

    def middle(r, carry):
        out[r + 2] = relax_row(tall[r + 2], columns, m_mid[r])
        return carry

    lax.fori_loop(0, rows - 4, middle, 0)


def body(distribution, velocity_order, cell_codes, knudsen, inflow):
    rows, count_y, count_z, width = distribution.shape
    peers = lax.axis_size("vert")
    total = width * peers
    chunks = width // LANES
    state = distribution.reshape(rows, count_y, 2, SUB, width)
    codes = cell_codes.reshape(rows, count_y * count_z)

    plane = VGY * VGZ
    n_x = 2 * (velocity_order // plane) - (VGX - 1)
    n_y = 2 * (velocity_order // VGZ % VGY) - (VGY - 1)
    n_z = 2 * (2 * (velocity_order % VGZ) - (VGZ - 1))
    square = n_x * n_x + n_y * n_y + n_z * n_z
    ones = jnp.ones_like(n_x)
    low_part = square % 8
    whole = jnp.stack([ones, n_x, n_y, n_z, square - low_part, low_part]).astype(F32)
    weights = jnp.pad(whole, ((0, 10), (0, 0))).astype(BF16)
    exponent = jnp.repeat(whole, 3, axis=0)
    exponent = jnp.pad(exponent, ((0, FEATURES - 18), (0, 0)))
    exponent = exponent.reshape(FEATURES, chunks, LANES)
    place = lax.broadcasted_iota(jnp.int32, (FEATURES, chunks, LANES), 0)
    factor = jnp.where((place >= 18) & (place < 21), 1.0, 0.0)
    table = jnp.concatenate([exponent, factor], axis=2)
    table = table.transpose(1, 0, 2).astype(BF16)
    coef = []
    for n, scale in ((n_x, 0.1), (n_y, 1.0 / 30.0), (n_z, 1.0 / 30.0)):
        courant = n.astype(F32) * UNIT * scale
        sign = jnp.where(n > 0, 1.0, -1.0)
        reach = jnp.abs(courant)
        coef.extend([reach, 0.5 * sign * (1.0 - reach), sign])
    coef = jnp.broadcast_to(jnp.stack(coef)[:, None, :], (9, SUB, width))

    def slab(n):
        return pl.BlockSpec((n, count_y, 2, SUB, LANES), lambda c: (0, 0, 0, 0, c))

    def slab_shape(n):
        return jax.ShapeDtypeStruct((n, count_y, 2, SUB, width), F32)

    cells = count_y * count_z
    whole_sums = pl.BlockSpec((5, rows, cells), lambda c: (0, 0, 0))
    inner_sums = pl.BlockSpec((5, rows - 4, cells), lambda c: (0, 0, 0))
    param_spec = pl.BlockSpec((6, rows, cells), lambda c: (0, 0, 0))
    edge_params = pl.BlockSpec((6, 2, cells), lambda c: (0, 0, 0))
    table_spec = pl.BlockSpec((1, FEATURES, 2 * LANES), lambda c: (c, 0, 0))
    coef_spec = pl.BlockSpec((9, SUB, LANES), lambda c: (0, 0, c))
    weight_spec = pl.BlockSpec((16, LANES), lambda c: (0, c))
    limits = pltpu.CompilerParams(
        dimension_semantics=("arbitrary",), vmem_limit_bytes=VMEM_LIMIT
    )

    def feature_scratch(n):
        return [pltpu.VMEM((n, FEATURES, cells), F32), pltpu.VMEM((n, cells, FEATURES), BF16)]

    def inner(relax, args):
        acc = pltpu.VMEM((rows - 4, SUB, cells), F32)
        sums = jax.ShapeDtypeStruct((5, rows - 4, cells), F32)
        if relax:
            return pl.pallas_call(
                functools.partial(inner_kernel, True, rows),
                grid=(chunks,),
                in_specs=[slab(2), slab(rows - 4), slab(2), param_spec, table_spec, coef_spec, weight_spec],
                out_specs=[slab(rows), slab(rows - 4), inner_sums],
                out_shape=[slab_shape(rows), slab_shape(rows - 4), sums],
                scratch_shapes=feature_scratch(rows) + [acc],
                compiler_params=limits,
                name="inner_relax",
            )(*args, table, coef, weights)
        return pl.pallas_call(
            functools.partial(inner_kernel, False, rows),
            grid=(chunks,),
            in_specs=[slab(rows), coef_spec, weight_spec],
            out_specs=[slab(rows - 4), inner_sums],
            out_shape=[slab_shape(rows - 4), sums],
            scratch_shapes=[acc],
            compiler_params=limits,
            name="inner_first",
        )(*args, coef, weights)

    def edge(relax, halos, params, state, sums):
        acc = pltpu.VMEM((4, SUB, cells), F32)
        out_specs = [slab(2), slab(2), whole_sums]
        out_shape = [slab_shape(2), slab_shape(2), jax.ShapeDtypeStruct((5, rows, cells), F32)]
        tail = [slab(rows), coef_spec, weight_spec, inner_sums]
        if relax:
            return pl.pallas_call(
                functools.partial(edge_kernel, True, rows),
                grid=(chunks,),
                in_specs=[slab(2), slab(2), edge_params, edge_params, table_spec] + tail,
                out_specs=out_specs,
                out_shape=out_shape,
                scratch_shapes=[
                    pltpu.VMEM((2, FEATURES, cells), F32),
                    pltpu.VMEM((2, 2, cells, FEATURES), BF16),
                    pltpu.VMEM((2, 2, count_y, 2, SUB, LANES), F32),
                    acc,
                ],
                compiler_params=limits,
                name="edge_relax",
            )(*halos, *params, table, state, coef, weights, sums)
        return pl.pallas_call(
            functools.partial(edge_kernel, False, rows),
            grid=(chunks,),
            in_specs=[slab(2), slab(2)] + tail,
            out_specs=out_specs,
            out_shape=out_shape,
            scratch_shapes=[acc],
            compiler_params=limits,
            name="edge_first",
        )(*halos, state, coef, weights, sums)

    smem = pl.BlockSpec(memory_space=pltpu.SMEM)
    vmem = pl.BlockSpec(memory_space=pltpu.VMEM)

    def cell_params(parts):
        return pl.pallas_call(
            functools.partial(param_kernel, total, len(parts)),
            in_specs=[vmem] * (len(parts) + 1) + [smem, smem],
            out_specs=[vmem] * 3,
            out_shape=[
                jax.ShapeDtypeStruct((6, n, cells), F32) for n in (rows, 2, 2)
            ],
            name="cell_params",
        )(*parts, codes, knudsen, inflow)

    def final(args):
        return pl.pallas_call(
            functools.partial(final_kernel, rows),
            grid=(chunks,),
            in_specs=[slab(2), slab(rows - 4), slab(2), param_spec, table_spec],
            out_specs=slab(rows),
            out_shape=slab_shape(rows),
            scratch_shapes=feature_scratch(rows),
            compiler_params=limits,
            name="final_relax",
        )(*args, table)

    line = lax.axis_size("gx")
    forward = [(i, i + 1) for i in range(line - 1)]
    backward = [(i + 1, i) for i in range(line - 1)]

    def exchange(low, high):
        return lax.ppermute(high, "gx", forward), lax.ppermute(low, "gx", backward)

    def gather(part):
        parts = [part]
        for shift in range(1, peers):
            pairs = [(i, (i + shift) % peers) for i in range(peers)]
            parts.append(lax.ppermute(part, "vert", pairs))
        return parts

    halos = exchange(state[:2], state[rows - 2 :])
    m_mid, sums = inner(False, (state,))
    m_low, m_high, sums = edge(False, halos, None, state, sums)
    for step in range(1, STEPS + 1):
        if step < STEPS:
            halos = exchange(m_low, m_high)
        params, p_low, p_high = cell_params(gather(sums))
        if step == STEPS:
            break
        p_halos = exchange(p_low, p_high)
        state, m_mid, sums = inner(True, (m_low, m_mid, m_high, params))
        m_low, m_high, sums = edge(True, halos, p_halos, state, sums)
    result = final((m_low, m_mid, m_high, params))
    return result.reshape(rows, count_y, count_z, width)


def solution(mesh):
    placed = (
        P(("groups", "gx"), None, None, "vert"),
        P("vert"),
        P(("groups", "gx"), None, None),
        P("groups"),
        P("groups"),
    )
    return jax.shard_map(
        body,
        mesh=mesh,
        in_specs=placed,
        out_specs=P(("groups", "gx"), None, None, "vert"),
        check_vma=False,
    )
```

profile of v0, /device:TPU:0, one launch (start us, length us, event | category | flops | bytes accessed | tf_op | source)
XLA Modules:
  0.0 142.2 jit_solution(7083251515027327183)
XLA Ops:
  0.0 2.8 %slice_bitcast_fusion = (f32[2,16,2,8,512]{4,3,2,1,0:T(8,128)S(1)}, f32[2,16,2,8,512]{4,3,2,1,0:T(8,128)}) fusion(f32[8,16,16,512]{3,2,1,0:T(8,128)} %param.5), kind=kLoop, calls=%fused_computation | loop fusion | bytes 4194304 | tf_op jit(solution)/shard_map/slice | solution.py:492
  2.8 2.4 %collective-permute-start = (f32[2,16,2,8,512]{4,3,2,1,0:T(8,128)}, f32[2,16,2,8,512]{4,3,2,1,0:T(8,128)S(1)}, u32[]{:S(2)}, u32[]{:S(2)}) collective-permute-start(f32[2,16,2,8,512]{4,3,2,1,0:T(8,128)} %get-tuple-element.58), channel_id=1, source_target_pairs={{0,4},{4,8},{8,12},{1,5},{5,9},{9,13},{2,6},{6,10},{10,14},{3,7},{... | collective-permute-start | bytes 3145736 | tf_op jit(solution)/shard_map/ppermute | solution.py:483
  5.3 1.3 collective-permute-start.1
  6.8 7.5 %inner_first.1 = (f32[4,16,2,8,512]{4,3,2,1,0:T(8,128)S(1)}, f32[5,4,256]{2,1,0:T(4,128)S(1)}) custom-call(f32[8,16,2,8,512]{4,3,2,1,0:T(8,128)} %bitcast.27, f32[9,8,512]{2,1,0:T(8,128)S(1)} %broadcast_in_dim.31.refs_1_.refs_3_.refs_5_.refs_6_, bf16[16,512]{1,0:T(8,128)(2,1)S(1)} %pad.10.refs_2_.refs_4_.refs_6_.refs_7_), custom_call_target="tpu_custom_call" | custom-call | tf_op jit(solution)/shard_map/inner_first/pallas_call | solution.py:409
  14.3 1.3 copy-done
  15.6 1.0 copy-done.4
  16.6 1.2 copy-done.5
  17.8 8.4 %edge_first.1 = (f32[2,16,2,8,512]{4,3,2,1,0:T(8,128)S(1)}, f32[2,16,2,8,512]{4,3,2,1,0:T(8,128)S(1)}, f32[5,8,256]{2,1,0:T(8,128)S(1)}) custom-call(f32[2,16,2,8,512]{4,3,2,1,0:T(8,128)S(1)} %collective-permute-done.refs_0_, f32[2,16,2,8,512]{4,3,2,1,0:T(8,128)S(1)} %copy-done.5, f32[8,16,2,8,512]{4,3,2,1,0:T(8,128)} %bitcast.28, ...), custom_call_target="tpu_custom_call" | custom-call | tf_op jit(solution)/shard_map/edge_first/pallas_call | solution.py:441
  26.3 10.2 %collective-permute-start.2 = (f32[2,16,2,8,512]{4,3,2,1,0:T(8,128)S(1)}, f32[2,16,2,8,512]{4,3,2,1,0:T(8,128)S(1)}, u32[]{:S(2)}, u32[]{:S(2)}) collective-permute-start(f32[2,16,2,8,512]{4,3,2,1,0:T(8,128)S(1)} %get-tuple-element.30.refs_2_), channel_id=1, source_target_pairs={{0,4},{4,8},{8,12},{1,5},{5,9},{9,13},{2,6},{6,10},{10,14},{3,7},{... | collective-permute-start | bytes 3145736 | tf_op jit(solution)/shard_map/ppermute | solution.py:483
  36.5 1.3 collective-permute-start.3
  37.9 1.6 %collective-permute-start.4 = (f32[5,8,256]{2,1,0:T(8,128)S(1)}, f32[5,8,256]{2,1,0:T(8,128)S(1)}, u32[]{:S(2)}, u32[]{:S(2)}) collective-permute-start(f32[5,8,256]{2,1,0:T(8,128)S(1)} %get-tuple-element.32.refs_0_), channel_id=1, source_target_pairs={{0,1},{1,2},{2,3},{3,0},{4,5},{5,6},{6,7},{7,4},{8,9},{9,10},{10,1... | collective-permute-start | bytes 122888 | tf_op jit(solution)/shard_map/ppermute | solution.py:489
  39.5 2.6 %collective-permute-start.5 = (f32[5,8,256]{2,1,0:T(8,128)S(1)}, f32[5,8,256]{2,1,0:T(8,128)}, u32[]{:S(2)}, u32[]{:S(2)}) collective-permute-start(f32[5,8,256]{2,1,0:T(8,128)S(1)} %get-tuple-element.32.refs_0_), channel_id=1, source_target_pairs={{0,2},{1,3},{2,0},{3,1},{4,6},{5,7},{6,4},{7,5},{8,10},{9,11},{10,... | collective-permute-start | bytes 122888 | tf_op jit(solution)/shard_map/ppermute | solution.py:489
  42.1 1.3 collective-permute-start.6
  43.5 0.7 reshape.21.refs_4_
  44.8 1.3 collective-permute-done.5.refs_2_
  46.3 1.6 %cell_params.3 = (f32[6,8,256]{2,1,0:T(8,128)}, f32[6,2,256]{2,1,0:T(2,128)}, f32[6,2,256]{2,1,0:T(2,128)}) custom-call(f32[5,8,256]{2,1,0:T(8,128)} %copy-done.11, f32[5,8,256]{2,1,0:T(8,128)} %copy-done.15, f32[5,8,256]{2,1,0:T(8,128)} %collective-permute-done.5.refs_2_, f32[5,8,256]{2,1,0:T(8,128)} %collective-permute-done.6.refs_3_, ...), custom_call_target="tpu_custom_call" | custom-call | tf_op jit(solution)/shard_map/cell_params/pallas_call | solution.py:456
  47.9 1.7 %collective-permute-start.7 = (f32[6,2,256]{2,1,0:T(2,128)}, f32[6,2,256]{2,1,0:T(2,128)S(1)}, u32[]{:S(2)}, u32[]{:S(2)}) collective-permute-start(f32[6,2,256]{2,1,0:T(2,128)} %get-tuple-element.33), channel_id=1, source_target_pairs={{0,4},{4,8},{8,12},{1,5},{5,9},{9,13},{2,6},{6,10},{10,14},{3,7},{... | collective-permute-start | bytes 36872 | tf_op jit(solution)/shard_map/ppermute | solution.py:483
  49.6 1.3 collective-permute-start.8
  51.0 0.8 copy-done.8
  51.8 12.9 %inner_relax.2 = (f32[8,16,2,8,512]{4,3,2,1,0:T(8,128)}, f32[4,16,2,8,512]{4,3,2,1,0:T(8,128)S(1)}, f32[5,4,256]{2,1,0:T(4,128)S(1)}) custom-call(f32[2,16,2,8,512]{4,3,2,1,0:T(8,128)S(1)} %get-tuple-element.31.refs_0_, f32[4,16,2,8,512]{4,3,2,1,0:T(8,128)} %copy-done, f32[2,16,2,8,512]{4,3,2,1,0:T(8,128)S(1)} %get-tuple-element.30.refs_2_, ...), custom_call_target="tpu_custom_call" | custom-call | tf_op jit(solution)/shard_map/inner_relax/pallas_call | solution.py:399
  64.7 1.3 copy-done.1
  66.1 1.0 copy-done.2
  67.1 1.2 copy-done.3
  68.3 10.2 %edge_relax.2 = (f32[2,16,2,8,512]{4,3,2,1,0:T(8,128)}, f32[2,16,2,8,512]{4,3,2,1,0:T(8,128)S(1)}, f32[5,8,256]{2,1,0:T(8,128)S(1)}) custom-call(f32[2,16,2,8,512]{4,3,2,1,0:T(8,128)S(1)} %copy-done.3, f32[2,16,2,8,512]{4,3,2,1,0:T(8,128)} %collective-permute-done.3.refs_1_, f32[6,2,256]{2,1,0:T(2,128)S(1)} %collective-permute-done.7.refs_2_, ...), custom_call_target="tpu_custom_call" | custom-call | tf_op jit(solution)/shard_map/edge_relax/pallas_call | solution.py:426
  78.5 1.3 collective-permute-start.10
  79.8 6.5 %collective-permute-start.9 = (f32[2,16,2,8,512]{4,3,2,1,0:T(8,128)S(1)}, f32[2,16,2,8,512]{4,3,2,1,0:T(8,128)}, u32[]{:S(2)}, u32[]{:S(2)}) collective-permute-start(f32[2,16,2,8,512]{4,3,2,1,0:T(8,128)S(1)} %get-tuple-element.39.refs_2_), channel_id=1, source_target_pairs={{0,4},{4,8},{8,12},{1,5},{5,9},{9,13},{2,6},{6,10},{10,14},{3,7},{... | collective-permute-start | bytes 3145736 | tf_op jit(solution)/shard_map/ppermute | solution.py:483
  86.7 3.3 %collective-permute-start.12 = (f32[5,8,256]{2,1,0:T(8,128)S(1)}, f32[5,8,256]{2,1,0:T(8,128)S(1)}, u32[]{:S(2)}, u32[]{:S(2)}) collective-permute-start(f32[5,8,256]{2,1,0:T(8,128)S(1)} %get-tuple-element.41.refs_0_), channel_id=1, source_target_pairs={{0,2},{1,3},{2,0},{3,1},{4,6},{5,7},{6,4},{7,5},{8,10},{9,11},{10,... | collective-permute-start | bytes 122888 | tf_op jit(solution)/shard_map/ppermute | solution.py:489
  90.2 2.5 %collective-permute-done.11.refs_1_ = f32[5,8,256]{2,1,0:T(8,128)S(1)} collective-permute-done((f32[5,8,256]{2,1,0:T(8,128)S(1)}, f32[5,8,256]{2,1,0:T(8,128)S(1)}, u32[]{:S(2)}, u32[]{:S(2)}) %collective-permute-start.11) | collective-permute-done | bytes 40992 | tf_op jit(solution)/shard_map/ppermute | solution.py:489
  92.7 1.5 %collective-permute-done.12.refs_2_ = f32[5,8,256]{2,1,0:T(8,128)S(1)} collective-permute-done((f32[5,8,256]{2,1,0:T(8,128)S(1)}, f32[5,8,256]{2,1,0:T(8,128)S(1)}, u32[]{:S(2)}, u32[]{:S(2)}) %collective-permute-start.12) | collective-permute-done | bytes 40992 | tf_op jit(solution)/shard_map/ppermute | solution.py:489
  94.8 0.6 copy-done.21
  95.5 1.6 %cell_params.4 = (f32[6,8,256]{2,1,0:T(8,128)}, f32[6,2,256]{2,1,0:T(2,128)}, f32[6,2,256]{2,1,0:T(2,128)}) custom-call(f32[5,8,256]{2,1,0:T(8,128)} %copy-done.12, f32[5,8,256]{2,1,0:T(8,128)} %copy-done.17, f32[5,8,256]{2,1,0:T(8,128)} %copy-done.19, f32[5,8,256]{2,1,0:T(8,128)} %copy-done.21, s32[8,256]{1,0:T(8,128)} %reshape.21.refs_4_, ...), custom_call_target="tpu_custom_call" | custom-call | tf_op jit(solution)/shard_map/cell_params/pallas_call | solution.py:456
  97.0 1.8 %collective-permute-start.14 = (f32[6,2,256]{2,1,0:T(2,128)}, f32[6,2,256]{2,1,0:T(2,128)S(1)}, u32[]{:S(2)}, u32[]{:S(2)}) collective-permute-start(f32[6,2,256]{2,1,0:T(2,128)} %get-tuple-element.42), channel_id=1, source_target_pairs={{0,4},{4,8},{8,12},{1,5},{5,9},{9,13},{2,6},{6,10},{10,14},{3,7},{... | collective-permute-start | bytes 36872 | tf_op jit(solution)/shard_map/ppermute | solution.py:483
  98.8 1.3 collective-permute-start.15
  100.1 0.8 copy-done.9
  100.9 12.9 %inner_relax.3 = (f32[8,16,2,8,512]{4,3,2,1,0:T(8,128)}, f32[4,16,2,8,512]{4,3,2,1,0:T(8,128)S(1)}, f32[5,4,256]{2,1,0:T(4,128)S(1)}) custom-call(f32[2,16,2,8,512]{4,3,2,1,0:T(8,128)} %get-tuple-element.40.refs_0_, f32[4,16,2,8,512]{4,3,2,1,0:T(8,128)} %copy-done.1, f32[2,16,2,8,512]{4,3,2,1,0:T(8,128)S(1)} %get-tuple-element.39.refs_2_, ...), custom_call_target="tpu_custom_call" | custom-call | tf_op jit(solution)/shard_map/inner_relax/pallas_call | solution.py:399
  113.8 9.6 %edge_relax.3 = (f32[2,16,2,8,512]{4,3,2,1,0:T(8,128)S(1)}, f32[2,16,2,8,512]{4,3,2,1,0:T(8,128)S(1)}, f32[5,8,256]{2,1,0:T(8,128)S(1)}) custom-call(f32[2,16,2,8,512]{4,3,2,1,0:T(8,128)} %collective-permute-done.9.refs_0_, f32[2,16,2,8,512]{4,3,2,1,0:T(8,128)} %collective-permute-done.10.refs_1_, f32[6,2,256]{2,1,0:T(2,128)S(1)} %collective-permute-done.14.refs_2_, ...), custom_call_target="tpu_custom_call" | custom-call | tf_op jit(solution)/shard_map/edge_relax/pallas_call | solution.py:426
  123.5 1.0 copy-done.6
  124.5 0.8 collective-permute-start.16
  125.3 1.6 %collective-permute-start.17 = (f32[5,8,256]{2,1,0:T(8,128)S(1)}, f32[5,8,256]{2,1,0:T(8,128)S(1)}, u32[]{:S(2)}, u32[]{:S(2)}) collective-permute-start(f32[5,8,256]{2,1,0:T(8,128)S(1)} %get-tuple-element.51.refs_0_), channel_id=1, source_target_pairs={{0,2},{1,3},{2,0},{3,1},{4,6},{5,7},{6,4},{7,5},{8,10},{9,11},{10,... | collective-permute-start | bytes 122888 | tf_op jit(solution)/shard_map/ppermute | solution.py:489
  126.9 1.4 collective-permute-start.18
  128.3 2.1 %collective-permute-done.16.refs_1_ = f32[5,8,256]{2,1,0:T(8,128)S(1)} collective-permute-done((f32[5,8,256]{2,1,0:T(8,128)S(1)}, f32[5,8,256]{2,1,0:T(8,128)S(1)}, u32[]{:S(2)}, u32[]{:S(2)}) %collective-permute-start.16) | collective-permute-done | bytes 40992 | tf_op jit(solution)/shard_map/ppermute | solution.py:489
  130.4 1.3 collective-permute-done.17.refs_2_
  131.7 0.6 copy-done.18
  132.3 0.6 copy-done.20
  132.9 1.6 %cell_params.5 = (f32[6,8,256]{2,1,0:T(8,128)}, f32[6,2,256]{2,1,0:T(2,128)}, f32[6,2,256]{2,1,0:T(2,128)}) custom-call(f32[5,8,256]{2,1,0:T(8,128)} %copy-done.13, f32[5,8,256]{2,1,0:T(8,128)} %copy-done.16, f32[5,8,256]{2,1,0:T(8,128)} %copy-done.18, f32[5,8,256]{2,1,0:T(8,128)} %copy-done.20, s32[8,256]{1,0:T(8,128)} %reshape.21.refs_4_, ...), custom_call_target="tpu_custom_call" | custom-call | tf_op jit(solution)/shard_map/cell_params/pallas_call | solution.py:456
  134.5 1.2 copy-done.7
  135.7 0.8 copy-done.10
  136.5 5.6 %final_relax.1 = f32[8,16,2,8,512]{4,3,2,1,0:T(8,128)} custom-call(f32[2,16,2,8,512]{4,3,2,1,0:T(8,128)S(1)} %get-tuple-element.48.refs_0_, f32[4,16,2,8,512]{4,3,2,1,0:T(8,128)S(1)} %get-tuple-element.49.refs_1_, f32[2,16,2,8,512]{4,3,2,1,0:T(8,128)S(1)} %copy-done.7, f32[6,8,256]{2,1,0:T(8,128)S(1)} %copy-done.10, ...), custom_call_target="tpu_custom_call" | custom-call | tf_op jit(solution)/shard_map/final_relax/pallas_call | solution.py:467
  (64 shorter events, 1.7 us)
Async XLA Ops:
  0.0 6.6 %copy-start.22 = (s32[512]{0:T(512)S(1)}, s32[512]{0:T(512)}, u32[]{:S(2)}) copy-start(s32[512]{0:T(512)} %param.6) | copy-start | bytes 6148
  2.8 12.8 %collective-permute-start = (f32[2,16,2,8,512]{4,3,2,1,0:T(8,128)}, f32[2,16,2,8,512]{4,3,2,1,0:T(8,128)S(1)}, u32[]{:S(2)}, u32[]{:S(2)}) collective-permute-start(f32[2,16,2,8,512]{4,3,2,1,0:T(8,128)} %get-tuple-element.58), channel_id=1, source_target_pairs={{0,4},{4,8},{8,12},{1,5},{5,9},{9,13},{2,6},{6,10},{10,14},{3,7},{... | collective-permute-start | bytes 3145736 | tf_op jit(solution)/shard_map/ppermute | solution.py:483
  5.3 10.4 %collective-permute-start.1 = (f32[2,16,2,8,512]{4,3,2,1,0:T(8,128)S(1)}, f32[2,16,2,8,512]{4,3,2,1,0:T(8,128)S(1)}, u32[]{:S(2)}, u32[]{:S(2)}) collective-permute-start(f32[2,16,2,8,512]{4,3,2,1,0:T(8,128)S(1)} %get-tuple-element.57), channel_id=1, source_target_pairs={{4,0},{8,4},{12,8},{5,1},{9,5},{13,9},{6,2},{10,6},{14,10},{7,3},{... | collective-permute-start | bytes 3145736 | tf_op jit(solution)/shard_map/ppermute | solution.py:483
  6.8 36.7 %copy-start.14 = (s32[8,16,16]{2,1,0:T(8,128)S(1)}, s32[8,16,16]{2,1,0:T(8,128)}, u32[]{:S(2)}) copy-start(s32[8,16,16]{2,1,0:T(8,128)} %param.7) | copy-start | bytes 24580
  14.3 1.3 copy-start
  15.6 1.0 copy-start.4
  16.6 1.2 copy-start.5
  26.3 20.1 %copy-start.11 = (f32[5,8,256]{2,1,0:T(8,128)}, f32[5,8,256]{2,1,0:T(8,128)S(1)}, u32[]{:S(2)}) copy-start(f32[5,8,256]{2,1,0:T(8,128)S(1)} %get-tuple-element.32.refs_0_) | copy-start | bytes 122884
  26.3 39.8 %collective-permute-start.2 = (f32[2,16,2,8,512]{4,3,2,1,0:T(8,128)S(1)}, f32[2,16,2,8,512]{4,3,2,1,0:T(8,128)S(1)}, u32[]{:S(2)}, u32[]{:S(2)}) collective-permute-start(f32[2,16,2,8,512]{4,3,2,1,0:T(8,128)S(1)} %get-tuple-element.30.refs_2_), channel_id=1, source_target_pairs={{0,4},{4,8},{8,12},{1,5},{5,9},{9,13},{2,6},{6,10},{10,14},{3,7},{... | collective-permute-start | bytes 3145736 | tf_op jit(solution)/shard_map/ppermute | solution.py:483
  36.5 30.6 %collective-permute-start.3 = (f32[2,16,2,8,512]{4,3,2,1,0:T(8,128)S(1)}, f32[2,16,2,8,512]{4,3,2,1,0:T(8,128)}, u32[]{:S(2)}, u32[]{:S(2)}) collective-permute-start(f32[2,16,2,8,512]{4,3,2,1,0:T(8,128)S(1)} %get-tuple-element.31.refs_0_), channel_id=1, source_target_pairs={{4,0},{8,4},{12,8},{5,1},{9,5},{13,9},{6,2},{10,6},{14,10},{7,3},{... | collective-permute-start | bytes 3145736 | tf_op jit(solution)/shard_map/ppermute | solution.py:483
  37.9 6.9 %collective-permute-start.4 = (f32[5,8,256]{2,1,0:T(8,128)S(1)}, f32[5,8,256]{2,1,0:T(8,128)S(1)}, u32[]{:S(2)}, u32[]{:S(2)}) collective-permute-start(f32[5,8,256]{2,1,0:T(8,128)S(1)} %get-tuple-element.32.refs_0_), channel_id=1, source_target_pairs={{0,1},{1,2},{2,3},{3,0},{4,5},{5,6},{6,7},{7,4},{8,9},{9,10},{10,1... | collective-permute-start | bytes 122888 | tf_op jit(solution)/shard_map/ppermute | solution.py:489
  39.5 6.6 %collective-permute-start.5 = (f32[5,8,256]{2,1,0:T(8,128)S(1)}, f32[5,8,256]{2,1,0:T(8,128)}, u32[]{:S(2)}, u32[]{:S(2)}) collective-permute-start(f32[5,8,256]{2,1,0:T(8,128)S(1)} %get-tuple-element.32.refs_0_), channel_id=1, source_target_pairs={{0,2},{1,3},{2,0},{3,1},{4,6},{5,7},{6,4},{7,5},{8,10},{9,11},{10,... | collective-permute-start | bytes 122888 | tf_op jit(solution)/shard_map/ppermute | solution.py:489
  42.1 4.2 %collective-permute-start.6 = (f32[5,8,256]{2,1,0:T(8,128)S(1)}, f32[5,8,256]{2,1,0:T(8,128)}, u32[]{:S(2)}, u32[]{:S(2)}) collective-permute-start(f32[5,8,256]{2,1,0:T(8,128)S(1)} %get-tuple-element.32.refs_0_), channel_id=1, source_target_pairs={{0,3},{1,0},{2,1},{3,2},{4,7},{5,4},{6,5},{7,6},{8,11},{9,8},{10,9... | collective-permute-start | bytes 122888 | tf_op jit(solution)/shard_map/ppermute | solution.py:489
  44.8 1.5 %copy-start.15 = (f32[5,8,256]{2,1,0:T(8,128)}, f32[5,8,256]{2,1,0:T(8,128)S(1)}, u32[]{:S(2)}) copy-start(f32[5,8,256]{2,1,0:T(8,128)S(1)} %collective-permute-done.4.refs_1_) | copy-start | bytes 122884
  47.9 18.2 %collective-permute-start.7 = (f32[6,2,256]{2,1,0:T(2,128)}, f32[6,2,256]{2,1,0:T(2,128)S(1)}, u32[]{:S(2)}, u32[]{:S(2)}) collective-permute-start(f32[6,2,256]{2,1,0:T(2,128)} %get-tuple-element.33), channel_id=1, source_target_pairs={{0,4},{4,8},{8,12},{1,5},{5,9},{9,13},{2,6},{6,10},{10,14},{3,7},{... | collective-permute-start | bytes 36872 | tf_op jit(solution)/shard_map/ppermute | solution.py:483
  49.6 16.5 %collective-permute-start.8 = (f32[6,2,256]{2,1,0:T(2,128)}, f32[6,2,256]{2,1,0:T(2,128)S(1)}, u32[]{:S(2)}, u32[]{:S(2)}) collective-permute-start(f32[6,2,256]{2,1,0:T(2,128)} %get-tuple-element.34), channel_id=1, source_target_pairs={{4,0},{8,4},{12,8},{5,1},{9,5},{13,9},{6,2},{10,6},{14,10},{7,3},{... | collective-permute-start | bytes 36872 | tf_op jit(solution)/shard_map/ppermute | solution.py:483
  51.0 0.8 copy-start.8
  64.7 1.3 copy-start.1
  66.1 1.0 copy-start.2
  67.1 1.2 copy-start.3
  78.5 16.0 %copy-start.12 = (f32[5,8,256]{2,1,0:T(8,128)}, f32[5,8,256]{2,1,0:T(8,128)S(1)}, u32[]{:S(2)}) copy-start(f32[5,8,256]{2,1,0:T(8,128)S(1)} %get-tuple-element.41.refs_0_) | copy-start | bytes 122884
  78.5 35.3 %collective-permute-start.10 = (f32[2,16,2,8,512]{4,3,2,1,0:T(8,128)}, f32[2,16,2,8,512]{4,3,2,1,0:T(8,128)}, u32[]{:S(2)}, u32[]{:S(2)}) collective-permute-start(f32[2,16,2,8,512]{4,3,2,1,0:T(8,128)} %get-tuple-element.40.refs_0_), channel_id=1, source_target_pairs={{4,0},{8,4},{12,8},{5,1},{9,5},{13,9},{6,2},{10,6},{14,10},{7,3},{... | collective-permute-start | bytes 3145736 | tf_op jit(solution)/shard_map/ppermute | solution.py:483
  79.8 34.0 %collective-permute-start.9 = (f32[2,16,2,8,512]{4,3,2,1,0:T(8,128)S(1)}, f32[2,16,2,8,512]{4,3,2,1,0:T(8,128)}, u32[]{:S(2)}, u32[]{:S(2)}) collective-permute-start(f32[2,16,2,8,512]{4,3,2,1,0:T(8,128)S(1)} %get-tuple-element.39.refs_2_), channel_id=1, source_target_pairs={{0,4},{4,8},{8,12},{1,5},{5,9},{9,13},{2,6},{6,10},{10,14},{3,7},{... | collective-permute-start | bytes 3145736 | tf_op jit(solution)/shard_map/ppermute | solution.py:483
  86.3 6.3 %collective-permute-start.11 = (f32[5,8,256]{2,1,0:T(8,128)S(1)}, f32[5,8,256]{2,1,0:T(8,128)S(1)}, u32[]{:S(2)}, u32[]{:S(2)}) collective-permute-start(f32[5,8,256]{2,1,0:T(8,128)S(1)} %get-tuple-element.41.refs_0_), channel_id=1, source_target_pairs={{0,1},{1,2},{2,3},{3,0},{4,5},{5,6},{6,7},{7,4},{8,9},{9,10},{10,1... | collective-permute-start | bytes 122888 | tf_op jit(solution)/shard_map/ppermute | solution.py:489
  86.7 7.5 %collective-permute-start.12 = (f32[5,8,256]{2,1,0:T(8,128)S(1)}, f32[5,8,256]{2,1,0:T(8,128)S(1)}, u32[]{:S(2)}, u32[]{:S(2)}) collective-permute-start(f32[5,8,256]{2,1,0:T(8,128)S(1)} %get-tuple-element.41.refs_0_), channel_id=1, source_target_pairs={{0,2},{1,3},{2,0},{3,1},{4,6},{5,7},{6,4},{7,5},{8,10},{9,11},{10,... | collective-permute-start | bytes 122888 | tf_op jit(solution)/shard_map/ppermute | solution.py:489
  90.1 4.5 %collective-permute-start.13 = (f32[5,8,256]{2,1,0:T(8,128)S(1)}, f32[5,8,256]{2,1,0:T(8,128)S(1)}, u32[]{:S(2)}, u32[]{:S(2)}) collective-permute-start(f32[5,8,256]{2,1,0:T(8,128)S(1)} %get-tuple-element.41.refs_0_), channel_id=1, source_target_pairs={{0,3},{1,0},{2,1},{3,2},{4,7},{5,4},{6,5},{7,6},{8,11},{9,8},{10,9... | collective-permute-start | bytes 122888 | tf_op jit(solution)/shard_map/ppermute | solution.py:489
  92.7 1.8 %copy-start.17 = (f32[5,8,256]{2,1,0:T(8,128)}, f32[5,8,256]{2,1,0:T(8,128)S(1)}, u32[]{:S(2)}) copy-start(f32[5,8,256]{2,1,0:T(8,128)S(1)} %collective-permute-done.11.refs_1_) | copy-start | bytes 122884
  94.2 0.6 copy-start.19
  94.8 0.6 copy-start.21
  97.0 16.8 %collective-permute-start.14 = (f32[6,2,256]{2,1,0:T(2,128)}, f32[6,2,256]{2,1,0:T(2,128)S(1)}, u32[]{:S(2)}, u32[]{:S(2)}) collective-permute-start(f32[6,2,256]{2,1,0:T(2,128)} %get-tuple-element.42), channel_id=1, source_target_pairs={{0,4},{4,8},{8,12},{1,5},{5,9},{9,13},{2,6},{6,10},{10,14},{3,7},{... | collective-permute-start | bytes 36872 | tf_op jit(solution)/shard_map/ppermute | solution.py:483
  98.8 15.0 %collective-permute-start.15 = (f32[6,2,256]{2,1,0:T(2,128)}, f32[6,2,256]{2,1,0:T(2,128)S(1)}, u32[]{:S(2)}, u32[]{:S(2)}) collective-permute-start(f32[6,2,256]{2,1,0:T(2,128)} %get-tuple-element.43), channel_id=1, source_target_pairs={{4,0},{8,4},{12,8},{5,1},{9,5},{13,9},{6,2},{10,6},{14,10},{7,3},{... | collective-permute-start | bytes 36872 | tf_op jit(solution)/shard_map/ppermute | solution.py:483
  100.1 0.8 copy-start.9
  123.5 1.0 copy-start.6
  124.5 7.3 %copy-start.13 = (f32[5,8,256]{2,1,0:T(8,128)}, f32[5,8,256]{2,1,0:T(8,128)S(1)}, u32[]{:S(2)}) copy-start(f32[5,8,256]{2,1,0:T(8,128)S(1)} %get-tuple-element.51.refs_0_) | copy-start | bytes 122884
  124.5 5.9 %collective-permute-start.16 = (f32[5,8,256]{2,1,0:T(8,128)S(1)}, f32[5,8,256]{2,1,0:T(8,128)S(1)}, u32[]{:S(2)}, u32[]{:S(2)}) collective-permute-start(f32[5,8,256]{2,1,0:T(8,128)S(1)} %get-tuple-element.51.refs_0_), channel_id=1, source_target_pairs={{0,1},{1,2},{2,3},{3,0},{4,5},{5,6},{6,7},{7,4},{8,9},{9,10},{10,1... | collective-permute-start | bytes 122888 | tf_op jit(solution)/shard_map/ppermute | solution.py:489
  125.3 6.4 %collective-permute-start.17 = (f32[5,8,256]{2,1,0:T(8,128)S(1)}, f32[5,8,256]{2,1,0:T(8,128)S(1)}, u32[]{:S(2)}, u32[]{:S(2)}) collective-permute-start(f32[5,8,256]{2,1,0:T(8,128)S(1)} %get-tuple-element.51.refs_0_), channel_id=1, source_target_pairs={{0,2},{1,3},{2,0},{3,1},{4,6},{5,7},{6,4},{7,5},{8,10},{9,11},{10,... | collective-permute-start | bytes 122888 | tf_op jit(solution)/shard_map/ppermute | solution.py:489
  126.9 4.8 %collective-permute-start.18 = (f32[5,8,256]{2,1,0:T(8,128)S(1)}, f32[5,8,256]{2,1,0:T(8,128)S(1)}, u32[]{:S(2)}, u32[]{:S(2)}) collective-permute-start(f32[5,8,256]{2,1,0:T(8,128)S(1)} %get-tuple-element.51.refs_0_), channel_id=1, source_target_pairs={{0,3},{1,0},{2,1},{3,2},{4,7},{5,4},{6,5},{7,6},{8,11},{9,8},{10,9... | collective-permute-start | bytes 122888 | tf_op jit(solution)/shard_map/ppermute | solution.py:489
  130.4 1.4 copy-start.16
  131.7 0.6 copy-start.18
  132.3 0.6 copy-start.20
  134.5 1.2 copy-start.7
  135.7 0.8 copy-start.10
where the time goes:
time: 143 us; the launch traced here: 142 us
  Pallas kernels  72 us (50%)
  starting transfers between devices  42.3 us (30%)
  local copies, waits for them, and re-layouts  17.6 us (12%)
  waiting for transfers between devices  9.31 us (7%)
    pallas_call x2, Pallas kernels, inner(): pl.pallas_call(functools.partial(inner_kernel, True, rows), grid=(chunks,...  25.9 us
    ppermute x5, starting transfers between devices, exchange(): lax.ppermute(high, 'gx', forward)  22.6 us
    pallas_call x2, Pallas kernels, edge(): pl.pallas_call(functools.partial(edge_kernel, True, rows), grid=(chunks,)...  19.9 us
    unnamed x46, local copies, waits for them, and re-layouts  13.8 us
    ppermute x9, starting transfers between devices, gather(): parts.append(lax.ppermute(part, 'vert', pairs))  13.2 us
    ppermute x9, waiting for transfers between devices, gather(): parts.append(lax.ppermute(part, 'vert', pairs))  9.28 us
    pallas_call x1, Pallas kernels, edge(): pl.pallas_call(functools.partial(edge_kernel, False, rows), grid=(chunks,...  8.42 us
    pallas_call x1, Pallas kernels, inner(): pl.pallas_call(functools.partial(inner_kernel, False, rows), grid=(chunks...  7.48 us
  transfers between devices with their start and end apart: 19, of which 7 were waited for; matrix products, arithmetic and copies ran while one was open for 1% of the time, Pallas kernels for 26%

commit v1 on v0

--- a/solution.py
+++ b/solution.py
@@ -16,7 +16,7 @@
 FEATURES = 32
 UNIT = 3.0 / 16.0
 LOG2E = 1.4426950408889634
-VMEM_LIMIT = 48 * 1024 * 1024
+VMEM_LIMIT = 14 * 1024 * 1024
 F32 = jnp.float32
 BF16 = jnp.bfloat16
 
@@ -460,6 +460,7 @@
             out_shape=[
                 jax.ShapeDtypeStruct((6, n, cells), F32) for n in (rows, 2, 2)
             ],
+            compiler_params=pltpu.CompilerParams(vmem_limit_bytes=4 * 1024 * 1024),
             name="cell_params",
         )(*parts, codes, knudsen, inflow)
 

time: 143 us -> 128 us (0.90)
  local copies, waits for them, and re-layouts: 17.6 us -> 8.68 us
  Pallas kernels: 72 us -> 67.2 us
    unnamed x46 -> x10, local copies, waits for them, and re-layouts: 13.8 us -> 4.36 us
    pallas_call x3, Pallas kernels: 4.68 us -> 2.51 us  [cell_params(): pl.pallas_call(functools.partial(param_kernel, total, len(parts)), in_spe...]
  transfers between devices with their start and end apart: 19 -> 19, of which waited for: 7 -> 8; matrix products, arithmetic and copies ran while one was open for 1% -> 1% of each run, Pallas kernels for 26% -> 26%
where the time goes in v1:
time: 128 us
  Pallas kernels  67.2 us (52%)
  starting transfers between devices  41 us (32%)
  waiting for transfers between devices  10 us (8%)
  local copies, waits for them, and re-layouts  8.68 us (7%)
    pallas_call x2, Pallas kernels, inner(): pl.pallas_call(functools.partial(inner_kernel, True, rows), grid=(chunks,...  24.8 us
    ppermute x5, starting transfers between devices, exchange(): lax.ppermute(high, 'gx', forward)  21.2 us
    pallas_call x2, Pallas kernels, edge(): pl.pallas_call(functools.partial(edge_kernel, True, rows), grid=(chunks,)...  18.6 us
    ppermute x9, starting transfers between devices, gather(): parts.append(lax.ppermute(part, 'vert', pairs))  13.3 us
    ppermute x9, waiting for transfers between devices, gather(): parts.append(lax.ppermute(part, 'vert', pairs))  9.98 us
    pallas_call x1, Pallas kernels, edge(): pl.pallas_call(functools.partial(edge_kernel, False, rows), grid=(chunks,...  8.87 us
    pallas_call x1, Pallas kernels, inner(): pl.pallas_call(functools.partial(inner_kernel, False, rows), grid=(chunks...  6.79 us
    ppermute x5, starting transfers between devices, exchange(): lax.ppermute(low, 'gx', backward)  6.45 us
  transfers between devices with their start and end apart: 19, of which 8 were waited for; matrix products, arithmetic and copies ran while one was open for 1% of the time, Pallas kernels for 26%

profile of v1, /device:TPU:0, one launch (start us, length us, event | category | flops | bytes accessed | tf_op | source)
XLA Modules:
  0.0 127.9 jit_solution(16452590523272390743)
XLA Ops:
  0.0 3.2 %slice_bitcast_fusion = (f32[2,16,2,8,512]{4,3,2,1,0:T(8,128)}, f32[2,16,2,8,512]{4,3,2,1,0:T(8,128)}) fusion(f32[8,16,16,512]{3,2,1,0:T(8,128)} %param.5), kind=kLoop, calls=%fused_computation | loop fusion | bytes 4194304 | tf_op jit(solution)/shard_map/slice | solution.py:493
  3.2 2.4 %collective-permute-start = (f32[2,16,2,8,512]{4,3,2,1,0:T(8,128)}, f32[2,16,2,8,512]{4,3,2,1,0:T(8,128)S(1)}, u32[]{:S(2)}, u32[]{:S(2)}) collective-permute-start(f32[2,16,2,8,512]{4,3,2,1,0:T(8,128)} %get-tuple-element.58), channel_id=1, source_target_pairs={{0,4},{4,8},{8,12},{1,5},{5,9},{9,13},{2,6},{6,10},{10,14},{3,7},{... | collective-permute-start | bytes 3145736 | tf_op jit(solution)/shard_map/ppermute | solution.py:484
  5.6 1.3 %collective-permute-start.1 = (f32[2,16,2,8,512]{4,3,2,1,0:T(8,128)}, f32[2,16,2,8,512]{4,3,2,1,0:T(8,128)}, u32[]{:S(2)}, u32[]{:S(2)}) collective-permute-start(f32[2,16,2,8,512]{4,3,2,1,0:T(8,128)} %get-tuple-element.57), channel_id=1, source_target_pairs={{4,0},{8,4},{12,8},{5,1},{9,5},{13,9},{6,2},{10,6},{14,10},{7,3},{... | collective-permute-start | bytes 3145736 | tf_op jit(solution)/shard_map/ppermute | solution.py:484
  7.0 0.1 stack.57
  7.1 0.0 copy-start
  7.1 2.2 %copy-done = f32[8,16,16,512]{3,2,1,0:T(8,128)S(1)} copy-done((f32[8,16,16,512]{3,2,1,0:T(8,128)S(1)}, f32[8,16,16,512]{3,2,1,0:T(8,128)}, u32[]{:S(2)}) %copy-start) | copy-done | bytes 4194328
  9.3 6.8 %inner_first.1 = (f32[4,16,2,8,512]{4,3,2,1,0:T(8,128)S(1)}, f32[5,4,256]{2,1,0:T(4,128)S(1)}) custom-call(f32[8,16,2,8,512]{4,3,2,1,0:T(8,128)S(1)} %bitcast.27, f32[9,8,512]{2,1,0:T(8,128)S(1)} %broadcast_in_dim.31.refs_1_.refs_3_.refs_5_.refs_6_, bf16[16,512]{1,0:T(8,128)(2,1)S(1)} %pad.10.refs_2_.refs_4_.refs_6_.refs_7_), custom_call_target="tpu_custom_call" | custom-call | tf_op jit(solution)/shard_map/inner_first/pallas_call | solution.py:409
  16.1 0.0 copy-start.3
  16.1 0.0 collective-permute-done.refs_0_
  16.1 0.9 copy-done.1
  17.1 1.2 copy-done.2
  18.3 8.9 %edge_first.1 = (f32[2,16,2,8,512]{4,3,2,1,0:T(8,128)S(1)}, f32[2,16,2,8,512]{4,3,2,1,0:T(8,128)}, f32[5,8,256]{2,1,0:T(8,128)S(1)}) custom-call(f32[2,16,2,8,512]{4,3,2,1,0:T(8,128)S(1)} %copy-done.2, f32[2,16,2,8,512]{4,3,2,1,0:T(8,128)} %collective-permute-done.1.refs_1_, f32[8,16,2,8,512]{4,3,2,1,0:T(8,128)S(1)} %bitcast.28, ...), custom_call_target="tpu_custom_call" | custom-call | tf_op jit(solution)/shard_map/edge_first/pallas_call | solution.py:441
  27.2 10.3 %collective-permute-start.2 = (f32[2,16,2,8,512]{4,3,2,1,0:T(8,128)}, f32[2,16,2,8,512]{4,3,2,1,0:T(8,128)}, u32[]{:S(2)}, u32[]{:S(2)}) collective-permute-start(f32[2,16,2,8,512]{4,3,2,1,0:T(8,128)} %get-tuple-element.30.refs_2_), channel_id=1, source_target_pairs={{0,4},{4,8},{8,12},{1,5},{5,9},{9,13},{2,6},{6,10},{10,14},{3,7},{... | collective-permute-start | bytes 3145736 | tf_op jit(solution)/shard_map/ppermute | solution.py:484
  37.5 1.3 %collective-permute-start.3 = (f32[2,16,2,8,512]{4,3,2,1,0:T(8,128)S(1)}, f32[2,16,2,8,512]{4,3,2,1,0:T(8,128)}, u32[]{:S(2)}, u32[]{:S(2)}) collective-permute-start(f32[2,16,2,8,512]{4,3,2,1,0:T(8,128)S(1)} %get-tuple-element.31.refs_0_), channel_id=1, source_target_pairs={{4,0},{8,4},{12,8},{5,1},{9,5},{13,9},{6,2},{10,6},{14,10},{7,3},{... | collective-permute-start | bytes 3145736 | tf_op jit(solution)/shard_map/ppermute | solution.py:484
  38.9 1.6 %collective-permute-start.4 = (f32[5,8,256]{2,1,0:T(8,128)S(1)}, f32[5,8,256]{2,1,0:T(8,128)S(1)}, u32[]{:S(2)}, u32[]{:S(2)}) collective-permute-start(f32[5,8,256]{2,1,0:T(8,128)S(1)} %get-tuple-element.32.refs_0_), channel_id=1, source_target_pairs={{0,1},{1,2},{2,3},{3,0},{4,5},{5,6},{6,7},{7,4},{8,9},{9,10},{10,1... | collective-permute-start | bytes 122888 | tf_op jit(solution)/shard_map/ppermute | solution.py:490
  40.5 2.6 %collective-permute-start.5 = (f32[5,8,256]{2,1,0:T(8,128)S(1)}, f32[5,8,256]{2,1,0:T(8,128)S(1)}, u32[]{:S(2)}, u32[]{:S(2)}) collective-permute-start(f32[5,8,256]{2,1,0:T(8,128)S(1)} %get-tuple-element.32.refs_0_), channel_id=1, source_target_pairs={{0,2},{1,3},{2,0},{3,1},{4,6},{5,7},{6,4},{7,5},{8,10},{9,11},{10,... | collective-permute-start | bytes 122888 | tf_op jit(solution)/shard_map/ppermute | solution.py:490
  43.1 1.3 %collective-permute-start.6 = (f32[5,8,256]{2,1,0:T(8,128)S(1)}, f32[5,8,256]{2,1,0:T(8,128)S(1)}, u32[]{:S(2)}, u32[]{:S(2)}) collective-permute-start(f32[5,8,256]{2,1,0:T(8,128)S(1)} %get-tuple-element.32.refs_0_), channel_id=1, source_target_pairs={{0,3},{1,0},{2,1},{3,2},{4,7},{5,4},{6,5},{7,6},{8,11},{9,8},{10,9... | collective-permute-start | bytes 122888 | tf_op jit(solution)/shard_map/ppermute | solution.py:490
  44.5 0.9 reshape.21.refs_4_
  46.0 1.0 collective-permute-done.5.refs_2_
  47.0 0.2 collective-permute-done.6.refs_3_
  47.2 0.6 cell_params.3
  47.9 1.7 %collective-permute-start.7 = (f32[6,2,256]{2,1,0:T(2,128)S(1)}, f32[6,2,256]{2,1,0:T(2,128)S(1)}, u32[]{:S(2)}, u32[]{:S(2)}) collective-permute-start(f32[6,2,256]{2,1,0:T(2,128)S(1)} %get-tuple-element.33), channel_id=1, source_target_pairs={{0,4},{4,8},{8,12},{1,5},{5,9},{9,13},{2,6},{6,10},{10,14},{3,7},{... | collective-permute-start | bytes 36872 | tf_op jit(solution)/shard_map/ppermute | solution.py:484
  49.6 1.3 %collective-permute-start.8 = (f32[6,2,256]{2,1,0:T(2,128)S(1)}, f32[6,2,256]{2,1,0:T(2,128)S(1)}, u32[]{:S(2)}, u32[]{:S(2)}) collective-permute-start(f32[6,2,256]{2,1,0:T(2,128)S(1)} %get-tuple-element.34), channel_id=1, source_target_pairs={{4,0},{8,4},{12,8},{5,1},{9,5},{13,9},{6,2},{10,6},{14,10},{7,3},{... | collective-permute-start | bytes 36872 | tf_op jit(solution)/shard_map/ppermute | solution.py:484
  50.9 0.1 iota.7
  51.0 12.7 %inner_relax.2 = (f32[8,16,2,8,512]{4,3,2,1,0:T(8,128)S(1)}, f32[4,16,2,8,512]{4,3,2,1,0:T(8,128)S(1)}, f32[5,4,256]{2,1,0:T(4,128)S(1)}) custom-call(f32[2,16,2,8,512]{4,3,2,1,0:T(8,128)S(1)} %get-tuple-element.31.refs_0_, f32[4,16,2,8,512]{4,3,2,1,0:T(8,128)S(1)} %get-tuple-element.35.refs_1_, f32[2,16,2,8,512]{4,3,2,1,0:T(8,128)} %get-tuple-element.30.refs_2_, ...), custom_call_target="tpu_custom_call" | custom-call | tf_op jit(solution)/shard_map/inner_relax/pallas_call | solution.py:399
  63.7 0.0 collective-permute-done.7.refs_2_
  63.7 9.5 %edge_relax.2 = (f32[2,16,2,8,512]{4,3,2,1,0:T(8,128)S(1)}, f32[2,16,2,8,512]{4,3,2,1,0:T(8,128)S(1)}, f32[5,8,256]{2,1,0:T(8,128)S(1)}) custom-call(f32[2,16,2,8,512]{4,3,2,1,0:T(8,128)} %collective-permute-done.2.refs_0_, f32[2,16,2,8,512]{4,3,2,1,0:T(8,128)} %collective-permute-done.3.refs_1_, f32[6,2,256]{2,1,0:T(2,128)S(1)} %collective-permute-done.7.refs_2_, ...), custom_call_target="tpu_custom_call" | custom-call | tf_op jit(solution)/shard_map/edge_relax/pallas_call | solution.py:426
  73.3 1.3 %collective-permute-start.10 = (f32[2,16,2,8,512]{4,3,2,1,0:T(8,128)S(1)}, f32[2,16,2,8,512]{4,3,2,1,0:T(8,128)S(1)}, u32[]{:S(2)}, u32[]{:S(2)}) collective-permute-start(f32[2,16,2,8,512]{4,3,2,1,0:T(8,128)S(1)} %get-tuple-element.40.refs_0_), channel_id=1, source_target_pairs={{4,0},{8,4},{12,8},{5,1},{9,5},{13,9},{6,2},{10,6},{14,10},{7,3},{... | collective-permute-start | bytes 3145736 | tf_op jit(solution)/shard_map/ppermute | solution.py:484
  74.6 4.7 %collective-permute-start.9 = (f32[2,16,2,8,512]{4,3,2,1,0:T(8,128)S(1)}, f32[2,16,2,8,512]{4,3,2,1,0:T(8,128)S(1)}, u32[]{:S(2)}, u32[]{:S(2)}) collective-permute-start(f32[2,16,2,8,512]{4,3,2,1,0:T(8,128)S(1)} %get-tuple-element.39.refs_2_), channel_id=1, source_target_pairs={{0,4},{4,8},{8,12},{1,5},{5,9},{9,13},{2,6},{6,10},{10,14},{3,7},{... | collective-permute-start | bytes 3145736 | tf_op jit(solution)/shard_map/ppermute | solution.py:484
  79.3 0.5 collective-permute-start.11
  79.8 3.3 %collective-permute-start.12 = (f32[5,8,256]{2,1,0:T(8,128)S(1)}, f32[5,8,256]{2,1,0:T(8,128)S(1)}, u32[]{:S(2)}, u32[]{:S(2)}) collective-permute-start(f32[5,8,256]{2,1,0:T(8,128)S(1)} %get-tuple-element.41.refs_0_), channel_id=1, source_target_pairs={{0,2},{1,3},{2,0},{3,1},{4,6},{5,7},{6,4},{7,5},{8,10},{9,11},{10,... | collective-permute-start | bytes 122888 | tf_op jit(solution)/shard_map/ppermute | solution.py:490
  83.1 0.1 collective-permute-start.13
  83.2 2.1 %collective-permute-done.11.refs_1_ = f32[5,8,256]{2,1,0:T(8,128)S(1)} collective-permute-done((f32[5,8,256]{2,1,0:T(8,128)S(1)}, f32[5,8,256]{2,1,0:T(8,128)S(1)}, u32[]{:S(2)}, u32[]{:S(2)}) %collective-permute-start.11) | collective-permute-done | bytes 40992 | tf_op jit(solution)/shard_map/ppermute | solution.py:490
  85.3 1.9 %collective-permute-done.12.refs_2_ = f32[5,8,256]{2,1,0:T(8,128)S(1)} collective-permute-done((f32[5,8,256]{2,1,0:T(8,128)S(1)}, f32[5,8,256]{2,1,0:T(8,128)S(1)}, u32[]{:S(2)}, u32[]{:S(2)}) %collective-permute-start.12) | collective-permute-done | bytes 40992 | tf_op jit(solution)/shard_map/ppermute | solution.py:490
  87.1 0.7 collective-permute-done.13.refs_3_
  87.8 0.6 cell_params.4
  88.5 2.0 %collective-permute-start.14 = (f32[6,2,256]{2,1,0:T(2,128)S(1)}, f32[6,2,256]{2,1,0:T(2,128)S(1)}, u32[]{:S(2)}, u32[]{:S(2)}) collective-permute-start(f32[6,2,256]{2,1,0:T(2,128)S(1)} %get-tuple-element.42), channel_id=1, source_target_pairs={{0,4},{4,8},{8,12},{1,5},{5,9},{9,13},{2,6},{6,10},{10,14},{3,7},{... | collective-permute-start | bytes 36872 | tf_op jit(solution)/shard_map/ppermute | solution.py:484
  90.5 1.3 %collective-permute-start.15 = (f32[6,2,256]{2,1,0:T(2,128)S(1)}, f32[6,2,256]{2,1,0:T(2,128)S(1)}, u32[]{:S(2)}, u32[]{:S(2)}) collective-permute-start(f32[6,2,256]{2,1,0:T(2,128)S(1)} %get-tuple-element.43), channel_id=1, source_target_pairs={{4,0},{8,4},{12,8},{5,1},{9,5},{13,9},{6,2},{10,6},{14,10},{7,3},{... | collective-permute-start | bytes 36872 | tf_op jit(solution)/shard_map/ppermute | solution.py:484
  91.8 12.1 %inner_relax.3 = (f32[8,16,2,8,512]{4,3,2,1,0:T(8,128)S(1)}, f32[4,16,2,8,512]{4,3,2,1,0:T(8,128)S(1)}, f32[5,4,256]{2,1,0:T(4,128)S(1)}) custom-call(f32[2,16,2,8,512]{4,3,2,1,0:T(8,128)S(1)} %get-tuple-element.40.refs_0_, f32[4,16,2,8,512]{4,3,2,1,0:T(8,128)S(1)} %get-tuple-element.44.refs_1_, f32[2,16,2,8,512]{4,3,2,1,0:T(8,128)S(1)} %get-tuple-element.39.refs_2_, ...), custom_call_target="tpu_custom_call" | custom-call | tf_op jit(solution)/shard_map/inner_relax/pallas_call | solution.py:399
  103.9 9.1 %edge_relax.3 = (f32[2,16,2,8,512]{4,3,2,1,0:T(8,128)S(1)}, f32[2,16,2,8,512]{4,3,2,1,0:T(8,128)S(1)}, f32[5,8,256]{2,1,0:T(8,128)S(1)}) custom-call(f32[2,16,2,8,512]{4,3,2,1,0:T(8,128)S(1)} %collective-permute-done.9.refs_0_, f32[2,16,2,8,512]{4,3,2,1,0:T(8,128)S(1)} %collective-permute-done.10.refs_1_, f32[6,2,256]{2,1,0:T(2,128)S(1)} %collective-permute-done.14.refs_2_, ...), custom_call_target="tpu_custom_call" | custom-call | tf_op jit(solution)/shard_map/edge_relax/pallas_call | solution.py:426
  113.0 0.7 collective-permute-start.16
  113.7 2.1 %collective-permute-start.17 = (f32[5,8,256]{2,1,0:T(8,128)S(1)}, f32[5,8,256]{2,1,0:T(8,128)S(1)}, u32[]{:S(2)}, u32[]{:S(2)}) collective-permute-start(f32[5,8,256]{2,1,0:T(8,128)S(1)} %get-tuple-element.51.refs_0_), channel_id=1, source_target_pairs={{0,2},{1,3},{2,0},{3,1},{4,6},{5,7},{6,4},{7,5},{8,10},{9,11},{10,... | collective-permute-start | bytes 122888 | tf_op jit(solution)/shard_map/ppermute | solution.py:490
  115.8 1.1 collective-permute-start.18
  116.9 2.1 %collective-permute-done.16.refs_1_ = f32[5,8,256]{2,1,0:T(8,128)S(1)} collective-permute-done((f32[5,8,256]{2,1,0:T(8,128)S(1)}, f32[5,8,256]{2,1,0:T(8,128)S(1)}, u32[]{:S(2)}, u32[]{:S(2)}) %collective-permute-start.16) | collective-permute-done | bytes 40992 | tf_op jit(solution)/shard_map/ppermute | solution.py:490
  118.9 1.1 collective-permute-done.17.refs_2_
  120.0 1.0 collective-permute-done.18.refs_3_
  121.0 1.2 cell_params.5
  122.2 5.6 %final_relax.1 = f32[8,16,2,8,512]{4,3,2,1,0:T(8,128)} custom-call(f32[2,16,2,8,512]{4,3,2,1,0:T(8,128)S(1)} %get-tuple-element.48.refs_0_, f32[4,16,2,8,512]{4,3,2,1,0:T(8,128)S(1)} %get-tuple-element.49.refs_1_, f32[2,16,2,8,512]{4,3,2,1,0:T(8,128)S(1)} %get-tuple-element.50.refs_2_, f32[6,8,256]{2,1,0:T(8,128)S(1)} %get-tuple-element.52.refs_3_, ...), custom_call_target="tpu_custom_call" | custom-call | tf_op jit(solution)/shard_map/final_relax/pallas_call | solution.py:468
  (28 shorter events, 0.2 us)
Async XLA Ops:
  0.0 6.9 %copy-start.4 = (s32[512]{0:T(512)S(1)}, s32[512]{0:T(512)}, u32[]{:S(2)}) copy-start(s32[512]{0:T(512)} %param.6) | copy-start | bytes 6148
  3.2 13.0 %collective-permute-start = (f32[2,16,2,8,512]{4,3,2,1,0:T(8,128)}, f32[2,16,2,8,512]{4,3,2,1,0:T(8,128)S(1)}, u32[]{:S(2)}, u32[]{:S(2)}) collective-permute-start(f32[2,16,2,8,512]{4,3,2,1,0:T(8,128)} %get-tuple-element.58), channel_id=1, source_target_pairs={{0,4},{4,8},{8,12},{1,5},{5,9},{9,13},{2,6},{6,10},{10,14},{3,7},{... | collective-permute-start | bytes 3145736 | tf_op jit(solution)/shard_map/ppermute | solution.py:484
  5.6 11.5 %collective-permute-start.1 = (f32[2,16,2,8,512]{4,3,2,1,0:T(8,128)}, f32[2,16,2,8,512]{4,3,2,1,0:T(8,128)}, u32[]{:S(2)}, u32[]{:S(2)}) collective-permute-start(f32[2,16,2,8,512]{4,3,2,1,0:T(8,128)} %get-tuple-element.57), channel_id=1, source_target_pairs={{4,0},{8,4},{12,8},{5,1},{9,5},{13,9},{6,2},{10,6},{14,10},{7,3},{... | collective-permute-start | bytes 3145736 | tf_op jit(solution)/shard_map/ppermute | solution.py:484
  7.1 2.2 %copy-start = (f32[8,16,16,512]{3,2,1,0:T(8,128)S(1)}, f32[8,16,16,512]{3,2,1,0:T(8,128)}, u32[]{:S(2)}) copy-start(f32[8,16,16,512]{3,2,1,0:T(8,128)} %param.5) | copy-start | bytes 12582916
  16.1 31.1 %copy-start.3 = (f32[4]{0:T(128)S(1)}, f32[4]{0:T(128)}, u32[]{:S(2)}) copy-start(f32[4]{0:T(128)} %refs_6_.5) | copy-start | bytes 52
  16.1 1.0 copy-start.1
  17.1 1.2 copy-start.2
  27.2 36.5 %collective-permute-start.2 = (f32[2,16,2,8,512]{4,3,2,1,0:T(8,128)}, f32[2,16,2,8,512]{4,3,2,1,0:T(8,128)}, u32[]{:S(2)}, u32[]{:S(2)}) collective-permute-start(f32[2,16,2,8,512]{4,3,2,1,0:T(8,128)} %get-tuple-element.30.refs_2_), channel_id=1, source_target_pairs={{0,4},{4,8},{8,12},{1,5},{5,9},{9,13},{2,6},{6,10},{10,14},{3,7},{... | collective-permute-start | bytes 3145736 | tf_op jit(solution)/shard_map/ppermute | solution.py:484
  37.5 26.2 %collective-permute-start.3 = (f32[2,16,2,8,512]{4,3,2,1,0:T(8,128)S(1)}, f32[2,16,2,8,512]{4,3,2,1,0:T(8,128)}, u32[]{:S(2)}, u32[]{:S(2)}) collective-permute-start(f32[2,16,2,8,512]{4,3,2,1,0:T(8,128)S(1)} %get-tuple-element.31.refs_0_), channel_id=1, source_target_pairs={{4,0},{8,4},{12,8},{5,1},{9,5},{13,9},{6,2},{10,6},{14,10},{7,3},{... | collective-permute-start | bytes 3145736 | tf_op jit(solution)/shard_map/ppermute | solution.py:484
  38.9 7.2 %collective-permute-start.4 = (f32[5,8,256]{2,1,0:T(8,128)S(1)}, f32[5,8,256]{2,1,0:T(8,128)S(1)}, u32[]{:S(2)}, u32[]{:S(2)}) collective-permute-start(f32[5,8,256]{2,1,0:T(8,128)S(1)} %get-tuple-element.32.refs_0_), channel_id=1, source_target_pairs={{0,1},{1,2},{2,3},{3,0},{4,5},{5,6},{6,7},{7,4},{8,9},{9,10},{10,1... | collective-permute-start | bytes 122888 | tf_op jit(solution)/shard_map/ppermute | solution.py:490
  40.5 6.5 %collective-permute-start.5 = (f32[5,8,256]{2,1,0:T(8,128)S(1)}, f32[5,8,256]{2,1,0:T(8,128)S(1)}, u32[]{:S(2)}, u32[]{:S(2)}) collective-permute-start(f32[5,8,256]{2,1,0:T(8,128)S(1)} %get-tuple-element.32.refs_0_), channel_id=1, source_target_pairs={{0,2},{1,3},{2,0},{3,1},{4,6},{5,7},{6,4},{7,5},{8,10},{9,11},{10,... | collective-permute-start | bytes 122888 | tf_op jit(solution)/shard_map/ppermute | solution.py:490
  43.1 4.1 %collective-permute-start.6 = (f32[5,8,256]{2,1,0:T(8,128)S(1)}, f32[5,8,256]{2,1,0:T(8,128)S(1)}, u32[]{:S(2)}, u32[]{:S(2)}) collective-permute-start(f32[5,8,256]{2,1,0:T(8,128)S(1)} %get-tuple-element.32.refs_0_), channel_id=1, source_target_pairs={{0,3},{1,0},{2,1},{3,2},{4,7},{5,4},{6,5},{7,6},{8,11},{9,8},{10,9... | collective-permute-start | bytes 122888 | tf_op jit(solution)/shard_map/ppermute | solution.py:490
  47.9 15.8 %collective-permute-start.7 = (f32[6,2,256]{2,1,0:T(2,128)S(1)}, f32[6,2,256]{2,1,0:T(2,128)S(1)}, u32[]{:S(2)}, u32[]{:S(2)}) collective-permute-start(f32[6,2,256]{2,1,0:T(2,128)S(1)} %get-tuple-element.33), channel_id=1, source_target_pairs={{0,4},{4,8},{8,12},{1,5},{5,9},{9,13},{2,6},{6,10},{10,14},{3,7},{... | collective-permute-start | bytes 36872 | tf_op jit(solution)/shard_map/ppermute | solution.py:484
  49.6 14.1 %collective-permute-start.8 = (f32[6,2,256]{2,1,0:T(2,128)S(1)}, f32[6,2,256]{2,1,0:T(2,128)S(1)}, u32[]{:S(2)}, u32[]{:S(2)}) collective-permute-start(f32[6,2,256]{2,1,0:T(2,128)S(1)} %get-tuple-element.34), channel_id=1, source_target_pairs={{4,0},{8,4},{12,8},{5,1},{9,5},{13,9},{6,2},{10,6},{14,10},{7,3},{... | collective-permute-start | bytes 36872 | tf_op jit(solution)/shard_map/ppermute | solution.py:484
  73.3 30.6 %collective-permute-start.10 = (f32[2,16,2,8,512]{4,3,2,1,0:T(8,128)S(1)}, f32[2,16,2,8,512]{4,3,2,1,0:T(8,128)S(1)}, u32[]{:S(2)}, u32[]{:S(2)}) collective-permute-start(f32[2,16,2,8,512]{4,3,2,1,0:T(8,128)S(1)} %get-tuple-element.40.refs_0_), channel_id=1, source_target_pairs={{4,0},{8,4},{12,8},{5,1},{9,5},{13,9},{6,2},{10,6},{14,10},{7,3},{... | collective-permute-start | bytes 3145736 | tf_op jit(solution)/shard_map/ppermute | solution.py:484
  74.6 29.3 %collective-permute-start.9 = (f32[2,16,2,8,512]{4,3,2,1,0:T(8,128)S(1)}, f32[2,16,2,8,512]{4,3,2,1,0:T(8,128)S(1)}, u32[]{:S(2)}, u32[]{:S(2)}) collective-permute-start(f32[2,16,2,8,512]{4,3,2,1,0:T(8,128)S(1)} %get-tuple-element.39.refs_2_), channel_id=1, source_target_pairs={{0,4},{4,8},{8,12},{1,5},{5,9},{9,13},{2,6},{6,10},{10,14},{3,7},{... | collective-permute-start | bytes 3145736 | tf_op jit(solution)/shard_map/ppermute | solution.py:484
  79.3 6.0 %collective-permute-start.11 = (f32[5,8,256]{2,1,0:T(8,128)S(1)}, f32[5,8,256]{2,1,0:T(8,128)S(1)}, u32[]{:S(2)}, u32[]{:S(2)}) collective-permute-start(f32[5,8,256]{2,1,0:T(8,128)S(1)} %get-tuple-element.41.refs_0_), channel_id=1, source_target_pairs={{0,1},{1,2},{2,3},{3,0},{4,5},{5,6},{6,7},{7,4},{8,9},{9,10},{10,1... | collective-permute-start | bytes 122888 | tf_op jit(solution)/shard_map/ppermute | solution.py:490
  79.8 7.3 %collective-permute-start.12 = (f32[5,8,256]{2,1,0:T(8,128)S(1)}, f32[5,8,256]{2,1,0:T(8,128)S(1)}, u32[]{:S(2)}, u32[]{:S(2)}) collective-permute-start(f32[5,8,256]{2,1,0:T(8,128)S(1)} %get-tuple-element.41.refs_0_), channel_id=1, source_target_pairs={{0,2},{1,3},{2,0},{3,1},{4,6},{5,7},{6,4},{7,5},{8,10},{9,11},{10,... | collective-permute-start | bytes 122888 | tf_op jit(solution)/shard_map/ppermute | solution.py:490
  83.1 4.8 %collective-permute-start.13 = (f32[5,8,256]{2,1,0:T(8,128)S(1)}, f32[5,8,256]{2,1,0:T(8,128)S(1)}, u32[]{:S(2)}, u32[]{:S(2)}) collective-permute-start(f32[5,8,256]{2,1,0:T(8,128)S(1)} %get-tuple-element.41.refs_0_), channel_id=1, source_target_pairs={{0,3},{1,0},{2,1},{3,2},{4,7},{5,4},{6,5},{7,6},{8,11},{9,8},{10,9... | collective-permute-start | bytes 122888 | tf_op jit(solution)/shard_map/ppermute | solution.py:490
  88.5 15.4 %collective-permute-start.14 = (f32[6,2,256]{2,1,0:T(2,128)S(1)}, f32[6,2,256]{2,1,0:T(2,128)S(1)}, u32[]{:S(2)}, u32[]{:S(2)}) collective-permute-start(f32[6,2,256]{2,1,0:T(2,128)S(1)} %get-tuple-element.42), channel_id=1, source_target_pairs={{0,4},{4,8},{8,12},{1,5},{5,9},{9,13},{2,6},{6,10},{10,14},{3,7},{... | collective-permute-start | bytes 36872 | tf_op jit(solution)/shard_map/ppermute | solution.py:484
  90.5 13.4 %collective-permute-start.15 = (f32[6,2,256]{2,1,0:T(2,128)S(1)}, f32[6,2,256]{2,1,0:T(2,128)S(1)}, u32[]{:S(2)}, u32[]{:S(2)}) collective-permute-start(f32[6,2,256]{2,1,0:T(2,128)S(1)} %get-tuple-element.43), channel_id=1, source_target_pairs={{4,0},{8,4},{12,8},{5,1},{9,5},{13,9},{6,2},{10,6},{14,10},{7,3},{... | collective-permute-start | bytes 36872 | tf_op jit(solution)/shard_map/ppermute | solution.py:484
  113.0 6.0 %collective-permute-start.16 = (f32[5,8,256]{2,1,0:T(8,128)S(1)}, f32[5,8,256]{2,1,0:T(8,128)S(1)}, u32[]{:S(2)}, u32[]{:S(2)}) collective-permute-start(f32[5,8,256]{2,1,0:T(8,128)S(1)} %get-tuple-element.51.refs_0_), channel_id=1, source_target_pairs={{0,1},{1,2},{2,3},{3,0},{4,5},{5,6},{6,7},{7,4},{8,9},{9,10},{10,1... | collective-permute-start | bytes 122888 | tf_op jit(solution)/shard_map/ppermute | solution.py:490
  113.7 6.4 %collective-permute-start.17 = (f32[5,8,256]{2,1,0:T(8,128)S(1)}, f32[5,8,256]{2,1,0:T(8,128)S(1)}, u32[]{:S(2)}, u32[]{:S(2)}) collective-permute-start(f32[5,8,256]{2,1,0:T(8,128)S(1)} %get-tuple-element.51.refs_0_), channel_id=1, source_target_pairs={{0,2},{1,3},{2,0},{3,1},{4,6},{5,7},{6,4},{7,5},{8,10},{9,11},{10,... | collective-permute-start | bytes 122888 | tf_op jit(solution)/shard_map/ppermute | solution.py:490
  115.8 5.2 %collective-permute-start.18 = (f32[5,8,256]{2,1,0:T(8,128)S(1)}, f32[5,8,256]{2,1,0:T(8,128)S(1)}, u32[]{:S(2)}, u32[]{:S(2)}) collective-permute-start(f32[5,8,256]{2,1,0:T(8,128)S(1)} %get-tuple-element.51.refs_0_), channel_id=1, source_target_pairs={{0,3},{1,0},{2,1},{3,2},{4,7},{5,4},{6,5},{7,6},{8,11},{9,8},{10,9... | collective-permute-start | bytes 122888 | tf_op jit(solution)/shard_map/ppermute | solution.py:490

commit v2 on v0

v2 whole, which is shorter than its diff:
```python
import functools

import jax
import jax.numpy as jnp
from jax import lax
from jax.experimental import pallas as pl
from jax.experimental.pallas import tpu as pltpu
from jax.sharding import PartitionSpec as P

VGX = 16
VGY = 16
VGZ = 8
STEPS = 3
LANES = 128
SUB = 8
FEATURES = 32
PAIR = 2 * LANES
UNIT = 3.0 / 16.0
LOG2E = 1.4426950408889634
LIMIT_MIB = 10
F32 = jnp.float32
BF16 = jnp.bfloat16


def minmod(lower, upper):
    return jnp.maximum(
        jnp.minimum(lower, upper), jnp.minimum(jnp.maximum(lower, upper), 0.0)
    )


def lanes_of(chunk):
    return pl.ds(pl.multiple_of(chunk * LANES, LANES), LANES)


def coefs_of(coef_ref, lanes):
    return [coef_ref[k, :, lanes] for k in range(9)]


def x_row(cells, rows, store, coef):
    reach, lean, ahead = coef[0], coef[1], coef[2] > 0.0
    first, last = rows[0], rows[-1]
    steps = {n: cells[n + 1] - cells[n] for n in range(first - 2, last + 2)}
    faces = {
        n: cells[n] + lean * minmod(steps[n - 1], steps[n])
        for n in range(first - 1, last + 2)
    }
    for n in rows:
        source = jnp.where(ahead, faces[n - 1], faces[n + 1])
        store(n, cells[n] - reach * (faces[n] - source))


def yz_row(source, out, row, lanes, coef, ring, face_ring):
    reach_y, lean_y, ahead_y = coef[3], coef[4], coef[5] > 0.0
    reach_z, lean_z, ahead_z = coef[6], coef[7], coef[8] > 0.0
    count = 16
    cells, steps, faces, z_faces = {}, {}, {}, {}

    def cell(y, t):
        y %= count
        if (y, t) not in cells:
            cells[y, t] = source[row, y, t, :, lanes]
        return cells[y, t]

    def step(y, t):
        y %= count
        if (y, t) not in steps:
            steps[y, t] = cell(y + 1, t) - cell(y, t)
        return steps[y, t]

    def face(y, t):
        y %= count
        if (y, t) not in faces:
            faces[y, t] = cell(y, t) + lean_y * minmod(step(y - 1, t), step(y, t))
        return faces[y, t]

    def lay(y):
        for t in range(2):
            ring[y, 8 + 8 * t : 16 + 8 * t, :] = cell(y, t)
        ring[y, 7:8, :] = source[row, y, 1, 7:8, lanes]
        ring[y, 24:25, :] = source[row, y, 0, 0:1, lanes]

    def lay_faces(y):
        for t in range(2):
            below = ring[y, 7 + 8 * t : 15 + 8 * t, :]
            above = ring[y, 9 + 8 * t : 17 + 8 * t, :]
            here = cell(y, t)
            z_faces[y, t] = here + lean_z * minmod(here - below, above - here)
            face_ring[y, 8 + 8 * t : 16 + 8 * t, :] = z_faces[y, t]
        face_ring[y, 7:8, :] = face_ring[y, 23:24, :]
        face_ring[y, 24:25, :] = face_ring[y, 8:9, :]

    def finish(y):
        for t in range(2):
            below = face_ring[y, 7 + 8 * t : 15 + 8 * t, :]
            above = face_ring[y, 9 + 8 * t : 17 + 8 * t, :]
            v = out[row, y, t, :, lanes]
            v -= reach_z * (z_faces[y, t] - jnp.where(ahead_z, below, above))
            upwind = jnp.where(ahead_y, face(y - 1, t), face(y + 1, t))
            v -= reach_y * (face(y, t) - upwind)
            out[row, y, t, :, lanes] = v

    for y in range(count + 2):
        if y < count:
            lay(y)
        if 0 <= y - 1 < count:
            lay_faces(y - 1)
        if 0 <= y - 2 < count:
            finish(y - 2)


def row_moments(block, weights):
    flat = block.reshape(256, LANES)
    high = flat.astype(BF16)
    rest = (flat - high.astype(F32)).astype(BF16)
    contract = (((1,), (1,)), ((), ()))
    total = lax.dot_general(weights, high, contract, preferred_element_type=F32)
    total += lax.dot_general(weights, rest, contract, preferred_element_type=F32)
    return total[:SUB]


def write_moments(out, place, value):
    for m in range(4):
        out[m, pl.ds(place, 1), :] = value[m : m + 1]
    out[4, pl.ds(place, 1), :] = value[4:5] + value[5:6]


def yz_rows(chunks, groups, coef_ref, weights, acc, ring, face_ring):
    for source, out, rows, place in groups:

        def one(i, carry, source=source, out=out, rows=rows, place=place):
            chunk, row = i // rows, i % rows
            lanes = lanes_of(chunk)
            yz_row(source, out, row, lanes, coefs_of(coef_ref, lanes), ring, face_ring)
            part = row_moments(out[row, :, :, :, lanes], weights[:, lanes])
            acc[place + row] = acc[place + row] + part
            return carry

        lax.fori_loop(0, chunks * rows, one, 0)


def three_parts(value):
    high = value.astype(BF16).astype(F32)
    rest = value - high
    middle = rest.astype(BF16).astype(F32)
    low = (rest - middle).astype(BF16).astype(F32)
    return high, middle, low


def spread_features(params, wide, tall, rows):
    alpha, beta_x, beta_y, beta_z, gamma, keep = params
    alpha = jnp.where(gamma == 0.0, -10000.0, alpha)
    zero = jnp.zeros_like(alpha)
    columns = []
    for value in (alpha, beta_x, beta_y, beta_z, gamma, gamma, keep):
        columns.extend(three_parts(value))
    columns.extend([zero] * (FEATURES - len(columns)))
    for k, value in enumerate(columns):
        for r in range(rows):
            wide[r, k : k + 1, :] = value[r : r + 1]
    for r in range(rows):
        tall[r] = wide[r].T.astype(BF16)


def relax_rows(source, out, tall, first, rows, table, factor, kept):
    width = source.shape[-1]

    def one(row, carry):
        features = tall[first + row]
        keep = jnp.dot(features, factor[...], preferred_element_type=F32)
        kept[...] = keep.reshape(16, 2, SUB, LANES)
        for pair in range(width // PAIR):
            power = jnp.dot(
                features, table[:, pair * PAIR : (pair + 1) * PAIR], preferred_element_type=F32
            )
            for half in range(2):
                lanes = pl.ds(pair * PAIR + half * LANES, LANES)
                shape = jnp.exp2(power[:, half * LANES : (half + 1) * LANES])
                shape = shape.reshape(16, 2, SUB, LANES)
                out[row, :, :, :, lanes] = kept[...] * source[row, :, :, :, lanes] + shape
        return carry

    lax.fori_loop(0, rows, one, 0)


def param_kernel(total, count, *refs):
    parts = refs[:count]
    codes, knudsen, inflow, out, out_low, out_high = refs[count:]
    sums = [parts[0][m] for m in range(5)]
    for part in parts[1:]:
        sums = [s + part[m] for m, s in enumerate(sums)]
    density = sums[0] * (1.0 / total)
    scale = UNIT / sums[0]
    u_x, u_y, u_z = (sums[m] * scale for m in (1, 2, 3))
    heat = (UNIT * sums[4] * scale - (u_x * u_x + u_y * u_y + u_z * u_z)) * (1.0 / 3.0)
    rate = 0.5 * density / (density + knudsen[0])
    code = codes[...]
    flowing, wall = code == 1, code == 2
    closed = flowing | wall
    u_x = jnp.where(flowing, inflow[1], jnp.where(wall, 0.0, u_x))
    u_y = jnp.where(closed, 0.0, u_y)
    u_z = jnp.where(closed, 0.0, u_z)
    heat = jnp.where(flowing, inflow[2], jnp.where(wall, inflow[3], heat))
    amount = jnp.where(flowing, inflow[0], jnp.where(wall, density, rate * density))
    keep = jnp.where(closed, 0.0, 1.0 - rate)
    g = (-0.5 * LOG2E) / heat

    def line(u, n, unit):
        s = None
        for i in range(n):
            gap = (i + 0.5 - n / 2) * unit - u
            e = jnp.exp2(g * (gap * gap))
            s = e if s is None else s + e
        return s

    norm = line(u_x, VGX, 6.0 / VGX) * line(u_y, VGY, 6.0 / VGY)
    norm = norm * line(u_z, VGZ, 6.0 / VGZ) * (1.0 / total)
    alpha = (jnp.log(amount) - jnp.log(norm)) * LOG2E
    alpha = alpha + g * (u_x * u_x + u_y * u_y + u_z * u_z)
    lean = (-2.0 * UNIT) * g
    params = (alpha, lean * u_x, lean * u_y, lean * u_z, g * (UNIT * UNIT), keep)
    rows = code.shape[0]
    for k, value in enumerate(params):
        out[k] = value
        out_low[k] = value[:2]
        out_high[k] = value[rows - 2 :]


def load_kernel(flags, state, cross, middle, inside, sems):
    rows = state.shape[0]
    copies = []
    for r in range(rows):
        place = jnp.where(flags[0] > 0, rows - 1 - r, r)
        if r < 2:
            target = cross.at[r]
        elif r < rows - 2:
            target = middle.at[r - 2]
        else:
            target = inside.at[r - rows + 2]
        copies.append(pltpu.make_async_copy(state.at[place], target, sems.at[r]))
    for copy in copies:
        copy.start()
    for copy in copies:
        copy.wait()


def inner_kernel(relax, rows, *refs):
    if relax:
        (m_cross, m_mid, m_in, params, table, factor, coef_ref, weights,
         cross, middle, inside, out, sums, wide, tall, kept, acc, ring, face_ring) = refs
        spread_features([params[k] for k in range(6)], wide, tall, rows)
        relax_rows(m_cross, cross, tall, 0, 2, table, factor, kept)
        relax_rows(m_mid, middle, tall, 2, rows - 4, table, factor, kept)
        relax_rows(m_in, inside, tall, rows - 2, 2, table, factor, kept)
    else:
        (cross, middle, inside, coef_ref, weights, out, sums, acc, ring, face_ring) = refs
    chunks = middle.shape[-1] // LANES
    inner = rows - 4
    acc[...] = jnp.zeros_like(acc)

    def along_x(i, carry):
        chunk, y = i // 16, i % 16
        lanes = lanes_of(chunk)
        coef = coefs_of(coef_ref, lanes)
        for t in range(2):
            cells = {}
            for n in range(rows):
                if n < 2:
                    cells[n] = cross[n, y, t, :, lanes]
                elif n < rows - 2:
                    cells[n] = middle[n - 2, y, t, :, lanes]
                else:
                    cells[n] = inside[n - rows + 2, y, t, :, lanes]

            def store(n, v, t=t):
                out[n - 2, y, t, :, lanes] = v

            x_row(cells, list(range(2, rows - 2)), store, coef)
        return carry

    lax.fori_loop(0, chunks * 16, along_x, 0, unroll=2)
    yz_rows(chunks, [(middle, out, inner, 0)], coef_ref, weights, acc, ring, face_ring)
    for r in range(inner):
        write_moments(sums, r, acc[r])


def edge_kernel(relax, rows, *refs):
    if relax:
        (flags, h_cross, h_in, p_cross, p_in, table, factor, cross, middle, inside, coef_ref,
         weights, inner_sums, out_cross, out_in, sums,
         wide, tall, kept, low, high, acc, ring, face_ring) = refs
        spread_features([p_cross[k] for k in range(6)], wide, tall, 2)
        relax_rows(h_cross, low, tall, 0, 2, table, factor, kept)
        spread_features([p_in[k] for k in range(6)], wide, tall, 2)
        relax_rows(h_in, high, tall, 0, 2, table, factor, kept)
    else:
        (flags, low, high, cross, middle, inside, coef_ref, weights, inner_sums,
         out_cross, out_in, sums, acc, ring, face_ring) = refs
    chunks = middle.shape[-1] // LANES
    acc[...] = jnp.zeros_like(acc)
    present = jnp.where(flags[1] > 0, 1.0, 0.0)

    def along_x(i, carry):
        chunk, y = i // 16, i % 16
        lanes = lanes_of(chunk)
        coef = coefs_of(coef_ref, lanes)
        for t in range(2):
            cells = {}
            for n in range(2):
                cells[-1 - n] = low[n, y, t, :, lanes] * present
                cells[n] = cross[n, y, t, :, lanes]
                cells[2 + n] = middle[n, y, t, :, lanes]

            def store(n, v, t=t):
                out_cross[n, y, t, :, lanes] = v

            x_row(cells, [0, 1], store, coef)
            cells = {}
            for n in range(2):
                cells[rows - 4 + n] = middle[rows - 6 + n, y, t, :, lanes]
                cells[rows - 2 + n] = inside[n, y, t, :, lanes]
                cells[rows + n] = high[1 - n, y, t, :, lanes]

            def store_in(n, v, t=t):
                out_in[n - rows + 2, y, t, :, lanes] = v

            x_row(cells, [rows - 2, rows - 1], store_in, coef)
        return carry

    lax.fori_loop(0, chunks * 16, along_x, 0)
    groups = [(cross, out_cross, 2, 0), (inside, out_in, 2, 2)]
    yz_rows(chunks, groups, coef_ref, weights, acc, ring, face_ring)
    for m in range(5):
        sums[m, 2 : rows - 2, :] = inner_sums[m]
    for r in range(2):
        write_moments(sums, r, acc[r])
        write_moments(sums, rows - 2 + r, acc[2 + r])


def final_kernel(rows, flags, m_cross, m_mid, m_in, params, table, factor, out,
                 wide, tall, kept, cross, middle, inside, sems):
    spread_features([params[k] for k in range(6)], wide, tall, rows)
    copies = []
    for source, target, first, count in (
        (m_cross, cross, 0, 2), (m_mid, middle, 2, rows - 4), (m_in, inside, rows - 2, 2)
    ):
        relax_rows(source, target, tall, first, count, table, factor, kept)
        for n in range(count):
            r = first + n
            place = jnp.where(flags[0] > 0, rows - 1 - r, r)
            copy = pltpu.make_async_copy(target.at[n], out.at[place], sems.at[r])
            copy.start()
            copies.append(copy)
    for copy in copies:
        copy.wait()


def body(distribution, velocity_order, cell_codes, knudsen, inflow):
    rows, count_y, count_z, width = distribution.shape
    peers = lax.axis_size("vert")
    line = lax.axis_size("gx")
    total = width * peers
    cells = count_y * count_z
    state = distribution.reshape(rows, count_y, 2, SUB, width)

    place = lax.axis_index("gx")
    mirrored = place % 2
    present = jnp.where((place == 0) | (place == line - 1), 0, 1)
    flags = jnp.stack([mirrored, present]).astype(jnp.int32)
    codes = cell_codes.reshape(rows, cells)
    codes = jnp.where(mirrored > 0, codes[::-1], codes)

    plane = VGY * VGZ
    n_x = 2 * (velocity_order // plane) - (VGX - 1)
    n_y = 2 * (velocity_order // VGZ % VGY) - (VGY - 1)
    n_z = 2 * (2 * (velocity_order % VGZ) - (VGZ - 1))
    square = n_x * n_x + n_y * n_y + n_z * n_z
    ones = jnp.ones_like(n_x)
    low_part = square % 8
    whole = jnp.stack([ones, n_x, n_y, n_z, square - low_part, low_part]).astype(F32)
    weights = jnp.pad(whole, ((0, 10), (0, 0))).astype(BF16)
    table = jnp.repeat(whole, 3, axis=0)
    table = jnp.pad(table, ((0, FEATURES - 18), (0, 0))).astype(BF16)
    slot = lax.broadcasted_iota(jnp.int32, (FEATURES, LANES), 0)
    factor = jnp.where((slot >= 18) & (slot < 21), 1.0, 0.0).astype(BF16)
    coef = []
    for n, scale in ((jnp.where(mirrored > 0, -n_x, n_x), 0.1), (n_y, 1.0 / 30.0), (n_z, 1.0 / 30.0)):
        reach = jnp.abs(n.astype(F32) * UNIT * scale)
        sign = jnp.where(n > 0, 1.0, -1.0)
        coef.extend([reach, 0.5 * sign * (1.0 - reach), sign])
    coef = jnp.broadcast_to(jnp.stack(coef)[:, None, :], (9, SUB, width))

    vmem = pl.BlockSpec(memory_space=pltpu.VMEM)
    smem = pl.BlockSpec(memory_space=pltpu.SMEM)
    hbm = pl.BlockSpec(memory_space=pl.ANY)

    def slab(n):
        return jax.ShapeDtypeStruct((n, count_y, 2, SUB, width), F32)

    def slab_scratch(n):
        return pltpu.VMEM((n, count_y, 2, SUB, width), F32)

    def feature_scratch(n):
        return [
            pltpu.VMEM((n, FEATURES, cells), F32),
            pltpu.VMEM((n, cells, FEATURES), BF16),
            pltpu.VMEM((count_y, 2, SUB, LANES), F32),
        ]

    def ring_scratch(n):
        return [pltpu.VMEM((n, SUB, cells), F32)] + [pltpu.VMEM((count_y, 32, LANES), F32)] * 2

    def limits(mib):
        return pltpu.CompilerParams(vmem_limit_bytes=mib * 1024 * 1024)

    def load():
        return pl.pallas_call(
            load_kernel,
            in_specs=[smem, hbm],
            out_specs=[vmem] * 3,
            out_shape=[slab(2), slab(rows - 4), slab(2)],
            scratch_shapes=[pltpu.SemaphoreType.DMA((rows,))],
            compiler_params=limits(6),
            name="load_rows",
        )(flags, state)

    def inner(relax, state, params):
        out_shape = [slab(rows - 4), jax.ShapeDtypeStruct((5, rows - 4, cells), F32)]
        scratch = ring_scratch(rows - 4)
        if relax:
            out_shape = [slab(2), slab(rows - 4), slab(2)] + out_shape
            scratch = feature_scratch(rows) + scratch
            args = (*state, params, table, factor, coef, weights)
        else:
            args = (*state, coef, weights)
        return pl.pallas_call(
            functools.partial(inner_kernel, relax, rows),
            in_specs=[vmem] * len(args),
            out_specs=[vmem] * len(out_shape),
            out_shape=out_shape,
            scratch_shapes=scratch,
            compiler_params=limits(LIMIT_MIB),
            name="inner_relax" if relax else "inner_first",
        )(*args)

    def edge(relax, halos, params, state, sums):
        scratch = ring_scratch(4)
        if relax:
            scratch = feature_scratch(2) + [slab_scratch(2)] * 2 + scratch
            args = (*halos, *params, table, factor, *state, coef, weights, sums)
        else:
            args = (*halos, *state, coef, weights, sums)
        return pl.pallas_call(
            functools.partial(edge_kernel, relax, rows),
            in_specs=[smem] + [vmem] * len(args),
            out_specs=[vmem] * 3,
            out_shape=[slab(2), slab(2), jax.ShapeDtypeStruct((5, rows, cells), F32)],
            scratch_shapes=scratch,
            compiler_params=limits(LIMIT_MIB),
            name="edge_relax" if relax else "edge_first",
        )(flags, *args)

    def cell_params(parts):
        return pl.pallas_call(
            functools.partial(param_kernel, total, len(parts)),
            in_specs=[vmem] * (len(parts) + 1) + [smem, smem],
            out_specs=[vmem] * 3,
            out_shape=[jax.ShapeDtypeStruct((6, n, cells), F32) for n in (rows, 2, 2)],
            compiler_params=limits(4),
            name="cell_params",
        )(*parts, codes, knudsen, inflow)

    def final(moved, params):
        return pl.pallas_call(
            functools.partial(final_kernel, rows),
            in_specs=[smem] + [vmem] * 6,
            out_specs=hbm,
            out_shape=slab(rows),
            scratch_shapes=feature_scratch(rows)
            + [slab_scratch(2), slab_scratch(rows - 4), slab_scratch(2)]
            + [pltpu.SemaphoreType.DMA((rows,))],
            compiler_params=limits(LIMIT_MIB),
            name="final_relax",
        )(flags, *moved, params, table, factor)

    across = [(0, 0), (line - 1, line - 1)]
    for i in range(1, line - 1, 2):
        across += [(i, i + 1), (i + 1, i)]
    within = []
    for i in range(0, line, 2):
        within += [(i, i + 1), (i + 1, i)]

    def exchange(cross, inside):
        return lax.ppermute(cross, "gx", across), lax.ppermute(inside, "gx", within)

    def gather(part):
        parts = [part]
        for shift in range(1, peers):
            pairs = [(i, (i + shift) % peers) for i in range(peers)]
            parts.append(lax.ppermute(part, "vert", pairs))
        return parts

    cross, middle, inside = load()
    halos = exchange(cross, inside)
    m_mid, sums = inner(False, (cross, middle, inside), None)
    m_cross, m_in, sums = edge(False, halos, None, (cross, middle, inside), sums)
    for _ in range(1, STEPS):
        halos = exchange(m_cross, m_in)
        params, p_cross, p_in = cell_params(gather(sums))
        p_halos = exchange(p_cross, p_in)
        moved = (m_cross, m_mid, m_in)
        cross, middle, inside, m_mid, sums = inner(True, moved, params)
        m_cross, m_in, sums = edge(True, halos, p_halos, (cross, middle, inside), sums)
    params, _, _ = cell_params(gather(sums))
    result = final((m_cross, m_mid, m_in), params)
    return result.reshape(rows, count_y, count_z, width)


def solution(mesh):
    placed = (
        P(("groups", "gx"), None, None, "vert"),
        P("vert"),
        P(("groups", "gx"), None, None),
        P("groups"),
        P("groups"),
    )
    return jax.shard_map(
        body,
        mesh=mesh,
        in_specs=placed,
        out_specs=P(("groups", "gx"), None, None, "vert"),
        check_vma=False,
    )
```

time: 143 us -> 111 us (0.78)
  local copies, waits for them, and re-layouts: 17.6 us -> 5.49 us
  Pallas kernels: 72 us -> 61.9 us
  starting transfers between devices: 42.3 us -> 33.4 us
    ppermute x10, starting transfers between devices: 29.1 us -> 19.9 us  [the longest x5 14.4 us: exchange(): lax.ppermute(inside, 'gx', within)]
    unnamed x46 -> x12, local copies, waits for them, and re-layouts: 13.8 us -> 5.11 us
    pallas_call x7 -> x8, Pallas kernels: 67.3 us -> 59.4 us  [the longest x3 28 us: edge(): pl.pallas_call(functools.partial(edge_kernel, relax, rows), in_specs=[sme...]
    slice x1 -> x0, local copies, waits for them, and re-layouts: 2.83 us -> none  [body(): halos = exchange(state[:2], state[rows - 2:])]
    pallas_call x3, Pallas kernels: 4.68 us -> 2.51 us  [cell_params(): pl.pallas_call(functools.partial(param_kernel, total, len(parts)), in_spe...]
  transfers between devices with their start and end apart: 19 -> 19, of which waited for: 7 -> 8; matrix products, arithmetic and copies ran while one was open for 1% -> 0% of each run, Pallas kernels for 26% -> 24%
where the time goes in v2:
time: 111 us
  Pallas kernels  61.9 us (56%)
  starting transfers between devices  33.4 us (30%)
  waiting for transfers between devices  9.27 us (8%)
  local copies, waits for them, and re-layouts  5.49 us (5%)
    pallas_call x3, Pallas kernels, edge(): pl.pallas_call(functools.partial(edge_kernel, relax, rows), in_specs=[sme...  28 us
    pallas_call x3, Pallas kernels, inner(): pl.pallas_call(functools.partial(inner_kernel, relax, rows), in_specs=[vm...  25.6 us
    ppermute x5, starting transfers between devices, exchange(): lax.ppermute(inside, 'gx', within)  14.4 us
    ppermute x9, starting transfers between devices, gather(): parts.append(lax.ppermute(part, 'vert', pairs))  13.4 us
    ppermute x9, waiting for transfers between devices, gather(): parts.append(lax.ppermute(part, 'vert', pairs))  9.24 us
    ppermute x5, starting transfers between devices, exchange(): lax.ppermute(cross, 'gx', across)  5.54 us
    unnamed x12, local copies, waits for them, and re-layouts  5.11 us
    pallas_call x1, Pallas kernels, final(): pl.pallas_call(functools.partial(final_kernel, rows), in_specs=[smem] + [...  3.89 us
  transfers between devices with their start and end apart: 19, of which 8 were waited for; matrix products, arithmetic and copies ran while one was open for 0% of the time, Pallas kernels for 24%

profile of v2, /device:TPU:0, one launch (start us, length us, event | category | flops | bytes accessed | tf_op | source)
XLA Modules:
  0.0 111.1 jit_solution(17888338883280871221)
XLA Ops:
  0.0 0.1 pad_add_fusion.flags.refs_0_
  0.1 2.2 %copy-done = f32[8,16,16,512]{3,2,1,0:T(8,128)S(1)} copy-done((f32[8,16,16,512]{3,2,1,0:T(8,128)S(1)}, f32[8,16,16,512]{3,2,1,0:T(8,128)}, u32[]{:S(2)}) %copy-start) | copy-done | bytes 4194328
  2.3 1.9 %load_rows.1 = (f32[2,16,2,8,512]{4,3,2,1,0:T(8,128)S(1)}, f32[4,16,2,8,512]{4,3,2,1,0:T(8,128)S(1)}, f32[2,16,2,8,512]{4,3,2,1,0:T(8,128)}) custom-call(s32[2]{0:T(128)S(1)} %pad_add_fusion.flags.refs_0_, f32[8,16,2,8,512]{4,3,2,1,0:T(8,128)S(1)} %bitcast.18), custom_call_target="tpu_custom_call" | custom-call | tf_op jit(solution)/shard_map/load_rows/pallas_call | solution.py:416
  4.2 1.6 %collective-permute-start = (f32[2,16,2,8,512]{4,3,2,1,0:T(8,128)S(1)}, f32[2,16,2,8,512]{4,3,2,1,0:T(8,128)}, u32[]{:S(2)}, u32[]{:S(2)}) collective-permute-start(f32[2,16,2,8,512]{4,3,2,1,0:T(8,128)S(1)} %get-tuple-element.36.refs_0_.refs_3_), channel_id=1, source_target_pairs={{0,0},{12,12},{4,8},{8,4},{1,1},{13,13},{5,9},{9,5},{2,2},{14,14},... | collective-permute-start | bytes 3145736 | tf_op jit(solution)/shard_map/ppermute | solution.py:493
  5.8 3.4 %collective-permute-start.1 = (f32[2,16,2,8,512]{4,3,2,1,0:T(8,128)}, f32[2,16,2,8,512]{4,3,2,1,0:T(8,128)}, u32[]{:S(2)}, u32[]{:S(2)}) collective-permute-start(f32[2,16,2,8,512]{4,3,2,1,0:T(8,128)} %get-tuple-element.37.refs_2_.refs_5_), channel_id=1, source_target_pairs={{0,4},{4,0},{8,12},{12,8},{1,5},{5,1},{9,13},{13,9},{2,6},{6,2},{1... | collective-permute-start | bytes 3145736 | tf_op jit(solution)/shard_map/ppermute | solution.py:493
  9.4 0.1 stack.69
  9.4 7.5 %inner_first.1 = (f32[4,16,2,8,512]{4,3,2,1,0:T(8,128)S(1)}, f32[5,4,256]{2,1,0:T(4,128)S(1)}) custom-call(f32[2,16,2,8,512]{4,3,2,1,0:T(8,128)S(1)} %get-tuple-element.36.refs_0_.refs_3_, f32[4,16,2,8,512]{4,3,2,1,0:T(8,128)S(1)} %get-tuple-element.38.refs_1_.refs_4_, f32[2,16,2,8,512]{4,3,2,1,0:T(8,128)} %get-tuple-element.37.refs_2_.refs_5_, ...), custom_call_target="tpu_custom_call" | custom-call | tf_op jit(solution)/shard_map/inner_first/pallas_call | solution.py:435
  16.9 0.0 copy-start.1
  16.9 1.3 %copy-done.1 = f32[4,16,2,8,512]{4,3,2,1,0:T(8,128)} copy-done((f32[4,16,2,8,512]{4,3,2,1,0:T(8,128)}, f32[4,16,2,8,512]{4,3,2,1,0:T(8,128)S(1)}, u32[]{:S(2)}) %copy-start.1) | copy-done | bytes 2097176
  18.3 0.0 copy-start.3
  18.3 10.2 %edge_first.1 = (f32[2,16,2,8,512]{4,3,2,1,0:T(8,128)}, f32[2,16,2,8,512]{4,3,2,1,0:T(8,128)}, f32[5,8,256]{2,1,0:T(8,128)S(1)}) custom-call(s32[2]{0:T(128)S(1)} %pad_add_fusion.flags.refs_0_, f32[2,16,2,8,512]{4,3,2,1,0:T(8,128)} %collective-permute-done.refs_1_, f32[2,16,2,8,512]{4,3,2,1,0:T(8,128)} %collective-permute-done.1.refs_2_, ...), custom_call_target="tpu_custom_call" | custom-call | tf_op jit(solution)/shard_map/edge_first/pallas_call | solution.py:452
  28.4 1.9 %collective-permute-start.2 = (f32[2,16,2,8,512]{4,3,2,1,0:T(8,128)}, f32[2,16,2,8,512]{4,3,2,1,0:T(8,128)S(1)}, u32[]{:S(2)}, u32[]{:S(2)}) collective-permute-start(f32[2,16,2,8,512]{4,3,2,1,0:T(8,128)} %get-tuple-element.40.refs_0_), channel_id=1, source_target_pairs={{0,0},{12,12},{4,8},{8,4},{1,1},{13,13},{5,9},{9,5},{2,2},{14,14},... | collective-permute-start | bytes 3145736 | tf_op jit(solution)/shard_map/ppermute | solution.py:493
  30.3 5.3 %collective-permute-start.3 = (f32[2,16,2,8,512]{4,3,2,1,0:T(8,128)}, f32[2,16,2,8,512]{4,3,2,1,0:T(8,128)S(1)}, u32[]{:S(2)}, u32[]{:S(2)}) collective-permute-start(f32[2,16,2,8,512]{4,3,2,1,0:T(8,128)} %get-tuple-element.41.refs_2_), channel_id=1, source_target_pairs={{0,4},{4,0},{8,12},{12,8},{1,5},{5,1},{9,13},{13,9},{2,6},{6,2},{1... | collective-permute-start | bytes 3145736 | tf_op jit(solution)/shard_map/ppermute | solution.py:493
  35.6 0.1 reshape.15
  35.7 0.1 rev.3
  35.7 1.6 %collective-permute-start.4 = (f32[5,8,256]{2,1,0:T(8,128)S(1)}, f32[5,8,256]{2,1,0:T(8,128)S(1)}, u32[]{:S(2)}, u32[]{:S(2)}) collective-permute-start(f32[5,8,256]{2,1,0:T(8,128)S(1)} %get-tuple-element.42.refs_0_), channel_id=1, source_target_pairs={{0,1},{1,2},{2,3},{3,0},{4,5},{5,6},{6,7},{7,4},{8,9},{9,10},{10,1... | collective-permute-start | bytes 122888 | tf_op jit(solution)/shard_map/ppermute | solution.py:499
  37.4 2.6 %collective-permute-start.5 = (f32[5,8,256]{2,1,0:T(8,128)S(1)}, f32[5,8,256]{2,1,0:T(8,128)S(1)}, u32[]{:S(2)}, u32[]{:S(2)}) collective-permute-start(f32[5,8,256]{2,1,0:T(8,128)S(1)} %get-tuple-element.42.refs_0_), channel_id=1, source_target_pairs={{0,2},{1,3},{2,0},{3,1},{4,6},{5,7},{6,4},{7,5},{8,10},{9,11},{10,... | collective-permute-start | bytes 122888 | tf_op jit(solution)/shard_map/ppermute | solution.py:499
  40.0 1.3 %collective-permute-start.6 = (f32[5,8,256]{2,1,0:T(8,128)S(1)}, f32[5,8,256]{2,1,0:T(8,128)S(1)}, u32[]{:S(2)}, u32[]{:S(2)}) collective-permute-start(f32[5,8,256]{2,1,0:T(8,128)S(1)} %get-tuple-element.42.refs_0_), channel_id=1, source_target_pairs={{0,3},{1,0},{2,1},{3,2},{4,7},{5,4},{6,5},{7,6},{8,11},{9,8},{10,9... | collective-permute-start | bytes 122888 | tf_op jit(solution)/shard_map/ppermute | solution.py:499
  42.0 1.0 collective-permute-done.5.refs_2_
  42.9 1.0 collective-permute-done.6.refs_3_
  44.0 0.6 cell_params.3
  44.6 0.7 collective-permute-start.7
  45.3 1.4 %collective-permute-start.8 = (f32[6,2,256]{2,1,0:T(2,128)S(1)}, f32[6,2,256]{2,1,0:T(2,128)S(1)}, u32[]{:S(2)}, u32[]{:S(2)}) collective-permute-start(f32[6,2,256]{2,1,0:T(2,128)S(1)} %get-tuple-element.44), channel_id=1, source_target_pairs={{0,4},{4,0},{8,12},{12,8},{1,5},{5,1},{9,13},{13,9},{2,6},{6,2},{1... | collective-permute-start | bytes 36872 | tf_op jit(solution)/shard_map/ppermute | solution.py:493
  46.7 0.1 iota.23.refs_5_.refs_6_.factor
  46.8 1.6 %copy-done.2 = f32[4,16,2,8,512]{4,3,2,1,0:T(8,128)S(1)} copy-done((f32[4,16,2,8,512]{4,3,2,1,0:T(8,128)S(1)}, f32[4,16,2,8,512]{4,3,2,1,0:T(8,128)}, u32[]{:S(2)}) %copy-start.2) | copy-done | bytes 2097176
  48.4 9.8 %inner_relax.2 = (f32[2,16,2,8,512]{4,3,2,1,0:T(8,128)S(1)}, f32[4,16,2,8,512]{4,3,2,1,0:T(8,128)S(1)}, f32[2,16,2,8,512]{4,3,2,1,0:T(8,128)S(1)}, f32[4,16,2,8,512]{4,3,2,1,0:T(8,128)S(1)}, f32[5,4,256]{2,1,0:T(4,128)S(1)}) custom-call(f32[2,16,2,8,512]{4,3,2,1,0:T(8,128)} %get-tuple-element.40.refs_0_, f32[4,16,2,8,512]{4,3,2,1,0:T(8,128)S(1)} %copy-done.2, ...), custom_call_target="tpu_custom_call" | custom-call | tf_op jit(solution)/shard_map/inner_relax/pallas_call | solution.py:435
  58.3 8.9 %edge_relax.2 = (f32[2,16,2,8,512]{4,3,2,1,0:T(8,128)S(1)}, f32[2,16,2,8,512]{4,3,2,1,0:T(8,128)S(1)}, f32[5,8,256]{2,1,0:T(8,128)S(1)}) custom-call(s32[2]{0:T(128)S(1)} %pad_add_fusion.flags.refs_0_, f32[2,16,2,8,512]{4,3,2,1,0:T(8,128)S(1)} %collective-permute-done.2.refs_1_, f32[2,16,2,8,512]{4,3,2,1,0:T(8,128)S(1)} %collective-permute-done.3.refs_2_, ...), custom_call_target="tpu_custom_call" | custom-call | tf_op jit(solution)/shard_map/edge_relax/pallas_call | solution.py:452
  67.2 0.1 collective-permute-start.10
  67.3 0.7 collective-permute-start.9
  68.0 0.9 collective-permute-start.11
  68.9 2.9 %collective-permute-start.12 = (f32[5,8,256]{2,1,0:T(8,128)S(1)}, f32[5,8,256]{2,1,0:T(8,128)S(1)}, u32[]{:S(2)}, u32[]{:S(2)}) collective-permute-start(f32[5,8,256]{2,1,0:T(8,128)S(1)} %get-tuple-element.53.refs_0_), channel_id=1, source_target_pairs={{0,2},{1,3},{2,0},{3,1},{4,6},{5,7},{6,4},{7,5},{8,10},{9,11},{10,... | collective-permute-start | bytes 122888 | tf_op jit(solution)/shard_map/ppermute | solution.py:499
  71.7 0.2 collective-permute-start.13
  72.0 2.0 %collective-permute-done.11.refs_1_ = f32[5,8,256]{2,1,0:T(8,128)S(1)} collective-permute-done((f32[5,8,256]{2,1,0:T(8,128)S(1)}, f32[5,8,256]{2,1,0:T(8,128)S(1)}, u32[]{:S(2)}, u32[]{:S(2)}) %collective-permute-start.11) | collective-permute-done | bytes 40992 | tf_op jit(solution)/shard_map/ppermute | solution.py:499
  74.0 1.1 collective-permute-done.12.refs_2_
  75.0 1.2 %collective-permute-done.13.refs_3_ = f32[5,8,256]{2,1,0:T(8,128)S(1)} collective-permute-done((f32[5,8,256]{2,1,0:T(8,128)S(1)}, f32[5,8,256]{2,1,0:T(8,128)S(1)}, u32[]{:S(2)}, u32[]{:S(2)}) %collective-permute-start.13) | collective-permute-done | bytes 40992 | tf_op jit(solution)/shard_map/ppermute | solution.py:499
  76.2 0.6 cell_params.4
  76.8 0.7 collective-permute-start.14
  77.5 4.3 %collective-permute-start.15 = (f32[6,2,256]{2,1,0:T(2,128)S(1)}, f32[6,2,256]{2,1,0:T(2,128)S(1)}, u32[]{:S(2)}, u32[]{:S(2)}) collective-permute-start(f32[6,2,256]{2,1,0:T(2,128)S(1)} %get-tuple-element.55), channel_id=1, source_target_pairs={{0,4},{4,0},{8,12},{12,8},{1,5},{5,1},{9,13},{13,9},{2,6},{6,2},{1... | collective-permute-start | bytes 36872 | tf_op jit(solution)/shard_map/ppermute | solution.py:493
  81.8 8.3 %inner_relax.3 = (f32[2,16,2,8,512]{4,3,2,1,0:T(8,128)S(1)}, f32[4,16,2,8,512]{4,3,2,1,0:T(8,128)S(1)}, f32[2,16,2,8,512]{4,3,2,1,0:T(8,128)S(1)}, f32[4,16,2,8,512]{4,3,2,1,0:T(8,128)S(1)}, f32[5,4,256]{2,1,0:T(4,128)S(1)}) custom-call(f32[2,16,2,8,512]{4,3,2,1,0:T(8,128)S(1)} %get-tuple-element.51.refs_0_, ...), custom_call_target="tpu_custom_call" | custom-call | tf_op jit(solution)/shard_map/inner_relax/pallas_call | solution.py:435
  90.1 8.9 %edge_relax.3 = (f32[2,16,2,8,512]{4,3,2,1,0:T(8,128)S(1)}, f32[2,16,2,8,512]{4,3,2,1,0:T(8,128)S(1)}, f32[5,8,256]{2,1,0:T(8,128)S(1)}) custom-call(s32[2]{0:T(128)S(1)} %pad_add_fusion.flags.refs_0_, f32[2,16,2,8,512]{4,3,2,1,0:T(8,128)S(1)} %collective-permute-done.9.refs_1_, f32[2,16,2,8,512]{4,3,2,1,0:T(8,128)S(1)} %collective-permute-done.10.refs_2_, ...), custom_call_target="tpu_custom_call" | custom-call | tf_op jit(solution)/shard_map/edge_relax/pallas_call | solution.py:452
  99.0 0.8 collective-permute-start.16
  99.8 2.1 %collective-permute-start.17 = (f32[5,8,256]{2,1,0:T(8,128)S(1)}, f32[5,8,256]{2,1,0:T(8,128)S(1)}, u32[]{:S(2)}, u32[]{:S(2)}) collective-permute-start(f32[5,8,256]{2,1,0:T(8,128)S(1)} %get-tuple-element.65.refs_0_), channel_id=1, source_target_pairs={{0,2},{1,3},{2,0},{3,1},{4,6},{5,7},{6,4},{7,5},{8,10},{9,11},{10,... | collective-permute-start | bytes 122888 | tf_op jit(solution)/shard_map/ppermute | solution.py:499
  101.9 1.0 collective-permute-start.18
  102.9 2.3 %collective-permute-done.16.refs_1_ = f32[5,8,256]{2,1,0:T(8,128)S(1)} collective-permute-done((f32[5,8,256]{2,1,0:T(8,128)S(1)}, f32[5,8,256]{2,1,0:T(8,128)S(1)}, u32[]{:S(2)}, u32[]{:S(2)}) %collective-permute-start.16) | collective-permute-done | bytes 40992 | tf_op jit(solution)/shard_map/ppermute | solution.py:499
  105.3 0.6 collective-permute-done.17.refs_2_
  105.8 0.1 collective-permute-done.18.refs_3_
  106.0 1.2 %cell_params.5 = (f32[6,8,256]{2,1,0:T(8,128)S(1)}, f32[6,2,256]{2,1,0:T(2,128)}, f32[6,2,256]{2,1,0:T(2,128)}) custom-call(f32[5,8,256]{2,1,0:T(8,128)S(1)} %get-tuple-element.65.refs_0_, f32[5,8,256]{2,1,0:T(8,128)S(1)} %collective-permute-done.16.refs_1_, f32[5,8,256]{2,1,0:T(8,128)S(1)} %collective-permute-done.17.refs_2_, ...), custom_call_target="tpu_custom_call" | custom-call | tf_op jit(solution)/shard_map/cell_params/pallas_call | solution.py:463
  107.2 3.9 %final_relax.1 = f32[8,16,2,8,512]{4,3,2,1,0:T(8,128)} custom-call(s32[2]{0:T(128)S(1)} %pad_add_fusion.flags.refs_0_, f32[2,16,2,8,512]{4,3,2,1,0:T(8,128)S(1)} %get-tuple-element.62.m_cross, f32[4,16,2,8,512]{4,3,2,1,0:T(8,128)S(1)} %get-tuple-element.63.m_mid, f32[2,16,2,8,512]{4,3,2,1,0:T(8,128)S(1)} %get-tuple-element.64.m_in, ...), custom_call_target="tpu_custom_call" | custom-call | tf_op jit(solution)/shard_map/final_relax/pallas_call | solution.py:473
  (32 shorter events, 0.2 us)
Async XLA Ops:
  0.1 2.2 %copy-start = (f32[8,16,16,512]{3,2,1,0:T(8,128)S(1)}, f32[8,16,16,512]{3,2,1,0:T(8,128)}, u32[]{:S(2)}) copy-start(f32[8,16,16,512]{3,2,1,0:T(8,128)} %param.5) | copy-start | bytes 12582916
  2.3 6.9 %copy-start.5 = (s32[512]{0:T(512)S(1)}, s32[512]{0:T(512)}, u32[]{:S(2)}) copy-start(s32[512]{0:T(512)} %param.6) | copy-start | bytes 6148
  4.2 14.1 %collective-permute-start = (f32[2,16,2,8,512]{4,3,2,1,0:T(8,128)S(1)}, f32[2,16,2,8,512]{4,3,2,1,0:T(8,128)}, u32[]{:S(2)}, u32[]{:S(2)}) collective-permute-start(f32[2,16,2,8,512]{4,3,2,1,0:T(8,128)S(1)} %get-tuple-element.36.refs_0_.refs_3_), channel_id=1, source_target_pairs={{0,0},{12,12},{4,8},{8,4},{1,1},{13,13},{5,9},{9,5},{2,2},{14,14},... | collective-permute-start | bytes 3145736 | tf_op jit(solution)/shard_map/ppermute | solution.py:493
  5.8 12.5 %collective-permute-start.1 = (f32[2,16,2,8,512]{4,3,2,1,0:T(8,128)}, f32[2,16,2,8,512]{4,3,2,1,0:T(8,128)}, u32[]{:S(2)}, u32[]{:S(2)}) collective-permute-start(f32[2,16,2,8,512]{4,3,2,1,0:T(8,128)} %get-tuple-element.37.refs_2_.refs_5_), channel_id=1, source_target_pairs={{0,4},{4,0},{8,12},{12,8},{1,5},{5,1},{9,13},{13,9},{2,6},{6,2},{1... | collective-permute-start | bytes 3145736 | tf_op jit(solution)/shard_map/ppermute | solution.py:493
  16.9 1.3 %copy-start.1 = (f32[4,16,2,8,512]{4,3,2,1,0:T(8,128)}, f32[4,16,2,8,512]{4,3,2,1,0:T(8,128)S(1)}, u32[]{:S(2)}) copy-start(f32[4,16,2,8,512]{4,3,2,1,0:T(8,128)S(1)} %get-tuple-element.45.refs_1_) | copy-start | bytes 6291460
  18.3 17.3 %copy-start.4 = (s32[8,16,16]{2,1,0:T(8,128)S(1)}, s32[8,16,16]{2,1,0:T(8,128)}, u32[]{:S(2)}) copy-start(s32[8,16,16]{2,1,0:T(8,128)} %param.7) | copy-start | bytes 24580
  18.3 25.7 %copy-start.3 = (f32[4]{0:T(128)S(1)}, f32[4]{0:T(128)}, u32[]{:S(2)}) copy-start(f32[4]{0:T(128)} %refs_6_.5) | copy-start | bytes 52
  28.4 29.8 %collective-permute-start.2 = (f32[2,16,2,8,512]{4,3,2,1,0:T(8,128)}, f32[2,16,2,8,512]{4,3,2,1,0:T(8,128)S(1)}, u32[]{:S(2)}, u32[]{:S(2)}) collective-permute-start(f32[2,16,2,8,512]{4,3,2,1,0:T(8,128)} %get-tuple-element.40.refs_0_), channel_id=1, source_target_pairs={{0,0},{12,12},{4,8},{8,4},{1,1},{13,13},{5,9},{9,5},{2,2},{14,14},... | collective-permute-start | bytes 3145736 | tf_op jit(solution)/shard_map/ppermute | solution.py:493
  30.3 28.0 %collective-permute-start.3 = (f32[2,16,2,8,512]{4,3,2,1,0:T(8,128)}, f32[2,16,2,8,512]{4,3,2,1,0:T(8,128)S(1)}, u32[]{:S(2)}, u32[]{:S(2)}) collective-permute-start(f32[2,16,2,8,512]{4,3,2,1,0:T(8,128)} %get-tuple-element.41.refs_2_), channel_id=1, source_target_pairs={{0,4},{4,0},{8,12},{12,8},{1,5},{5,1},{9,13},{13,9},{2,6},{6,2},{1... | collective-permute-start | bytes 3145736 | tf_op jit(solution)/shard_map/ppermute | solution.py:493
  35.7 6.2 %collective-permute-start.4 = (f32[5,8,256]{2,1,0:T(8,128)S(1)}, f32[5,8,256]{2,1,0:T(8,128)S(1)}, u32[]{:S(2)}, u32[]{:S(2)}) collective-permute-start(f32[5,8,256]{2,1,0:T(8,128)S(1)} %get-tuple-element.42.refs_0_), channel_id=1, source_target_pairs={{0,1},{1,2},{2,3},{3,0},{4,5},{5,6},{6,7},{7,4},{8,9},{9,10},{10,1... | collective-permute-start | bytes 122888 | tf_op jit(solution)/shard_map/ppermute | solution.py:499
  37.4 5.6 %collective-permute-start.5 = (f32[5,8,256]{2,1,0:T(8,128)S(1)}, f32[5,8,256]{2,1,0:T(8,128)S(1)}, u32[]{:S(2)}, u32[]{:S(2)}) collective-permute-start(f32[5,8,256]{2,1,0:T(8,128)S(1)} %get-tuple-element.42.refs_0_), channel_id=1, source_target_pairs={{0,2},{1,3},{2,0},{3,1},{4,6},{5,7},{6,4},{7,5},{8,10},{9,11},{10,... | collective-permute-start | bytes 122888 | tf_op jit(solution)/shard_map/ppermute | solution.py:499
  40.0 4.0 %collective-permute-start.6 = (f32[5,8,256]{2,1,0:T(8,128)S(1)}, f32[5,8,256]{2,1,0:T(8,128)S(1)}, u32[]{:S(2)}, u32[]{:S(2)}) collective-permute-start(f32[5,8,256]{2,1,0:T(8,128)S(1)} %get-tuple-element.42.refs_0_), channel_id=1, source_target_pairs={{0,3},{1,0},{2,1},{3,2},{4,7},{5,4},{6,5},{7,6},{8,11},{9,8},{10,9... | collective-permute-start | bytes 122888 | tf_op jit(solution)/shard_map/ppermute | solution.py:499
  44.6 13.6 %collective-permute-start.7 = (f32[6,2,256]{2,1,0:T(2,128)S(1)}, f32[6,2,256]{2,1,0:T(2,128)S(1)}, u32[]{:S(2)}, u32[]{:S(2)}) collective-permute-start(f32[6,2,256]{2,1,0:T(2,128)S(1)} %get-tuple-element.43), channel_id=1, source_target_pairs={{0,0},{12,12},{4,8},{8,4},{1,1},{13,13},{5,9},{9,5},{2,2},{14,14},... | collective-permute-start | bytes 36872 | tf_op jit(solution)/shard_map/ppermute | solution.py:493
  45.3 13.0 %collective-permute-start.8 = (f32[6,2,256]{2,1,0:T(2,128)S(1)}, f32[6,2,256]{2,1,0:T(2,128)S(1)}, u32[]{:S(2)}, u32[]{:S(2)}) collective-permute-start(f32[6,2,256]{2,1,0:T(2,128)S(1)} %get-tuple-element.44), channel_id=1, source_target_pairs={{0,4},{4,0},{8,12},{12,8},{1,5},{5,1},{9,13},{13,9},{2,6},{6,2},{1... | collective-permute-start | bytes 36872 | tf_op jit(solution)/shard_map/ppermute | solution.py:493
  46.8 1.6 %copy-start.2 = (f32[4,16,2,8,512]{4,3,2,1,0:T(8,128)S(1)}, f32[4,16,2,8,512]{4,3,2,1,0:T(8,128)}, u32[]{:S(2)}) copy-start(f32[4,16,2,8,512]{4,3,2,1,0:T(8,128)} %copy-done.1) | copy-start | bytes 6291460
  67.2 22.9 %collective-permute-start.10 = (f32[2,16,2,8,512]{4,3,2,1,0:T(8,128)S(1)}, f32[2,16,2,8,512]{4,3,2,1,0:T(8,128)S(1)}, u32[]{:S(2)}, u32[]{:S(2)}) collective-permute-start(f32[2,16,2,8,512]{4,3,2,1,0:T(8,128)S(1)} %get-tuple-element.52.refs_2_), channel_id=1, source_target_pairs={{0,4},{4,0},{8,12},{12,8},{1,5},{5,1},{9,13},{13,9},{2,6},{6,2},{1... | collective-permute-start | bytes 3145736 | tf_op jit(solution)/shard_map/ppermute | solution.py:493
  67.3 22.8 %collective-permute-start.9 = (f32[2,16,2,8,512]{4,3,2,1,0:T(8,128)S(1)}, f32[2,16,2,8,512]{4,3,2,1,0:T(8,128)S(1)}, u32[]{:S(2)}, u32[]{:S(2)}) collective-permute-start(f32[2,16,2,8,512]{4,3,2,1,0:T(8,128)S(1)} %get-tuple-element.51.refs_0_), channel_id=1, source_target_pairs={{0,0},{12,12},{4,8},{8,4},{1,1},{13,13},{5,9},{9,5},{2,2},{14,14},... | collective-permute-start | bytes 3145736 | tf_op jit(solution)/shard_map/ppermute | solution.py:493
  68.0 6.0 %collective-permute-start.11 = (f32[5,8,256]{2,1,0:T(8,128)S(1)}, f32[5,8,256]{2,1,0:T(8,128)S(1)}, u32[]{:S(2)}, u32[]{:S(2)}) collective-permute-start(f32[5,8,256]{2,1,0:T(8,128)S(1)} %get-tuple-element.53.refs_0_), channel_id=1, source_target_pairs={{0,1},{1,2},{2,3},{3,0},{4,5},{5,6},{6,7},{7,4},{8,9},{9,10},{10,1... | collective-permute-start | bytes 122888 | tf_op jit(solution)/shard_map/ppermute | solution.py:499
  68.9 6.2 %collective-permute-start.12 = (f32[5,8,256]{2,1,0:T(8,128)S(1)}, f32[5,8,256]{2,1,0:T(8,128)S(1)}, u32[]{:S(2)}, u32[]{:S(2)}) collective-permute-start(f32[5,8,256]{2,1,0:T(8,128)S(1)} %get-tuple-element.53.refs_0_), channel_id=1, source_target_pairs={{0,2},{1,3},{2,0},{3,1},{4,6},{5,7},{6,4},{7,5},{8,10},{9,11},{10,... | collective-permute-start | bytes 122888 | tf_op jit(solution)/shard_map/ppermute | solution.py:499
  71.7 4.5 %collective-permute-start.13 = (f32[5,8,256]{2,1,0:T(8,128)S(1)}, f32[5,8,256]{2,1,0:T(8,128)S(1)}, u32[]{:S(2)}, u32[]{:S(2)}) collective-permute-start(f32[5,8,256]{2,1,0:T(8,128)S(1)} %get-tuple-element.53.refs_0_), channel_id=1, source_target_pairs={{0,3},{1,0},{2,1},{3,2},{4,7},{5,4},{6,5},{7,6},{8,11},{9,8},{10,9... | collective-permute-start | bytes 122888 | tf_op jit(solution)/shard_map/ppermute | solution.py:499
  76.8 13.2 %collective-permute-start.14 = (f32[6,2,256]{2,1,0:T(2,128)S(1)}, f32[6,2,256]{2,1,0:T(2,128)S(1)}, u32[]{:S(2)}, u32[]{:S(2)}) collective-permute-start(f32[6,2,256]{2,1,0:T(2,128)S(1)} %get-tuple-element.54), channel_id=1, source_target_pairs={{0,0},{12,12},{4,8},{8,4},{1,1},{13,13},{5,9},{9,5},{2,2},{14,14},... | collective-permute-start | bytes 36872 | tf_op jit(solution)/shard_map/ppermute | solution.py:493
  77.5 12.6 %collective-permute-start.15 = (f32[6,2,256]{2,1,0:T(2,128)S(1)}, f32[6,2,256]{2,1,0:T(2,128)S(1)}, u32[]{:S(2)}, u32[]{:S(2)}) collective-permute-start(f32[6,2,256]{2,1,0:T(2,128)S(1)} %get-tuple-element.55), channel_id=1, source_target_pairs={{0,4},{4,0},{8,12},{12,8},{1,5},{5,1},{9,13},{13,9},{2,6},{6,2},{1... | collective-permute-start | bytes 36872 | tf_op jit(solution)/shard_map/ppermute | solution.py:493
  99.0 6.2 %collective-permute-start.16 = (f32[5,8,256]{2,1,0:T(8,128)S(1)}, f32[5,8,256]{2,1,0:T(8,128)S(1)}, u32[]{:S(2)}, u32[]{:S(2)}) collective-permute-start(f32[5,8,256]{2,1,0:T(8,128)S(1)} %get-tuple-element.65.refs_0_), channel_id=1, source_target_pairs={{0,1},{1,2},{2,3},{3,0},{4,5},{5,6},{6,7},{7,4},{8,9},{9,10},{10,1... | collective-permute-start | bytes 122888 | tf_op jit(solution)/shard_map/ppermute | solution.py:499
  99.8 6.0 %collective-permute-start.17 = (f32[5,8,256]{2,1,0:T(8,128)S(1)}, f32[5,8,256]{2,1,0:T(8,128)S(1)}, u32[]{:S(2)}, u32[]{:S(2)}) collective-permute-start(f32[5,8,256]{2,1,0:T(8,128)S(1)} %get-tuple-element.65.refs_0_), channel_id=1, source_target_pairs={{0,2},{1,3},{2,0},{3,1},{4,6},{5,7},{6,4},{7,5},{8,10},{9,11},{10,... | collective-permute-start | bytes 122888 | tf_op jit(solution)/shard_map/ppermute | solution.py:499
  101.9 4.1 %collective-permute-start.18 = (f32[5,8,256]{2,1,0:T(8,128)S(1)}, f32[5,8,256]{2,1,0:T(8,128)S(1)}, u32[]{:S(2)}, u32[]{:S(2)}) collective-permute-start(f32[5,8,256]{2,1,0:T(8,128)S(1)} %get-tuple-element.65.refs_0_), channel_id=1, source_target_pairs={{0,3},{1,0},{2,1},{3,2},{4,7},{5,4},{6,5},{7,6},{8,11},{9,8},{10,9... | collective-permute-start | bytes 122888 | tf_op jit(solution)/shard_map/ppermute | solution.py:499

commit v3 on v2

--- a/solution.py
+++ b/solution.py
@@ -36,7 +36,7 @@
     return [coef_ref[k, :, lanes] for k in range(9)]
 
 
-def x_row(cells, rows, store, coef):
+def x_row(cells, rows, store, coef, change=False):
     reach, lean, ahead = coef[0], coef[1], coef[2] > 0.0
     first, last = rows[0], rows[-1]
     steps = {n: cells[n + 1] - cells[n] for n in range(first - 2, last + 2)}
@@ -46,10 +46,11 @@
     }
     for n in rows:
         source = jnp.where(ahead, faces[n - 1], faces[n + 1])
-        store(n, cells[n] - reach * (faces[n] - source))
-
-
-def yz_row(source, out, row, lanes, coef, ring, face_ring):
+        v = reach * (faces[n] - source)
+        store(n, v if change else cells[n] - v)
+
+
+def yz_row(source, out, fresh, row, lanes, coef, ring, face_ring):
     reach_y, lean_y, ahead_y = coef[3], coef[4], coef[5] > 0.0
     reach_z, lean_z, ahead_z = coef[6], coef[7], coef[8] > 0.0
     count = 16
@@ -93,7 +94,7 @@
         for t in range(2):
             below = face_ring[y, 7 + 8 * t : 15 + 8 * t, :]
             above = face_ring[y, 9 + 8 * t : 17 + 8 * t, :]
-            v = out[row, y, t, :, lanes]
+            v = cell(y, t) if fresh else out[row, y, t, :, lanes]
             v -= reach_z * (z_faces[y, t] - jnp.where(ahead_z, below, above))
             upwind = jnp.where(ahead_y, face(y - 1, t), face(y + 1, t))
             v -= reach_y * (face(y, t) - upwind)
@@ -108,34 +109,32 @@
             finish(y - 2)
 
 
-def row_moments(block, weights):
-    flat = block.reshape(256, LANES)
-    high = flat.astype(BF16)
-    rest = (flat - high.astype(F32)).astype(BF16)
-    contract = (((1,), (1,)), ((), ()))
-    total = lax.dot_general(weights, high, contract, preferred_element_type=F32)
-    total += lax.dot_general(weights, rest, contract, preferred_element_type=F32)
-    return total[:SUB]
-
-
-def write_moments(out, place, value):
-    for m in range(4):
-        out[m, pl.ds(place, 1), :] = value[m : m + 1]
-    out[4, pl.ds(place, 1), :] = value[4:5] + value[5:6]
-
-
-def yz_rows(chunks, groups, coef_ref, weights, acc, ring, face_ring):
-    for source, out, rows, place in groups:
-
-        def one(i, carry, source=source, out=out, rows=rows, place=place):
-            chunk, row = i // rows, i % rows
-            lanes = lanes_of(chunk)
-            yz_row(source, out, row, lanes, coefs_of(coef_ref, lanes), ring, face_ring)
-            part = row_moments(out[row, :, :, :, lanes], weights[:, lanes])
-            acc[place + row] = acc[place + row] + part
-            return carry
-
-        lax.fori_loop(0, chunks * rows, one, 0)
+def row_moments(out, count, weights, sums, first):
+    width = out.shape[-1]
+    for r in range(count):
+        flat = out[r].reshape(256, width)
+        high = flat.astype(BF16)
+        rest = (flat - high.astype(F32)).astype(BF16)
+        both = jnp.concatenate([high, rest], axis=1)
+        contract = (((1,), (1,)), ((), ()))
+        part = lax.dot_general(weights[...], both, contract, preferred_element_type=F32)
+        place = first + r
+        for m in range(4):
+            sums[m, place : place + 1, :] = part[m : m + 1]
+        sums[4, place : place + 1, :] = part[4:5] + part[5:6]
+
+
+def yz_rows(source, out, fresh, rows, coef_ref, ring, face_ring):
+    chunks = source.shape[-1] // LANES
+
+    def one(i, carry):
+        chunk, row = i // rows, i % rows
+        lanes = lanes_of(chunk)
+        coef = coefs_of(coef_ref, lanes)
+        yz_row(source, out, fresh, row, lanes, coef, ring, face_ring)
+        return carry
+
+    lax.fori_loop(0, chunks * rows, one, 0)
 
 
 def three_parts(value):
@@ -164,22 +163,23 @@
 def relax_rows(source, out, tall, first, rows, table, factor, kept):
     width = source.shape[-1]
 
-    def one(row, carry):
-        features = tall[first + row]
-        keep = jnp.dot(features, factor[...], preferred_element_type=F32)
-        kept[...] = keep.reshape(16, 2, SUB, LANES)
-        for pair in range(width // PAIR):
-            power = jnp.dot(
-                features, table[:, pair * PAIR : (pair + 1) * PAIR], preferred_element_type=F32
-            )
-            for half in range(2):
-                lanes = pl.ds(pair * PAIR + half * LANES, LANES)
-                shape = jnp.exp2(power[:, half * LANES : (half + 1) * LANES])
-                shape = shape.reshape(16, 2, SUB, LANES)
-                out[row, :, :, :, lanes] = kept[...] * source[row, :, :, :, lanes] + shape
+    def two(i, carry):
+        for u in range(2):
+            keep = jnp.dot(tall[first + 2 * i + u], factor[...], preferred_element_type=F32)
+            kept[u] = keep.reshape(16, 2, SUB, LANES)
+        for u in range(2):
+            row = 2 * i + u
+            for pair in range(width // PAIR):
+                columns = table[:, pair * PAIR : (pair + 1) * PAIR]
+                power = jnp.dot(tall[first + row], columns, preferred_element_type=F32)
+                for half in range(2):
+                    lanes = pl.ds(pair * PAIR + half * LANES, LANES)
+                    shape = jnp.exp2(power[:, half * LANES : (half + 1) * LANES])
+                    shape = shape.reshape(16, 2, SUB, LANES)
+                    out[row, :, :, :, lanes] = kept[u] * source[row, :, :, :, lanes] + shape
         return carry
 
-    lax.fori_loop(0, rows, one, 0)
+    lax.fori_loop(0, rows // 2, two, 0)
 
 
 def param_kernel(total, count, *refs):
@@ -246,16 +246,15 @@
 def inner_kernel(relax, rows, *refs):
     if relax:
         (m_cross, m_mid, m_in, params, table, factor, coef_ref, weights,
-         cross, middle, inside, out, sums, wide, tall, kept, acc, ring, face_ring) = refs
+         cross, middle, inside, out, e_cross, e_in, sums, wide, tall, kept, ring, face_ring) = refs
         spread_features([params[k] for k in range(6)], wide, tall, rows)
         relax_rows(m_cross, cross, tall, 0, 2, table, factor, kept)
         relax_rows(m_mid, middle, tall, 2, rows - 4, table, factor, kept)
         relax_rows(m_in, inside, tall, rows - 2, 2, table, factor, kept)
     else:
-        (cross, middle, inside, coef_ref, weights, out, sums, acc, ring, face_ring) = refs
+        (cross, middle, inside, coef_ref, weights, out, e_cross, e_in, sums, ring, face_ring) = refs
     chunks = middle.shape[-1] // LANES
     inner = rows - 4
-    acc[...] = jnp.zeros_like(acc)
 
     def along_x(i, carry):
         chunk, y = i // 16, i % 16
@@ -278,25 +277,25 @@
         return carry
 
     lax.fori_loop(0, chunks * 16, along_x, 0, unroll=2)
-    yz_rows(chunks, [(middle, out, inner, 0)], coef_ref, weights, acc, ring, face_ring)
-    for r in range(inner):
-        write_moments(sums, r, acc[r])
+    yz_rows(middle, out, False, inner, coef_ref, ring, face_ring)
+    yz_rows(cross, e_cross, True, 2, coef_ref, ring, face_ring)
+    yz_rows(inside, e_in, True, 2, coef_ref, ring, face_ring)
+    row_moments(out, inner, weights, sums, 0)
 
 
 def edge_kernel(relax, rows, *refs):
     if relax:
-        (flags, h_cross, h_in, p_cross, p_in, table, factor, cross, middle, inside, coef_ref,
-         weights, inner_sums, out_cross, out_in, sums,
-         wide, tall, kept, low, high, acc, ring, face_ring) = refs
+        (flags, h_cross, h_in, p_cross, p_in, table, factor, cross, middle, inside, e_cross,
+         e_in, coef_ref, weights, inner_sums, out_cross, out_in, sums,
+         wide, tall, kept, low, high) = refs
         spread_features([p_cross[k] for k in range(6)], wide, tall, 2)
         relax_rows(h_cross, low, tall, 0, 2, table, factor, kept)
         spread_features([p_in[k] for k in range(6)], wide, tall, 2)
         relax_rows(h_in, high, tall, 0, 2, table, factor, kept)
     else:
-        (flags, low, high, cross, middle, inside, coef_ref, weights, inner_sums,
-         out_cross, out_in, sums, acc, ring, face_ring) = refs
+        (flags, low, high, cross, middle, inside, e_cross, e_in, coef_ref, weights,
+         inner_sums, out_cross, out_in, sums) = refs
     chunks = middle.shape[-1] // LANES
-    acc[...] = jnp.zeros_like(acc)
     present = jnp.where(flags[1] > 0, 1.0, 0.0)
 
     def along_x(i, carry):
@@ -311,9 +310,9 @@
                 cells[2 + n] = middle[n, y, t, :, lanes]
 
             def store(n, v, t=t):
-                out_cross[n, y, t, :, lanes] = v
-
-            x_row(cells, [0, 1], store, coef)
+                out_cross[n, y, t, :, lanes] = e_cross[n, y, t, :, lanes] - v
+
+            x_row(cells, [0, 1], store, coef, True)
             cells = {}
             for n in range(2):
                 cells[rows - 4 + n] = middle[rows - 6 + n, y, t, :, lanes]
@@ -321,19 +320,17 @@
                 cells[rows + n] = high[1 - n, y, t, :, lanes]
 
             def store_in(n, v, t=t):
-                out_in[n - rows + 2, y, t, :, lanes] = v
-
-            x_row(cells, [rows - 2, rows - 1], store_in, coef)
+                r = n - rows + 2
+                out_in[r, y, t, :, lanes] = e_in[r, y, t, :, lanes] - v
+
+            x_row(cells, [rows - 2, rows - 1], store_in, coef, True)
         return carry
 
-    lax.fori_loop(0, chunks * 16, along_x, 0)
-    groups = [(cross, out_cross, 2, 0), (inside, out_in, 2, 2)]
-    yz_rows(chunks, groups, coef_ref, weights, acc, ring, face_ring)
+    lax.fori_loop(0, chunks * 16, along_x, 0, unroll=2)
     for m in range(5):
         sums[m, 2 : rows - 2, :] = inner_sums[m]
-    for r in range(2):
-        write_moments(sums, r, acc[r])
-        write_moments(sums, rows - 2 + r, acc[2 + r])
+    row_moments(out_cross, 2, weights, sums, 0)
+    row_moments(out_in, 2, weights, sums, rows - 2)
 
 
 def final_kernel(rows, flags, m_cross, m_mid, m_in, params, table, factor, out,
@@ -378,6 +375,7 @@
     low_part = square % 8
     whole = jnp.stack([ones, n_x, n_y, n_z, square - low_part, low_part]).astype(F32)
     weights = jnp.pad(whole, ((0, 10), (0, 0))).astype(BF16)
+    weights = jnp.concatenate([weights, weights], axis=1)
     table = jnp.repeat(whole, 3, axis=0)
     table = jnp.pad(table, ((0, FEATURES - 18), (0, 0))).astype(BF16)
     slot = lax.broadcasted_iota(jnp.int32, (FEATURES, LANES), 0)
@@ -391,7 +389,7 @@
 
     vmem = pl.BlockSpec(memory_space=pltpu.VMEM)
     smem = pl.BlockSpec(memory_space=pltpu.SMEM)
-    hbm = pl.BlockSpec(memory_space=pl.ANY)
+    hbm = pl.BlockSpec(memory_space=pltpu.HBM)
 
     def slab(n):
         return jax.ShapeDtypeStruct((n, count_y, 2, SUB, width), F32)
@@ -403,11 +401,10 @@
         return [
             pltpu.VMEM((n, FEATURES, cells), F32),
             pltpu.VMEM((n, cells, FEATURES), BF16),
-            pltpu.VMEM((count_y, 2, SUB, LANES), F32),
+            pltpu.VMEM((2, count_y, 2, SUB, LANES), F32),
         ]
 
-    def ring_scratch(n):
-        return [pltpu.VMEM((n, SUB, cells), F32)] + [pltpu.VMEM((count_y, 32, LANES), F32)] * 2
+    ring_scratch = [pltpu.VMEM((count_y, 32, LANES), F32)] * 2
 
     def limits(mib):
         return pltpu.CompilerParams(vmem_limit_bytes=mib * 1024 * 1024)
@@ -421,11 +418,12 @@
             scratch_shapes=[pltpu.SemaphoreType.DMA((rows,))],
             compiler_params=limits(6),
             name="load_rows",
-        )(flags, state)
+        )(flags, pltpu.with_memory_space_constraint(state, pltpu.HBM))
 
     def inner(relax, state, params):
-        out_shape = [slab(rows - 4), jax.ShapeDtypeStruct((5, rows - 4, cells), F32)]
-        scratch = ring_scratch(rows - 4)
+        sums = jax.ShapeDtypeStruct((5, rows - 4, cells), F32)
+        out_shape = [slab(rows - 4), slab(2), slab(2), sums]
+        scratch = ring_scratch
         if relax:
             out_shape = [slab(2), slab(rows - 4), slab(2)] + out_shape
             scratch = feature_scratch(rows) + scratch
@@ -442,13 +440,13 @@
             name="inner_relax" if relax else "inner_first",
         )(*args)
 
-    def edge(relax, halos, params, state, sums):
-        scratch = ring_scratch(4)
+    def edge(relax, halos, params, state, edges, sums):
+        scratch = []
+        args = (*state, *edges, coef, weights, sums)
         if relax:
-            scratch = feature_scratch(2) + [slab_scratch(2)] * 2 + scratch
-            args = (*halos, *params, table, factor, *state, coef, weights, sums)
-        else:
-            args = (*halos, *state, coef, weights, sums)
+            scratch = feature_scratch(2) + [slab_scratch(2)] * 2
+            args = (*params, table, factor, *args)
+        args = (*halos, *args)
         return pl.pallas_call(
             functools.partial(edge_kernel, relax, rows),
             in_specs=[smem] + [vmem] * len(args),
@@ -482,15 +480,23 @@
             name="final_relax",
         )(flags, *moved, params, table, factor)
 
-    across = [(0, 0), (line - 1, line - 1)]
-    for i in range(1, line - 1, 2):
-        across += [(i, i + 1), (i + 1, i)]
+    parts = lax.axis_size("groups")
+    across = []
+    for p in range(parts):
+        for i in (0, line - 1):
+            other = p ^ 1 if (p ^ 1) < parts else p
+            across.append((p * line + i, other * line + i))
+        for i in range(1, line - 1, 2):
+            across += [(p * line + i, p * line + i + 1), (p * line + i + 1, p * line + i)]
     within = []
     for i in range(0, line, 2):
         within += [(i, i + 1), (i + 1, i)]
 
     def exchange(cross, inside):
-        return lax.ppermute(cross, "gx", across), lax.ppermute(inside, "gx", within)
+        return (
+            lax.ppermute(cross, ("groups", "gx"), across),
+            lax.ppermute(inside, "gx", within),
+        )
 
     def gather(part):
         parts = [part]
@@ -499,17 +505,22 @@
             parts.append(lax.ppermute(part, "vert", pairs))
         return parts
 
+    flags, codes, weights, table, factor, coef = lax.optimization_barrier(
+        (flags, codes, weights, table, factor, coef)
+    )
     cross, middle, inside = load()
     halos = exchange(cross, inside)
-    m_mid, sums = inner(False, (cross, middle, inside), None)
-    m_cross, m_in, sums = edge(False, halos, None, (cross, middle, inside), sums)
+    m_mid, e_cross, e_in, sums = inner(False, (cross, middle, inside), None)
+    m_cross, m_in, sums = edge(
+        False, halos, None, (cross, middle, inside), (e_cross, e_in), sums
+    )
     for _ in range(1, STEPS):
         halos = exchange(m_cross, m_in)
         params, p_cross, p_in = cell_params(gather(sums))
         p_halos = exchange(p_cross, p_in)
         moved = (m_cross, m_mid, m_in)
-        cross, middle, inside, m_mid, sums = inner(True, moved, params)
-        m_cross, m_in, sums = edge(True, halos, p_halos, (cross, middle, inside), sums)
+        *state, m_mid, e_cross, e_in, sums = inner(True, moved, params)
+        m_cross, m_in, sums = edge(True, halos, p_halos, state, (e_cross, e_in), sums)
     params, _, _ = cell_params(gather(sums))
     result = final((m_cross, m_mid, m_in), params)
     return result.reshape(rows, count_y, count_z, width)

time: 111 us -> 84.5 us (0.76)
  Pallas kernels: 61.9 us -> 44.6 us
  starting transfers between devices: 33.4 us -> 22.1 us
  waiting for transfers between devices: 9.27 us -> 14.7 us
  local copies, waits for them, and re-layouts: 5.49 us -> 1.22 us
    pallas_call x3, Pallas kernels: 28 us -> 10.5 us  [edge(): pl.pallas_call(functools.partial(edge_kernel, relax, rows), in_specs=[sme...]
    ppermute x5, starting transfers between devices: 14.4 us -> 0.6 us  [exchange(): lax.ppermute(inside, 'gx', within)]
    ppermute x5, waiting for transfers between devices: 0.01 us -> 5.29 us  [exchange(): lax.ppermute(cross, ('groups', 'gx'), across)]
    unnamed x12 -> x2, local copies, waits for them, and re-layouts: 5.11 us -> 0.01 us
    ppermute x5, starting transfers between devices: 5.54 us -> 8.24 us  [exchange(): lax.ppermute(cross, ('groups', 'gx'), across)]
  transfers between devices with their start and end apart: 19 -> 19, of which waited for: 8 -> 8; matrix products, arithmetic and copies ran while one was open for 0% -> 0% of each run, Pallas kernels for 24% -> 32%
where the time goes in v3:
time: 84.5 us; the launch traced here: 84.3 us
  Pallas kernels  44.6 us (53%)
  starting transfers between devices  22.1 us (26%)
  waiting for transfers between devices  14.7 us (17%)
  local copies, waits for them, and re-layouts  1.22 us (1%)
  between operations  0.85 us (1%)
    pallas_call x3, Pallas kernels, inner(): pl.pallas_call(functools.partial(inner_kernel, relax, rows), in_specs=[vm...  25.3 us
    ppermute x9, starting transfers between devices, gather(): parts.append(lax.ppermute(part, 'vert', pairs))  13.3 us
    pallas_call x3, Pallas kernels, edge(): pl.pallas_call(functools.partial(edge_kernel, relax, rows), in_specs=[sme...  10.5 us
    ppermute x9, waiting for transfers between devices, gather(): parts.append(lax.ppermute(part, 'vert', pairs))  9.4 us
    ppermute x5, starting transfers between devices, exchange(): lax.ppermute(cross, ('groups', 'gx'), across)  8.24 us
    ppermute x5, waiting for transfers between devices, exchange(): lax.ppermute(cross, ('groups', 'gx'), across)  5.29 us
    pallas_call x1, Pallas kernels, final(): pl.pallas_call(functools.partial(final_kernel, rows), in_specs=[smem] + [...  3.47 us
    pallas_call x1, Pallas kernels, load(): pl.pallas_call(load_kernel, in_specs=[smem, hbm], out_specs=[vmem] * 3, o...  2.76 us
  transfers between devices with their start and end apart: 19, of which 8 were waited for; matrix products, arithmetic and copies ran while one was open for 0% of the time, Pallas kernels for 32%

profile of v3, /device:TPU:0, one launch (start us, length us, event | category | flops | bytes accessed | tf_op | source)
XLA Modules:
  0.0 84.3 jit_solution(4549217851164610121)
XLA Ops:
  0.0 0.7 compare_select_fusion
  0.9 0.9 %reshape.14 = s32[8,256]{1,0:T(8,128)S(1)} reshape(s32[8,16,16]{2,1,0:T(8,128)} %param.7) | data formatting | bytes 16384 | tf_op jit(solution)/shard_map/reshape | solution.py:366
  1.8 0.1 rev.3
  1.9 0.1 pad_add_fusion.flags.refs_0_
  2.0 0.1 stack.75
  2.1 0.1 iota.7.refs_5_.refs_6_.factor
  2.1 2.8 %load_rows.1 = (f32[2,16,2,8,512]{4,3,2,1,0:T(8,128)S(1)}, f32[4,16,2,8,512]{4,3,2,1,0:T(8,128)S(1)}, f32[2,16,2,8,512]{4,3,2,1,0:T(8,128)S(1)}) custom-call(s32[2]{0:T(128)S(1)} %pad_add_fusion.flags.refs_0_, f32[8,16,2,8,512]{4,3,2,1,0:T(8,128)} %bitcast.18), custom_call_target="tpu_custom_call" | custom-call | tf_op jit(solution)/shard_map/load_rows/pallas_call | solution.py:413
  4.9 3.0 %collective-permute-start = (f32[2,16,2,8,512]{4,3,2,1,0:T(8,128)S(1)}, f32[2,16,2,8,512]{4,3,2,1,0:T(8,128)S(1)}, u32[]{:S(2)}, u32[]{:S(2)}) collective-permute-start(f32[2,16,2,8,512]{4,3,2,1,0:T(8,128)S(1)} %get-tuple-element.49.refs_0_.refs_3_), channel_id=1, source_target_pairs={{0,16},{12,28},{4,8},{8,4},{16,0},{28,12},{20,24},{24,20},{1,17},{... | collective-permute-start | bytes 3145736 | tf_op jit(solution)/shard_map/ppermute | solution.py:497
  7.9 0.1 collective-permute-start.1
  8.0 7.4 %inner_first.1 = (f32[4,16,2,8,512]{4,3,2,1,0:T(8,128)S(1)}, f32[2,16,2,8,512]{4,3,2,1,0:T(8,128)S(1)}, f32[2,16,2,8,512]{4,3,2,1,0:T(8,128)S(1)}, f32[5,4,256]{2,1,0:T(4,128)S(1)}) custom-call(f32[2,16,2,8,512]{4,3,2,1,0:T(8,128)S(1)} %get-tuple-element.49.refs_0_.refs_3_, f32[4,16,2,8,512]{4,3,2,1,0:T(8,128)S(1)} %get-tuple-element.51.refs_1_.refs_4_, ...), custom_call_target="tpu_custom_call" | custom-call | tf_op jit(solution)/shard_map/inner_first/pallas_call | solution.py:433
  15.5 5.3 %collective-permute-done.refs_1_ = f32[2,16,2,8,512]{4,3,2,1,0:T(8,128)S(1)} collective-permute-done((f32[2,16,2,8,512]{4,3,2,1,0:T(8,128)S(1)}, f32[2,16,2,8,512]{4,3,2,1,0:T(8,128)S(1)}, u32[]{:S(2)}, u32[]{:S(2)}) %collective-permute-start) | collective-permute-done | bytes 1048608 | tf_op jit(solution)/shard_map/ppermute | solution.py:497
  20.7 0.0 collective-permute-done.1.refs_2_
  20.7 3.1 %edge_first.1 = (f32[2,16,2,8,512]{4,3,2,1,0:T(8,128)S(1)}, f32[2,16,2,8,512]{4,3,2,1,0:T(8,128)S(1)}, f32[5,8,256]{2,1,0:T(8,128)S(1)}) custom-call(s32[2]{0:T(128)S(1)} %pad_add_fusion.flags.refs_0_, f32[2,16,2,8,512]{4,3,2,1,0:T(8,128)S(1)} %collective-permute-done.refs_1_, f32[2,16,2,8,512]{4,3,2,1,0:T(8,128)S(1)} %collective-permute-done.1.refs_2_, ...), custom_call_target="tpu_custom_call" | custom-call | tf_op jit(solution)/shard_map/edge_first/pallas_call | solution.py:450
  23.8 2.0 %collective-permute-start.2 = (f32[2,16,2,8,512]{4,3,2,1,0:T(8,128)S(1)}, f32[2,16,2,8,512]{4,3,2,1,0:T(8,128)S(1)}, u32[]{:S(2)}, u32[]{:S(2)}) collective-permute-start(f32[2,16,2,8,512]{4,3,2,1,0:T(8,128)S(1)} %get-tuple-element.57.refs_0_), channel_id=1, source_target_pairs={{0,16},{12,28},{4,8},{8,4},{16,0},{28,12},{20,24},{24,20},{1,17},{... | collective-permute-start | bytes 3145736 | tf_op jit(solution)/shard_map/ppermute | solution.py:497
  25.8 1.6 %collective-permute-start.4 = (f32[5,8,256]{2,1,0:T(8,128)S(1)}, f32[5,8,256]{2,1,0:T(8,128)S(1)}, u32[]{:S(2)}, u32[]{:S(2)}) collective-permute-start(f32[5,8,256]{2,1,0:T(8,128)S(1)} %get-tuple-element.59.refs_0_), channel_id=1, source_target_pairs={{0,1},{1,2},{2,3},{3,0},{4,5},{5,6},{6,7},{7,4},{8,9},{9,10},{10,1... | collective-permute-start | bytes 122888 | tf_op jit(solution)/shard_map/ppermute | solution.py:505
  27.4 2.6 %collective-permute-start.5 = (f32[5,8,256]{2,1,0:T(8,128)S(1)}, f32[5,8,256]{2,1,0:T(8,128)S(1)}, u32[]{:S(2)}, u32[]{:S(2)}) collective-permute-start(f32[5,8,256]{2,1,0:T(8,128)S(1)} %get-tuple-element.59.refs_0_), channel_id=1, source_target_pairs={{0,2},{1,3},{2,0},{3,1},{4,6},{5,7},{6,4},{7,5},{8,10},{9,11},{10,... | collective-permute-start | bytes 122888 | tf_op jit(solution)/shard_map/ppermute | solution.py:505
  30.0 1.3 %collective-permute-start.6 = (f32[5,8,256]{2,1,0:T(8,128)S(1)}, f32[5,8,256]{2,1,0:T(8,128)S(1)}, u32[]{:S(2)}, u32[]{:S(2)}) collective-permute-start(f32[5,8,256]{2,1,0:T(8,128)S(1)} %get-tuple-element.59.refs_0_), channel_id=1, source_target_pairs={{0,3},{1,0},{2,1},{3,2},{4,7},{5,4},{6,5},{7,6},{8,11},{9,8},{10,9... | collective-permute-start | bytes 122888 | tf_op jit(solution)/shard_map/ppermute | solution.py:505
  32.0 1.6 %collective-permute-done.5.refs_2_ = f32[5,8,256]{2,1,0:T(8,128)S(1)} collective-permute-done((f32[5,8,256]{2,1,0:T(8,128)S(1)}, f32[5,8,256]{2,1,0:T(8,128)S(1)}, u32[]{:S(2)}, u32[]{:S(2)}) %collective-permute-start.5) | collective-permute-done | bytes 40992 | tf_op jit(solution)/shard_map/ppermute | solution.py:505
  33.6 0.4 collective-permute-done.6.refs_3_
  34.1 0.6 cell_params.3
  34.7 1.1 %collective-permute-start.7 = (f32[6,2,256]{2,1,0:T(2,128)S(1)}, f32[6,2,256]{2,1,0:T(2,128)S(1)}, u32[]{:S(2)}, u32[]{:S(2)}) collective-permute-start(f32[6,2,256]{2,1,0:T(2,128)S(1)} %get-tuple-element.61), channel_id=1, source_target_pairs={{0,16},{12,28},{4,8},{8,4},{16,0},{28,12},{20,24},{24,20},{1,17},{... | collective-permute-start | bytes 36872 | tf_op jit(solution)/shard_map/ppermute | solution.py:497
  35.8 0.0 collective-permute-start.8
  35.8 8.9 %inner_relax.2 = (f32[2,16,2,8,512]{4,3,2,1,0:T(8,128)S(1)}, f32[4,16,2,8,512]{4,3,2,1,0:T(8,128)S(1)}, f32[2,16,2,8,512]{4,3,2,1,0:T(8,128)S(1)}, f32[4,16,2,8,...) custom-call(f32[2,16,2,8,512]{4,3,2,1,0:T(8,128)S(1)} %get-tuple-ele, ...), custom_call_target="tpu_custom_call" | custom-call | tf_op jit(solution)/shard_map/inner_relax/pallas_call | solution.py:433
  44.7 0.0 collective-permute-done.7.refs_3_
  44.7 0.0 collective-permute-done.8.refs_4_
  44.7 0.0 collective-permute-done.3.refs_2_
  44.8 3.7 %edge_relax.2 = (f32[2,16,2,8,512]{4,3,2,1,0:T(8,128)S(1)}, f32[2,16,2,8,512]{4,3,2,1,0:T(8,128)S(1)}, f32[5,8,256]{2,1,0:T(8,128)S(1)}) custom-call(s32[2]{0:T(128)S(1)} %pad_add_fusion.flags.refs_0_, f32[2,16,2,8,512]{4,3,2,1,0:T(8,128)S(1)} %collective-permute-done.2.refs_1_, f32[2,16,2,8,512]{4,3,2,1,0:T(8,128)S(1)} %collective-permute-done.3.refs_2_, ...), custom_call_target="tpu_custom_call" | custom-call | tf_op jit(solution)/shard_map/edge_relax/pallas_call | solution.py:450
  48.5 0.5 collective-permute-start.10
  49.0 1.0 %collective-permute-start.9 = (f32[2,16,2,8,512]{4,3,2,1,0:T(8,128)S(1)}, f32[2,16,2,8,512]{4,3,2,1,0:T(8,128)S(1)}, u32[]{:S(2)}, u32[]{:S(2)}) collective-permute-start(f32[2,16,2,8,512]{4,3,2,1,0:T(8,128)S(1)} %get-tuple-element.73.refs_0_), channel_id=1, source_target_pairs={{0,16},{12,28},{4,8},{8,4},{16,0},{28,12},{20,24},{24,20},{1,17},{... | collective-permute-start | bytes 3145736 | tf_op jit(solution)/shard_map/ppermute | solution.py:497
  50.0 0.8 collective-permute-start.11
  50.8 2.9 %collective-permute-start.12 = (f32[5,8,256]{2,1,0:T(8,128)S(1)}, f32[5,8,256]{2,1,0:T(8,128)S(1)}, u32[]{:S(2)}, u32[]{:S(2)}) collective-permute-start(f32[5,8,256]{2,1,0:T(8,128)S(1)} %get-tuple-element.75.refs_0_), channel_id=1, source_target_pairs={{0,2},{1,3},{2,0},{3,1},{4,6},{5,7},{6,4},{7,5},{8,10},{9,11},{10,... | collective-permute-start | bytes 122888 | tf_op jit(solution)/shard_map/ppermute | solution.py:505
  53.7 0.2 collective-permute-start.13
  53.9 2.0 %collective-permute-done.11.refs_1_ = f32[5,8,256]{2,1,0:T(8,128)S(1)} collective-permute-done((f32[5,8,256]{2,1,0:T(8,128)S(1)}, f32[5,8,256]{2,1,0:T(8,128)S(1)}, u32[]{:S(2)}, u32[]{:S(2)}) %collective-permute-start.11) | collective-permute-done | bytes 40992 | tf_op jit(solution)/shard_map/ppermute | solution.py:505
  55.9 0.8 collective-permute-done.12.refs_2_
  56.7 1.0 %collective-permute-done.13.refs_3_ = f32[5,8,256]{2,1,0:T(8,128)S(1)} collective-permute-done((f32[5,8,256]{2,1,0:T(8,128)S(1)}, f32[5,8,256]{2,1,0:T(8,128)S(1)}, u32[]{:S(2)}, u32[]{:S(2)}) %collective-permute-start.13) | collective-permute-done | bytes 40992 | tf_op jit(solution)/shard_map/ppermute | solution.py:505
  57.7 0.6 cell_params.4
  58.3 1.1 %collective-permute-start.14 = (f32[6,2,256]{2,1,0:T(2,128)S(1)}, f32[6,2,256]{2,1,0:T(2,128)S(1)}, u32[]{:S(2)}, u32[]{:S(2)}) collective-permute-start(f32[6,2,256]{2,1,0:T(2,128)S(1)} %get-tuple-element.76), channel_id=1, source_target_pairs={{0,16},{12,28},{4,8},{8,4},{16,0},{28,12},{20,24},{24,20},{1,17},{... | collective-permute-start | bytes 36872 | tf_op jit(solution)/shard_map/ppermute | solution.py:497
  59.4 8.9 %inner_relax.3 = (f32[2,16,2,8,512]{4,3,2,1,0:T(8,128)S(1)}, f32[4,16,2,8,512]{4,3,2,1,0:T(8,128)S(1)}, f32[2,16,2,8,512]{4,3,2,1,0:T(8,128)S(1)}, f32[4,16,2,8,...) custom-call(f32[2,16,2,8,512]{4,3,2,1,0:T(8,128)S(1)} %get-tuple-ele, ...), custom_call_target="tpu_custom_call" | custom-call | tf_op jit(solution)/shard_map/inner_relax/pallas_call | solution.py:433
  68.4 0.0 collective-permute-done.14.refs_3_
  68.4 0.0 collective-permute-done.15.refs_4_
  68.4 3.7 %edge_relax.3 = (f32[2,16,2,8,512]{4,3,2,1,0:T(8,128)S(1)}, f32[2,16,2,8,512]{4,3,2,1,0:T(8,128)S(1)}, f32[5,8,256]{2,1,0:T(8,128)S(1)}) custom-call(s32[2]{0:T(128)S(1)} %pad_add_fusion.flags.refs_0_, f32[2,16,2,8,512]{4,3,2,1,0:T(8,128)S(1)} %collective-permute-done.9.refs_1_, f32[2,16,2,8,512]{4,3,2,1,0:T(8,128)S(1)} %collective-permute-done.10.refs_2_, ...), custom_call_target="tpu_custom_call" | custom-call | tf_op jit(solution)/shard_map/edge_relax/pallas_call | solution.py:450
  72.1 0.7 collective-permute-start.16
  72.9 2.1 %collective-permute-start.17 = (f32[5,8,256]{2,1,0:T(8,128)S(1)}, f32[5,8,256]{2,1,0:T(8,128)S(1)}, u32[]{:S(2)}, u32[]{:S(2)}) collective-permute-start(f32[5,8,256]{2,1,0:T(8,128)S(1)} %get-tuple-element.89.refs_0_), channel_id=1, source_target_pairs={{0,2},{1,3},{2,0},{3,1},{4,6},{5,7},{6,4},{7,5},{8,10},{9,11},{10,... | collective-permute-start | bytes 122888 | tf_op jit(solution)/shard_map/ppermute | solution.py:505
  75.0 1.0 %collective-permute-start.18 = (f32[5,8,256]{2,1,0:T(8,128)S(1)}, f32[5,8,256]{2,1,0:T(8,128)S(1)}, u32[]{:S(2)}, u32[]{:S(2)}) collective-permute-start(f32[5,8,256]{2,1,0:T(8,128)S(1)} %get-tuple-element.89.refs_0_), channel_id=1, source_target_pairs={{0,3},{1,0},{2,1},{3,2},{4,7},{5,4},{6,5},{7,6},{8,11},{9,8},{10,9... | collective-permute-start | bytes 122888 | tf_op jit(solution)/shard_map/ppermute | solution.py:505
  76.0 2.4 %collective-permute-done.16.refs_1_ = f32[5,8,256]{2,1,0:T(8,128)S(1)} collective-permute-done((f32[5,8,256]{2,1,0:T(8,128)S(1)}, f32[5,8,256]{2,1,0:T(8,128)S(1)}, u32[]{:S(2)}, u32[]{:S(2)}) %collective-permute-start.16) | collective-permute-done | bytes 40992 | tf_op jit(solution)/shard_map/ppermute | solution.py:505
  78.4 1.2 %collective-permute-done.17.refs_2_ = f32[5,8,256]{2,1,0:T(8,128)S(1)} collective-permute-done((f32[5,8,256]{2,1,0:T(8,128)S(1)}, f32[5,8,256]{2,1,0:T(8,128)S(1)}, u32[]{:S(2)}, u32[]{:S(2)}) %collective-permute-start.17) | collective-permute-done | bytes 40992 | tf_op jit(solution)/shard_map/ppermute | solution.py:505
  79.6 1.2 %cell_params.5 = (f32[6,8,256]{2,1,0:T(8,128)S(1)}, f32[6,2,256]{2,1,0:T(2,128)}, f32[6,2,256]{2,1,0:T(2,128)}) custom-call(f32[5,8,256]{2,1,0:T(8,128)S(1)} %get-tuple-element.89.refs_0_, f32[5,8,256]{2,1,0:T(8,128)S(1)} %collective-permute-done.16.refs_1_, f32[5,8,256]{2,1,0:T(8,128)S(1)} %collective-permute-done.17.refs_2_, ...), custom_call_target="tpu_custom_call" | custom-call | tf_op jit(solution)/shard_map/cell_params/pallas_call | solution.py:461
  80.9 3.5 %final_relax.1 = f32[8,16,2,8,512]{4,3,2,1,0:T(8,128)} custom-call(s32[2]{0:T(128)S(1)} %pad_add_fusion.flags.refs_0_, f32[2,16,2,8,512]{4,3,2,1,0:T(8,128)S(1)} %get-tuple-element.86.m_cross, f32[4,16,2,8,512]{4,3,2,1,0:T(8,128)S(1)} %get-tuple-element.87.m_mid, f32[2,16,2,8,512]{4,3,2,1,0:T(8,128)S(1)} %get-tuple-element.88.m_in, ...), custom_call_target="tpu_custom_call" | custom-call | tf_op jit(solution)/shard_map/final_relax/pallas_call | solution.py:471
  (22 shorter events, 0.2 us)
Async XLA Ops:
  4.9 15.8 %collective-permute-start = (f32[2,16,2,8,512]{4,3,2,1,0:T(8,128)S(1)}, f32[2,16,2,8,512]{4,3,2,1,0:T(8,128)S(1)}, u32[]{:S(2)}, u32[]{:S(2)}) collective-permute-start(f32[2,16,2,8,512]{4,3,2,1,0:T(8,128)S(1)} %get-tuple-element.49.refs_0_.refs_3_), channel_id=1, source_target_pairs={{0,16},{12,28},{4,8},{8,4},{16,0},{28,12},{20,24},{24,20},{1,17},{... | collective-permute-start | bytes 3145736 | tf_op jit(solution)/shard_map/ppermute | solution.py:497
  7.9 12.8 %collective-permute-start.1 = (f32[2,16,2,8,512]{4,3,2,1,0:T(8,128)S(1)}, f32[2,16,2,8,512]{4,3,2,1,0:T(8,128)S(1)}, u32[]{:S(2)}, u32[]{:S(2)}) collective-permute-start(f32[2,16,2,8,512]{4,3,2,1,0:T(8,128)S(1)} %get-tuple-element.50.refs_2_.refs_5_), channel_id=1, source_target_pairs={{0,4},{4,0},{8,12},{12,8},{1,5},{5,1},{9,13},{13,9},{2,6},{6,2},{1... | collective-permute-start | bytes 3145736 | tf_op jit(solution)/shard_map/ppermute | solution.py:498
  20.7 13.3 %copy-start = (f32[4]{0:T(128)S(1)}, f32[4]{0:T(128)}, u32[]{:S(2)}) copy-start(f32[4]{0:T(128)} %refs_6_.5) | copy-start | bytes 52
  23.8 20.9 %collective-permute-start.2 = (f32[2,16,2,8,512]{4,3,2,1,0:T(8,128)S(1)}, f32[2,16,2,8,512]{4,3,2,1,0:T(8,128)S(1)}, u32[]{:S(2)}, u32[]{:S(2)}) collective-permute-start(f32[2,16,2,8,512]{4,3,2,1,0:T(8,128)S(1)} %get-tuple-element.57.refs_0_), channel_id=1, source_target_pairs={{0,16},{12,28},{4,8},{8,4},{16,0},{28,12},{20,24},{24,20},{1,17},{... | collective-permute-start | bytes 3145736 | tf_op jit(solution)/shard_map/ppermute | solution.py:497
  25.8 18.9 %collective-permute-start.3 = (f32[2,16,2,8,512]{4,3,2,1,0:T(8,128)S(1)}, f32[2,16,2,8,512]{4,3,2,1,0:T(8,128)S(1)}, u32[]{:S(2)}, u32[]{:S(2)}) collective-permute-start(f32[2,16,2,8,512]{4,3,2,1,0:T(8,128)S(1)} %get-tuple-element.58.refs_2_), channel_id=1, source_target_pairs={{0,4},{4,0},{8,12},{12,8},{1,5},{5,1},{9,13},{13,9},{2,6},{6,2},{1... | collective-permute-start | bytes 3145736 | tf_op jit(solution)/shard_map/ppermute | solution.py:498
  25.8 6.2 %collective-permute-start.4 = (f32[5,8,256]{2,1,0:T(8,128)S(1)}, f32[5,8,256]{2,1,0:T(8,128)S(1)}, u32[]{:S(2)}, u32[]{:S(2)}) collective-permute-start(f32[5,8,256]{2,1,0:T(8,128)S(1)} %get-tuple-element.59.refs_0_), channel_id=1, source_target_pairs={{0,1},{1,2},{2,3},{3,0},{4,5},{5,6},{6,7},{7,4},{8,9},{9,10},{10,1... | collective-permute-start | bytes 122888 | tf_op jit(solution)/shard_map/ppermute | solution.py:505
  27.4 6.2 %collective-permute-start.5 = (f32[5,8,256]{2,1,0:T(8,128)S(1)}, f32[5,8,256]{2,1,0:T(8,128)S(1)}, u32[]{:S(2)}, u32[]{:S(2)}) collective-permute-start(f32[5,8,256]{2,1,0:T(8,128)S(1)} %get-tuple-element.59.refs_0_), channel_id=1, source_target_pairs={{0,2},{1,3},{2,0},{3,1},{4,6},{5,7},{6,4},{7,5},{8,10},{9,11},{10,... | collective-permute-start | bytes 122888 | tf_op jit(solution)/shard_map/ppermute | solution.py:505
  30.0 4.0 %collective-permute-start.6 = (f32[5,8,256]{2,1,0:T(8,128)S(1)}, f32[5,8,256]{2,1,0:T(8,128)S(1)}, u32[]{:S(2)}, u32[]{:S(2)}) collective-permute-start(f32[5,8,256]{2,1,0:T(8,128)S(1)} %get-tuple-element.59.refs_0_), channel_id=1, source_target_pairs={{0,3},{1,0},{2,1},{3,2},{4,7},{5,4},{6,5},{7,6},{8,11},{9,8},{10,9... | collective-permute-start | bytes 122888 | tf_op jit(solution)/shard_map/ppermute | solution.py:505
  34.7 10.0 %collective-permute-start.7 = (f32[6,2,256]{2,1,0:T(2,128)S(1)}, f32[6,2,256]{2,1,0:T(2,128)S(1)}, u32[]{:S(2)}, u32[]{:S(2)}) collective-permute-start(f32[6,2,256]{2,1,0:T(2,128)S(1)} %get-tuple-element.61), channel_id=1, source_target_pairs={{0,16},{12,28},{4,8},{8,4},{16,0},{28,12},{20,24},{24,20},{1,17},{... | collective-permute-start | bytes 36872 | tf_op jit(solution)/shard_map/ppermute | solution.py:497
  35.8 9.0 %collective-permute-start.8 = (f32[6,2,256]{2,1,0:T(2,128)S(1)}, f32[6,2,256]{2,1,0:T(2,128)S(1)}, u32[]{:S(2)}, u32[]{:S(2)}) collective-permute-start(f32[6,2,256]{2,1,0:T(2,128)S(1)} %get-tuple-element.62), channel_id=1, source_target_pairs={{0,4},{4,0},{8,12},{12,8},{1,5},{5,1},{9,13},{13,9},{2,6},{6,2},{1... | collective-permute-start | bytes 36872 | tf_op jit(solution)/shard_map/ppermute | solution.py:498
  48.5 19.9 %collective-permute-start.10 = (f32[2,16,2,8,512]{4,3,2,1,0:T(8,128)S(1)}, f32[2,16,2,8,512]{4,3,2,1,0:T(8,128)S(1)}, u32[]{:S(2)}, u32[]{:S(2)}) collective-permute-start(f32[2,16,2,8,512]{4,3,2,1,0:T(8,128)S(1)} %get-tuple-element.74.refs_2_), channel_id=1, source_target_pairs={{0,4},{4,0},{8,12},{12,8},{1,5},{5,1},{9,13},{13,9},{2,6},{6,2},{1... | collective-permute-start | bytes 3145736 | tf_op jit(solution)/shard_map/ppermute | solution.py:498
  49.0 19.4 %collective-permute-start.9 = (f32[2,16,2,8,512]{4,3,2,1,0:T(8,128)S(1)}, f32[2,16,2,8,512]{4,3,2,1,0:T(8,128)S(1)}, u32[]{:S(2)}, u32[]{:S(2)}) collective-permute-start(f32[2,16,2,8,512]{4,3,2,1,0:T(8,128)S(1)} %get-tuple-element.73.refs_0_), channel_id=1, source_target_pairs={{0,16},{12,28},{4,8},{8,4},{16,0},{28,12},{20,24},{24,20},{1,17},{... | collective-permute-start | bytes 3145736 | tf_op jit(solution)/shard_map/ppermute | solution.py:497
  50.0 5.9 %collective-permute-start.11 = (f32[5,8,256]{2,1,0:T(8,128)S(1)}, f32[5,8,256]{2,1,0:T(8,128)S(1)}, u32[]{:S(2)}, u32[]{:S(2)}) collective-permute-start(f32[5,8,256]{2,1,0:T(8,128)S(1)} %get-tuple-element.75.refs_0_), channel_id=1, source_target_pairs={{0,1},{1,2},{2,3},{3,0},{4,5},{5,6},{6,7},{7,4},{8,9},{9,10},{10,1... | collective-permute-start | bytes 122888 | tf_op jit(solution)/shard_map/ppermute | solution.py:505
  50.8 5.9 %collective-permute-start.12 = (f32[5,8,256]{2,1,0:T(8,128)S(1)}, f32[5,8,256]{2,1,0:T(8,128)S(1)}, u32[]{:S(2)}, u32[]{:S(2)}) collective-permute-start(f32[5,8,256]{2,1,0:T(8,128)S(1)} %get-tuple-element.75.refs_0_), channel_id=1, source_target_pairs={{0,2},{1,3},{2,0},{3,1},{4,6},{5,7},{6,4},{7,5},{8,10},{9,11},{10,... | collective-permute-start | bytes 122888 | tf_op jit(solution)/shard_map/ppermute | solution.py:505
  53.7 4.0 %collective-permute-start.13 = (f32[5,8,256]{2,1,0:T(8,128)S(1)}, f32[5,8,256]{2,1,0:T(8,128)S(1)}, u32[]{:S(2)}, u32[]{:S(2)}) collective-permute-start(f32[5,8,256]{2,1,0:T(8,128)S(1)} %get-tuple-element.75.refs_0_), channel_id=1, source_target_pairs={{0,3},{1,0},{2,1},{3,2},{4,7},{5,4},{6,5},{7,6},{8,11},{9,8},{10,9... | collective-permute-start | bytes 122888 | tf_op jit(solution)/shard_map/ppermute | solution.py:505
  58.3 10.0 %collective-permute-start.14 = (f32[6,2,256]{2,1,0:T(2,128)S(1)}, f32[6,2,256]{2,1,0:T(2,128)S(1)}, u32[]{:S(2)}, u32[]{:S(2)}) collective-permute-start(f32[6,2,256]{2,1,0:T(2,128)S(1)} %get-tuple-element.76), channel_id=1, source_target_pairs={{0,16},{12,28},{4,8},{8,4},{16,0},{28,12},{20,24},{24,20},{1,17},{... | collective-permute-start | bytes 36872 | tf_op jit(solution)/shard_map/ppermute | solution.py:497
  59.4 9.0 %collective-permute-start.15 = (f32[6,2,256]{2,1,0:T(2,128)S(1)}, f32[6,2,256]{2,1,0:T(2,128)S(1)}, u32[]{:S(2)}, u32[]{:S(2)}) collective-permute-start(f32[6,2,256]{2,1,0:T(2,128)S(1)} %get-tuple-element.77), channel_id=1, source_target_pairs={{0,4},{4,0},{8,12},{12,8},{1,5},{5,1},{9,13},{13,9},{2,6},{6,2},{1... | collective-permute-start | bytes 36872 | tf_op jit(solution)/shard_map/ppermute | solution.py:498
  72.1 6.3 %collective-permute-start.16 = (f32[5,8,256]{2,1,0:T(8,128)S(1)}, f32[5,8,256]{2,1,0:T(8,128)S(1)}, u32[]{:S(2)}, u32[]{:S(2)}) collective-permute-start(f32[5,8,256]{2,1,0:T(8,128)S(1)} %get-tuple-element.89.refs_0_), channel_id=1, source_target_pairs={{0,1},{1,2},{2,3},{3,0},{4,5},{5,6},{6,7},{7,4},{8,9},{9,10},{10,1... | collective-permute-start | bytes 122888 | tf_op jit(solution)/shard_map/ppermute | solution.py:505
  72.9 6.8 %collective-permute-start.17 = (f32[5,8,256]{2,1,0:T(8,128)S(1)}, f32[5,8,256]{2,1,0:T(8,128)S(1)}, u32[]{:S(2)}, u32[]{:S(2)}) collective-permute-start(f32[5,8,256]{2,1,0:T(8,128)S(1)} %get-tuple-element.89.refs_0_), channel_id=1, source_target_pairs={{0,2},{1,3},{2,0},{3,1},{4,6},{5,7},{6,4},{7,5},{8,10},{9,11},{10,... | collective-permute-start | bytes 122888 | tf_op jit(solution)/shard_map/ppermute | solution.py:505
  75.0 4.6 %collective-permute-start.18 = (f32[5,8,256]{2,1,0:T(8,128)S(1)}, f32[5,8,256]{2,1,0:T(8,128)S(1)}, u32[]{:S(2)}, u32[]{:S(2)}) collective-permute-start(f32[5,8,256]{2,1,0:T(8,128)S(1)} %get-tuple-element.89.refs_0_), channel_id=1, source_target_pairs={{0,3},{1,0},{2,1},{3,2},{4,7},{5,4},{6,5},{7,6},{8,11},{9,8},{10,9... | collective-permute-start | bytes 122888 | tf_op jit(solution)/shard_map/ppermute | solution.py:505

commit v4 on v3

--- a/solution.py
+++ b/solution.py
@@ -184,7 +184,7 @@
 
 def param_kernel(total, count, *refs):
     parts = refs[:count]
-    codes, knudsen, inflow, out, out_low, out_high = refs[count:]
+    codes, knudsen, inflow, out, *edges = refs[count:]
     sums = [parts[0][m] for m in range(5)]
     for part in parts[1:]:
         sums = [s + part[m] for m, s in enumerate(sums)]
@@ -221,24 +221,75 @@
     rows = code.shape[0]
     for k, value in enumerate(params):
         out[k] = value
-        out_low[k] = value[:2]
-        out_high[k] = value[rows - 2 :]
-
-
-def load_kernel(flags, state, cross, middle, inside, sems):
+        if edges:
+            edges[0][k] = value[:2]
+            edges[1][k] = value[rows - 2 :]
+
+
+def row_copies(mirrored, state, target, first, sems):
     rows = state.shape[0]
     copies = []
+    for n in range(target.shape[0]):
+        place = jnp.where(mirrored > 0, rows - 1 - first - n, first + n)
+        copies.append(pltpu.make_async_copy(state.at[place], target.at[n], sems.at[n]))
+    return copies
+
+
+def load_kernel(order_in, codes_in, state, cross, inside, codes, table, factor, weights, coef,
+                order, raw, flat, cross_sems, inside_sems, more_sems):
+    rows, width = state.shape[0], order.shape[-1]
+    mirrored = lax.axis_index("gx") % 2
+    more = [
+        pltpu.make_async_copy(order_in, order, more_sems.at[0]),
+        pltpu.make_async_copy(codes_in, raw, more_sems.at[1]),
+    ]
+    copies = row_copies(mirrored, state, cross, 0, cross_sems)
+    copies += row_copies(mirrored, state, inside, rows - 2, inside_sems)
+    for copy in more + copies:
+        copy.start()
+    for copy in more:
+        copy.wait()
+
+    slots = jnp.broadcast_to(order[...], (SUB, width))
+    n_x = 2 * (slots // (VGY * VGZ)) - (VGX - 1)
+    n_y = 2 * (slots // VGZ % VGY) - (VGY - 1)
+    n_z = 2 * (2 * (slots % VGZ) - (VGZ - 1))
+    square = n_x * n_x + n_y * n_y + n_z * n_z
+    low_part = square % 8
+    whole = [n.astype(F32) for n in (n_x, n_y, n_z, square - low_part, low_part)]
+    whole = [jnp.ones_like(whole[0])] + whole
+
+    def pick(values, index):
+        out = jnp.zeros_like(values[0])
+        for k, value in enumerate(values):
+            out = jnp.where(index == k, value, out)
+        return out
+
+    line = lax.broadcasted_iota(jnp.int32, (SUB, width), 0)
+    moments = jnp.concatenate([pick(whole, line), jnp.zeros((SUB, width), F32)], axis=0)
+    moments = moments.astype(BF16)
+    weights[:, :width] = moments
+    weights[:, width:] = moments
+    table[...] = jnp.concatenate(
+        [pick(whole, (line + SUB * g) // 3) for g in range(FEATURES // SUB)], axis=0
+    ).astype(BF16)
+    slot = lax.broadcasted_iota(jnp.int32, (FEATURES, LANES), 0)
+    factor[...] = jnp.where((slot >= 18) & (slot < 21), 1.0, 0.0).astype(BF16)
+    turn = jnp.where(mirrored > 0, -1.0, 1.0)
+    for k, (n, scale) in enumerate(
+        ((whole[1] * turn, 0.1), (whole[2], 1.0 / 30.0), (whole[3], 1.0 / 30.0))
+    ):
+        reach = jnp.abs(n * UNIT * scale)
+        sign = jnp.where(n > 0.0, 1.0, -1.0)
+        coef[3 * k] = reach
+        coef[3 * k + 1] = 0.5 * sign * (1.0 - reach)
+        coef[3 * k + 2] = sign
+
+    for y in range(raw.shape[1]):
+        flat[:, y * raw.shape[2] : (y + 1) * raw.shape[2]] = raw[:, y, :]
     for r in range(rows):
-        place = jnp.where(flags[0] > 0, rows - 1 - r, r)
-        if r < 2:
-            target = cross.at[r]
-        elif r < rows - 2:
-            target = middle.at[r - 2]
-        else:
-            target = inside.at[r - rows + 2]
-        copies.append(pltpu.make_async_copy(state.at[place], target, sems.at[r]))
-    for copy in copies:
-        copy.start()
+        place = jnp.where(mirrored > 0, rows - 1 - r, r)
+        codes[r : r + 1, :] = flat[pl.ds(place, 1), :]
     for copy in copies:
         copy.wait()
 
@@ -252,7 +303,17 @@
         relax_rows(m_mid, middle, tall, 2, rows - 4, table, factor, kept)
         relax_rows(m_in, inside, tall, rows - 2, 2, table, factor, kept)
     else:
-        (cross, middle, inside, coef_ref, weights, out, e_cross, e_in, sums, ring, face_ring) = refs
+        (cross, inside, state, coef_ref, weights, middle, out, e_cross, e_in, sums,
+         ring, face_ring, sems) = refs
+        mirrored = lax.axis_index("gx") % 2
+        copies = row_copies(mirrored, state, middle, 2, sems)
+        for copy in copies:
+            copy.start()
+    yz_rows(cross, e_cross, True, 2, coef_ref, ring, face_ring)
+    yz_rows(inside, e_in, True, 2, coef_ref, ring, face_ring)
+    if not relax:
+        for copy in copies:
+            copy.wait()
     chunks = middle.shape[-1] // LANES
     inner = rows - 4
 
@@ -278,14 +339,12 @@
 
     lax.fori_loop(0, chunks * 16, along_x, 0, unroll=2)
     yz_rows(middle, out, False, inner, coef_ref, ring, face_ring)
-    yz_rows(cross, e_cross, True, 2, coef_ref, ring, face_ring)
-    yz_rows(inside, e_in, True, 2, coef_ref, ring, face_ring)
     row_moments(out, inner, weights, sums, 0)
 
 
-def edge_kernel(relax, rows, *refs):
+def edge_kernel(relax, rows, line, *refs):
     if relax:
-        (flags, h_cross, h_in, p_cross, p_in, table, factor, cross, middle, inside, e_cross,
+        (h_cross, h_in, p_cross, p_in, table, factor, cross, middle, inside, e_cross,
          e_in, coef_ref, weights, inner_sums, out_cross, out_in, sums,
          wide, tall, kept, low, high) = refs
         spread_features([p_cross[k] for k in range(6)], wide, tall, 2)
@@ -293,10 +352,11 @@
         spread_features([p_in[k] for k in range(6)], wide, tall, 2)
         relax_rows(h_in, high, tall, 0, 2, table, factor, kept)
     else:
-        (flags, low, high, cross, middle, inside, e_cross, e_in, coef_ref, weights,
+        (low, high, cross, middle, inside, e_cross, e_in, coef_ref, weights,
          inner_sums, out_cross, out_in, sums) = refs
     chunks = middle.shape[-1] // LANES
-    present = jnp.where(flags[1] > 0, 1.0, 0.0)
+    place = lax.axis_index("gx")
+    present = jnp.where((place == 0) | (place == line - 1), 0.0, 1.0)
 
     def along_x(i, carry):
         chunk, y = i // 16, i % 16
@@ -333,8 +393,9 @@
     row_moments(out_in, 2, weights, sums, rows - 2)
 
 
-def final_kernel(rows, flags, m_cross, m_mid, m_in, params, table, factor, out,
+def final_kernel(rows, m_cross, m_mid, m_in, params, table, factor, out,
                  wide, tall, kept, cross, middle, inside, sems):
+    mirrored = lax.axis_index("gx") % 2
     spread_features([params[k] for k in range(6)], wide, tall, rows)
     copies = []
     for source, target, first, count in (
@@ -343,7 +404,7 @@
         relax_rows(source, target, tall, first, count, table, factor, kept)
         for n in range(count):
             r = first + n
-            place = jnp.where(flags[0] > 0, rows - 1 - r, r)
+            place = jnp.where(mirrored > 0, rows - 1 - r, r)
             copy = pltpu.make_async_copy(target.at[n], out.at[place], sems.at[r])
             copy.start()
             copies.append(copy)
@@ -359,34 +420,6 @@
     cells = count_y * count_z
     state = distribution.reshape(rows, count_y, 2, SUB, width)
 
-    place = lax.axis_index("gx")
-    mirrored = place % 2
-    present = jnp.where((place == 0) | (place == line - 1), 0, 1)
-    flags = jnp.stack([mirrored, present]).astype(jnp.int32)
-    codes = cell_codes.reshape(rows, cells)
-    codes = jnp.where(mirrored > 0, codes[::-1], codes)
-
-    plane = VGY * VGZ
-    n_x = 2 * (velocity_order // plane) - (VGX - 1)
-    n_y = 2 * (velocity_order // VGZ % VGY) - (VGY - 1)
-    n_z = 2 * (2 * (velocity_order % VGZ) - (VGZ - 1))
-    square = n_x * n_x + n_y * n_y + n_z * n_z
-    ones = jnp.ones_like(n_x)
-    low_part = square % 8
-    whole = jnp.stack([ones, n_x, n_y, n_z, square - low_part, low_part]).astype(F32)
-    weights = jnp.pad(whole, ((0, 10), (0, 0))).astype(BF16)
-    weights = jnp.concatenate([weights, weights], axis=1)
-    table = jnp.repeat(whole, 3, axis=0)
-    table = jnp.pad(table, ((0, FEATURES - 18), (0, 0))).astype(BF16)
-    slot = lax.broadcasted_iota(jnp.int32, (FEATURES, LANES), 0)
-    factor = jnp.where((slot >= 18) & (slot < 21), 1.0, 0.0).astype(BF16)
-    coef = []
-    for n, scale in ((jnp.where(mirrored > 0, -n_x, n_x), 0.1), (n_y, 1.0 / 30.0), (n_z, 1.0 / 30.0)):
-        reach = jnp.abs(n.astype(F32) * UNIT * scale)
-        sign = jnp.where(n > 0, 1.0, -1.0)
-        coef.extend([reach, 0.5 * sign * (1.0 - reach), sign])
-    coef = jnp.broadcast_to(jnp.stack(coef)[:, None, :], (9, SUB, width))
-
     vmem = pl.BlockSpec(memory_space=pltpu.VMEM)
     smem = pl.BlockSpec(memory_space=pltpu.SMEM)
     hbm = pl.BlockSpec(memory_space=pltpu.HBM)
@@ -409,16 +442,34 @@
     def limits(mib):
         return pltpu.CompilerParams(vmem_limit_bytes=mib * 1024 * 1024)
 
+    def in_hbm(array):
+        return pltpu.with_memory_space_constraint(array, pltpu.HBM)
+
     def load():
         return pl.pallas_call(
             load_kernel,
-            in_specs=[smem, hbm],
-            out_specs=[vmem] * 3,
-            out_shape=[slab(2), slab(rows - 4), slab(2)],
-            scratch_shapes=[pltpu.SemaphoreType.DMA((rows,))],
+            in_specs=[hbm] * 3,
+            out_specs=[vmem] * 7,
+            out_shape=[
+                slab(2),
+                slab(2),
+                jax.ShapeDtypeStruct((rows, cells), jnp.int32),
+                jax.ShapeDtypeStruct((FEATURES, width), BF16),
+                jax.ShapeDtypeStruct((FEATURES, LANES), BF16),
+                jax.ShapeDtypeStruct((16, 2 * width), BF16),
+                jax.ShapeDtypeStruct((9, SUB, width), F32),
+            ],
+            scratch_shapes=[
+                pltpu.VMEM((1, width), jnp.int32),
+                pltpu.VMEM((rows, count_y, count_z), jnp.int32),
+                pltpu.VMEM((rows, cells), jnp.int32),
+                pltpu.SemaphoreType.DMA((2,)),
+                pltpu.SemaphoreType.DMA((2,)),
+                pltpu.SemaphoreType.DMA((2,)),
+            ],
             compiler_params=limits(6),
-            name="load_rows",
-        )(flags, pltpu.with_memory_space_constraint(state, pltpu.HBM))
+            name="load_edges",
+        )(in_hbm(velocity_order.reshape(1, width)), in_hbm(cell_codes), in_hbm(state))
 
     def inner(relax, state, params):
         sums = jax.ShapeDtypeStruct((5, rows - 4, cells), F32)
@@ -429,10 +480,12 @@
             scratch = feature_scratch(rows) + scratch
             args = (*state, params, table, factor, coef, weights)
         else:
+            out_shape = [slab(rows - 4)] + out_shape
+            scratch = scratch + [pltpu.SemaphoreType.DMA((rows - 4,))]
             args = (*state, coef, weights)
         return pl.pallas_call(
             functools.partial(inner_kernel, relax, rows),
-            in_specs=[vmem] * len(args),
+            in_specs=[vmem if relax or n != 2 else hbm for n in range(len(args))],
             out_specs=[vmem] * len(out_shape),
             out_shape=out_shape,
             scratch_shapes=scratch,
@@ -448,21 +501,21 @@
             args = (*params, table, factor, *args)
         args = (*halos, *args)
         return pl.pallas_call(
-            functools.partial(edge_kernel, relax, rows),
-            in_specs=[smem] + [vmem] * len(args),
+            functools.partial(edge_kernel, relax, rows, line),
+            in_specs=[vmem] * len(args),
             out_specs=[vmem] * 3,
             out_shape=[slab(2), slab(2), jax.ShapeDtypeStruct((5, rows, cells), F32)],
             scratch_shapes=scratch,
             compiler_params=limits(LIMIT_MIB),
             name="edge_relax" if relax else "edge_first",
-        )(flags, *args)
-
-    def cell_params(parts):
+        )(*args)
+
+    def cell_params(parts, *sizes):
         return pl.pallas_call(
             functools.partial(param_kernel, total, len(parts)),
             in_specs=[vmem] * (len(parts) + 1) + [smem, smem],
-            out_specs=[vmem] * 3,
-            out_shape=[jax.ShapeDtypeStruct((6, n, cells), F32) for n in (rows, 2, 2)],
+            out_specs=[vmem] * len(sizes),
+            out_shape=[jax.ShapeDtypeStruct((6, n, cells), F32) for n in sizes],
             compiler_params=limits(4),
             name="cell_params",
         )(*parts, codes, knudsen, inflow)
@@ -470,7 +523,7 @@
     def final(moved, params):
         return pl.pallas_call(
             functools.partial(final_kernel, rows),
-            in_specs=[smem] + [vmem] * 6,
+            in_specs=[vmem] * 6,
             out_specs=hbm,
             out_shape=slab(rows),
             scratch_shapes=feature_scratch(rows)
@@ -478,7 +531,7 @@
             + [pltpu.SemaphoreType.DMA((rows,))],
             compiler_params=limits(LIMIT_MIB),
             name="final_relax",
-        )(flags, *moved, params, table, factor)
+        )(*moved, params, table, factor)
 
     parts = lax.axis_size("groups")
     across = []
@@ -505,23 +558,20 @@
             parts.append(lax.ppermute(part, "vert", pairs))
         return parts
 
-    flags, codes, weights, table, factor, coef = lax.optimization_barrier(
-        (flags, codes, weights, table, factor, coef)
-    )
-    cross, middle, inside = load()
+    cross, inside, codes, table, factor, weights, coef = load()
     halos = exchange(cross, inside)
-    m_mid, e_cross, e_in, sums = inner(False, (cross, middle, inside), None)
+    middle, m_mid, e_cross, e_in, sums = inner(False, (cross, inside, in_hbm(state)), None)
     m_cross, m_in, sums = edge(
         False, halos, None, (cross, middle, inside), (e_cross, e_in), sums
     )
     for _ in range(1, STEPS):
         halos = exchange(m_cross, m_in)
-        params, p_cross, p_in = cell_params(gather(sums))
+        params, p_cross, p_in = cell_params(gather(sums), rows, 2, 2)
         p_halos = exchange(p_cross, p_in)
         moved = (m_cross, m_mid, m_in)
         *state, m_mid, e_cross, e_in, sums = inner(True, moved, params)
         m_cross, m_in, sums = edge(True, halos, p_halos, state, (e_cross, e_in), sums)
-    params, _, _ = cell_params(gather(sums))
+    (params,) = cell_params(gather(sums), rows)
     result = final((m_cross, m_mid, m_in), params)
     return result.reshape(rows, count_y, count_z, width)
 

time: 84.5 us -> 78.5 us (0.929)
  Pallas kernels: 44.6 us -> 40.8 us
  local copies, waits for them, and re-layouts: 1.22 us -> 0.01 us
    pallas_call x5, Pallas kernels: 16.8 us -> 13.5 us  [the longest x3 8.92 us: edge(): pl.pallas_call(functools.partial(edge_kernel, relax, rows, line), in_spec...]
    reshape x2 -> x0, local copies, waits for them, and re-layouts: 0.95 us -> none  [the longest x1 0.93 us: body(): codes = cell_codes.reshape(rows, cells)]
  transfers between devices with their start and end apart: 19 -> 19, of which waited for: 8 -> 8; matrix products, arithmetic and copies ran while one was open for 0% -> 0% of each run, Pallas kernels for 32% -> 34%
where the time goes in v4:
time: 78.5 us; the launch traced here: 78.3 us
  Pallas kernels  40.8 us (52%)
  starting transfers between devices  22.1 us (28%)
  waiting for transfers between devices  14.6 us (19%)
    pallas_call x3, Pallas kernels, inner(): pl.pallas_call(functools.partial(inner_kernel, relax, rows), in_specs=[vm...  25.4 us
    ppermute x9, starting transfers between devices, gather(): parts.append(lax.ppermute(part, 'vert', pairs))  13.3 us
    ppermute x9, waiting for transfers between devices, gather(): parts.append(lax.ppermute(part, 'vert', pairs))  9.38 us
    pallas_call x3, Pallas kernels, edge(): pl.pallas_call(functools.partial(edge_kernel, relax, rows, line), in_spec...  8.92 us
    ppermute x5, starting transfers between devices, exchange(): lax.ppermute(cross, ('groups', 'gx'), across)  8.25 us
    ppermute x5, waiting for transfers between devices, exchange(): lax.ppermute(cross, ('groups', 'gx'), across)  5.2 us
    pallas_call x1, Pallas kernels, final(): pl.pallas_call(functools.partial(final_kernel, rows), in_specs=[vmem] * 6...  2.94 us
    pallas_call x3, Pallas kernels, cell_params(): pl.pallas_call(functools.partial(param_kernel, total, len(parts)), in_spe...  1.92 us
  transfers between devices with their start and end apart: 19, of which 8 were waited for; matrix products, arithmetic and copies ran while one was open for 0% of the time, Pallas kernels for 34%

profile of v4, /device:TPU:0, one launch (start us, length us, event | category | flops | bytes accessed | tf_op | source)
XLA Modules:
  0.0 78.3 jit_solution(7597591698797862913)
XLA Ops:
  0.0 1.6 %load_edges.1 = (f32[2,16,2,8,512]{4,3,2,1,0:T(8,128)S(1)}, f32[2,16,2,8,512]{4,3,2,1,0:T(8,128)S(1)}, s32[8,256]{1,0:T(8,128)S(1)}, bf16[32,512]{1,0:T(8,128)(2...) custom-call(s32[1,512]{1,0:T(1,128)} %bitcast.5, ...), custom_call_target="tpu_custom_call" | custom-call | tf_op jit(solution)/shard_map/load_edges/pallas_call | solution.py:449
  1.6 3.0 %collective-permute-start = (f32[2,16,2,8,512]{4,3,2,1,0:T(8,128)S(1)}, f32[2,16,2,8,512]{4,3,2,1,0:T(8,128)S(1)}, u32[]{:S(2)}, u32[]{:S(2)}) collective-permute-start(f32[2,16,2,8,512]{4,3,2,1,0:T(8,128)S(1)} %get-tuple-element.46.refs_0_.refs_2_), channel_id=1, source_target_pairs={{0,16},{12,28},{4,8},{8,4},{16,0},{28,12},{20,24},{24,20},{1,17},{... | collective-permute-start | bytes 3145736 | tf_op jit(solution)/shard_map/ppermute | solution.py:550
  4.7 0.1 collective-permute-start.1
  4.7 7.5 %inner_first.1 = (f32[4,16,2,8,512]{4,3,2,1,0:T(8,128)S(1)}, f32[4,16,2,8,512]{4,3,2,1,0:T(8,128)S(1)}, f32[2,16,2,8,512]{4,3,2,1,0:T(8,128)S(1)}, f32[2,16,2,8,512]{4,3,2,1,0:T(8,128)S(1)}, f32[5,4,256]{2,1,0:T(4,128)S(1)}) custom-call(f32[2,16,2,8,512]{4,3,2,1,0:T(8,128)S(1)} %get-tuple-element.46.refs_0_.refs_2_, ...), custom_call_target="tpu_custom_call" | custom-call | tf_op jit(solution)/shard_map/inner_first/pallas_call | solution.py:486
  12.3 5.2 %collective-permute-done.refs_0_ = f32[2,16,2,8,512]{4,3,2,1,0:T(8,128)S(1)} collective-permute-done((f32[2,16,2,8,512]{4,3,2,1,0:T(8,128)S(1)}, f32[2,16,2,8,512]{4,3,2,1,0:T(8,128)S(1)}, u32[]{:S(2)}, u32[]{:S(2)}) %collective-permute-start) | collective-permute-done | bytes 1048608 | tf_op jit(solution)/shard_map/ppermute | solution.py:550
  17.4 0.0 collective-permute-done.1.refs_1_
  17.4 2.5 %edge_first.1 = (f32[2,16,2,8,512]{4,3,2,1,0:T(8,128)S(1)}, f32[2,16,2,8,512]{4,3,2,1,0:T(8,128)S(1)}, f32[5,8,256]{2,1,0:T(8,128)S(1)}) custom-call(f32[2,16,2,8,512]{4,3,2,1,0:T(8,128)S(1)} %collective-permute-done.refs_0_, f32[2,16,2,8,512]{4,3,2,1,0:T(8,128)S(1)} %collective-permute-done.1.refs_1_, ...), custom_call_target="tpu_custom_call" | custom-call | tf_op jit(solution)/shard_map/edge_first/pallas_call | solution.py:503
  20.0 2.0 %collective-permute-start.2 = (f32[2,16,2,8,512]{4,3,2,1,0:T(8,128)S(1)}, f32[2,16,2,8,512]{4,3,2,1,0:T(8,128)S(1)}, u32[]{:S(2)}, u32[]{:S(2)}) collective-permute-start(f32[2,16,2,8,512]{4,3,2,1,0:T(8,128)S(1)} %get-tuple-element.54.refs_0_), channel_id=1, source_target_pairs={{0,16},{12,28},{4,8},{8,4},{16,0},{28,12},{20,24},{24,20},{1,17},{... | collective-permute-start | bytes 3145736 | tf_op jit(solution)/shard_map/ppermute | solution.py:550
  22.0 0.0 collective-permute-start.3
  22.0 1.6 %collective-permute-start.4 = (f32[5,8,256]{2,1,0:T(8,128)S(1)}, f32[5,8,256]{2,1,0:T(8,128)S(1)}, u32[]{:S(2)}, u32[]{:S(2)}) collective-permute-start(f32[5,8,256]{2,1,0:T(8,128)S(1)} %get-tuple-element.56.refs_0_), channel_id=1, source_target_pairs={{0,1},{1,2},{2,3},{3,0},{4,5},{5,6},{6,7},{7,4},{8,9},{9,10},{10,1... | collective-permute-start | bytes 122888 | tf_op jit(solution)/shard_map/ppermute | solution.py:558
  23.6 2.6 %collective-permute-start.5 = (f32[5,8,256]{2,1,0:T(8,128)S(1)}, f32[5,8,256]{2,1,0:T(8,128)S(1)}, u32[]{:S(2)}, u32[]{:S(2)}) collective-permute-start(f32[5,8,256]{2,1,0:T(8,128)S(1)} %get-tuple-element.56.refs_0_), channel_id=1, source_target_pairs={{0,2},{1,3},{2,0},{3,1},{4,6},{5,7},{6,4},{7,5},{8,10},{9,11},{10,... | collective-permute-start | bytes 122888 | tf_op jit(solution)/shard_map/ppermute | solution.py:558
  26.2 1.3 %collective-permute-start.6 = (f32[5,8,256]{2,1,0:T(8,128)S(1)}, f32[5,8,256]{2,1,0:T(8,128)S(1)}, u32[]{:S(2)}, u32[]{:S(2)}) collective-permute-start(f32[5,8,256]{2,1,0:T(8,128)S(1)} %get-tuple-element.56.refs_0_), channel_id=1, source_target_pairs={{0,3},{1,0},{2,1},{3,2},{4,7},{5,4},{6,5},{7,6},{8,11},{9,8},{10,9... | collective-permute-start | bytes 122888 | tf_op jit(solution)/shard_map/ppermute | solution.py:558
  28.2 0.0 collective-permute-done.4.refs_1_
  28.2 1.6 %collective-permute-done.5.refs_2_ = f32[5,8,256]{2,1,0:T(8,128)S(1)} collective-permute-done((f32[5,8,256]{2,1,0:T(8,128)S(1)}, f32[5,8,256]{2,1,0:T(8,128)S(1)}, u32[]{:S(2)}, u32[]{:S(2)}) %collective-permute-start.5) | collective-permute-done | bytes 40992 | tf_op jit(solution)/shard_map/ppermute | solution.py:558
  29.8 0.4 collective-permute-done.6.refs_3_
  30.2 0.6 cell_params.3
  30.9 1.1 %collective-permute-start.7 = (f32[6,2,256]{2,1,0:T(2,128)S(1)}, f32[6,2,256]{2,1,0:T(2,128)S(1)}, u32[]{:S(2)}, u32[]{:S(2)}) collective-permute-start(f32[6,2,256]{2,1,0:T(2,128)S(1)} %get-tuple-element.58), channel_id=1, source_target_pairs={{0,16},{12,28},{4,8},{8,4},{16,0},{28,12},{20,24},{24,20},{1,17},{... | collective-permute-start | bytes 36872 | tf_op jit(solution)/shard_map/ppermute | solution.py:550
  31.9 0.0 collective-permute-start.8
  31.9 9.0 %inner_relax.2 = (f32[2,16,2,8,512]{4,3,2,1,0:T(8,128)S(1)}, f32[4,16,2,8,512]{4,3,2,1,0:T(8,128)S(1)}, f32[2,16,2,8,512]{4,3,2,1,0:T(8,128)S(1)}, f32[4,16,2,8,...) custom-call(f32[2,16,2,8,512]{4,3,2,1,0:T(8,128)S(1)} %get-tuple-ele, ...), custom_call_target="tpu_custom_call" | custom-call | tf_op jit(solution)/shard_map/inner_relax/pallas_call | solution.py:486
  40.9 0.0 collective-permute-done.7.refs_2_
  40.9 0.0 collective-permute-done.8.refs_3_
  40.9 0.0 collective-permute-done.2.refs_0_
  40.9 0.0 collective-permute-done.3.refs_1_
  40.9 3.2 %edge_relax.2 = (f32[2,16,2,8,512]{4,3,2,1,0:T(8,128)S(1)}, f32[2,16,2,8,512]{4,3,2,1,0:T(8,128)S(1)}, f32[5,8,256]{2,1,0:T(8,128)S(1)}) custom-call(f32[2,16,2,8,512]{4,3,2,1,0:T(8,128)S(1)} %collective-permute-done.2.refs_0_, f32[2,16,2,8,512]{4,3,2,1,0:T(8,128)S(1)} %collective-permute-done.3.refs_1_, f32[6,2,256]{2,1,0:T(2,128)S(1)} %collective-permute-done.7.refs_2_, ...), custom_call_target="tpu_custom_call" | custom-call | tf_op jit(solution)/shard_map/edge_relax/pallas_call | solution.py:503
  44.1 0.5 collective-permute-start.10
  44.6 1.0 %collective-permute-start.9 = (f32[2,16,2,8,512]{4,3,2,1,0:T(8,128)S(1)}, f32[2,16,2,8,512]{4,3,2,1,0:T(8,128)S(1)}, u32[]{:S(2)}, u32[]{:S(2)}) collective-permute-start(f32[2,16,2,8,512]{4,3,2,1,0:T(8,128)S(1)} %get-tuple-element.70.refs_0_), channel_id=1, source_target_pairs={{0,16},{12,28},{4,8},{8,4},{16,0},{28,12},{20,24},{24,20},{1,17},{... | collective-permute-start | bytes 3145736 | tf_op jit(solution)/shard_map/ppermute | solution.py:550
  45.7 0.9 %collective-permute-start.11 = (f32[5,8,256]{2,1,0:T(8,128)S(1)}, f32[5,8,256]{2,1,0:T(8,128)S(1)}, u32[]{:S(2)}, u32[]{:S(2)}) collective-permute-start(f32[5,8,256]{2,1,0:T(8,128)S(1)} %get-tuple-element.72.refs_0_), channel_id=1, source_target_pairs={{0,1},{1,2},{2,3},{3,0},{4,5},{5,6},{6,7},{7,4},{8,9},{9,10},{10,1... | collective-permute-start | bytes 122888 | tf_op jit(solution)/shard_map/ppermute | solution.py:558
  46.5 2.8 %collective-permute-start.12 = (f32[5,8,256]{2,1,0:T(8,128)S(1)}, f32[5,8,256]{2,1,0:T(8,128)S(1)}, u32[]{:S(2)}, u32[]{:S(2)}) collective-permute-start(f32[5,8,256]{2,1,0:T(8,128)S(1)} %get-tuple-element.72.refs_0_), channel_id=1, source_target_pairs={{0,2},{1,3},{2,0},{3,1},{4,6},{5,7},{6,4},{7,5},{8,10},{9,11},{10,... | collective-permute-start | bytes 122888 | tf_op jit(solution)/shard_map/ppermute | solution.py:558
  49.4 0.2 collective-permute-start.13
  49.6 2.0 %collective-permute-done.11.refs_1_ = f32[5,8,256]{2,1,0:T(8,128)S(1)} collective-permute-done((f32[5,8,256]{2,1,0:T(8,128)S(1)}, f32[5,8,256]{2,1,0:T(8,128)S(1)}, u32[]{:S(2)}, u32[]{:S(2)}) %collective-permute-start.11) | collective-permute-done | bytes 40992 | tf_op jit(solution)/shard_map/ppermute | solution.py:558
  51.6 0.8 %collective-permute-done.12.refs_2_ = f32[5,8,256]{2,1,0:T(8,128)S(1)} collective-permute-done((f32[5,8,256]{2,1,0:T(8,128)S(1)}, f32[5,8,256]{2,1,0:T(8,128)S(1)}, u32[]{:S(2)}, u32[]{:S(2)}) %collective-permute-start.12) | collective-permute-done | bytes 40992 | tf_op jit(solution)/shard_map/ppermute | solution.py:558
  52.4 1.0 %collective-permute-done.13.refs_3_ = f32[5,8,256]{2,1,0:T(8,128)S(1)} collective-permute-done((f32[5,8,256]{2,1,0:T(8,128)S(1)}, f32[5,8,256]{2,1,0:T(8,128)S(1)}, u32[]{:S(2)}, u32[]{:S(2)}) %collective-permute-start.13) | collective-permute-done | bytes 40992 | tf_op jit(solution)/shard_map/ppermute | solution.py:558
  53.4 0.6 cell_params.4
  54.0 1.1 %collective-permute-start.14 = (f32[6,2,256]{2,1,0:T(2,128)S(1)}, f32[6,2,256]{2,1,0:T(2,128)S(1)}, u32[]{:S(2)}, u32[]{:S(2)}) collective-permute-start(f32[6,2,256]{2,1,0:T(2,128)S(1)} %get-tuple-element.73), channel_id=1, source_target_pairs={{0,16},{12,28},{4,8},{8,4},{16,0},{28,12},{20,24},{24,20},{1,17},{... | collective-permute-start | bytes 36872 | tf_op jit(solution)/shard_map/ppermute | solution.py:550
  55.1 0.0 collective-permute-start.15
  55.1 8.9 %inner_relax.3 = (f32[2,16,2,8,512]{4,3,2,1,0:T(8,128)S(1)}, f32[4,16,2,8,512]{4,3,2,1,0:T(8,128)S(1)}, f32[2,16,2,8,512]{4,3,2,1,0:T(8,128)S(1)}, f32[4,16,2,8,...) custom-call(f32[2,16,2,8,512]{4,3,2,1,0:T(8,128)S(1)} %get-tuple-ele, ...), custom_call_target="tpu_custom_call" | custom-call | tf_op jit(solution)/shard_map/inner_relax/pallas_call | solution.py:486
  64.1 0.0 collective-permute-done.14.refs_2_
  64.1 0.0 collective-permute-done.15.refs_3_
  64.1 0.0 collective-permute-done.10.refs_1_
  64.1 0.0 collective-permute-done.9.refs_0_
  64.1 3.2 %edge_relax.3 = (f32[2,16,2,8,512]{4,3,2,1,0:T(8,128)S(1)}, f32[2,16,2,8,512]{4,3,2,1,0:T(8,128)S(1)}, f32[5,8,256]{2,1,0:T(8,128)S(1)}) custom-call(f32[2,16,2,8,512]{4,3,2,1,0:T(8,128)S(1)} %collective-permute-done.9.refs_0_, f32[2,16,2,8,512]{4,3,2,1,0:T(8,128)S(1)} %collective-permute-done.10.refs_1_, f32[6,2,256]{2,1,0:T(2,128)S(1)} %collective-permute-done.14.refs_2_, ...), custom_call_target="tpu_custom_call" | custom-call | tf_op jit(solution)/shard_map/edge_relax/pallas_call | solution.py:503
  67.3 0.7 collective-permute-start.16
  68.0 2.2 %collective-permute-start.17 = (f32[5,8,256]{2,1,0:T(8,128)S(1)}, f32[5,8,256]{2,1,0:T(8,128)S(1)}, u32[]{:S(2)}, u32[]{:S(2)}) collective-permute-start(f32[5,8,256]{2,1,0:T(8,128)S(1)} %get-tuple-element.86.refs_0_), channel_id=1, source_target_pairs={{0,2},{1,3},{2,0},{3,1},{4,6},{5,7},{6,4},{7,5},{8,10},{9,11},{10,... | collective-permute-start | bytes 122888 | tf_op jit(solution)/shard_map/ppermute | solution.py:558
  70.1 1.0 %collective-permute-start.18 = (f32[5,8,256]{2,1,0:T(8,128)S(1)}, f32[5,8,256]{2,1,0:T(8,128)S(1)}, u32[]{:S(2)}, u32[]{:S(2)}) collective-permute-start(f32[5,8,256]{2,1,0:T(8,128)S(1)} %get-tuple-element.86.refs_0_), channel_id=1, source_target_pairs={{0,3},{1,0},{2,1},{3,2},{4,7},{5,4},{6,5},{7,6},{8,11},{9,8},{10,9... | collective-permute-start | bytes 122888 | tf_op jit(solution)/shard_map/ppermute | solution.py:558
  71.2 2.4 %collective-permute-done.16.refs_1_ = f32[5,8,256]{2,1,0:T(8,128)S(1)} collective-permute-done((f32[5,8,256]{2,1,0:T(8,128)S(1)}, f32[5,8,256]{2,1,0:T(8,128)S(1)}, u32[]{:S(2)}, u32[]{:S(2)}) %collective-permute-start.16) | collective-permute-done | bytes 40992 | tf_op jit(solution)/shard_map/ppermute | solution.py:558
  73.6 1.2 %collective-permute-done.17.refs_2_ = f32[5,8,256]{2,1,0:T(8,128)S(1)} collective-permute-done((f32[5,8,256]{2,1,0:T(8,128)S(1)}, f32[5,8,256]{2,1,0:T(8,128)S(1)}, u32[]{:S(2)}, u32[]{:S(2)}) %collective-permute-start.17) | collective-permute-done | bytes 40992 | tf_op jit(solution)/shard_map/ppermute | solution.py:558
  74.7 0.6 cell_params.5.params
  75.4 2.9 %final_relax.1 = f32[8,16,2,8,512]{4,3,2,1,0:T(8,128)} custom-call(f32[2,16,2,8,512]{4,3,2,1,0:T(8,128)S(1)} %get-tuple-element.83.m_cross, f32[4,16,2,8,512]{4,3,2,1,0:T(8,128)S(1)} %get-tuple-element.84.m_mid, f32[2,16,2,8,512]{4,3,2,1,0:T(8,128)S(1)} %get-tuple-element.85.m_in, f32[6,8,256]{2,1,0:T(8,128)S(1)} %cell_params.5.params, ...), custom_call_target="tpu_custom_call" | custom-call | tf_op jit(solution)/shard_map/final_relax/pallas_call | solution.py:524
  (3 shorter events, 0.0 us)
Async XLA Ops:
  1.6 15.8 %collective-permute-start = (f32[2,16,2,8,512]{4,3,2,1,0:T(8,128)S(1)}, f32[2,16,2,8,512]{4,3,2,1,0:T(8,128)S(1)}, u32[]{:S(2)}, u32[]{:S(2)}) collective-permute-start(f32[2,16,2,8,512]{4,3,2,1,0:T(8,128)S(1)} %get-tuple-element.46.refs_0_.refs_2_), channel_id=1, source_target_pairs={{0,16},{12,28},{4,8},{8,4},{16,0},{28,12},{20,24},{24,20},{1,17},{... | collective-permute-start | bytes 3145736 | tf_op jit(solution)/shard_map/ppermute | solution.py:550
  4.7 12.8 %collective-permute-start.1 = (f32[2,16,2,8,512]{4,3,2,1,0:T(8,128)S(1)}, f32[2,16,2,8,512]{4,3,2,1,0:T(8,128)S(1)}, u32[]{:S(2)}, u32[]{:S(2)}) collective-permute-start(f32[2,16,2,8,512]{4,3,2,1,0:T(8,128)S(1)} %get-tuple-element.47.refs_1_.refs_4_), channel_id=1, source_target_pairs={{0,4},{4,0},{8,12},{12,8},{1,5},{5,1},{9,13},{13,9},{2,6},{6,2},{1... | collective-permute-start | bytes 3145736 | tf_op jit(solution)/shard_map/ppermute | solution.py:551
  17.4 12.8 %copy-start = (f32[4]{0:T(128)S(1)}, f32[4]{0:T(128)}, u32[]{:S(2)}) copy-start(f32[4]{0:T(128)} %refs_6_.5) | copy-start | bytes 52
  20.0 20.9 %collective-permute-start.2 = (f32[2,16,2,8,512]{4,3,2,1,0:T(8,128)S(1)}, f32[2,16,2,8,512]{4,3,2,1,0:T(8,128)S(1)}, u32[]{:S(2)}, u32[]{:S(2)}) collective-permute-start(f32[2,16,2,8,512]{4,3,2,1,0:T(8,128)S(1)} %get-tuple-element.54.refs_0_), channel_id=1, source_target_pairs={{0,16},{12,28},{4,8},{8,4},{16,0},{28,12},{20,24},{24,20},{1,17},{... | collective-permute-start | bytes 3145736 | tf_op jit(solution)/shard_map/ppermute | solution.py:550
  22.0 18.9 %collective-permute-start.3 = (f32[2,16,2,8,512]{4,3,2,1,0:T(8,128)S(1)}, f32[2,16,2,8,512]{4,3,2,1,0:T(8,128)S(1)}, u32[]{:S(2)}, u32[]{:S(2)}) collective-permute-start(f32[2,16,2,8,512]{4,3,2,1,0:T(8,128)S(1)} %get-tuple-element.55.refs_2_), channel_id=1, source_target_pairs={{0,4},{4,0},{8,12},{12,8},{1,5},{5,1},{9,13},{13,9},{2,6},{6,2},{1... | collective-permute-start | bytes 3145736 | tf_op jit(solution)/shard_map/ppermute | solution.py:551
  22.0 6.2 %collective-permute-start.4 = (f32[5,8,256]{2,1,0:T(8,128)S(1)}, f32[5,8,256]{2,1,0:T(8,128)S(1)}, u32[]{:S(2)}, u32[]{:S(2)}) collective-permute-start(f32[5,8,256]{2,1,0:T(8,128)S(1)} %get-tuple-element.56.refs_0_), channel_id=1, source_target_pairs={{0,1},{1,2},{2,3},{3,0},{4,5},{5,6},{6,7},{7,4},{8,9},{9,10},{10,1... | collective-permute-start | bytes 122888 | tf_op jit(solution)/shard_map/ppermute | solution.py:558
  23.6 6.2 %collective-permute-start.5 = (f32[5,8,256]{2,1,0:T(8,128)S(1)}, f32[5,8,256]{2,1,0:T(8,128)S(1)}, u32[]{:S(2)}, u32[]{:S(2)}) collective-permute-start(f32[5,8,256]{2,1,0:T(8,128)S(1)} %get-tuple-element.56.refs_0_), channel_id=1, source_target_pairs={{0,2},{1,3},{2,0},{3,1},{4,6},{5,7},{6,4},{7,5},{8,10},{9,11},{10,... | collective-permute-start | bytes 122888 | tf_op jit(solution)/shard_map/ppermute | solution.py:558
  26.2 4.0 %collective-permute-start.6 = (f32[5,8,256]{2,1,0:T(8,128)S(1)}, f32[5,8,256]{2,1,0:T(8,128)S(1)}, u32[]{:S(2)}, u32[]{:S(2)}) collective-permute-start(f32[5,8,256]{2,1,0:T(8,128)S(1)} %get-tuple-element.56.refs_0_), channel_id=1, source_target_pairs={{0,3},{1,0},{2,1},{3,2},{4,7},{5,4},{6,5},{7,6},{8,11},{9,8},{10,9... | collective-permute-start | bytes 122888 | tf_op jit(solution)/shard_map/ppermute | solution.py:558
  30.9 10.0 %collective-permute-start.7 = (f32[6,2,256]{2,1,0:T(2,128)S(1)}, f32[6,2,256]{2,1,0:T(2,128)S(1)}, u32[]{:S(2)}, u32[]{:S(2)}) collective-permute-start(f32[6,2,256]{2,1,0:T(2,128)S(1)} %get-tuple-element.58), channel_id=1, source_target_pairs={{0,16},{12,28},{4,8},{8,4},{16,0},{28,12},{20,24},{24,20},{1,17},{... | collective-permute-start | bytes 36872 | tf_op jit(solution)/shard_map/ppermute | solution.py:550
  31.9 9.0 %collective-permute-start.8 = (f32[6,2,256]{2,1,0:T(2,128)S(1)}, f32[6,2,256]{2,1,0:T(2,128)S(1)}, u32[]{:S(2)}, u32[]{:S(2)}) collective-permute-start(f32[6,2,256]{2,1,0:T(2,128)S(1)} %get-tuple-element.59), channel_id=1, source_target_pairs={{0,4},{4,0},{8,12},{12,8},{1,5},{5,1},{9,13},{13,9},{2,6},{6,2},{1... | collective-permute-start | bytes 36872 | tf_op jit(solution)/shard_map/ppermute | solution.py:551
  44.1 19.9 %collective-permute-start.10 = (f32[2,16,2,8,512]{4,3,2,1,0:T(8,128)S(1)}, f32[2,16,2,8,512]{4,3,2,1,0:T(8,128)S(1)}, u32[]{:S(2)}, u32[]{:S(2)}) collective-permute-start(f32[2,16,2,8,512]{4,3,2,1,0:T(8,128)S(1)} %get-tuple-element.71.refs_2_), channel_id=1, source_target_pairs={{0,4},{4,0},{8,12},{12,8},{1,5},{5,1},{9,13},{13,9},{2,6},{6,2},{1... | collective-permute-start | bytes 3145736 | tf_op jit(solution)/shard_map/ppermute | solution.py:551
  44.6 19.5 %collective-permute-start.9 = (f32[2,16,2,8,512]{4,3,2,1,0:T(8,128)S(1)}, f32[2,16,2,8,512]{4,3,2,1,0:T(8,128)S(1)}, u32[]{:S(2)}, u32[]{:S(2)}) collective-permute-start(f32[2,16,2,8,512]{4,3,2,1,0:T(8,128)S(1)} %get-tuple-element.70.refs_0_), channel_id=1, source_target_pairs={{0,16},{12,28},{4,8},{8,4},{16,0},{28,12},{20,24},{24,20},{1,17},{... | collective-permute-start | bytes 3145736 | tf_op jit(solution)/shard_map/ppermute | solution.py:550
  45.7 5.9 %collective-permute-start.11 = (f32[5,8,256]{2,1,0:T(8,128)S(1)}, f32[5,8,256]{2,1,0:T(8,128)S(1)}, u32[]{:S(2)}, u32[]{:S(2)}) collective-permute-start(f32[5,8,256]{2,1,0:T(8,128)S(1)} %get-tuple-element.72.refs_0_), channel_id=1, source_target_pairs={{0,1},{1,2},{2,3},{3,0},{4,5},{5,6},{6,7},{7,4},{8,9},{9,10},{10,1... | collective-permute-start | bytes 122888 | tf_op jit(solution)/shard_map/ppermute | solution.py:558
  46.5 5.9 %collective-permute-start.12 = (f32[5,8,256]{2,1,0:T(8,128)S(1)}, f32[5,8,256]{2,1,0:T(8,128)S(1)}, u32[]{:S(2)}, u32[]{:S(2)}) collective-permute-start(f32[5,8,256]{2,1,0:T(8,128)S(1)} %get-tuple-element.72.refs_0_), channel_id=1, source_target_pairs={{0,2},{1,3},{2,0},{3,1},{4,6},{5,7},{6,4},{7,5},{8,10},{9,11},{10,... | collective-permute-start | bytes 122888 | tf_op jit(solution)/shard_map/ppermute | solution.py:558
  49.4 4.0 %collective-permute-start.13 = (f32[5,8,256]{2,1,0:T(8,128)S(1)}, f32[5,8,256]{2,1,0:T(8,128)S(1)}, u32[]{:S(2)}, u32[]{:S(2)}) collective-permute-start(f32[5,8,256]{2,1,0:T(8,128)S(1)} %get-tuple-element.72.refs_0_), channel_id=1, source_target_pairs={{0,3},{1,0},{2,1},{3,2},{4,7},{5,4},{6,5},{7,6},{8,11},{9,8},{10,9... | collective-permute-start | bytes 122888 | tf_op jit(solution)/shard_map/ppermute | solution.py:558
  54.0 10.1 %collective-permute-start.14 = (f32[6,2,256]{2,1,0:T(2,128)S(1)}, f32[6,2,256]{2,1,0:T(2,128)S(1)}, u32[]{:S(2)}, u32[]{:S(2)}) collective-permute-start(f32[6,2,256]{2,1,0:T(2,128)S(1)} %get-tuple-element.73), channel_id=1, source_target_pairs={{0,16},{12,28},{4,8},{8,4},{16,0},{28,12},{20,24},{24,20},{1,17},{... | collective-permute-start | bytes 36872 | tf_op jit(solution)/shard_map/ppermute | solution.py:550
  55.1 9.0 %collective-permute-start.15 = (f32[6,2,256]{2,1,0:T(2,128)S(1)}, f32[6,2,256]{2,1,0:T(2,128)S(1)}, u32[]{:S(2)}, u32[]{:S(2)}) collective-permute-start(f32[6,2,256]{2,1,0:T(2,128)S(1)} %get-tuple-element.74), channel_id=1, source_target_pairs={{0,4},{4,0},{8,12},{12,8},{1,5},{5,1},{9,13},{13,9},{2,6},{6,2},{1... | collective-permute-start | bytes 36872 | tf_op jit(solution)/shard_map/ppermute | solution.py:551
  67.3 6.3 %collective-permute-start.16 = (f32[5,8,256]{2,1,0:T(8,128)S(1)}, f32[5,8,256]{2,1,0:T(8,128)S(1)}, u32[]{:S(2)}, u32[]{:S(2)}) collective-permute-start(f32[5,8,256]{2,1,0:T(8,128)S(1)} %get-tuple-element.86.refs_0_), channel_id=1, source_target_pairs={{0,1},{1,2},{2,3},{3,0},{4,5},{5,6},{6,7},{7,4},{8,9},{9,10},{10,1... | collective-permute-start | bytes 122888 | tf_op jit(solution)/shard_map/ppermute | solution.py:558
  68.0 6.8 %collective-permute-start.17 = (f32[5,8,256]{2,1,0:T(8,128)S(1)}, f32[5,8,256]{2,1,0:T(8,128)S(1)}, u32[]{:S(2)}, u32[]{:S(2)}) collective-permute-start(f32[5,8,256]{2,1,0:T(8,128)S(1)} %get-tuple-element.86.refs_0_), channel_id=1, source_target_pairs={{0,2},{1,3},{2,0},{3,1},{4,6},{5,7},{6,4},{7,5},{8,10},{9,11},{10,... | collective-permute-start | bytes 122888 | tf_op jit(solution)/shard_map/ppermute | solution.py:558
  70.1 4.6 %collective-permute-start.18 = (f32[5,8,256]{2,1,0:T(8,128)S(1)}, f32[5,8,256]{2,1,0:T(8,128)S(1)}, u32[]{:S(2)}, u32[]{:S(2)}) collective-permute-start(f32[5,8,256]{2,1,0:T(8,128)S(1)} %get-tuple-element.86.refs_0_), channel_id=1, source_target_pairs={{0,3},{1,0},{2,1},{3,2},{4,7},{5,4},{6,5},{7,6},{8,11},{9,8},{10,9... | collective-permute-start | bytes 122888 | tf_op jit(solution)/shard_map/ppermute | solution.py:558

commit v5 on v4

--- a/solution.py
+++ b/solution.py
@@ -50,11 +50,11 @@
         store(n, v if change else cells[n] - v)
 
 
-def yz_row(source, out, fresh, row, lanes, coef, ring, face_ring):
+def yz_row(source, out, fresh, row, lanes, coef):
     reach_y, lean_y, ahead_y = coef[3], coef[4], coef[5] > 0.0
     reach_z, lean_z, ahead_z = coef[6], coef[7], coef[8] > 0.0
     count = 16
-    cells, steps, faces, z_faces = {}, {}, {}, {}
+    cells, steps, faces = {}, {}, {}
 
     def cell(y, t):
         y %= count
@@ -74,39 +74,40 @@
             faces[y, t] = cell(y, t) + lean_y * minmod(step(y - 1, t), step(y, t))
         return faces[y, t]
 
-    def lay(y):
-        for t in range(2):
-            ring[y, 8 + 8 * t : 16 + 8 * t, :] = cell(y, t)
-        ring[y, 7:8, :] = source[row, y, 1, 7:8, lanes]
-        ring[y, 24:25, :] = source[row, y, 0, 0:1, lanes]
-
-    def lay_faces(y):
-        for t in range(2):
-            below = ring[y, 7 + 8 * t : 15 + 8 * t, :]
-            above = ring[y, 9 + 8 * t : 17 + 8 * t, :]
-            here = cell(y, t)
-            z_faces[y, t] = here + lean_z * minmod(here - below, above - here)
-            face_ring[y, 8 + 8 * t : 16 + 8 * t, :] = z_faces[y, t]
-        face_ring[y, 7:8, :] = face_ring[y, 23:24, :]
-        face_ring[y, 24:25, :] = face_ring[y, 8:9, :]
-
-    def finish(y):
-        for t in range(2):
-            below = face_ring[y, 7 + 8 * t : 15 + 8 * t, :]
-            above = face_ring[y, 9 + 8 * t : 17 + 8 * t, :]
+    def up(v):
+        return pltpu.roll(v, SUB - 1, 0)
+
+    def down(v):
+        return pltpu.roll(v, 1, 0)
+
+    for y in range(count):
+        even, odd = cell(y, 0), cell(y, 1)
+        step_even = odd - even
+        step_odd = up(even) - odd
+        face_even = even + lean_z * minmod(down(step_odd), step_even)
+        face_odd = odd + lean_z * minmod(step_even, step_odd)
+        winds = (
+            jnp.where(ahead_z, down(face_odd), face_odd),
+            jnp.where(ahead_z, face_even, up(face_even)),
+        )
+        for t, z_face in enumerate((face_even, face_odd)):
             v = cell(y, t) if fresh else out[row, y, t, :, lanes]
-            v -= reach_z * (z_faces[y, t] - jnp.where(ahead_z, below, above))
+            v -= reach_z * (z_face - winds[t])
             upwind = jnp.where(ahead_y, face(y - 1, t), face(y + 1, t))
             v -= reach_y * (face(y, t) - upwind)
             out[row, y, t, :, lanes] = v
 
-    for y in range(count + 2):
-        if y < count:
-            lay(y)
-        if 0 <= y - 1 < count:
-            lay_faces(y - 1)
-        if 0 <= y - 2 < count:
-            finish(y - 2)
+
+def yz_rows(source, out, fresh, rows, coef_ref):
+    chunks = source.shape[-1] // LANES
+
+    def one(i, carry):
+        chunk, row = i // rows, i % rows
+        lanes = lanes_of(chunk)
+        yz_row(source, out, fresh, row, lanes, coefs_of(coef_ref, lanes))
+        return carry
+
+    lax.fori_loop(0, chunks * rows, one, 0, unroll=2)
 
 
 def row_moments(out, count, weights, sums, first):
@@ -124,19 +125,6 @@
         sums[4, place : place + 1, :] = part[4:5] + part[5:6]
 
 
-def yz_rows(source, out, fresh, rows, coef_ref, ring, face_ring):
-    chunks = source.shape[-1] // LANES
-
-    def one(i, carry):
-        chunk, row = i // rows, i % rows
-        lanes = lanes_of(chunk)
-        coef = coefs_of(coef_ref, lanes)
-        yz_row(source, out, fresh, row, lanes, coef, ring, face_ring)
-        return carry
-
-    lax.fori_loop(0, chunks * rows, one, 0)
-
-
 def three_parts(value):
     high = value.astype(BF16).astype(F32)
     rest = value - high
@@ -176,7 +164,11 @@
                     lanes = pl.ds(pair * PAIR + half * LANES, LANES)
                     shape = jnp.exp2(power[:, half * LANES : (half + 1) * LANES])
                     shape = shape.reshape(16, 2, SUB, LANES)
-                    out[row, :, :, :, lanes] = kept[u] * source[row, :, :, :, lanes] + shape
+                    value = kept[u] * source[row, :, :, :, lanes] + shape
+                    if callable(out):
+                        out(row, 2 * pair + half, value)
+                    else:
+                        out[row, :, :, :, lanes] = value
         return carry
 
     lax.fori_loop(0, rows // 2, two, 0)
@@ -226,25 +218,43 @@
             edges[1][k] = value[rows - 2 :]
 
 
-def row_copies(mirrored, state, target, first, sems):
-    rows = state.shape[0]
+def row_copies(mirrored, whole, staged, first, sems, out=False):
+    rows = whole.shape[0]
     copies = []
-    for n in range(target.shape[0]):
+    for n in range(staged.shape[0]):
         place = jnp.where(mirrored > 0, rows - 1 - first - n, first + n)
-        copies.append(pltpu.make_async_copy(state.at[place], target.at[n], sems.at[n]))
+        for c in range(staged.shape[2]):
+            far = whole.at[place, :, :, pl.ds(c * LANES, LANES)]
+            near = staged.at[n, :, c]
+            pair = (near, far) if out else (far, near)
+            copies.append(pltpu.make_async_copy(*pair, sems.at[n, c]))
     return copies
 
 
+def unstage(staged, out):
+    count = staged.shape[1]
+
+    def one(i, carry):
+        n, y = i // count, i % count
+        for c in range(staged.shape[2]):
+            for t in range(2):
+                v = staged[n, y, c, pl.ds(t, SUB, stride=2), :]
+                out[n, y, t, :, pl.ds(c * LANES, LANES)] = v
+        return carry
+
+    lax.fori_loop(0, staged.shape[0] * count, one, 0, unroll=4)
+
+
 def load_kernel(order_in, codes_in, state, cross, inside, codes, table, factor, weights, coef,
-                order, raw, flat, cross_sems, inside_sems, more_sems):
+                order, raw, flat, near_cross, near_inside, cross_sems, inside_sems, more_sems):
     rows, width = state.shape[0], order.shape[-1]
     mirrored = lax.axis_index("gx") % 2
     more = [
         pltpu.make_async_copy(order_in, order, more_sems.at[0]),
         pltpu.make_async_copy(codes_in, raw, more_sems.at[1]),
     ]
-    copies = row_copies(mirrored, state, cross, 0, cross_sems)
-    copies += row_copies(mirrored, state, inside, rows - 2, inside_sems)
+    copies = row_copies(mirrored, state, near_cross, 0, cross_sems)
+    copies += row_copies(mirrored, state, near_inside, rows - 2, inside_sems)
     for copy in more + copies:
         copy.start()
     for copy in more:
@@ -285,35 +295,45 @@
         coef[3 * k + 1] = 0.5 * sign * (1.0 - reach)
         coef[3 * k + 2] = sign
 
+    span = raw.shape[2]
+    z = lax.broadcasted_iota(jnp.int32, (span, span), 0)
+    goes = lax.broadcasted_iota(jnp.int32, (span, span), 1)
+    shuffle = jnp.where(goes == z % 2 * SUB + z // 2, 1.0, 0.0).astype(BF16)
+    lined = raw[...].reshape(rows * raw.shape[1], span).astype(F32).astype(BF16)
+    lined = jnp.dot(lined, shuffle, preferred_element_type=F32).astype(jnp.int32)
+    raw[...] = lined.reshape(rows, raw.shape[1], span)
     for y in range(raw.shape[1]):
-        flat[:, y * raw.shape[2] : (y + 1) * raw.shape[2]] = raw[:, y, :]
+        flat[:, y * span : (y + 1) * span] = raw[:, y, :]
     for r in range(rows):
         place = jnp.where(mirrored > 0, rows - 1 - r, r)
         codes[r : r + 1, :] = flat[pl.ds(place, 1), :]
     for copy in copies:
         copy.wait()
+    unstage(near_cross, cross)
+    unstage(near_inside, inside)
 
 
 def inner_kernel(relax, rows, *refs):
     if relax:
         (m_cross, m_mid, m_in, params, table, factor, coef_ref, weights,
-         cross, middle, inside, out, e_cross, e_in, sums, wide, tall, kept, ring, face_ring) = refs
+         cross, middle, inside, out, e_cross, e_in, sums, wide, tall, kept) = refs
         spread_features([params[k] for k in range(6)], wide, tall, rows)
         relax_rows(m_cross, cross, tall, 0, 2, table, factor, kept)
         relax_rows(m_mid, middle, tall, 2, rows - 4, table, factor, kept)
         relax_rows(m_in, inside, tall, rows - 2, 2, table, factor, kept)
     else:
         (cross, inside, state, coef_ref, weights, middle, out, e_cross, e_in, sums,
-         ring, face_ring, sems) = refs
+         near, sems) = refs
         mirrored = lax.axis_index("gx") % 2
-        copies = row_copies(mirrored, state, middle, 2, sems)
+        copies = row_copies(mirrored, state, near, 2, sems)
         for copy in copies:
             copy.start()
-    yz_rows(cross, e_cross, True, 2, coef_ref, ring, face_ring)
-    yz_rows(inside, e_in, True, 2, coef_ref, ring, face_ring)
+    yz_rows(cross, e_cross, True, 2, coef_ref)
+    yz_rows(inside, e_in, True, 2, coef_ref)
     if not relax:
         for copy in copies:
             copy.wait()
+        unstage(near, middle)
     chunks = middle.shape[-1] // LANES
     inner = rows - 4
 
@@ -338,7 +358,7 @@
         return carry
 
     lax.fori_loop(0, chunks * 16, along_x, 0, unroll=2)
-    yz_rows(middle, out, False, inner, coef_ref, ring, face_ring)
+    yz_rows(middle, out, False, inner, coef_ref)
     row_moments(out, inner, weights, sums, 0)
 
 
@@ -394,20 +414,23 @@
 
 
 def final_kernel(rows, m_cross, m_mid, m_in, params, table, factor, out,
-                 wide, tall, kept, cross, middle, inside, sems):
+                 wide, tall, kept, staged, sems):
     mirrored = lax.axis_index("gx") % 2
     spread_features([params[k] for k in range(6)], wide, tall, rows)
     copies = []
-    for source, target, first, count in (
-        (m_cross, cross, 0, 2), (m_mid, middle, 2, rows - 4), (m_in, inside, rows - 2, 2)
-    ):
-        relax_rows(source, target, tall, first, count, table, factor, kept)
-        for n in range(count):
-            r = first + n
-            place = jnp.where(mirrored > 0, rows - 1 - r, r)
-            copy = pltpu.make_async_copy(target.at[n], out.at[place], sems.at[r])
+    for source, first, count in ((m_cross, 0, 2), (m_mid, 2, rows - 4), (m_in, rows - 2, 2)):
+        near = staged.at[pl.ds(first, count)]
+
+        def store(row, chunk, value, near=near):
+            for y in range(16):
+                for t in range(2):
+                    near[row, y, chunk, pl.ds(t, SUB, stride=2), :] = value[y, t]
+
+        relax_rows(source, store, tall, first, count, table, factor, kept)
+        more = row_copies(mirrored, out, near, first, sems.at[pl.ds(first, count)], True)
+        for copy in more:
             copy.start()
-            copies.append(copy)
+        copies += more
     for copy in copies:
         copy.wait()
 
@@ -418,7 +441,7 @@
     line = lax.axis_size("gx")
     total = width * peers
     cells = count_y * count_z
-    state = distribution.reshape(rows, count_y, 2, SUB, width)
+    chunks = width // LANES
 
     vmem = pl.BlockSpec(memory_space=pltpu.VMEM)
     smem = pl.BlockSpec(memory_space=pltpu.SMEM)
@@ -437,7 +460,11 @@
             pltpu.VMEM((2, count_y, 2, SUB, LANES), F32),
         ]
 
-    ring_scratch = [pltpu.VMEM((count_y, 32, LANES), F32)] * 2
+    def staging(n):
+        return [
+            pltpu.VMEM((n, count_y, chunks, count_z, LANES), F32),
+            pltpu.SemaphoreType.DMA((n, chunks)),
+        ]
 
     def limits(mib):
         return pltpu.CompilerParams(vmem_limit_bytes=mib * 1024 * 1024)
@@ -463,25 +490,27 @@
                 pltpu.VMEM((1, width), jnp.int32),
                 pltpu.VMEM((rows, count_y, count_z), jnp.int32),
                 pltpu.VMEM((rows, cells), jnp.int32),
-                pltpu.SemaphoreType.DMA((2,)),
-                pltpu.SemaphoreType.DMA((2,)),
+                staging(2)[0],
+                staging(2)[0],
+                staging(2)[1],
+                staging(2)[1],
                 pltpu.SemaphoreType.DMA((2,)),
             ],
             compiler_params=limits(6),
             name="load_edges",
-        )(in_hbm(velocity_order.reshape(1, width)), in_hbm(cell_codes), in_hbm(state))
+        )(in_hbm(velocity_order.reshape(1, width)), in_hbm(cell_codes), in_hbm(distribution))
 
     def inner(relax, state, params):
         sums = jax.ShapeDtypeStruct((5, rows - 4, cells), F32)
         out_shape = [slab(rows - 4), slab(2), slab(2), sums]
-        scratch = ring_scratch
+        scratch = []
         if relax:
             out_shape = [slab(2), slab(rows - 4), slab(2)] + out_shape
-            scratch = feature_scratch(rows) + scratch
+            scratch = feature_scratch(rows)
             args = (*state, params, table, factor, coef, weights)
         else:
             out_shape = [slab(rows - 4)] + out_shape
-            scratch = scratch + [pltpu.SemaphoreType.DMA((rows - 4,))]
+            scratch = staging(rows - 4)
             args = (*state, coef, weights)
         return pl.pallas_call(
             functools.partial(inner_kernel, relax, rows),
@@ -525,10 +554,8 @@
             functools.partial(final_kernel, rows),
             in_specs=[vmem] * 6,
             out_specs=hbm,
-            out_shape=slab(rows),
-            scratch_shapes=feature_scratch(rows)
-            + [slab_scratch(2), slab_scratch(rows - 4), slab_scratch(2)]
-            + [pltpu.SemaphoreType.DMA((rows,))],
+            out_shape=jax.ShapeDtypeStruct(distribution.shape, F32),
+            scratch_shapes=feature_scratch(rows) + staging(rows),
             compiler_params=limits(LIMIT_MIB),
             name="final_relax",
         )(*moved, params, table, factor)
@@ -560,7 +587,7 @@
 
     cross, inside, codes, table, factor, weights, coef = load()
     halos = exchange(cross, inside)
-    middle, m_mid, e_cross, e_in, sums = inner(False, (cross, inside, in_hbm(state)), None)
+    middle, m_mid, e_cross, e_in, sums = inner(False, (cross, inside, in_hbm(distribution)), None)
     m_cross, m_in, sums = edge(
         False, halos, None, (cross, middle, inside), (e_cross, e_in), sums
     )
@@ -572,8 +599,7 @@
         *state, m_mid, e_cross, e_in, sums = inner(True, moved, params)
         m_cross, m_in, sums = edge(True, halos, p_halos, state, (e_cross, e_in), sums)
     (params,) = cell_params(gather(sums), rows)
-    result = final((m_cross, m_mid, m_in), params)
-    return result.reshape(rows, count_y, count_z, width)
+    return final((m_cross, m_mid, m_in), params)
 
 
 def solution(mesh):

time: 78.5 us -> 76 us (0.968)
  Pallas kernels: 40.8 us -> 37.3 us
  waiting for transfers between devices: 14.6 us -> 15.6 us
    pallas_call x3, Pallas kernels: 25.4 us -> 20.9 us  [inner(): pl.pallas_call(functools.partial(inner_kernel, relax, rows), in_specs=[vm...]
    ppermute x5, waiting for transfers between devices: 5.2 us -> 6.21 us  [exchange(): lax.ppermute(cross, ('groups', 'gx'), across)]
    pallas_call x1, Pallas kernels: 1.62 us -> 2.42 us  [load(): pl.pallas_call(load_kernel, in_specs=[hbm] * 3, out_specs=[vmem] * 7, out...]
  transfers between devices with their start and end apart: 19 -> 19, of which waited for: 8 -> 8; matrix products, arithmetic and copies ran while one was open for 0% -> 0% of each run, Pallas kernels for 34% -> 29%
where the time goes in v5:
time: 76 us; the launch traced here: 75.8 us
  Pallas kernels  37.3 us (49%)
  starting transfers between devices  22.1 us (29%)
  waiting for transfers between devices  15.6 us (21%)
  between operations  0.76 us (1%)
    pallas_call x3, Pallas kernels, inner(): pl.pallas_call(functools.partial(inner_kernel, relax, rows), in_specs=[vm...  20.9 us
    ppermute x9, starting transfers between devices, gather(): parts.append(lax.ppermute(part, 'vert', pairs))  13.2 us
    ppermute x9, waiting for transfers between devices, gather(): parts.append(lax.ppermute(part, 'vert', pairs))  9.39 us
    pallas_call x3, Pallas kernels, edge(): pl.pallas_call(functools.partial(edge_kernel, relax, rows, line), in_spec...  8.92 us
    ppermute x5, starting transfers between devices, exchange(): lax.ppermute(cross, ('groups', 'gx'), across)  8.25 us
    ppermute x5, waiting for transfers between devices, exchange(): lax.ppermute(cross, ('groups', 'gx'), across)  6.21 us
    pallas_call x1, Pallas kernels, final(): pl.pallas_call(functools.partial(final_kernel, rows), in_specs=[vmem] * 6...  3.15 us
    pallas_call x1, Pallas kernels, load(): pl.pallas_call(load_kernel, in_specs=[hbm] * 3, out_specs=[vmem] * 7, out...  2.42 us
  transfers between devices with their start and end apart: 19, of which 8 were waited for; matrix products, arithmetic and copies ran while one was open for 0% of the time, Pallas kernels for 29%

profile of v5, /device:TPU:0, one launch (start us, length us, event | category | flops | bytes accessed | tf_op | source)
XLA Modules:
  0.0 75.8 jit_solution(384337506241696041)
XLA Ops:
  0.0 2.4 %load_edges.1 = (f32[2,16,2,8,512]{4,3,2,1,0:T(8,128)S(1)}, f32[2,16,2,8,512]{4,3,2,1,0:T(8,128)S(1)}, s32[8,256]{1,0:T(8,128)S(1)}, bf16[32,512]{1,0:T(8,128)(2...) custom-call(s32[1,512]{1,0:T(1,128)} %bitcast.1, ...), custom_call_target="tpu_custom_call" | custom-call | tf_op jit(solution)/shard_map/load_edges/pallas_call | solution.py:476
  2.4 3.0 %collective-permute-start = (f32[2,16,2,8,512]{4,3,2,1,0:T(8,128)S(1)}, f32[2,16,2,8,512]{4,3,2,1,0:T(8,128)S(1)}, u32[]{:S(2)}, u32[]{:S(2)}) collective-permute-start(f32[2,16,2,8,512]{4,3,2,1,0:T(8,128)S(1)} %get-tuple-element.46.refs_0_.refs_2_), channel_id=1, source_target_pairs={{0,16},{12,28},{4,8},{8,4},{16,0},{28,12},{20,24},{24,20},{1,17},{... | collective-permute-start | bytes 3145736 | tf_op jit(solution)/shard_map/ppermute | solution.py:577
  5.5 0.1 collective-permute-start.1
  5.6 6.5 %inner_first.1 = (f32[4,16,2,8,512]{4,3,2,1,0:T(8,128)S(1)}, f32[4,16,2,8,512]{4,3,2,1,0:T(8,128)S(1)}, f32[2,16,2,8,512]{4,3,2,1,0:T(8,128)S(1)}, f32[2,16,2,8,512]{4,3,2,1,0:T(8,128)S(1)}, f32[5,4,256]{2,1,0:T(4,128)S(1)}) custom-call(f32[2,16,2,8,512]{4,3,2,1,0:T(8,128)S(1)} %get-tuple-element.46.refs_0_.refs_2_, ...), custom_call_target="tpu_custom_call" | custom-call | tf_op jit(solution)/shard_map/inner_first/pallas_call | solution.py:515
  12.1 6.2 %collective-permute-done.refs_0_ = f32[2,16,2,8,512]{4,3,2,1,0:T(8,128)S(1)} collective-permute-done((f32[2,16,2,8,512]{4,3,2,1,0:T(8,128)S(1)}, f32[2,16,2,8,512]{4,3,2,1,0:T(8,128)S(1)}, u32[]{:S(2)}, u32[]{:S(2)}) %collective-permute-start) | collective-permute-done | bytes 1048608 | tf_op jit(solution)/shard_map/ppermute | solution.py:577
  18.2 0.0 collective-permute-done.1.refs_1_
  18.2 2.5 %edge_first.1 = (f32[2,16,2,8,512]{4,3,2,1,0:T(8,128)S(1)}, f32[2,16,2,8,512]{4,3,2,1,0:T(8,128)S(1)}, f32[5,8,256]{2,1,0:T(8,128)S(1)}) custom-call(f32[2,16,2,8,512]{4,3,2,1,0:T(8,128)S(1)} %collective-permute-done.refs_0_, f32[2,16,2,8,512]{4,3,2,1,0:T(8,128)S(1)} %collective-permute-done.1.refs_1_, ...), custom_call_target="tpu_custom_call" | custom-call | tf_op jit(solution)/shard_map/edge_first/pallas_call | solution.py:532
  20.8 2.0 %collective-permute-start.2 = (f32[2,16,2,8,512]{4,3,2,1,0:T(8,128)S(1)}, f32[2,16,2,8,512]{4,3,2,1,0:T(8,128)S(1)}, u32[]{:S(2)}, u32[]{:S(2)}) collective-permute-start(f32[2,16,2,8,512]{4,3,2,1,0:T(8,128)S(1)} %get-tuple-element.54.refs_0_), channel_id=1, source_target_pairs={{0,16},{12,28},{4,8},{8,4},{16,0},{28,12},{20,24},{24,20},{1,17},{... | collective-permute-start | bytes 3145736 | tf_op jit(solution)/shard_map/ppermute | solution.py:577
  22.8 0.0 collective-permute-start.3
  22.8 1.6 %collective-permute-start.4 = (f32[5,8,256]{2,1,0:T(8,128)S(1)}, f32[5,8,256]{2,1,0:T(8,128)S(1)}, u32[]{:S(2)}, u32[]{:S(2)}) collective-permute-start(f32[5,8,256]{2,1,0:T(8,128)S(1)} %get-tuple-element.56.refs_0_), channel_id=1, source_target_pairs={{0,1},{1,2},{2,3},{3,0},{4,5},{5,6},{6,7},{7,4},{8,9},{9,10},{10,1... | collective-permute-start | bytes 122888 | tf_op jit(solution)/shard_map/ppermute | solution.py:585
  24.4 2.6 %collective-permute-start.5 = (f32[5,8,256]{2,1,0:T(8,128)S(1)}, f32[5,8,256]{2,1,0:T(8,128)S(1)}, u32[]{:S(2)}, u32[]{:S(2)}) collective-permute-start(f32[5,8,256]{2,1,0:T(8,128)S(1)} %get-tuple-element.56.refs_0_), channel_id=1, source_target_pairs={{0,2},{1,3},{2,0},{3,1},{4,6},{5,7},{6,4},{7,5},{8,10},{9,11},{10,... | collective-permute-start | bytes 122888 | tf_op jit(solution)/shard_map/ppermute | solution.py:585
  27.0 1.3 %collective-permute-start.6 = (f32[5,8,256]{2,1,0:T(8,128)S(1)}, f32[5,8,256]{2,1,0:T(8,128)S(1)}, u32[]{:S(2)}, u32[]{:S(2)}) collective-permute-start(f32[5,8,256]{2,1,0:T(8,128)S(1)} %get-tuple-element.56.refs_0_), channel_id=1, source_target_pairs={{0,3},{1,0},{2,1},{3,2},{4,7},{5,4},{6,5},{7,6},{8,11},{9,8},{10,9... | collective-permute-start | bytes 122888 | tf_op jit(solution)/shard_map/ppermute | solution.py:585
  29.0 0.0 collective-permute-done.4.refs_1_
  29.0 1.6 %collective-permute-done.5.refs_2_ = f32[5,8,256]{2,1,0:T(8,128)S(1)} collective-permute-done((f32[5,8,256]{2,1,0:T(8,128)S(1)}, f32[5,8,256]{2,1,0:T(8,128)S(1)}, u32[]{:S(2)}, u32[]{:S(2)}) %collective-permute-start.5) | collective-permute-done | bytes 40992 | tf_op jit(solution)/shard_map/ppermute | solution.py:585
  30.6 0.4 collective-permute-done.6.refs_3_
  31.0 0.6 cell_params.3
  31.7 1.1 %collective-permute-start.7 = (f32[6,2,256]{2,1,0:T(2,128)S(1)}, f32[6,2,256]{2,1,0:T(2,128)S(1)}, u32[]{:S(2)}, u32[]{:S(2)}) collective-permute-start(f32[6,2,256]{2,1,0:T(2,128)S(1)} %get-tuple-element.58), channel_id=1, source_target_pairs={{0,16},{12,28},{4,8},{8,4},{16,0},{28,12},{20,24},{24,20},{1,17},{... | collective-permute-start | bytes 36872 | tf_op jit(solution)/shard_map/ppermute | solution.py:577
  32.7 0.0 collective-permute-start.8
  32.7 7.2 %inner_relax.2 = (f32[2,16,2,8,512]{4,3,2,1,0:T(8,128)S(1)}, f32[4,16,2,8,512]{4,3,2,1,0:T(8,128)S(1)}, f32[2,16,2,8,512]{4,3,2,1,0:T(8,128)S(1)}, f32[4,16,2,8,...) custom-call(f32[2,16,2,8,512]{4,3,2,1,0:T(8,128)S(1)} %get-tuple-ele, ...), custom_call_target="tpu_custom_call" | custom-call | tf_op jit(solution)/shard_map/inner_relax/pallas_call | solution.py:515
  39.9 0.0 collective-permute-done.7.refs_2_
  39.9 0.0 collective-permute-done.8.refs_3_
  40.0 0.0 collective-permute-done.2.refs_0_
  40.0 0.0 collective-permute-done.3.refs_1_
  40.0 3.2 %edge_relax.2 = (f32[2,16,2,8,512]{4,3,2,1,0:T(8,128)S(1)}, f32[2,16,2,8,512]{4,3,2,1,0:T(8,128)S(1)}, f32[5,8,256]{2,1,0:T(8,128)S(1)}) custom-call(f32[2,16,2,8,512]{4,3,2,1,0:T(8,128)S(1)} %collective-permute-done.2.refs_0_, f32[2,16,2,8,512]{4,3,2,1,0:T(8,128)S(1)} %collective-permute-done.3.refs_1_, f32[6,2,256]{2,1,0:T(2,128)S(1)} %collective-permute-done.7.refs_2_, ...), custom_call_target="tpu_custom_call" | custom-call | tf_op jit(solution)/shard_map/edge_relax/pallas_call | solution.py:532
  43.2 0.5 collective-permute-start.10
  43.7 1.0 %collective-permute-start.9 = (f32[2,16,2,8,512]{4,3,2,1,0:T(8,128)S(1)}, f32[2,16,2,8,512]{4,3,2,1,0:T(8,128)S(1)}, u32[]{:S(2)}, u32[]{:S(2)}) collective-permute-start(f32[2,16,2,8,512]{4,3,2,1,0:T(8,128)S(1)} %get-tuple-element.70.refs_0_), channel_id=1, source_target_pairs={{0,16},{12,28},{4,8},{8,4},{16,0},{28,12},{20,24},{24,20},{1,17},{... | collective-permute-start | bytes 3145736 | tf_op jit(solution)/shard_map/ppermute | solution.py:577
  44.7 0.8 %collective-permute-start.11 = (f32[5,8,256]{2,1,0:T(8,128)S(1)}, f32[5,8,256]{2,1,0:T(8,128)S(1)}, u32[]{:S(2)}, u32[]{:S(2)}) collective-permute-start(f32[5,8,256]{2,1,0:T(8,128)S(1)} %get-tuple-element.72.refs_0_), channel_id=1, source_target_pairs={{0,1},{1,2},{2,3},{3,0},{4,5},{5,6},{6,7},{7,4},{8,9},{9,10},{10,1... | collective-permute-start | bytes 122888 | tf_op jit(solution)/shard_map/ppermute | solution.py:585
  45.5 2.8 %collective-permute-start.12 = (f32[5,8,256]{2,1,0:T(8,128)S(1)}, f32[5,8,256]{2,1,0:T(8,128)S(1)}, u32[]{:S(2)}, u32[]{:S(2)}) collective-permute-start(f32[5,8,256]{2,1,0:T(8,128)S(1)} %get-tuple-element.72.refs_0_), channel_id=1, source_target_pairs={{0,2},{1,3},{2,0},{3,1},{4,6},{5,7},{6,4},{7,5},{8,10},{9,11},{10,... | collective-permute-start | bytes 122888 | tf_op jit(solution)/shard_map/ppermute | solution.py:585
  48.4 0.2 collective-permute-start.13
  48.6 2.0 %collective-permute-done.11.refs_1_ = f32[5,8,256]{2,1,0:T(8,128)S(1)} collective-permute-done((f32[5,8,256]{2,1,0:T(8,128)S(1)}, f32[5,8,256]{2,1,0:T(8,128)S(1)}, u32[]{:S(2)}, u32[]{:S(2)}) %collective-permute-start.11) | collective-permute-done | bytes 40992 | tf_op jit(solution)/shard_map/ppermute | solution.py:585
  50.6 0.8 %collective-permute-done.12.refs_2_ = f32[5,8,256]{2,1,0:T(8,128)S(1)} collective-permute-done((f32[5,8,256]{2,1,0:T(8,128)S(1)}, f32[5,8,256]{2,1,0:T(8,128)S(1)}, u32[]{:S(2)}, u32[]{:S(2)}) %collective-permute-start.12) | collective-permute-done | bytes 40992 | tf_op jit(solution)/shard_map/ppermute | solution.py:585
  51.5 0.9 %collective-permute-done.13.refs_3_ = f32[5,8,256]{2,1,0:T(8,128)S(1)} collective-permute-done((f32[5,8,256]{2,1,0:T(8,128)S(1)}, f32[5,8,256]{2,1,0:T(8,128)S(1)}, u32[]{:S(2)}, u32[]{:S(2)}) %collective-permute-start.13) | collective-permute-done | bytes 40992 | tf_op jit(solution)/shard_map/ppermute | solution.py:585
  52.4 0.6 cell_params.4
  53.0 1.1 %collective-permute-start.14 = (f32[6,2,256]{2,1,0:T(2,128)S(1)}, f32[6,2,256]{2,1,0:T(2,128)S(1)}, u32[]{:S(2)}, u32[]{:S(2)}) collective-permute-start(f32[6,2,256]{2,1,0:T(2,128)S(1)} %get-tuple-element.73), channel_id=1, source_target_pairs={{0,16},{12,28},{4,8},{8,4},{16,0},{28,12},{20,24},{24,20},{1,17},{... | collective-permute-start | bytes 36872 | tf_op jit(solution)/shard_map/ppermute | solution.py:577
  54.1 0.0 collective-permute-start.15
  54.1 7.2 %inner_relax.3 = (f32[2,16,2,8,512]{4,3,2,1,0:T(8,128)S(1)}, f32[4,16,2,8,512]{4,3,2,1,0:T(8,128)S(1)}, f32[2,16,2,8,512]{4,3,2,1,0:T(8,128)S(1)}, f32[4,16,2,8,...) custom-call(f32[2,16,2,8,512]{4,3,2,1,0:T(8,128)S(1)} %get-tuple-ele, ...), custom_call_target="tpu_custom_call" | custom-call | tf_op jit(solution)/shard_map/inner_relax/pallas_call | solution.py:515
  61.3 0.0 collective-permute-done.14.refs_2_
  61.4 0.0 collective-permute-done.15.refs_3_
  61.4 0.0 collective-permute-done.10.refs_1_
  61.4 3.2 %edge_relax.3 = (f32[2,16,2,8,512]{4,3,2,1,0:T(8,128)S(1)}, f32[2,16,2,8,512]{4,3,2,1,0:T(8,128)S(1)}, f32[5,8,256]{2,1,0:T(8,128)S(1)}) custom-call(f32[2,16,2,8,512]{4,3,2,1,0:T(8,128)S(1)} %collective-permute-done.9.refs_0_, f32[2,16,2,8,512]{4,3,2,1,0:T(8,128)S(1)} %collective-permute-done.10.refs_1_, f32[6,2,256]{2,1,0:T(2,128)S(1)} %collective-permute-done.14.refs_2_, ...), custom_call_target="tpu_custom_call" | custom-call | tf_op jit(solution)/shard_map/edge_relax/pallas_call | solution.py:532
  64.6 0.7 collective-permute-start.16
  65.3 2.1 %collective-permute-start.17 = (f32[5,8,256]{2,1,0:T(8,128)S(1)}, f32[5,8,256]{2,1,0:T(8,128)S(1)}, u32[]{:S(2)}, u32[]{:S(2)}) collective-permute-start(f32[5,8,256]{2,1,0:T(8,128)S(1)} %get-tuple-element.86.refs_0_), channel_id=1, source_target_pairs={{0,2},{1,3},{2,0},{3,1},{4,6},{5,7},{6,4},{7,5},{8,10},{9,11},{10,... | collective-permute-start | bytes 122888 | tf_op jit(solution)/shard_map/ppermute | solution.py:585
  67.4 1.0 %collective-permute-start.18 = (f32[5,8,256]{2,1,0:T(8,128)S(1)}, f32[5,8,256]{2,1,0:T(8,128)S(1)}, u32[]{:S(2)}, u32[]{:S(2)}) collective-permute-start(f32[5,8,256]{2,1,0:T(8,128)S(1)} %get-tuple-element.86.refs_0_), channel_id=1, source_target_pairs={{0,3},{1,0},{2,1},{3,2},{4,7},{5,4},{6,5},{7,6},{8,11},{9,8},{10,9... | collective-permute-start | bytes 122888 | tf_op jit(solution)/shard_map/ppermute | solution.py:585
  68.4 2.4 %collective-permute-done.16.refs_1_ = f32[5,8,256]{2,1,0:T(8,128)S(1)} collective-permute-done((f32[5,8,256]{2,1,0:T(8,128)S(1)}, f32[5,8,256]{2,1,0:T(8,128)S(1)}, u32[]{:S(2)}, u32[]{:S(2)}) %collective-permute-start.16) | collective-permute-done | bytes 40992 | tf_op jit(solution)/shard_map/ppermute | solution.py:585
  70.8 1.2 %collective-permute-done.17.refs_2_ = f32[5,8,256]{2,1,0:T(8,128)S(1)} collective-permute-done((f32[5,8,256]{2,1,0:T(8,128)S(1)}, f32[5,8,256]{2,1,0:T(8,128)S(1)}, u32[]{:S(2)}, u32[]{:S(2)}) %collective-permute-start.17) | collective-permute-done | bytes 40992 | tf_op jit(solution)/shard_map/ppermute | solution.py:585
  72.0 0.0 collective-permute-done.18.refs_3_
  72.0 0.6 cell_params.5.params
  72.7 3.1 %final_relax.1 = f32[8,16,16,512]{3,2,1,0:T(8,128)} custom-call(f32[2,16,2,8,512]{4,3,2,1,0:T(8,128)S(1)} %get-tuple-element.83.m_cross, f32[4,16,2,8,512]{4,3,2,1,0:T(8,128)S(1)} %get-tuple-element.84.m_mid, f32[2,16,2,8,512]{4,3,2,1,0:T(8,128)S(1)} %get-tuple-element.85.m_in, f32[6,8,256]{2,1,0:T(8,128)S(1)} %cell_params.5.params, ...), custom_call_target="tpu_custom_call" | custom-call | tf_op jit(solution)/shard_map/final_relax/pallas_call | solution.py:553
  (3 shorter events, 0.0 us)
Async XLA Ops:
  2.4 15.8 %collective-permute-start = (f32[2,16,2,8,512]{4,3,2,1,0:T(8,128)S(1)}, f32[2,16,2,8,512]{4,3,2,1,0:T(8,128)S(1)}, u32[]{:S(2)}, u32[]{:S(2)}) collective-permute-start(f32[2,16,2,8,512]{4,3,2,1,0:T(8,128)S(1)} %get-tuple-element.46.refs_0_.refs_2_), channel_id=1, source_target_pairs={{0,16},{12,28},{4,8},{8,4},{16,0},{28,12},{20,24},{24,20},{1,17},{... | collective-permute-start | bytes 3145736 | tf_op jit(solution)/shard_map/ppermute | solution.py:577
  5.5 12.8 %collective-permute-start.1 = (f32[2,16,2,8,512]{4,3,2,1,0:T(8,128)S(1)}, f32[2,16,2,8,512]{4,3,2,1,0:T(8,128)S(1)}, u32[]{:S(2)}, u32[]{:S(2)}) collective-permute-start(f32[2,16,2,8,512]{4,3,2,1,0:T(8,128)S(1)} %get-tuple-element.47.refs_1_.refs_4_), channel_id=1, source_target_pairs={{0,4},{4,0},{8,12},{12,8},{1,5},{5,1},{9,13},{13,9},{2,6},{6,2},{1... | collective-permute-start | bytes 3145736 | tf_op jit(solution)/shard_map/ppermute | solution.py:578
  18.2 12.8 %copy-start = (f32[4]{0:T(128)S(1)}, f32[4]{0:T(128)}, u32[]{:S(2)}) copy-start(f32[4]{0:T(128)} %refs_6_.5) | copy-start | bytes 52
  20.8 19.2 %collective-permute-start.2 = (f32[2,16,2,8,512]{4,3,2,1,0:T(8,128)S(1)}, f32[2,16,2,8,512]{4,3,2,1,0:T(8,128)S(1)}, u32[]{:S(2)}, u32[]{:S(2)}) collective-permute-start(f32[2,16,2,8,512]{4,3,2,1,0:T(8,128)S(1)} %get-tuple-element.54.refs_0_), channel_id=1, source_target_pairs={{0,16},{12,28},{4,8},{8,4},{16,0},{28,12},{20,24},{24,20},{1,17},{... | collective-permute-start | bytes 3145736 | tf_op jit(solution)/shard_map/ppermute | solution.py:577
  22.8 17.2 %collective-permute-start.3 = (f32[2,16,2,8,512]{4,3,2,1,0:T(8,128)S(1)}, f32[2,16,2,8,512]{4,3,2,1,0:T(8,128)S(1)}, u32[]{:S(2)}, u32[]{:S(2)}) collective-permute-start(f32[2,16,2,8,512]{4,3,2,1,0:T(8,128)S(1)} %get-tuple-element.55.refs_2_), channel_id=1, source_target_pairs={{0,4},{4,0},{8,12},{12,8},{1,5},{5,1},{9,13},{13,9},{2,6},{6,2},{1... | collective-permute-start | bytes 3145736 | tf_op jit(solution)/shard_map/ppermute | solution.py:578
  22.8 6.2 %collective-permute-start.4 = (f32[5,8,256]{2,1,0:T(8,128)S(1)}, f32[5,8,256]{2,1,0:T(8,128)S(1)}, u32[]{:S(2)}, u32[]{:S(2)}) collective-permute-start(f32[5,8,256]{2,1,0:T(8,128)S(1)} %get-tuple-element.56.refs_0_), channel_id=1, source_target_pairs={{0,1},{1,2},{2,3},{3,0},{4,5},{5,6},{6,7},{7,4},{8,9},{9,10},{10,1... | collective-permute-start | bytes 122888 | tf_op jit(solution)/shard_map/ppermute | solution.py:585
  24.4 6.2 %collective-permute-start.5 = (f32[5,8,256]{2,1,0:T(8,128)S(1)}, f32[5,8,256]{2,1,0:T(8,128)S(1)}, u32[]{:S(2)}, u32[]{:S(2)}) collective-permute-start(f32[5,8,256]{2,1,0:T(8,128)S(1)} %get-tuple-element.56.refs_0_), channel_id=1, source_target_pairs={{0,2},{1,3},{2,0},{3,1},{4,6},{5,7},{6,4},{7,5},{8,10},{9,11},{10,... | collective-permute-start | bytes 122888 | tf_op jit(solution)/shard_map/ppermute | solution.py:585
  27.0 4.0 %collective-permute-start.6 = (f32[5,8,256]{2,1,0:T(8,128)S(1)}, f32[5,8,256]{2,1,0:T(8,128)S(1)}, u32[]{:S(2)}, u32[]{:S(2)}) collective-permute-start(f32[5,8,256]{2,1,0:T(8,128)S(1)} %get-tuple-element.56.refs_0_), channel_id=1, source_target_pairs={{0,3},{1,0},{2,1},{3,2},{4,7},{5,4},{6,5},{7,6},{8,11},{9,8},{10,9... | collective-permute-start | bytes 122888 | tf_op jit(solution)/shard_map/ppermute | solution.py:585
  31.7 8.3 %collective-permute-start.7 = (f32[6,2,256]{2,1,0:T(2,128)S(1)}, f32[6,2,256]{2,1,0:T(2,128)S(1)}, u32[]{:S(2)}, u32[]{:S(2)}) collective-permute-start(f32[6,2,256]{2,1,0:T(2,128)S(1)} %get-tuple-element.58), channel_id=1, source_target_pairs={{0,16},{12,28},{4,8},{8,4},{16,0},{28,12},{20,24},{24,20},{1,17},{... | collective-permute-start | bytes 36872 | tf_op jit(solution)/shard_map/ppermute | solution.py:577
  32.7 7.2 %collective-permute-start.8 = (f32[6,2,256]{2,1,0:T(2,128)S(1)}, f32[6,2,256]{2,1,0:T(2,128)S(1)}, u32[]{:S(2)}, u32[]{:S(2)}) collective-permute-start(f32[6,2,256]{2,1,0:T(2,128)S(1)} %get-tuple-element.59), channel_id=1, source_target_pairs={{0,4},{4,0},{8,12},{12,8},{1,5},{5,1},{9,13},{13,9},{2,6},{6,2},{1... | collective-permute-start | bytes 36872 | tf_op jit(solution)/shard_map/ppermute | solution.py:578
  43.2 18.2 %collective-permute-start.10 = (f32[2,16,2,8,512]{4,3,2,1,0:T(8,128)S(1)}, f32[2,16,2,8,512]{4,3,2,1,0:T(8,128)S(1)}, u32[]{:S(2)}, u32[]{:S(2)}) collective-permute-start(f32[2,16,2,8,512]{4,3,2,1,0:T(8,128)S(1)} %get-tuple-element.71.refs_2_), channel_id=1, source_target_pairs={{0,4},{4,0},{8,12},{12,8},{1,5},{5,1},{9,13},{13,9},{2,6},{6,2},{1... | collective-permute-start | bytes 3145736 | tf_op jit(solution)/shard_map/ppermute | solution.py:578
  43.7 17.7 %collective-permute-start.9 = (f32[2,16,2,8,512]{4,3,2,1,0:T(8,128)S(1)}, f32[2,16,2,8,512]{4,3,2,1,0:T(8,128)S(1)}, u32[]{:S(2)}, u32[]{:S(2)}) collective-permute-start(f32[2,16,2,8,512]{4,3,2,1,0:T(8,128)S(1)} %get-tuple-element.70.refs_0_), channel_id=1, source_target_pairs={{0,16},{12,28},{4,8},{8,4},{16,0},{28,12},{20,24},{24,20},{1,17},{... | collective-permute-start | bytes 3145736 | tf_op jit(solution)/shard_map/ppermute | solution.py:577
  44.7 5.9 %collective-permute-start.11 = (f32[5,8,256]{2,1,0:T(8,128)S(1)}, f32[5,8,256]{2,1,0:T(8,128)S(1)}, u32[]{:S(2)}, u32[]{:S(2)}) collective-permute-start(f32[5,8,256]{2,1,0:T(8,128)S(1)} %get-tuple-element.72.refs_0_), channel_id=1, source_target_pairs={{0,1},{1,2},{2,3},{3,0},{4,5},{5,6},{6,7},{7,4},{8,9},{9,10},{10,1... | collective-permute-start | bytes 122888 | tf_op jit(solution)/shard_map/ppermute | solution.py:585
  45.5 5.9 %collective-permute-start.12 = (f32[5,8,256]{2,1,0:T(8,128)S(1)}, f32[5,8,256]{2,1,0:T(8,128)S(1)}, u32[]{:S(2)}, u32[]{:S(2)}) collective-permute-start(f32[5,8,256]{2,1,0:T(8,128)S(1)} %get-tuple-element.72.refs_0_), channel_id=1, source_target_pairs={{0,2},{1,3},{2,0},{3,1},{4,6},{5,7},{6,4},{7,5},{8,10},{9,11},{10,... | collective-permute-start | bytes 122888 | tf_op jit(solution)/shard_map/ppermute | solution.py:585
  48.4 4.0 %collective-permute-start.13 = (f32[5,8,256]{2,1,0:T(8,128)S(1)}, f32[5,8,256]{2,1,0:T(8,128)S(1)}, u32[]{:S(2)}, u32[]{:S(2)}) collective-permute-start(f32[5,8,256]{2,1,0:T(8,128)S(1)} %get-tuple-element.72.refs_0_), channel_id=1, source_target_pairs={{0,3},{1,0},{2,1},{3,2},{4,7},{5,4},{6,5},{7,6},{8,11},{9,8},{10,9... | collective-permute-start | bytes 122888 | tf_op jit(solution)/shard_map/ppermute | solution.py:585
  53.0 8.3 %collective-permute-start.14 = (f32[6,2,256]{2,1,0:T(2,128)S(1)}, f32[6,2,256]{2,1,0:T(2,128)S(1)}, u32[]{:S(2)}, u32[]{:S(2)}) collective-permute-start(f32[6,2,256]{2,1,0:T(2,128)S(1)} %get-tuple-element.73), channel_id=1, source_target_pairs={{0,16},{12,28},{4,8},{8,4},{16,0},{28,12},{20,24},{24,20},{1,17},{... | collective-permute-start | bytes 36872 | tf_op jit(solution)/shard_map/ppermute | solution.py:577
  54.1 7.2 %collective-permute-start.15 = (f32[6,2,256]{2,1,0:T(2,128)S(1)}, f32[6,2,256]{2,1,0:T(2,128)S(1)}, u32[]{:S(2)}, u32[]{:S(2)}) collective-permute-start(f32[6,2,256]{2,1,0:T(2,128)S(1)} %get-tuple-element.74), channel_id=1, source_target_pairs={{0,4},{4,0},{8,12},{12,8},{1,5},{5,1},{9,13},{13,9},{2,6},{6,2},{1... | collective-permute-start | bytes 36872 | tf_op jit(solution)/shard_map/ppermute | solution.py:578
  64.6 6.3 %collective-permute-start.16 = (f32[5,8,256]{2,1,0:T(8,128)S(1)}, f32[5,8,256]{2,1,0:T(8,128)S(1)}, u32[]{:S(2)}, u32[]{:S(2)}) collective-permute-start(f32[5,8,256]{2,1,0:T(8,128)S(1)} %get-tuple-element.86.refs_0_), channel_id=1, source_target_pairs={{0,1},{1,2},{2,3},{3,0},{4,5},{5,6},{6,7},{7,4},{8,9},{9,10},{10,1... | collective-permute-start | bytes 122888 | tf_op jit(solution)/shard_map/ppermute | solution.py:585
  65.3 6.7 %collective-permute-start.17 = (f32[5,8,256]{2,1,0:T(8,128)S(1)}, f32[5,8,256]{2,1,0:T(8,128)S(1)}, u32[]{:S(2)}, u32[]{:S(2)}) collective-permute-start(f32[5,8,256]{2,1,0:T(8,128)S(1)} %get-tuple-element.86.refs_0_), channel_id=1, source_target_pairs={{0,2},{1,3},{2,0},{3,1},{4,6},{5,7},{6,4},{7,5},{8,10},{9,11},{10,... | collective-permute-start | bytes 122888 | tf_op jit(solution)/shard_map/ppermute | solution.py:585
  67.4 4.6 %collective-permute-start.18 = (f32[5,8,256]{2,1,0:T(8,128)S(1)}, f32[5,8,256]{2,1,0:T(8,128)S(1)}, u32[]{:S(2)}, u32[]{:S(2)}) collective-permute-start(f32[5,8,256]{2,1,0:T(8,128)S(1)} %get-tuple-element.86.refs_0_), channel_id=1, source_target_pairs={{0,3},{1,0},{2,1},{3,2},{4,7},{5,4},{6,5},{7,6},{8,11},{9,8},{10,9... | collective-permute-start | bytes 122888 | tf_op jit(solution)/shard_map/ppermute | solution.py:585

commit v6 on v5

--- a/solution.py
+++ b/solution.py
@@ -110,16 +110,14 @@
     lax.fori_loop(0, chunks * rows, one, 0, unroll=2)
 
 
-def row_moments(out, count, weights, sums, first):
-    width = out.shape[-1]
-    for r in range(count):
-        flat = out[r].reshape(256, width)
+def row_moments(rows, weights, sums):
+    for row, place in rows:
+        flat = row[...].reshape(256, row.shape[-1])
         high = flat.astype(BF16)
         rest = (flat - high.astype(F32)).astype(BF16)
         both = jnp.concatenate([high, rest], axis=1)
         contract = (((1,), (1,)), ((), ()))
         part = lax.dot_general(weights[...], both, contract, preferred_element_type=F32)
-        place = first + r
         for m in range(4):
             sums[m, place : place + 1, :] = part[m : m + 1]
         sums[4, place : place + 1, :] = part[4:5] + part[5:6]
@@ -148,30 +146,27 @@
         tall[r] = wide[r].T.astype(BF16)
 
 
-def relax_rows(source, out, tall, first, rows, table, factor, kept):
-    width = source.shape[-1]
-
-    def two(i, carry):
-        for u in range(2):
-            keep = jnp.dot(tall[first + 2 * i + u], factor[...], preferred_element_type=F32)
-            kept[u] = keep.reshape(16, 2, SUB, LANES)
-        for u in range(2):
-            row = 2 * i + u
-            for pair in range(width // PAIR):
-                columns = table[:, pair * PAIR : (pair + 1) * PAIR]
-                power = jnp.dot(tall[first + row], columns, preferred_element_type=F32)
-                for half in range(2):
-                    lanes = pl.ds(pair * PAIR + half * LANES, LANES)
-                    shape = jnp.exp2(power[:, half * LANES : (half + 1) * LANES])
-                    shape = shape.reshape(16, 2, SUB, LANES)
-                    value = kept[u] * source[row, :, :, :, lanes] + shape
-                    if callable(out):
-                        out(row, 2 * pair + half, value)
-                    else:
-                        out[row, :, :, :, lanes] = value
-        return carry
-
-    lax.fori_loop(0, rows // 2, two, 0)
+def relax_group(group, tall, table, factor, kept):
+    for u, (place, _, _) in enumerate(group):
+        keep = jnp.dot(tall[place], factor[...], preferred_element_type=F32)
+        kept[u] = keep.reshape(16, 2, SUB, LANES)
+    for u, (place, moved, store) in enumerate(group):
+        for pair in range(moved.shape[-1] // PAIR):
+            columns = table[:, pair * PAIR : (pair + 1) * PAIR]
+            power = jnp.dot(tall[place], columns, preferred_element_type=F32)
+            for half in range(2):
+                chunk = 2 * pair + half
+                shape = jnp.exp2(power[:, half * LANES : (half + 1) * LANES])
+                shape = shape.reshape(16, 2, SUB, LANES)
+                lanes = pl.ds(chunk * LANES, LANES)
+                store(chunk, kept[u] * moved[:, :, :, lanes] + shape)
+
+
+def into(row):
+    def store(chunk, v):
+        row[:, :, :, pl.ds(chunk * LANES, LANES)] = v
+
+    return store
 
 
 def param_kernel(total, count, *refs):
@@ -307,9 +302,12 @@
     for r in range(rows):
         place = jnp.where(mirrored > 0, rows - 1 - r, r)
         codes[r : r + 1, :] = flat[pl.ds(place, 1), :]
-    for copy in copies:
+    half = len(copies) // 2
+    for copy in copies[:half]:
         copy.wait()
     unstage(near_cross, cross)
+    for copy in copies[half:]:
+        copy.wait()
     unstage(near_inside, inside)
 
 
@@ -318,9 +316,15 @@
         (m_cross, m_mid, m_in, params, table, factor, coef_ref, weights,
          cross, middle, inside, out, e_cross, e_in, sums, wide, tall, kept) = refs
         spread_features([params[k] for k in range(6)], wide, tall, rows)
-        relax_rows(m_cross, cross, tall, 0, 2, table, factor, kept)
-        relax_rows(m_mid, middle, tall, 2, rows - 4, table, factor, kept)
-        relax_rows(m_in, inside, tall, rows - 2, 2, table, factor, kept)
+        group = [(r, m_cross.at[r], into(cross.at[r])) for r in range(2)]
+        group += [(rows - 2 + r, m_in.at[r], into(inside.at[r])) for r in range(2)]
+        relax_group(group, tall, table, factor, kept)
+        for first in range(0, rows - 4, 4):
+            group = [
+                (2 + r, m_mid.at[r], into(middle.at[r]))
+                for r in range(first, min(first + 4, rows - 4))
+            ]
+            relax_group(group, tall, table, factor, kept)
     else:
         (cross, inside, state, coef_ref, weights, middle, out, e_cross, e_in, sums,
          near, sems) = refs
@@ -357,9 +361,9 @@
             x_row(cells, list(range(2, rows - 2)), store, coef)
         return carry
 
-    lax.fori_loop(0, chunks * 16, along_x, 0, unroll=2)
+    lax.fori_loop(0, chunks * 16, along_x, 0, unroll=4)
     yz_rows(middle, out, False, inner, coef_ref)
-    row_moments(out, inner, weights, sums, 0)
+    row_moments([(out.at[r], r) for r in range(inner)], weights, sums)
 
 
 def edge_kernel(relax, rows, line, *refs):
@@ -367,10 +371,11 @@
         (h_cross, h_in, p_cross, p_in, table, factor, cross, middle, inside, e_cross,
          e_in, coef_ref, weights, inner_sums, out_cross, out_in, sums,
          wide, tall, kept, low, high) = refs
-        spread_features([p_cross[k] for k in range(6)], wide, tall, 2)
-        relax_rows(h_cross, low, tall, 0, 2, table, factor, kept)
-        spread_features([p_in[k] for k in range(6)], wide, tall, 2)
-        relax_rows(h_in, high, tall, 0, 2, table, factor, kept)
+        params = [jnp.concatenate([p_cross[k], p_in[k]], axis=0) for k in range(6)]
+        spread_features(params, wide, tall, 4)
+        group = [(r, h_cross.at[r], into(low.at[r])) for r in range(2)]
+        group += [(2 + r, h_in.at[r], into(high.at[r])) for r in range(2)]
+        relax_group(group, tall, table, factor, kept)
     else:
         (low, high, cross, middle, inside, e_cross, e_in, coef_ref, weights,
          inner_sums, out_cross, out_in, sums) = refs
@@ -406,28 +411,34 @@
             x_row(cells, [rows - 2, rows - 1], store_in, coef, True)
         return carry
 
-    lax.fori_loop(0, chunks * 16, along_x, 0, unroll=2)
+    lax.fori_loop(0, chunks * 16, along_x, 0, unroll=4)
     for m in range(5):
         sums[m, 2 : rows - 2, :] = inner_sums[m]
-    row_moments(out_cross, 2, weights, sums, 0)
-    row_moments(out_in, 2, weights, sums, rows - 2)
+    edges = [(out_cross.at[r], r) for r in range(2)]
+    edges += [(out_in.at[r], rows - 2 + r) for r in range(2)]
+    row_moments(edges, weights, sums)
 
 
 def final_kernel(rows, m_cross, m_mid, m_in, params, table, factor, out,
                  wide, tall, kept, staged, sems):
     mirrored = lax.axis_index("gx") % 2
     spread_features([params[k] for k in range(6)], wide, tall, rows)
+    moved = [m_cross.at[r] for r in range(2)] + [m_mid.at[r] for r in range(rows - 4)]
+    moved += [m_in.at[r] for r in range(2)]
     copies = []
-    for source, first, count in ((m_cross, 0, 2), (m_mid, 2, rows - 4), (m_in, rows - 2, 2)):
-        near = staged.at[pl.ds(first, count)]
-
-        def store(row, chunk, value, near=near):
-            for y in range(16):
-                for t in range(2):
-                    near[row, y, chunk, pl.ds(t, SUB, stride=2), :] = value[y, t]
-
-        relax_rows(source, store, tall, first, count, table, factor, kept)
-        more = row_copies(mirrored, out, near, first, sems.at[pl.ds(first, count)], True)
+    for first in range(0, rows, 2):
+        near = staged.at[pl.ds(first, 2)]
+        group = []
+        for r in range(2):
+
+            def store(chunk, v, row=near.at[r]):
+                for y in range(16):
+                    for t in range(2):
+                        row[y, chunk, pl.ds(t, SUB, stride=2), :] = v[y, t]
+
+            group.append((first + r, moved[first + r], store))
+        relax_group(group, tall, table, factor, kept)
+        more = row_copies(mirrored, out, near, first, sems.at[pl.ds(first, 2)], True)
         for copy in more:
             copy.start()
         copies += more
@@ -457,7 +468,7 @@
         return [
             pltpu.VMEM((n, FEATURES, cells), F32),
             pltpu.VMEM((n, cells, FEATURES), BF16),
-            pltpu.VMEM((2, count_y, 2, SUB, LANES), F32),
+            pltpu.VMEM((4, count_y, 2, SUB, LANES), F32),
         ]
 
     def staging(n):
@@ -526,7 +537,7 @@
         scratch = []
         args = (*state, *edges, coef, weights, sums)
         if relax:
-            scratch = feature_scratch(2) + [slab_scratch(2)] * 2
+            scratch = feature_scratch(4) + [slab_scratch(2)] * 2
             args = (*params, table, factor, *args)
         args = (*halos, *args)
         return pl.pallas_call(

time: 76 us -> 73.1 us (0.962)
  Pallas kernels: 37.3 us -> 34.2 us
    pallas_call x3, Pallas kernels: 20.9 us -> 19.3 us  [inner(): pl.pallas_call(functools.partial(inner_kernel, relax, rows), in_specs=[vm...]
    pallas_call x3, Pallas kernels: 8.92 us -> 8.05 us  [edge(): pl.pallas_call(functools.partial(edge_kernel, relax, rows, line), in_spec...]
  transfers between devices with their start and end apart: 19 -> 19, of which waited for: 8 -> 8; matrix products, arithmetic and copies ran while one was open for 0% -> 0% of each run, Pallas kernels for 29% -> 28%
where the time goes in v6:
time: 73.1 us; the launch traced here: 73 us
  Pallas kernels  34.2 us (47%)
  starting transfers between devices  22.1 us (30%)
  waiting for transfers between devices  15.9 us (22%)
  between operations  0.76 us (1%)
    pallas_call x3, Pallas kernels, inner(): pl.pallas_call(functools.partial(inner_kernel, relax, rows), in_specs=[vm...  19.3 us
    ppermute x9, starting transfers between devices, gather(): parts.append(lax.ppermute(part, 'vert', pairs))  13.3 us
    ppermute x9, waiting for transfers between devices, gather(): parts.append(lax.ppermute(part, 'vert', pairs))  9.41 us
    ppermute x5, starting transfers between devices, exchange(): lax.ppermute(cross, ('groups', 'gx'), across)  8.25 us
    pallas_call x3, Pallas kernels, edge(): pl.pallas_call(functools.partial(edge_kernel, relax, rows, line), in_spec...  8.05 us
    ppermute x5, waiting for transfers between devices, exchange(): lax.ppermute(cross, ('groups', 'gx'), across)  6.46 us
    pallas_call x1, Pallas kernels, final(): pl.pallas_call(functools.partial(final_kernel, rows), in_specs=[vmem] * 6...  2.8 us
    pallas_call x1, Pallas kernels, load(): pl.pallas_call(load_kernel, in_specs=[hbm] * 3, out_specs=[vmem] * 7, out...  2.11 us
  transfers between devices with their start and end apart: 19, of which 8 were waited for; matrix products, arithmetic and copies ran while one was open for 0% of the time, Pallas kernels for 28%

profile of v6, /device:TPU:0, one launch (start us, length us, event | category | flops | bytes accessed | tf_op | source)
XLA Modules:
  0.0 73.0 jit_solution(6080081713072541727)
XLA Ops:
  0.0 2.1 %load_edges.1 = (f32[2,16,2,8,512]{4,3,2,1,0:T(8,128)S(1)}, f32[2,16,2,8,512]{4,3,2,1,0:T(8,128)S(1)}, s32[8,256]{1,0:T(8,128)S(1)}, bf16[32,512]{1,0:T(8,128)(2...) custom-call(s32[1,512]{1,0:T(1,128)} %bitcast.1, ...), custom_call_target="tpu_custom_call" | custom-call | tf_op jit(solution)/shard_map/load_edges/pallas_call | solution.py:487
  2.1 3.0 %collective-permute-start = (f32[2,16,2,8,512]{4,3,2,1,0:T(8,128)S(1)}, f32[2,16,2,8,512]{4,3,2,1,0:T(8,128)S(1)}, u32[]{:S(2)}, u32[]{:S(2)}) collective-permute-start(f32[2,16,2,8,512]{4,3,2,1,0:T(8,128)S(1)} %get-tuple-element.46.refs_0_.refs_2_), channel_id=1, source_target_pairs={{0,16},{12,28},{4,8},{8,4},{16,0},{28,12},{20,24},{24,20},{1,17},{... | collective-permute-start | bytes 3145736 | tf_op jit(solution)/shard_map/ppermute | solution.py:588
  5.2 0.1 collective-permute-start.1
  5.2 6.3 %inner_first.1 = (f32[4,16,2,8,512]{4,3,2,1,0:T(8,128)S(1)}, f32[4,16,2,8,512]{4,3,2,1,0:T(8,128)S(1)}, f32[2,16,2,8,512]{4,3,2,1,0:T(8,128)S(1)}, f32[2,16,2,8,512]{4,3,2,1,0:T(8,128)S(1)}, f32[5,4,256]{2,1,0:T(4,128)S(1)}) custom-call(f32[2,16,2,8,512]{4,3,2,1,0:T(8,128)S(1)} %get-tuple-element.46.refs_0_.refs_2_, ...), custom_call_target="tpu_custom_call" | custom-call | tf_op jit(solution)/shard_map/inner_first/pallas_call | solution.py:526
  11.5 6.4 %collective-permute-done.refs_0_ = f32[2,16,2,8,512]{4,3,2,1,0:T(8,128)S(1)} collective-permute-done((f32[2,16,2,8,512]{4,3,2,1,0:T(8,128)S(1)}, f32[2,16,2,8,512]{4,3,2,1,0:T(8,128)S(1)}, u32[]{:S(2)}, u32[]{:S(2)}) %collective-permute-start) | collective-permute-done | bytes 1048608 | tf_op jit(solution)/shard_map/ppermute | solution.py:588
  17.9 0.0 collective-permute-done.1.refs_1_
  17.9 2.2 %edge_first.1 = (f32[2,16,2,8,512]{4,3,2,1,0:T(8,128)S(1)}, f32[2,16,2,8,512]{4,3,2,1,0:T(8,128)S(1)}, f32[5,8,256]{2,1,0:T(8,128)S(1)}) custom-call(f32[2,16,2,8,512]{4,3,2,1,0:T(8,128)S(1)} %collective-permute-done.refs_0_, f32[2,16,2,8,512]{4,3,2,1,0:T(8,128)S(1)} %collective-permute-done.1.refs_1_, ...), custom_call_target="tpu_custom_call" | custom-call | tf_op jit(solution)/shard_map/edge_first/pallas_call | solution.py:543
  20.2 2.0 %collective-permute-start.2 = (f32[2,16,2,8,512]{4,3,2,1,0:T(8,128)S(1)}, f32[2,16,2,8,512]{4,3,2,1,0:T(8,128)S(1)}, u32[]{:S(2)}, u32[]{:S(2)}) collective-permute-start(f32[2,16,2,8,512]{4,3,2,1,0:T(8,128)S(1)} %get-tuple-element.54.refs_0_), channel_id=1, source_target_pairs={{0,16},{12,28},{4,8},{8,4},{16,0},{28,12},{20,24},{24,20},{1,17},{... | collective-permute-start | bytes 3145736 | tf_op jit(solution)/shard_map/ppermute | solution.py:588
  22.2 0.0 collective-permute-start.3
  22.2 1.6 %collective-permute-start.4 = (f32[5,8,256]{2,1,0:T(8,128)S(1)}, f32[5,8,256]{2,1,0:T(8,128)S(1)}, u32[]{:S(2)}, u32[]{:S(2)}) collective-permute-start(f32[5,8,256]{2,1,0:T(8,128)S(1)} %get-tuple-element.56.refs_0_), channel_id=1, source_target_pairs={{0,1},{1,2},{2,3},{3,0},{4,5},{5,6},{6,7},{7,4},{8,9},{9,10},{10,1... | collective-permute-start | bytes 122888 | tf_op jit(solution)/shard_map/ppermute | solution.py:596
  23.8 2.6 %collective-permute-start.5 = (f32[5,8,256]{2,1,0:T(8,128)S(1)}, f32[5,8,256]{2,1,0:T(8,128)S(1)}, u32[]{:S(2)}, u32[]{:S(2)}) collective-permute-start(f32[5,8,256]{2,1,0:T(8,128)S(1)} %get-tuple-element.56.refs_0_), channel_id=1, source_target_pairs={{0,2},{1,3},{2,0},{3,1},{4,6},{5,7},{6,4},{7,5},{8,10},{9,11},{10,... | collective-permute-start | bytes 122888 | tf_op jit(solution)/shard_map/ppermute | solution.py:596
  26.4 1.3 %collective-permute-start.6 = (f32[5,8,256]{2,1,0:T(8,128)S(1)}, f32[5,8,256]{2,1,0:T(8,128)S(1)}, u32[]{:S(2)}, u32[]{:S(2)}) collective-permute-start(f32[5,8,256]{2,1,0:T(8,128)S(1)} %get-tuple-element.56.refs_0_), channel_id=1, source_target_pairs={{0,3},{1,0},{2,1},{3,2},{4,7},{5,4},{6,5},{7,6},{8,11},{9,8},{10,9... | collective-permute-start | bytes 122888 | tf_op jit(solution)/shard_map/ppermute | solution.py:596
  28.4 0.0 collective-permute-done.4.refs_1_
  28.4 1.6 %collective-permute-done.5.refs_2_ = f32[5,8,256]{2,1,0:T(8,128)S(1)} collective-permute-done((f32[5,8,256]{2,1,0:T(8,128)S(1)}, f32[5,8,256]{2,1,0:T(8,128)S(1)}, u32[]{:S(2)}, u32[]{:S(2)}) %collective-permute-start.5) | collective-permute-done | bytes 40992 | tf_op jit(solution)/shard_map/ppermute | solution.py:596
  30.0 0.4 collective-permute-done.6.refs_3_
  30.4 0.6 cell_params.3
  31.1 1.1 %collective-permute-start.7 = (f32[6,2,256]{2,1,0:T(2,128)S(1)}, f32[6,2,256]{2,1,0:T(2,128)S(1)}, u32[]{:S(2)}, u32[]{:S(2)}) collective-permute-start(f32[6,2,256]{2,1,0:T(2,128)S(1)} %get-tuple-element.58), channel_id=1, source_target_pairs={{0,16},{12,28},{4,8},{8,4},{16,0},{28,12},{20,24},{24,20},{1,17},{... | collective-permute-start | bytes 36872 | tf_op jit(solution)/shard_map/ppermute | solution.py:588
  32.1 0.0 collective-permute-start.8
  32.1 6.5 %inner_relax.2 = (f32[2,16,2,8,512]{4,3,2,1,0:T(8,128)S(1)}, f32[4,16,2,8,512]{4,3,2,1,0:T(8,128)S(1)}, f32[2,16,2,8,512]{4,3,2,1,0:T(8,128)S(1)}, f32[4,16,2,8,...) custom-call(f32[2,16,2,8,512]{4,3,2,1,0:T(8,128)S(1)} %get-tuple-ele, ...), custom_call_target="tpu_custom_call" | custom-call | tf_op jit(solution)/shard_map/inner_relax/pallas_call | solution.py:526
  38.7 0.0 collective-permute-done.7.refs_2_
  38.7 0.0 collective-permute-done.8.refs_3_
  38.7 0.0 collective-permute-done.2.refs_0_
  38.7 0.0 collective-permute-done.3.refs_1_
  38.7 2.9 %edge_relax.2 = (f32[2,16,2,8,512]{4,3,2,1,0:T(8,128)S(1)}, f32[2,16,2,8,512]{4,3,2,1,0:T(8,128)S(1)}, f32[5,8,256]{2,1,0:T(8,128)S(1)}) custom-call(f32[2,16,2,8,512]{4,3,2,1,0:T(8,128)S(1)} %collective-permute-done.2.refs_0_, f32[2,16,2,8,512]{4,3,2,1,0:T(8,128)S(1)} %collective-permute-done.3.refs_1_, f32[6,2,256]{2,1,0:T(2,128)S(1)} %collective-permute-done.7.refs_2_, ...), custom_call_target="tpu_custom_call" | custom-call | tf_op jit(solution)/shard_map/edge_relax/pallas_call | solution.py:543
  41.6 0.5 collective-permute-start.10
  42.1 1.0 %collective-permute-start.9 = (f32[2,16,2,8,512]{4,3,2,1,0:T(8,128)S(1)}, f32[2,16,2,8,512]{4,3,2,1,0:T(8,128)S(1)}, u32[]{:S(2)}, u32[]{:S(2)}) collective-permute-start(f32[2,16,2,8,512]{4,3,2,1,0:T(8,128)S(1)} %get-tuple-element.70.refs_0_), channel_id=1, source_target_pairs={{0,16},{12,28},{4,8},{8,4},{16,0},{28,12},{20,24},{24,20},{1,17},{... | collective-permute-start | bytes 3145736 | tf_op jit(solution)/shard_map/ppermute | solution.py:588
  43.2 0.8 %collective-permute-start.11 = (f32[5,8,256]{2,1,0:T(8,128)S(1)}, f32[5,8,256]{2,1,0:T(8,128)S(1)}, u32[]{:S(2)}, u32[]{:S(2)}) collective-permute-start(f32[5,8,256]{2,1,0:T(8,128)S(1)} %get-tuple-element.72.refs_0_), channel_id=1, source_target_pairs={{0,1},{1,2},{2,3},{3,0},{4,5},{5,6},{6,7},{7,4},{8,9},{9,10},{10,1... | collective-permute-start | bytes 122888 | tf_op jit(solution)/shard_map/ppermute | solution.py:596
  44.0 2.8 %collective-permute-start.12 = (f32[5,8,256]{2,1,0:T(8,128)S(1)}, f32[5,8,256]{2,1,0:T(8,128)S(1)}, u32[]{:S(2)}, u32[]{:S(2)}) collective-permute-start(f32[5,8,256]{2,1,0:T(8,128)S(1)} %get-tuple-element.72.refs_0_), channel_id=1, source_target_pairs={{0,2},{1,3},{2,0},{3,1},{4,6},{5,7},{6,4},{7,5},{8,10},{9,11},{10,... | collective-permute-start | bytes 122888 | tf_op jit(solution)/shard_map/ppermute | solution.py:596
  46.8 0.2 collective-permute-start.13
  47.1 2.0 %collective-permute-done.11.refs_1_ = f32[5,8,256]{2,1,0:T(8,128)S(1)} collective-permute-done((f32[5,8,256]{2,1,0:T(8,128)S(1)}, f32[5,8,256]{2,1,0:T(8,128)S(1)}, u32[]{:S(2)}, u32[]{:S(2)}) %collective-permute-start.11) | collective-permute-done | bytes 40992 | tf_op jit(solution)/shard_map/ppermute | solution.py:596
  49.1 0.8 %collective-permute-done.12.refs_2_ = f32[5,8,256]{2,1,0:T(8,128)S(1)} collective-permute-done((f32[5,8,256]{2,1,0:T(8,128)S(1)}, f32[5,8,256]{2,1,0:T(8,128)S(1)}, u32[]{:S(2)}, u32[]{:S(2)}) %collective-permute-start.12) | collective-permute-done | bytes 40992 | tf_op jit(solution)/shard_map/ppermute | solution.py:596
  49.9 1.0 %collective-permute-done.13.refs_3_ = f32[5,8,256]{2,1,0:T(8,128)S(1)} collective-permute-done((f32[5,8,256]{2,1,0:T(8,128)S(1)}, f32[5,8,256]{2,1,0:T(8,128)S(1)}, u32[]{:S(2)}, u32[]{:S(2)}) %collective-permute-start.13) | collective-permute-done | bytes 40992 | tf_op jit(solution)/shard_map/ppermute | solution.py:596
  50.8 0.6 cell_params.4
  51.5 1.1 %collective-permute-start.14 = (f32[6,2,256]{2,1,0:T(2,128)S(1)}, f32[6,2,256]{2,1,0:T(2,128)S(1)}, u32[]{:S(2)}, u32[]{:S(2)}) collective-permute-start(f32[6,2,256]{2,1,0:T(2,128)S(1)} %get-tuple-element.73), channel_id=1, source_target_pairs={{0,16},{12,28},{4,8},{8,4},{16,0},{28,12},{20,24},{24,20},{1,17},{... | collective-permute-start | bytes 36872 | tf_op jit(solution)/shard_map/ppermute | solution.py:588
  52.6 0.0 collective-permute-start.15
  52.6 6.5 %inner_relax.3 = (f32[2,16,2,8,512]{4,3,2,1,0:T(8,128)S(1)}, f32[4,16,2,8,512]{4,3,2,1,0:T(8,128)S(1)}, f32[2,16,2,8,512]{4,3,2,1,0:T(8,128)S(1)}, f32[4,16,2,8,...) custom-call(f32[2,16,2,8,512]{4,3,2,1,0:T(8,128)S(1)} %get-tuple-ele, ...), custom_call_target="tpu_custom_call" | custom-call | tf_op jit(solution)/shard_map/inner_relax/pallas_call | solution.py:526
  59.1 0.0 collective-permute-done.14.refs_2_
  59.1 0.0 collective-permute-done.15.refs_3_
  59.2 0.0 collective-permute-done.10.refs_1_
  59.2 0.0 collective-permute-done.9.refs_0_
  59.2 2.9 %edge_relax.3 = (f32[2,16,2,8,512]{4,3,2,1,0:T(8,128)S(1)}, f32[2,16,2,8,512]{4,3,2,1,0:T(8,128)S(1)}, f32[5,8,256]{2,1,0:T(8,128)S(1)}) custom-call(f32[2,16,2,8,512]{4,3,2,1,0:T(8,128)S(1)} %collective-permute-done.9.refs_0_, f32[2,16,2,8,512]{4,3,2,1,0:T(8,128)S(1)} %collective-permute-done.10.refs_1_, f32[6,2,256]{2,1,0:T(2,128)S(1)} %collective-permute-done.14.refs_2_, ...), custom_call_target="tpu_custom_call" | custom-call | tf_op jit(solution)/shard_map/edge_relax/pallas_call | solution.py:543
  62.1 0.7 collective-permute-start.16
  62.8 2.1 %collective-permute-start.17 = (f32[5,8,256]{2,1,0:T(8,128)S(1)}, f32[5,8,256]{2,1,0:T(8,128)S(1)}, u32[]{:S(2)}, u32[]{:S(2)}) collective-permute-start(f32[5,8,256]{2,1,0:T(8,128)S(1)} %get-tuple-element.86.refs_0_), channel_id=1, source_target_pairs={{0,2},{1,3},{2,0},{3,1},{4,6},{5,7},{6,4},{7,5},{8,10},{9,11},{10,... | collective-permute-start | bytes 122888 | tf_op jit(solution)/shard_map/ppermute | solution.py:596
  64.9 1.0 %collective-permute-start.18 = (f32[5,8,256]{2,1,0:T(8,128)S(1)}, f32[5,8,256]{2,1,0:T(8,128)S(1)}, u32[]{:S(2)}, u32[]{:S(2)}) collective-permute-start(f32[5,8,256]{2,1,0:T(8,128)S(1)} %get-tuple-element.86.refs_0_), channel_id=1, source_target_pairs={{0,3},{1,0},{2,1},{3,2},{4,7},{5,4},{6,5},{7,6},{8,11},{9,8},{10,9... | collective-permute-start | bytes 122888 | tf_op jit(solution)/shard_map/ppermute | solution.py:596
  65.9 2.4 %collective-permute-done.16.refs_1_ = f32[5,8,256]{2,1,0:T(8,128)S(1)} collective-permute-done((f32[5,8,256]{2,1,0:T(8,128)S(1)}, f32[5,8,256]{2,1,0:T(8,128)S(1)}, u32[]{:S(2)}, u32[]{:S(2)}) %collective-permute-start.16) | collective-permute-done | bytes 40992 | tf_op jit(solution)/shard_map/ppermute | solution.py:596
  68.4 1.2 %collective-permute-done.17.refs_2_ = f32[5,8,256]{2,1,0:T(8,128)S(1)} collective-permute-done((f32[5,8,256]{2,1,0:T(8,128)S(1)}, f32[5,8,256]{2,1,0:T(8,128)S(1)}, u32[]{:S(2)}, u32[]{:S(2)}) %collective-permute-start.17) | collective-permute-done | bytes 40992 | tf_op jit(solution)/shard_map/ppermute | solution.py:596
  69.5 0.6 cell_params.5.params
  70.2 2.8 %final_relax.1 = f32[8,16,16,512]{3,2,1,0:T(8,128)} custom-call(f32[2,16,2,8,512]{4,3,2,1,0:T(8,128)S(1)} %get-tuple-element.83.m_cross, f32[4,16,2,8,512]{4,3,2,1,0:T(8,128)S(1)} %get-tuple-element.84.m_mid, f32[2,16,2,8,512]{4,3,2,1,0:T(8,128)S(1)} %get-tuple-element.85.m_in, f32[6,8,256]{2,1,0:T(8,128)S(1)} %cell_params.5.params, ...), custom_call_target="tpu_custom_call" | custom-call | tf_op jit(solution)/shard_map/final_relax/pallas_call | solution.py:564
  (3 shorter events, 0.0 us)
Async XLA Ops:
  2.1 15.8 %collective-permute-start = (f32[2,16,2,8,512]{4,3,2,1,0:T(8,128)S(1)}, f32[2,16,2,8,512]{4,3,2,1,0:T(8,128)S(1)}, u32[]{:S(2)}, u32[]{:S(2)}) collective-permute-start(f32[2,16,2,8,512]{4,3,2,1,0:T(8,128)S(1)} %get-tuple-element.46.refs_0_.refs_2_), channel_id=1, source_target_pairs={{0,16},{12,28},{4,8},{8,4},{16,0},{28,12},{20,24},{24,20},{1,17},{... | collective-permute-start | bytes 3145736 | tf_op jit(solution)/shard_map/ppermute | solution.py:588
  5.2 12.8 %collective-permute-start.1 = (f32[2,16,2,8,512]{4,3,2,1,0:T(8,128)S(1)}, f32[2,16,2,8,512]{4,3,2,1,0:T(8,128)S(1)}, u32[]{:S(2)}, u32[]{:S(2)}) collective-permute-start(f32[2,16,2,8,512]{4,3,2,1,0:T(8,128)S(1)} %get-tuple-element.47.refs_1_.refs_4_), channel_id=1, source_target_pairs={{0,4},{4,0},{8,12},{12,8},{1,5},{5,1},{9,13},{13,9},{2,6},{6,2},{1... | collective-permute-start | bytes 3145736 | tf_op jit(solution)/shard_map/ppermute | solution.py:589
  17.9 12.5 %copy-start = (f32[4]{0:T(128)S(1)}, f32[4]{0:T(128)}, u32[]{:S(2)}) copy-start(f32[4]{0:T(128)} %refs_6_.5) | copy-start | bytes 52
  20.2 18.5 %collective-permute-start.2 = (f32[2,16,2,8,512]{4,3,2,1,0:T(8,128)S(1)}, f32[2,16,2,8,512]{4,3,2,1,0:T(8,128)S(1)}, u32[]{:S(2)}, u32[]{:S(2)}) collective-permute-start(f32[2,16,2,8,512]{4,3,2,1,0:T(8,128)S(1)} %get-tuple-element.54.refs_0_), channel_id=1, source_target_pairs={{0,16},{12,28},{4,8},{8,4},{16,0},{28,12},{20,24},{24,20},{1,17},{... | collective-permute-start | bytes 3145736 | tf_op jit(solution)/shard_map/ppermute | solution.py:588
  22.2 16.5 %collective-permute-start.3 = (f32[2,16,2,8,512]{4,3,2,1,0:T(8,128)S(1)}, f32[2,16,2,8,512]{4,3,2,1,0:T(8,128)S(1)}, u32[]{:S(2)}, u32[]{:S(2)}) collective-permute-start(f32[2,16,2,8,512]{4,3,2,1,0:T(8,128)S(1)} %get-tuple-element.55.refs_2_), channel_id=1, source_target_pairs={{0,4},{4,0},{8,12},{12,8},{1,5},{5,1},{9,13},{13,9},{2,6},{6,2},{1... | collective-permute-start | bytes 3145736 | tf_op jit(solution)/shard_map/ppermute | solution.py:589
  22.2 6.2 %collective-permute-start.4 = (f32[5,8,256]{2,1,0:T(8,128)S(1)}, f32[5,8,256]{2,1,0:T(8,128)S(1)}, u32[]{:S(2)}, u32[]{:S(2)}) collective-permute-start(f32[5,8,256]{2,1,0:T(8,128)S(1)} %get-tuple-element.56.refs_0_), channel_id=1, source_target_pairs={{0,1},{1,2},{2,3},{3,0},{4,5},{5,6},{6,7},{7,4},{8,9},{9,10},{10,1... | collective-permute-start | bytes 122888 | tf_op jit(solution)/shard_map/ppermute | solution.py:596
  23.8 6.2 %collective-permute-start.5 = (f32[5,8,256]{2,1,0:T(8,128)S(1)}, f32[5,8,256]{2,1,0:T(8,128)S(1)}, u32[]{:S(2)}, u32[]{:S(2)}) collective-permute-start(f32[5,8,256]{2,1,0:T(8,128)S(1)} %get-tuple-element.56.refs_0_), channel_id=1, source_target_pairs={{0,2},{1,3},{2,0},{3,1},{4,6},{5,7},{6,4},{7,5},{8,10},{9,11},{10,... | collective-permute-start | bytes 122888 | tf_op jit(solution)/shard_map/ppermute | solution.py:596
  26.4 4.0 %collective-permute-start.6 = (f32[5,8,256]{2,1,0:T(8,128)S(1)}, f32[5,8,256]{2,1,0:T(8,128)S(1)}, u32[]{:S(2)}, u32[]{:S(2)}) collective-permute-start(f32[5,8,256]{2,1,0:T(8,128)S(1)} %get-tuple-element.56.refs_0_), channel_id=1, source_target_pairs={{0,3},{1,0},{2,1},{3,2},{4,7},{5,4},{6,5},{7,6},{8,11},{9,8},{10,9... | collective-permute-start | bytes 122888 | tf_op jit(solution)/shard_map/ppermute | solution.py:596
  31.1 7.6 %collective-permute-start.7 = (f32[6,2,256]{2,1,0:T(2,128)S(1)}, f32[6,2,256]{2,1,0:T(2,128)S(1)}, u32[]{:S(2)}, u32[]{:S(2)}) collective-permute-start(f32[6,2,256]{2,1,0:T(2,128)S(1)} %get-tuple-element.58), channel_id=1, source_target_pairs={{0,16},{12,28},{4,8},{8,4},{16,0},{28,12},{20,24},{24,20},{1,17},{... | collective-permute-start | bytes 36872 | tf_op jit(solution)/shard_map/ppermute | solution.py:588
  32.1 6.6 %collective-permute-start.8 = (f32[6,2,256]{2,1,0:T(2,128)S(1)}, f32[6,2,256]{2,1,0:T(2,128)S(1)}, u32[]{:S(2)}, u32[]{:S(2)}) collective-permute-start(f32[6,2,256]{2,1,0:T(2,128)S(1)} %get-tuple-element.59), channel_id=1, source_target_pairs={{0,4},{4,0},{8,12},{12,8},{1,5},{5,1},{9,13},{13,9},{2,6},{6,2},{1... | collective-permute-start | bytes 36872 | tf_op jit(solution)/shard_map/ppermute | solution.py:589
  41.6 17.5 %collective-permute-start.10 = (f32[2,16,2,8,512]{4,3,2,1,0:T(8,128)S(1)}, f32[2,16,2,8,512]{4,3,2,1,0:T(8,128)S(1)}, u32[]{:S(2)}, u32[]{:S(2)}) collective-permute-start(f32[2,16,2,8,512]{4,3,2,1,0:T(8,128)S(1)} %get-tuple-element.71.refs_2_), channel_id=1, source_target_pairs={{0,4},{4,0},{8,12},{12,8},{1,5},{5,1},{9,13},{13,9},{2,6},{6,2},{1... | collective-permute-start | bytes 3145736 | tf_op jit(solution)/shard_map/ppermute | solution.py:589
  42.1 17.0 %collective-permute-start.9 = (f32[2,16,2,8,512]{4,3,2,1,0:T(8,128)S(1)}, f32[2,16,2,8,512]{4,3,2,1,0:T(8,128)S(1)}, u32[]{:S(2)}, u32[]{:S(2)}) collective-permute-start(f32[2,16,2,8,512]{4,3,2,1,0:T(8,128)S(1)} %get-tuple-element.70.refs_0_), channel_id=1, source_target_pairs={{0,16},{12,28},{4,8},{8,4},{16,0},{28,12},{20,24},{24,20},{1,17},{... | collective-permute-start | bytes 3145736 | tf_op jit(solution)/shard_map/ppermute | solution.py:588
  43.2 5.9 %collective-permute-start.11 = (f32[5,8,256]{2,1,0:T(8,128)S(1)}, f32[5,8,256]{2,1,0:T(8,128)S(1)}, u32[]{:S(2)}, u32[]{:S(2)}) collective-permute-start(f32[5,8,256]{2,1,0:T(8,128)S(1)} %get-tuple-element.72.refs_0_), channel_id=1, source_target_pairs={{0,1},{1,2},{2,3},{3,0},{4,5},{5,6},{6,7},{7,4},{8,9},{9,10},{10,1... | collective-permute-start | bytes 122888 | tf_op jit(solution)/shard_map/ppermute | solution.py:596
  44.0 5.9 %collective-permute-start.12 = (f32[5,8,256]{2,1,0:T(8,128)S(1)}, f32[5,8,256]{2,1,0:T(8,128)S(1)}, u32[]{:S(2)}, u32[]{:S(2)}) collective-permute-start(f32[5,8,256]{2,1,0:T(8,128)S(1)} %get-tuple-element.72.refs_0_), channel_id=1, source_target_pairs={{0,2},{1,3},{2,0},{3,1},{4,6},{5,7},{6,4},{7,5},{8,10},{9,11},{10,... | collective-permute-start | bytes 122888 | tf_op jit(solution)/shard_map/ppermute | solution.py:596
  46.8 4.0 %collective-permute-start.13 = (f32[5,8,256]{2,1,0:T(8,128)S(1)}, f32[5,8,256]{2,1,0:T(8,128)S(1)}, u32[]{:S(2)}, u32[]{:S(2)}) collective-permute-start(f32[5,8,256]{2,1,0:T(8,128)S(1)} %get-tuple-element.72.refs_0_), channel_id=1, source_target_pairs={{0,3},{1,0},{2,1},{3,2},{4,7},{5,4},{6,5},{7,6},{8,11},{9,8},{10,9... | collective-permute-start | bytes 122888 | tf_op jit(solution)/shard_map/ppermute | solution.py:596
  51.5 7.6 %collective-permute-start.14 = (f32[6,2,256]{2,1,0:T(2,128)S(1)}, f32[6,2,256]{2,1,0:T(2,128)S(1)}, u32[]{:S(2)}, u32[]{:S(2)}) collective-permute-start(f32[6,2,256]{2,1,0:T(2,128)S(1)} %get-tuple-element.73), channel_id=1, source_target_pairs={{0,16},{12,28},{4,8},{8,4},{16,0},{28,12},{20,24},{24,20},{1,17},{... | collective-permute-start | bytes 36872 | tf_op jit(solution)/shard_map/ppermute | solution.py:588
  52.6 6.6 %collective-permute-start.15 = (f32[6,2,256]{2,1,0:T(2,128)S(1)}, f32[6,2,256]{2,1,0:T(2,128)S(1)}, u32[]{:S(2)}, u32[]{:S(2)}) collective-permute-start(f32[6,2,256]{2,1,0:T(2,128)S(1)} %get-tuple-element.74), channel_id=1, source_target_pairs={{0,4},{4,0},{8,12},{12,8},{1,5},{5,1},{9,13},{13,9},{2,6},{6,2},{1... | collective-permute-start | bytes 36872 | tf_op jit(solution)/shard_map/ppermute | solution.py:589
  62.1 6.3 %collective-permute-start.16 = (f32[5,8,256]{2,1,0:T(8,128)S(1)}, f32[5,8,256]{2,1,0:T(8,128)S(1)}, u32[]{:S(2)}, u32[]{:S(2)}) collective-permute-start(f32[5,8,256]{2,1,0:T(8,128)S(1)} %get-tuple-element.86.refs_0_), channel_id=1, source_target_pairs={{0,1},{1,2},{2,3},{3,0},{4,5},{5,6},{6,7},{7,4},{8,9},{9,10},{10,1... | collective-permute-start | bytes 122888 | tf_op jit(solution)/shard_map/ppermute | solution.py:596
  62.8 6.8 %collective-permute-start.17 = (f32[5,8,256]{2,1,0:T(8,128)S(1)}, f32[5,8,256]{2,1,0:T(8,128)S(1)}, u32[]{:S(2)}, u32[]{:S(2)}) collective-permute-start(f32[5,8,256]{2,1,0:T(8,128)S(1)} %get-tuple-element.86.refs_0_), channel_id=1, source_target_pairs={{0,2},{1,3},{2,0},{3,1},{4,6},{5,7},{6,4},{7,5},{8,10},{9,11},{10,... | collective-permute-start | bytes 122888 | tf_op jit(solution)/shard_map/ppermute | solution.py:596
  64.9 4.6 %collective-permute-start.18 = (f32[5,8,256]{2,1,0:T(8,128)S(1)}, f32[5,8,256]{2,1,0:T(8,128)S(1)}, u32[]{:S(2)}, u32[]{:S(2)}) collective-permute-start(f32[5,8,256]{2,1,0:T(8,128)S(1)} %get-tuple-element.86.refs_0_), channel_id=1, source_target_pairs={{0,3},{1,0},{2,1},{3,2},{4,7},{5,4},{6,5},{7,6},{8,11},{9,8},{10,9... | collective-permute-start | bytes 122888 | tf_op jit(solution)/shard_map/ppermute | solution.py:596

commit v7 on v6

--- a/solution.py
+++ b/solution.py
@@ -171,7 +171,11 @@
 
 def param_kernel(total, count, *refs):
     parts = refs[:count]
-    codes, knudsen, inflow, out, *edges = refs[count:]
+    if len(refs) == count + 4:
+        codes, knudsen, inflow, out = refs[count:]
+    else:
+        (codes, knudsen, inflow, m_in, table, factor, out, p_cross, inside,
+         wide, tall, kept) = refs[count:]
     sums = [parts[0][m] for m in range(5)]
     for part in parts[1:]:
         sums = [s + part[m] for m, s in enumerate(sums)]
@@ -208,9 +212,12 @@
     rows = code.shape[0]
     for k, value in enumerate(params):
         out[k] = value
-        if edges:
-            edges[0][k] = value[:2]
-            edges[1][k] = value[rows - 2 :]
+    if len(refs) > count + 4:
+        for k, value in enumerate(params):
+            p_cross[k] = value[:2]
+        spread_features([value[rows - 2 :] for value in params], wide, tall, 2)
+        group = [(r, m_in.at[r], into(inside.at[r])) for r in range(2)]
+        relax_group(group, tall, table, factor, kept)
 
 
 def row_copies(mirrored, whole, staged, first, sems, out=False):
@@ -313,18 +320,13 @@
 
 def inner_kernel(relax, rows, *refs):
     if relax:
-        (m_cross, m_mid, m_in, params, table, factor, coef_ref, weights,
-         cross, middle, inside, out, e_cross, e_in, sums, wide, tall, kept) = refs
-        spread_features([params[k] for k in range(6)], wide, tall, rows)
+        (m_cross, m_mid, inside, params, table, factor, coef_ref, weights,
+         cross, middle, out, e_cross, e_in, sums, wide, tall, kept) = refs
+        spread_features([params[k] for k in range(6)], wide, tall, rows - 2)
         group = [(r, m_cross.at[r], into(cross.at[r])) for r in range(2)]
-        group += [(rows - 2 + r, m_in.at[r], into(inside.at[r])) for r in range(2)]
-        relax_group(group, tall, table, factor, kept)
-        for first in range(0, rows - 4, 4):
-            group = [
-                (2 + r, m_mid.at[r], into(middle.at[r]))
-                for r in range(first, min(first + 4, rows - 4))
-            ]
-            relax_group(group, tall, table, factor, kept)
+        group += [(2 + r, m_mid.at[r], into(middle.at[r])) for r in range(rows - 4)]
+        for first in range(0, rows - 2, 3):
+            relax_group(group[first : first + 3], tall, table, factor, kept)
     else:
         (cross, inside, state, coef_ref, weights, middle, out, e_cross, e_in, sums,
          near, sems) = refs
@@ -366,19 +368,32 @@
     row_moments([(out.at[r], r) for r in range(inner)], weights, sums)
 
 
-def edge_kernel(relax, rows, line, *refs):
+def edge_kernel(sides, relax, rows, line, *refs):
+    refs = list(refs)
+    take = lambda n: [refs.pop(0) for _ in range(n)]
+    if "cross" in sides:
+        low, cross, e_cross, inner_sums = take(4)
+        if relax:
+            params, table, factor = take(3)
+    if "in" in sides:
+        high, inside, e_in = take(3)
+    elif "cross" in sides:
+        (in_sums,) = take(1)
+    middle, coef_ref, weights, sums = take(4)
+    edges = []
+    if "cross" in sides:
+        (out_cross,) = take(1)
+        edges += [(out_cross.at[r], r) for r in range(2)]
+    if "in" in sides:
+        (out_in,) = take(1)
+        first = rows - 2 if "cross" in sides else 0
+        edges += [(out_in.at[r], first + r) for r in range(2)]
     if relax:
-        (h_cross, h_in, p_cross, p_in, table, factor, cross, middle, inside, e_cross,
-         e_in, coef_ref, weights, inner_sums, out_cross, out_in, sums,
-         wide, tall, kept, low, high) = refs
-        params = [jnp.concatenate([p_cross[k], p_in[k]], axis=0) for k in range(6)]
-        spread_features(params, wide, tall, 4)
-        group = [(r, h_cross.at[r], into(low.at[r])) for r in range(2)]
-        group += [(2 + r, h_in.at[r], into(high.at[r])) for r in range(2)]
+        wide, tall, kept, relaxed = take(4)
+        spread_features([params[k] for k in range(6)], wide, tall, 2)
+        group = [(r, low.at[r], into(relaxed.at[r])) for r in range(2)]
         relax_group(group, tall, table, factor, kept)
-    else:
-        (low, high, cross, middle, inside, e_cross, e_in, coef_ref, weights,
-         inner_sums, out_cross, out_in, sums) = refs
+        low = relaxed
     chunks = middle.shape[-1] // LANES
     place = lax.axis_index("gx")
     present = jnp.where((place == 0) | (place == line - 1), 0.0, 1.0)
@@ -388,34 +403,37 @@
         lanes = lanes_of(chunk)
         coef = coefs_of(coef_ref, lanes)
         for t in range(2):
-            cells = {}
-            for n in range(2):
-                cells[-1 - n] = low[n, y, t, :, lanes] * present
-                cells[n] = cross[n, y, t, :, lanes]
-                cells[2 + n] = middle[n, y, t, :, lanes]
-
-            def store(n, v, t=t):
-                out_cross[n, y, t, :, lanes] = e_cross[n, y, t, :, lanes] - v
-
-            x_row(cells, [0, 1], store, coef, True)
-            cells = {}
-            for n in range(2):
-                cells[rows - 4 + n] = middle[rows - 6 + n, y, t, :, lanes]
-                cells[rows - 2 + n] = inside[n, y, t, :, lanes]
-                cells[rows + n] = high[1 - n, y, t, :, lanes]
-
-            def store_in(n, v, t=t):
-                r = n - rows + 2
-                out_in[r, y, t, :, lanes] = e_in[r, y, t, :, lanes] - v
-
-            x_row(cells, [rows - 2, rows - 1], store_in, coef, True)
+            if "cross" in sides:
+                cells = {}
+                for n in range(2):
+                    cells[-1 - n] = low[n, y, t, :, lanes] * present
+                    cells[n] = cross[n, y, t, :, lanes]
+                    cells[2 + n] = middle[n, y, t, :, lanes]
+
+                def store(n, v, t=t):
+                    out_cross[n, y, t, :, lanes] = e_cross[n, y, t, :, lanes] - v
+
+                x_row(cells, [0, 1], store, coef, True)
+            if "in" in sides:
+                cells = {}
+                for n in range(2):
+                    cells[rows - 4 + n] = middle[rows - 6 + n, y, t, :, lanes]
+                    cells[rows - 2 + n] = inside[n, y, t, :, lanes]
+                    cells[rows + n] = high[1 - n, y, t, :, lanes]
+
+                def store_in(n, v, t=t):
+                    r = n - rows + 2
+                    out_in[r, y, t, :, lanes] = e_in[r, y, t, :, lanes] - v
+
+                x_row(cells, [rows - 2, rows - 1], store_in, coef, True)
         return carry
 
     lax.fori_loop(0, chunks * 16, along_x, 0, unroll=4)
-    for m in range(5):
-        sums[m, 2 : rows - 2, :] = inner_sums[m]
-    edges = [(out_cross.at[r], r) for r in range(2)]
-    edges += [(out_in.at[r], rows - 2 + r) for r in range(2)]
+    if "cross" in sides:
+        for m in range(5):
+            sums[m, 2 : rows - 2, :] = inner_sums[m]
+            if "in" not in sides:
+                sums[m, rows - 2 :, :] = in_sums[m]
     row_moments(edges, weights, sums)
 
 
@@ -468,7 +486,7 @@
         return [
             pltpu.VMEM((n, FEATURES, cells), F32),
             pltpu.VMEM((n, cells, FEATURES), BF16),
-            pltpu.VMEM((4, count_y, 2, SUB, LANES), F32),
+            pltpu.VMEM((min(n, 4), count_y, 2, SUB, LANES), F32),
         ]
 
     def staging(n):
@@ -516,8 +534,8 @@
         out_shape = [slab(rows - 4), slab(2), slab(2), sums]
         scratch = []
         if relax:
-            out_shape = [slab(2), slab(rows - 4), slab(2)] + out_shape
-            scratch = feature_scratch(rows)
+            out_shape = [slab(2), slab(rows - 4)] + out_shape
+            scratch = feature_scratch(rows - 2)
             args = (*state, params, table, factor, coef, weights)
         else:
             out_shape = [slab(rows - 4)] + out_shape
@@ -533,32 +551,32 @@
             name="inner_relax" if relax else "inner_first",
         )(*args)
 
-    def edge(relax, halos, params, state, edges, sums):
-        scratch = []
-        args = (*state, *edges, coef, weights, sums)
-        if relax:
-            scratch = feature_scratch(4) + [slab_scratch(2)] * 2
-            args = (*params, table, factor, *args)
-        args = (*halos, *args)
+    def edge(sides, relax, *args):
+        scratch = feature_scratch(2) + [slab_scratch(2)] if relax else []
         return pl.pallas_call(
-            functools.partial(edge_kernel, relax, rows, line),
-            in_specs=[vmem] * len(args),
-            out_specs=[vmem] * 3,
-            out_shape=[slab(2), slab(2), jax.ShapeDtypeStruct((5, rows, cells), F32)],
+            functools.partial(edge_kernel, sides, relax, rows, line),
+            in_specs=[vmem] * (len(args) + 2),
+            out_specs=[vmem] * (1 + len(sides)),
+            out_shape=[jax.ShapeDtypeStruct((5, rows if "cross" in sides else 2, cells), F32)]
+            + [slab(2)] * len(sides),
             scratch_shapes=scratch,
             compiler_params=limits(LIMIT_MIB),
-            name="edge_relax" if relax else "edge_first",
-        )(*args)
-
-    def cell_params(parts, *sizes):
+            name="edge_" + "_".join(sides),
+        )(*args, coef, weights)
+
+    def cell_params(parts, *edge_args):
+        out_shape = [jax.ShapeDtypeStruct((6, rows, cells), F32)]
+        if edge_args:
+            out_shape += [jax.ShapeDtypeStruct((6, 2, cells), F32), slab(2)]
         return pl.pallas_call(
             functools.partial(param_kernel, total, len(parts)),
-            in_specs=[vmem] * (len(parts) + 1) + [smem, smem],
-            out_specs=[vmem] * len(sizes),
-            out_shape=[jax.ShapeDtypeStruct((6, n, cells), F32) for n in sizes],
+            in_specs=[vmem] * (len(parts) + 1) + [smem, smem] + [vmem] * len(edge_args),
+            out_specs=[vmem] * len(out_shape),
+            out_shape=out_shape,
+            scratch_shapes=feature_scratch(2) if edge_args else [],
             compiler_params=limits(4),
             name="cell_params",
-        )(*parts, codes, knudsen, inflow)
+        )(*parts, codes, knudsen, inflow, *edge_args)
 
     def final(moved, params):
         return pl.pallas_call(
@@ -583,11 +601,11 @@
     for i in range(0, line, 2):
         within += [(i, i + 1), (i + 1, i)]
 
-    def exchange(cross, inside):
-        return (
-            lax.ppermute(cross, ("groups", "gx"), across),
-            lax.ppermute(inside, "gx", within),
-        )
+    def swap_across(x):
+        return lax.ppermute(x, ("groups", "gx"), across)
+
+    def swap_within(x):
+        return lax.ppermute(x, "gx", within)
 
     def gather(part):
         parts = [part]
@@ -597,19 +615,21 @@
         return parts
 
     cross, inside, codes, table, factor, weights, coef = load()
-    halos = exchange(cross, inside)
+    low, high = swap_across(cross), swap_within(inside)
     middle, m_mid, e_cross, e_in, sums = inner(False, (cross, inside, in_hbm(distribution)), None)
-    m_cross, m_in, sums = edge(
-        False, halos, None, (cross, middle, inside), (e_cross, e_in), sums
-    )
+    in_sums, m_in = edge(("in",), False, high, inside, e_in, middle)
+    sums, m_cross = edge(("cross",), False, low, cross, e_cross, sums, in_sums, middle)
     for _ in range(1, STEPS):
-        halos = exchange(m_cross, m_in)
-        params, p_cross, p_in = cell_params(gather(sums), rows, 2, 2)
-        p_halos = exchange(p_cross, p_in)
-        moved = (m_cross, m_mid, m_in)
-        *state, m_mid, e_cross, e_in, sums = inner(True, moved, params)
-        m_cross, m_in, sums = edge(True, halos, p_halos, state, (e_cross, e_in), sums)
-    (params,) = cell_params(gather(sums), rows)
+        low = swap_across(m_cross)
+        params, p_cross, inside = cell_params(gather(sums), m_in, table, factor)
+        p_low, high = swap_across(p_cross), swap_within(inside)
+        cross, middle, m_mid, e_cross, e_in, sums = inner(
+            True, (m_cross, m_mid, inside), params
+        )
+        far = (low, cross, e_cross, sums, p_low, table, factor)
+        near = (high, inside, e_in)
+        sums, m_cross, m_in = edge(("cross", "in"), True, *far, *near, middle)
+    (params,) = cell_params(gather(sums))
     return final((m_cross, m_mid, m_in), params)
 
 

time: 73.1 us -> 76.4 us (1.045)
  waiting for transfers between devices: 15.9 us -> 17.4 us
  starting transfers between devices: 22.1 us -> 23.5 us
    ppermute x10 -> x8, waiting for transfers between devices: 6.47 us -> 9.18 us  [the longest x5 9.17 us: swap_across(): return lax.ppermute(x, ('groups', 'gx'), across)]
    ppermute x9, waiting for transfers between devices: 9.41 us -> 8.24 us  [gather(): parts.append(lax.ppermute(part, 'vert', pairs))]
    pallas_call x3, Pallas kernels: 1.92 us -> 2.78 us  [cell_params(): pl.pallas_call(functools.partial(param_kernel, total, len(parts)), in_spe...]
    ppermute x10 -> x8, starting transfers between devices: 8.87 us -> 9.53 us  [the longest x5 8.87 us: swap_across(): return lax.ppermute(x, ('groups', 'gx'), across)]
    pallas_call x3 -> x4, Pallas kernels: 8.05 us -> 8.08 us  [edge(): pl.pallas_call(functools.partial(edge_kernel, sides, relax, rows, line),...]
  transfers between devices with their start and end apart: 19 -> 17, of which waited for: 8 -> 9; matrix products, arithmetic and copies ran while one was open for 0% -> 0% of each run, Pallas kernels for 28% -> 29%
where the time goes in v7:
time: 76.4 us; the launch traced here: 76.3 us
  Pallas kernels  34.7 us (45%)
  starting transfers between devices  23.5 us (31%)
  waiting for transfers between devices  17.4 us (23%)
    pallas_call x3, Pallas kernels, inner(): pl.pallas_call(functools.partial(inner_kernel, relax, rows), in_specs=[vm...  18.9 us
    ppermute x9, starting transfers between devices, gather(): parts.append(lax.ppermute(part, 'vert', pairs))  13.9 us
    ppermute x5, waiting for transfers between devices, swap_across(): return lax.ppermute(x, ('groups', 'gx'), across)  9.17 us
    ppermute x5, starting transfers between devices, swap_across(): return lax.ppermute(x, ('groups', 'gx'), across)  8.87 us
    ppermute x9, waiting for transfers between devices, gather(): parts.append(lax.ppermute(part, 'vert', pairs))  8.24 us
    pallas_call x4, Pallas kernels, edge(): pl.pallas_call(functools.partial(edge_kernel, sides, relax, rows, line),...  8.08 us
    pallas_call x1, Pallas kernels, final(): pl.pallas_call(functools.partial(final_kernel, rows), in_specs=[vmem] * 6...  2.8 us
    pallas_call x3, Pallas kernels, cell_params(): pl.pallas_call(functools.partial(param_kernel, total, len(parts)), in_spe...  2.78 us
  transfers between devices with their start and end apart: 17, of which 9 were waited for; matrix products, arithmetic and copies ran while one was open for 0% of the time, Pallas kernels for 29%

profile of v7, /device:TPU:0, one launch (start us, length us, event | category | flops | bytes accessed | tf_op | source)
XLA Modules:
  0.0 76.3 jit_solution(13070943281116499564)
XLA Ops:
  0.0 2.1 %load_edges.1 = (f32[2,16,2,8,512]{4,3,2,1,0:T(8,128)S(1)}, f32[2,16,2,8,512]{4,3,2,1,0:T(8,128)S(1)}, s32[8,256]{1,0:T(8,128)S(1)}, bf16[32,512]{1,0:T(8,128)(2...) custom-call(s32[1,512]{1,0:T(1,128)} %bitcast.1, ...), custom_call_target="tpu_custom_call" | custom-call | tf_op jit(solution)/shard_map/load_edges/pallas_call | solution.py:505
  2.1 0.5 collective-permute-start.1
  2.6 2.6 %collective-permute-start = (f32[2,16,2,8,512]{4,3,2,1,0:T(8,128)S(1)}, f32[2,16,2,8,512]{4,3,2,1,0:T(8,128)S(1)}, u32[]{:S(2)}, u32[]{:S(2)}) collective-permute-start(f32[2,16,2,8,512]{4,3,2,1,0:T(8,128)S(1)} %get-tuple-element.45.refs_0_.refs_1_), channel_id=1, source_target_pairs={{0,16},{12,28},{4,8},{8,4},{16,0},{28,12},{20,24},{24,20},{1,17},{... | collective-permute-start | bytes 3145736 | tf_op jit(solution)/shard_map/ppermute | solution.py:605
  5.2 6.3 %inner_first.1 = (f32[4,16,2,8,512]{4,3,2,1,0:T(8,128)S(1)}, f32[4,16,2,8,512]{4,3,2,1,0:T(8,128)S(1)}, f32[2,16,2,8,512]{4,3,2,1,0:T(8,128)S(1)}, f32[2,16,2,8,512]{4,3,2,1,0:T(8,128)S(1)}, f32[5,4,256]{2,1,0:T(4,128)S(1)}) custom-call(f32[2,16,2,8,512]{4,3,2,1,0:T(8,128)S(1)} %get-tuple-element.45.refs_0_.refs_1_, ...), custom_call_target="tpu_custom_call" | custom-call | tf_op jit(solution)/shard_map/inner_first/pallas_call | solution.py:544
  11.5 0.0 collective-permute-done.1.refs_0_
  11.5 1.3 %edge_in.1 = (f32[5,2,256]{2,1,0:T(2,128)S(1)}, f32[2,16,2,8,512]{4,3,2,1,0:T(8,128)S(1)}) custom-call(f32[2,16,2,8,512]{4,3,2,1,0:T(8,128)S(1)} %collective-permute-done.1.refs_0_, f32[2,16,2,8,512]{4,3,2,1,0:T(8,128)S(1)} %get-tuple-element.46.refs_1_, f32[2,16,2,8,512]{4,3,2,1,0:T(8,128)S(1)} %get-tuple-element.51.refs_2_, ...), custom_call_target="tpu_custom_call" | custom-call | tf_op jit(solution)/shard_map/edge_in/pallas_call | solution.py:556
  12.9 5.2 %collective-permute-done.refs_0_ = f32[2,16,2,8,512]{4,3,2,1,0:T(8,128)S(1)} collective-permute-done((f32[2,16,2,8,512]{4,3,2,1,0:T(8,128)S(1)}, f32[2,16,2,8,512]{4,3,2,1,0:T(8,128)S(1)}, u32[]{:S(2)}, u32[]{:S(2)}) %collective-permute-start) | collective-permute-done | bytes 1048608 | tf_op jit(solution)/shard_map/ppermute | solution.py:605
  18.0 0.0 copy-start
  18.0 1.3 %edge_cross.1 = (f32[5,8,256]{2,1,0:T(8,128)S(1)}, f32[2,16,2,8,512]{4,3,2,1,0:T(8,128)S(1)}) custom-call(f32[2,16,2,8,512]{4,3,2,1,0:T(8,128)S(1)} %collective-permute-done.refs_0_, f32[2,16,2,8,512]{4,3,2,1,0:T(8,128)S(1)} %get-tuple-element.45.refs_0_.refs_1_, f32[2,16,2,8,512]{4,3,2,1,0:T(8,128)S(1)} %get-tuple-element.49.refs_2_, ...), custom_call_target="tpu_custom_call" | custom-call | tf_op jit(solution)/shard_map/edge_cross/pallas_call | solution.py:556
  19.4 2.1 %collective-permute-start.3 = (f32[5,8,256]{2,1,0:T(8,128)S(1)}, f32[5,8,256]{2,1,0:T(8,128)S(1)}, u32[]{:S(2)}, u32[]{:S(2)}) collective-permute-start(f32[5,8,256]{2,1,0:T(8,128)S(1)} %get-tuple-element.56.refs_0_), channel_id=1, source_target_pairs={{0,1},{1,2},{2,3},{3,0},{4,5},{5,6},{6,7},{7,4},{8,9},{9,10},{10,1... | collective-permute-start | bytes 122888 | tf_op jit(solution)/shard_map/ppermute | solution.py:614
  21.4 2.6 %collective-permute-start.4 = (f32[5,8,256]{2,1,0:T(8,128)S(1)}, f32[5,8,256]{2,1,0:T(8,128)S(1)}, u32[]{:S(2)}, u32[]{:S(2)}) collective-permute-start(f32[5,8,256]{2,1,0:T(8,128)S(1)} %get-tuple-element.56.refs_0_), channel_id=1, source_target_pairs={{0,2},{1,3},{2,0},{3,1},{4,6},{5,7},{6,4},{7,5},{8,10},{9,11},{10,... | collective-permute-start | bytes 122888 | tf_op jit(solution)/shard_map/ppermute | solution.py:614
  24.0 1.3 %collective-permute-start.5 = (f32[5,8,256]{2,1,0:T(8,128)S(1)}, f32[5,8,256]{2,1,0:T(8,128)S(1)}, u32[]{:S(2)}, u32[]{:S(2)}) collective-permute-start(f32[5,8,256]{2,1,0:T(8,128)S(1)} %get-tuple-element.56.refs_0_), channel_id=1, source_target_pairs={{0,3},{1,0},{2,1},{3,2},{4,7},{5,4},{6,5},{7,6},{8,11},{9,8},{10,9... | collective-permute-start | bytes 122888 | tf_op jit(solution)/shard_map/ppermute | solution.py:614
  26.0 1.6 %collective-permute-start.2 = (f32[2,16,2,8,512]{4,3,2,1,0:T(8,128)S(1)}, f32[2,16,2,8,512]{4,3,2,1,0:T(8,128)S(1)}, u32[]{:S(2)}, u32[]{:S(2)}) collective-permute-start(f32[2,16,2,8,512]{4,3,2,1,0:T(8,128)S(1)} %get-tuple-element.54.refs_0_), channel_id=1, source_target_pairs={{0,16},{12,28},{4,8},{8,4},{16,0},{28,12},{20,24},{24,20},{1,17},{... | collective-permute-start | bytes 3145736 | tf_op jit(solution)/shard_map/ppermute | solution.py:605
  27.6 0.0 collective-permute-done.3.refs_1_
  27.6 0.0 collective-permute-done.4.refs_2_
  27.6 0.4 collective-permute-done.5.refs_3_
  28.0 0.0 copy-done
  28.0 1.1 %cell_params.3 = (f32[6,8,256]{2,1,0:T(8,128)S(1)}, f32[6,2,256]{2,1,0:T(2,128)S(1)}, f32[2,16,2,8,512]{4,3,2,1,0:T(8,128)S(1)}) custom-call(f32[5,8,256]{2,1,0:T(8,128)S(1)} %get-tuple-element.56.refs_0_, f32[5,8,256]{2,1,0:T(8,128)S(1)} %collective-permute-done.3.refs_1_, f32[5,8,256]{2,1,0:T(8,128)S(1)} %collective-permute-done.4.refs_2_, ...), custom_call_target="tpu_custom_call" | custom-call | tf_op jit(solution)/shard_map/cell_params/pallas_call | solution.py:571
  29.1 0.1 collective-permute-start.7
  29.2 1.6 %collective-permute-start.6 = (f32[6,2,256]{2,1,0:T(2,128)S(1)}, f32[6,2,256]{2,1,0:T(2,128)S(1)}, u32[]{:S(2)}, u32[]{:S(2)}) collective-permute-start(f32[6,2,256]{2,1,0:T(2,128)S(1)} %get-tuple-element.66), channel_id=1, source_target_pairs={{0,16},{12,28},{4,8},{8,4},{16,0},{28,12},{20,24},{24,20},{1,17},{... | collective-permute-start | bytes 36872 | tf_op jit(solution)/shard_map/ppermute | solution.py:605
  30.8 6.3 %inner_relax.2 = (f32[2,16,2,8,512]{4,3,2,1,0:T(8,128)S(1)}, f32[4,16,2,8,512]{4,3,2,1,0:T(8,128)S(1)}, f32[4,16,2,8,512]{4,3,2,1,0:T(8,128)S(1)}, f32[2,16,2,8,...) custom-call(f32[2,16,2,8,512]{4,3,2,1,0:T(8,128)S(1)} %get-tuple-element.54.refs_0_, ...), custom_call_target="tpu_custom_call" | custom-call | tf_op jit(solution)/shard_map/inner_relax/pallas_call | solution.py:544
  37.1 3.9 %collective-permute-done.6.refs_4_ = f32[6,2,256]{2,1,0:T(2,128)S(1)} collective-permute-done((f32[6,2,256]{2,1,0:T(2,128)S(1)}, f32[6,2,256]{2,1,0:T(2,128)S(1)}, u32[]{:S(2)}, u32[]{:S(2)}) %collective-permute-start.6) | collective-permute-done | bytes 12320 | tf_op jit(solution)/shard_map/ppermute | solution.py:605
  41.0 0.0 collective-permute-done.2.refs_0_
  41.0 0.0 collective-permute-done.7.refs_7_
  41.0 2.7 %edge_cross_in.2 = (f32[5,8,256]{2,1,0:T(8,128)S(1)}, f32[2,16,2,8,512]{4,3,2,1,0:T(8,128)S(1)}, f32[2,16,2,8,512]{4,3,2,1,0:T(8,128)S(1)}) custom-call(f32[2,16,2,8,512]{4,3,2,1,0:T(8,128)S(1)} %collective-permute-done.2.refs_0_, f32[2,16,2,8,512]{4,3,2,1,0:T(8,128)S(1)} %get-tuple-element.63.refs_1_, f32[2,16,2,8,512]{4,3,2,1,0:T(8,128)S(1)} %get-tuple-element.64.refs_2_, ...), custom_call_target="tpu_custom_call" | custom-call | tf_op jit(solution)/shard_map/edge_cross_in/pallas_call | solution.py:556
  43.7 0.2 collective-permute-start.10
  43.9 2.9 %collective-permute-start.11 = (f32[5,8,256]{2,1,0:T(8,128)S(1)}, f32[5,8,256]{2,1,0:T(8,128)S(1)}, u32[]{:S(2)}, u32[]{:S(2)}) collective-permute-start(f32[5,8,256]{2,1,0:T(8,128)S(1)} %get-tuple-element.71.refs_0_), channel_id=1, source_target_pairs={{0,3},{1,0},{2,1},{3,2},{4,7},{5,4},{6,5},{7,6},{8,11},{9,8},{10,9... | collective-permute-start | bytes 122888 | tf_op jit(solution)/shard_map/ppermute | solution.py:614
  46.8 0.0 collective-permute-start.9
  46.8 1.5 %collective-permute-start.8 = (f32[2,16,2,8,512]{4,3,2,1,0:T(8,128)S(1)}, f32[2,16,2,8,512]{4,3,2,1,0:T(8,128)S(1)}, u32[]{:S(2)}, u32[]{:S(2)}) collective-permute-start(f32[2,16,2,8,512]{4,3,2,1,0:T(8,128)S(1)} %get-tuple-element.69.refs_0_), channel_id=1, source_target_pairs={{0,16},{12,28},{4,8},{8,4},{16,0},{28,12},{20,24},{24,20},{1,17},{... | collective-permute-start | bytes 3145736 | tf_op jit(solution)/shard_map/ppermute | solution.py:605
  48.3 0.8 %collective-permute-done.10.refs_2_ = f32[5,8,256]{2,1,0:T(8,128)S(1)} collective-permute-done((f32[5,8,256]{2,1,0:T(8,128)S(1)}, f32[5,8,256]{2,1,0:T(8,128)S(1)}, u32[]{:S(2)}, u32[]{:S(2)}) %collective-permute-start.10) | collective-permute-done | bytes 40992 | tf_op jit(solution)/shard_map/ppermute | solution.py:614
  49.1 0.0 collective-permute-done.11.refs_3_
  49.1 3.5 %collective-permute-done.9.refs_1_ = f32[5,8,256]{2,1,0:T(8,128)S(1)} collective-permute-done((f32[5,8,256]{2,1,0:T(8,128)S(1)}, f32[5,8,256]{2,1,0:T(8,128)S(1)}, u32[]{:S(2)}, u32[]{:S(2)}) %collective-permute-start.9) | collective-permute-done | bytes 40992 | tf_op jit(solution)/shard_map/ppermute | solution.py:614
  52.6 1.1 %cell_params.4 = (f32[6,8,256]{2,1,0:T(8,128)S(1)}, f32[6,2,256]{2,1,0:T(2,128)S(1)}, f32[2,16,2,8,512]{4,3,2,1,0:T(8,128)S(1)}) custom-call(f32[5,8,256]{2,1,0:T(8,128)S(1)} %get-tuple-element.71.refs_0_, f32[5,8,256]{2,1,0:T(8,128)S(1)} %collective-permute-done.9.refs_1_, f32[5,8,256]{2,1,0:T(8,128)S(1)} %collective-permute-done.10.refs_2_, ...), custom_call_target="tpu_custom_call" | custom-call | tf_op jit(solution)/shard_map/cell_params/pallas_call | solution.py:571
  53.7 0.1 collective-permute-start.13
  53.7 1.6 %collective-permute-start.12 = (f32[6,2,256]{2,1,0:T(2,128)S(1)}, f32[6,2,256]{2,1,0:T(2,128)S(1)}, u32[]{:S(2)}, u32[]{:S(2)}) collective-permute-start(f32[6,2,256]{2,1,0:T(2,128)S(1)} %get-tuple-element.78), channel_id=1, source_target_pairs={{0,16},{12,28},{4,8},{8,4},{16,0},{28,12},{20,24},{24,20},{1,17},{... | collective-permute-start | bytes 36872 | tf_op jit(solution)/shard_map/ppermute | solution.py:605
  55.3 6.3 %inner_relax.3 = (f32[2,16,2,8,512]{4,3,2,1,0:T(8,128)S(1)}, f32[4,16,2,8,512]{4,3,2,1,0:T(8,128)S(1)}, f32[4,16,2,8,512]{4,3,2,1,0:T(8,128)S(1)}, f32[2,16,2,8,...) custom-call(f32[2,16,2,8,512]{4,3,2,1,0:T(8,128)S(1)} %get-tuple-element.69.refs_0_, ...), custom_call_target="tpu_custom_call" | custom-call | tf_op jit(solution)/shard_map/inner_relax/pallas_call | solution.py:544
  61.7 0.1 collective-permute-done.12.refs_4_
  61.7 0.0 collective-permute-done.8.refs_0_
  61.7 0.0 collective-permute-done.13.refs_7_
  61.7 2.7 %edge_cross_in.3 = (f32[5,8,256]{2,1,0:T(8,128)S(1)}, f32[2,16,2,8,512]{4,3,2,1,0:T(8,128)S(1)}, f32[2,16,2,8,512]{4,3,2,1,0:T(8,128)S(1)}) custom-call(f32[2,16,2,8,512]{4,3,2,1,0:T(8,128)S(1)} %collective-permute-done.8.refs_0_, f32[2,16,2,8,512]{4,3,2,1,0:T(8,128)S(1)} %get-tuple-element.75.refs_1_, f32[2,16,2,8,512]{4,3,2,1,0:T(8,128)S(1)} %get-tuple-element.76.refs_2_, ...), custom_call_target="tpu_custom_call" | custom-call | tf_op jit(solution)/shard_map/edge_cross_in/pallas_call | solution.py:556
  64.4 0.5 collective-permute-start.14
  64.9 3.9 %collective-permute-start.15 = (f32[5,8,256]{2,1,0:T(8,128)S(1)}, f32[5,8,256]{2,1,0:T(8,128)S(1)}, u32[]{:S(2)}, u32[]{:S(2)}) collective-permute-start(f32[5,8,256]{2,1,0:T(8,128)S(1)} %get-tuple-element.84.refs_0_), channel_id=1, source_target_pairs={{0,2},{1,3},{2,0},{3,1},{4,6},{5,7},{6,4},{7,5},{8,10},{9,11},{10,... | collective-permute-start | bytes 122888 | tf_op jit(solution)/shard_map/ppermute | solution.py:614
  68.8 0.4 collective-permute-start.16
  69.3 1.0 %collective-permute-done.14.refs_1_ = f32[5,8,256]{2,1,0:T(8,128)S(1)} collective-permute-done((f32[5,8,256]{2,1,0:T(8,128)S(1)}, f32[5,8,256]{2,1,0:T(8,128)S(1)}, u32[]{:S(2)}, u32[]{:S(2)}) %collective-permute-start.14) | collective-permute-done | bytes 40992 | tf_op jit(solution)/shard_map/ppermute | solution.py:614
  70.2 0.6 collective-permute-done.15.refs_2_
  70.8 2.0 %collective-permute-done.16.refs_3_ = f32[5,8,256]{2,1,0:T(8,128)S(1)} collective-permute-done((f32[5,8,256]{2,1,0:T(8,128)S(1)}, f32[5,8,256]{2,1,0:T(8,128)S(1)}, u32[]{:S(2)}, u32[]{:S(2)}) %collective-permute-start.16) | collective-permute-done | bytes 40992 | tf_op jit(solution)/shard_map/ppermute | solution.py:614
  72.8 0.6 cell_params.5.params
  73.5 2.8 %final_relax.1 = f32[8,16,16,512]{3,2,1,0:T(8,128)} custom-call(f32[2,16,2,8,512]{4,3,2,1,0:T(8,128)S(1)} %get-tuple-element.81.m_cross, f32[4,16,2,8,512]{4,3,2,1,0:T(8,128)S(1)} %get-tuple-element.82.m_mid, f32[2,16,2,8,512]{4,3,2,1,0:T(8,128)S(1)} %get-tuple-element.83.m_in, f32[6,8,256]{2,1,0:T(8,128)S(1)} %cell_params.5.params, ...), custom_call_target="tpu_custom_call" | custom-call | tf_op jit(solution)/shard_map/final_relax/pallas_call | solution.py:582
Async XLA Ops:
  2.1 9.4 %collective-permute-start.1 = (f32[2,16,2,8,512]{4,3,2,1,0:T(8,128)S(1)}, f32[2,16,2,8,512]{4,3,2,1,0:T(8,128)S(1)}, u32[]{:S(2)}, u32[]{:S(2)}) collective-permute-start(f32[2,16,2,8,512]{4,3,2,1,0:T(8,128)S(1)} %get-tuple-element.46.refs_1_), channel_id=1, source_target_pairs={{0,4},{4,0},{8,12},{12,8},{1,5},{5,1},{9,13},{13,9},{2,6},{6,2},{1... | collective-permute-start | bytes 3145736 | tf_op jit(solution)/shard_map/ppermute | solution.py:608
  2.6 15.4 %collective-permute-start = (f32[2,16,2,8,512]{4,3,2,1,0:T(8,128)S(1)}, f32[2,16,2,8,512]{4,3,2,1,0:T(8,128)S(1)}, u32[]{:S(2)}, u32[]{:S(2)}) collective-permute-start(f32[2,16,2,8,512]{4,3,2,1,0:T(8,128)S(1)} %get-tuple-element.45.refs_0_.refs_1_), channel_id=1, source_target_pairs={{0,16},{12,28},{4,8},{8,4},{16,0},{28,12},{20,24},{24,20},{1,17},{... | collective-permute-start | bytes 3145736 | tf_op jit(solution)/shard_map/ppermute | solution.py:605
  18.0 10.0 %copy-start = (f32[4]{0:T(128)S(1)}, f32[4]{0:T(128)}, u32[]{:S(2)}) copy-start(f32[4]{0:T(128)} %refs_6_.5) | copy-start | bytes 52
  19.4 8.3 %collective-permute-start.3 = (f32[5,8,256]{2,1,0:T(8,128)S(1)}, f32[5,8,256]{2,1,0:T(8,128)S(1)}, u32[]{:S(2)}, u32[]{:S(2)}) collective-permute-start(f32[5,8,256]{2,1,0:T(8,128)S(1)} %get-tuple-element.56.refs_0_), channel_id=1, source_target_pairs={{0,1},{1,2},{2,3},{3,0},{4,5},{5,6},{6,7},{7,4},{8,9},{9,10},{10,1... | collective-permute-start | bytes 122888 | tf_op jit(solution)/shard_map/ppermute | solution.py:614
  21.4 6.2 %collective-permute-start.4 = (f32[5,8,256]{2,1,0:T(8,128)S(1)}, f32[5,8,256]{2,1,0:T(8,128)S(1)}, u32[]{:S(2)}, u32[]{:S(2)}) collective-permute-start(f32[5,8,256]{2,1,0:T(8,128)S(1)} %get-tuple-element.56.refs_0_), channel_id=1, source_target_pairs={{0,2},{1,3},{2,0},{3,1},{4,6},{5,7},{6,4},{7,5},{8,10},{9,11},{10,... | collective-permute-start | bytes 122888 | tf_op jit(solution)/shard_map/ppermute | solution.py:614
  24.0 4.0 %collective-permute-start.5 = (f32[5,8,256]{2,1,0:T(8,128)S(1)}, f32[5,8,256]{2,1,0:T(8,128)S(1)}, u32[]{:S(2)}, u32[]{:S(2)}) collective-permute-start(f32[5,8,256]{2,1,0:T(8,128)S(1)} %get-tuple-element.56.refs_0_), channel_id=1, source_target_pairs={{0,3},{1,0},{2,1},{3,2},{4,7},{5,4},{6,5},{7,6},{8,11},{9,8},{10,9... | collective-permute-start | bytes 122888 | tf_op jit(solution)/shard_map/ppermute | solution.py:614
  26.0 15.0 %collective-permute-start.2 = (f32[2,16,2,8,512]{4,3,2,1,0:T(8,128)S(1)}, f32[2,16,2,8,512]{4,3,2,1,0:T(8,128)S(1)}, u32[]{:S(2)}, u32[]{:S(2)}) collective-permute-start(f32[2,16,2,8,512]{4,3,2,1,0:T(8,128)S(1)} %get-tuple-element.54.refs_0_), channel_id=1, source_target_pairs={{0,16},{12,28},{4,8},{8,4},{16,0},{28,12},{20,24},{24,20},{1,17},{... | collective-permute-start | bytes 3145736 | tf_op jit(solution)/shard_map/ppermute | solution.py:605
  29.1 11.9 %collective-permute-start.7 = (f32[2,16,2,8,512]{4,3,2,1,0:T(8,128)S(1)}, f32[2,16,2,8,512]{4,3,2,1,0:T(8,128)S(1)}, u32[]{:S(2)}, u32[]{:S(2)}) collective-permute-start(f32[2,16,2,8,512]{4,3,2,1,0:T(8,128)S(1)} %get-tuple-element.61.refs_2_.refs_8_), channel_id=1, source_target_pairs={{0,4},{4,0},{8,12},{12,8},{1,5},{5,1},{9,13},{13,9},{2,6},{6,2},{1... | collective-permute-start | bytes 3145736 | tf_op jit(solution)/shard_map/ppermute | solution.py:608
  29.2 11.8 %collective-permute-start.6 = (f32[6,2,256]{2,1,0:T(2,128)S(1)}, f32[6,2,256]{2,1,0:T(2,128)S(1)}, u32[]{:S(2)}, u32[]{:S(2)}) collective-permute-start(f32[6,2,256]{2,1,0:T(2,128)S(1)} %get-tuple-element.66), channel_id=1, source_target_pairs={{0,16},{12,28},{4,8},{8,4},{16,0},{28,12},{20,24},{24,20},{1,17},{... | collective-permute-start | bytes 36872 | tf_op jit(solution)/shard_map/ppermute | solution.py:605
  43.7 5.4 %collective-permute-start.10 = (f32[5,8,256]{2,1,0:T(8,128)S(1)}, f32[5,8,256]{2,1,0:T(8,128)S(1)}, u32[]{:S(2)}, u32[]{:S(2)}) collective-permute-start(f32[5,8,256]{2,1,0:T(8,128)S(1)} %get-tuple-element.71.refs_0_), channel_id=1, source_target_pairs={{0,2},{1,3},{2,0},{3,1},{4,6},{5,7},{6,4},{7,5},{8,10},{9,11},{10,... | collective-permute-start | bytes 122888 | tf_op jit(solution)/shard_map/ppermute | solution.py:614
  43.9 5.2 %collective-permute-start.11 = (f32[5,8,256]{2,1,0:T(8,128)S(1)}, f32[5,8,256]{2,1,0:T(8,128)S(1)}, u32[]{:S(2)}, u32[]{:S(2)}) collective-permute-start(f32[5,8,256]{2,1,0:T(8,128)S(1)} %get-tuple-element.71.refs_0_), channel_id=1, source_target_pairs={{0,3},{1,0},{2,1},{3,2},{4,7},{5,4},{6,5},{7,6},{8,11},{9,8},{10,9... | collective-permute-start | bytes 122888 | tf_op jit(solution)/shard_map/ppermute | solution.py:614
  46.8 5.8 %collective-permute-start.9 = (f32[5,8,256]{2,1,0:T(8,128)S(1)}, f32[5,8,256]{2,1,0:T(8,128)S(1)}, u32[]{:S(2)}, u32[]{:S(2)}) collective-permute-start(f32[5,8,256]{2,1,0:T(8,128)S(1)} %get-tuple-element.71.refs_0_), channel_id=1, source_target_pairs={{0,1},{1,2},{2,3},{3,0},{4,5},{5,6},{6,7},{7,4},{8,9},{9,10},{10,1... | collective-permute-start | bytes 122888 | tf_op jit(solution)/shard_map/ppermute | solution.py:614
  46.8 14.9 %collective-permute-start.8 = (f32[2,16,2,8,512]{4,3,2,1,0:T(8,128)S(1)}, f32[2,16,2,8,512]{4,3,2,1,0:T(8,128)S(1)}, u32[]{:S(2)}, u32[]{:S(2)}) collective-permute-start(f32[2,16,2,8,512]{4,3,2,1,0:T(8,128)S(1)} %get-tuple-element.69.refs_0_), channel_id=1, source_target_pairs={{0,16},{12,28},{4,8},{8,4},{16,0},{28,12},{20,24},{24,20},{1,17},{... | collective-permute-start | bytes 3145736 | tf_op jit(solution)/shard_map/ppermute | solution.py:605
  53.7 8.1 %collective-permute-start.13 = (f32[2,16,2,8,512]{4,3,2,1,0:T(8,128)S(1)}, f32[2,16,2,8,512]{4,3,2,1,0:T(8,128)S(1)}, u32[]{:S(2)}, u32[]{:S(2)}) collective-permute-start(f32[2,16,2,8,512]{4,3,2,1,0:T(8,128)S(1)} %get-tuple-element.73.refs_2_.refs_8_), channel_id=1, source_target_pairs={{0,4},{4,0},{8,12},{12,8},{1,5},{5,1},{9,13},{13,9},{2,6},{6,2},{1... | collective-permute-start | bytes 3145736 | tf_op jit(solution)/shard_map/ppermute | solution.py:608
  53.7 8.0 %collective-permute-start.12 = (f32[6,2,256]{2,1,0:T(2,128)S(1)}, f32[6,2,256]{2,1,0:T(2,128)S(1)}, u32[]{:S(2)}, u32[]{:S(2)}) collective-permute-start(f32[6,2,256]{2,1,0:T(2,128)S(1)} %get-tuple-element.78), channel_id=1, source_target_pairs={{0,16},{12,28},{4,8},{8,4},{16,0},{28,12},{20,24},{24,20},{1,17},{... | collective-permute-start | bytes 36872 | tf_op jit(solution)/shard_map/ppermute | solution.py:605
  64.4 5.8 %collective-permute-start.14 = (f32[5,8,256]{2,1,0:T(8,128)S(1)}, f32[5,8,256]{2,1,0:T(8,128)S(1)}, u32[]{:S(2)}, u32[]{:S(2)}) collective-permute-start(f32[5,8,256]{2,1,0:T(8,128)S(1)} %get-tuple-element.84.refs_0_), channel_id=1, source_target_pairs={{0,1},{1,2},{2,3},{3,0},{4,5},{5,6},{6,7},{7,4},{8,9},{9,10},{10,1... | collective-permute-start | bytes 122888 | tf_op jit(solution)/shard_map/ppermute | solution.py:614
  64.9 5.9 %collective-permute-start.15 = (f32[5,8,256]{2,1,0:T(8,128)S(1)}, f32[5,8,256]{2,1,0:T(8,128)S(1)}, u32[]{:S(2)}, u32[]{:S(2)}) collective-permute-start(f32[5,8,256]{2,1,0:T(8,128)S(1)} %get-tuple-element.84.refs_0_), channel_id=1, source_target_pairs={{0,2},{1,3},{2,0},{3,1},{4,6},{5,7},{6,4},{7,5},{8,10},{9,11},{10,... | collective-permute-start | bytes 122888 | tf_op jit(solution)/shard_map/ppermute | solution.py:614
  68.8 4.0 %collective-permute-start.16 = (f32[5,8,256]{2,1,0:T(8,128)S(1)}, f32[5,8,256]{2,1,0:T(8,128)S(1)}, u32[]{:S(2)}, u32[]{:S(2)}) collective-permute-start(f32[5,8,256]{2,1,0:T(8,128)S(1)} %get-tuple-element.84.refs_0_), channel_id=1, source_target_pairs={{0,3},{1,0},{2,1},{3,2},{4,7},{5,4},{6,5},{7,6},{8,11},{9,8},{10,9... | collective-permute-start | bytes 122888 | tf_op jit(solution)/shard_map/ppermute | solution.py:614

commit v8 on v6

--- a/solution.py
+++ b/solution.py
@@ -366,52 +366,82 @@
     row_moments([(out.at[r], r) for r in range(inner)], weights, sums)
 
 
-def edge_kernel(relax, rows, line, *refs):
-    if relax:
-        (h_cross, h_in, p_cross, p_in, table, factor, cross, middle, inside, e_cross,
-         e_in, coef_ref, weights, inner_sums, out_cross, out_in, sums,
-         wide, tall, kept, low, high) = refs
-        params = [jnp.concatenate([p_cross[k], p_in[k]], axis=0) for k in range(6)]
-        spread_features(params, wide, tall, 4)
-        group = [(r, h_cross.at[r], into(low.at[r])) for r in range(2)]
-        group += [(2 + r, h_in.at[r], into(high.at[r])) for r in range(2)]
-        relax_group(group, tall, table, factor, kept)
-    else:
-        (low, high, cross, middle, inside, e_cross, e_in, coef_ref, weights,
-         inner_sums, out_cross, out_in, sums) = refs
-    chunks = middle.shape[-1] // LANES
+def presence(line):
     place = lax.axis_index("gx")
-    present = jnp.where((place == 0) | (place == line - 1), 0.0, 1.0)
-
-    def along_x(i, carry):
-        chunk, y = i // 16, i % 16
-        lanes = lanes_of(chunk)
+    return jnp.where((place == 0) | (place == line - 1), 0.0, 1.0)
+
+
+def cross_x(low, cross, middle, before, out, y, t, lanes, coef, present):
+    cells = {}
+    for n in range(2):
+        cells[-1 - n] = low[n, y, t, :, lanes] * present
+        cells[n] = cross[n, y, t, :, lanes]
+        cells[2 + n] = middle[n, y, t, :, lanes]
+
+    def store(n, v):
+        out[n, y, t, :, lanes] = before[n, y, t, :, lanes] - v
+
+    x_row(cells, [0, 1], store, coef, True)
+
+
+def in_x(high, inside, middle, before, out, y, t, lanes, coef):
+    last = middle.shape[0]
+    cells = {}
+    for n in range(2):
+        cells[n] = middle[last - 2 + n, y, t, :, lanes]
+        cells[2 + n] = inside[n, y, t, :, lanes]
+        cells[4 + n] = high[1 - n, y, t, :, lanes]
+
+    def store(n, v):
+        out[n - 2, y, t, :, lanes] = before[n - 2, y, t, :, lanes] - v
+
+    x_row(cells, [2, 3], store, coef, True)
+
+
+def each_place(middle, coef_ref, work):
+    def one(i, carry):
+        lanes = lanes_of(i // 16)
         coef = coefs_of(coef_ref, lanes)
         for t in range(2):
-            cells = {}
-            for n in range(2):
-                cells[-1 - n] = low[n, y, t, :, lanes] * present
-                cells[n] = cross[n, y, t, :, lanes]
-                cells[2 + n] = middle[n, y, t, :, lanes]
-
-            def store(n, v, t=t):
-                out_cross[n, y, t, :, lanes] = e_cross[n, y, t, :, lanes] - v
-
-            x_row(cells, [0, 1], store, coef, True)
-            cells = {}
-            for n in range(2):
-                cells[rows - 4 + n] = middle[rows - 6 + n, y, t, :, lanes]
-                cells[rows - 2 + n] = inside[n, y, t, :, lanes]
-                cells[rows + n] = high[1 - n, y, t, :, lanes]
-
-            def store_in(n, v, t=t):
-                r = n - rows + 2
-                out_in[r, y, t, :, lanes] = e_in[r, y, t, :, lanes] - v
-
-            x_row(cells, [rows - 2, rows - 1], store_in, coef, True)
+            work(i % 16, t, lanes, coef)
         return carry
 
-    lax.fori_loop(0, chunks * 16, along_x, 0, unroll=4)
+    lax.fori_loop(0, middle.shape[-1] // LANES * 16, one, 0, unroll=4)
+
+
+def first_in_kernel(high, inside, e_in, middle, coef_ref, weights, out, sums):
+    each_place(middle, coef_ref, lambda *at: in_x(high, inside, middle, e_in, out, *at))
+    row_moments([(out.at[r], r) for r in range(2)], weights, sums)
+
+
+def first_cross_kernel(line, low, cross, e_cross, middle, coef_ref, weights, inner_sums, in_sums,
+                       out, sums):
+    present = presence(line)
+    each_place(
+        middle, coef_ref, lambda *at: cross_x(low, cross, middle, e_cross, out, *at, present)
+    )
+    rows = sums.shape[1]
+    for m in range(5):
+        sums[m, 2 : rows - 2, :] = inner_sums[m]
+        sums[m, rows - 2 :, :] = in_sums[m]
+    row_moments([(out.at[r], r) for r in range(2)], weights, sums)
+
+
+def edge_kernel(rows, line, h_cross, h_in, p_cross, p_in, table, factor, cross, middle, inside,
+                e_cross, e_in, coef_ref, weights, inner_sums, out_cross, out_in, sums,
+                wide, tall, kept, low, high):
+    params = [jnp.concatenate([p_cross[k], p_in[k]], axis=0) for k in range(6)]
+    spread_features(params, wide, tall, 4)
+    group = [(r, h_cross.at[r], into(low.at[r])) for r in range(2)]
+    group += [(2 + r, h_in.at[r], into(high.at[r])) for r in range(2)]
+    relax_group(group, tall, table, factor, kept)
+    present = presence(line)
+
+    def work(*at):
+        cross_x(low, cross, middle, e_cross, out_cross, *at, present)
+        in_x(high, inside, middle, e_in, out_in, *at)
+
+    each_place(middle, coef_ref, work)
     for m in range(5):
         sums[m, 2 : rows - 2, :] = inner_sums[m]
     edges = [(out_cross.at[r], r) for r in range(2)]
@@ -533,21 +563,39 @@
             name="inner_relax" if relax else "inner_first",
         )(*args)
 
-    def edge(relax, halos, params, state, edges, sums):
-        scratch = []
-        args = (*state, *edges, coef, weights, sums)
-        if relax:
-            scratch = feature_scratch(4) + [slab_scratch(2)] * 2
-            args = (*params, table, factor, *args)
-        args = (*halos, *args)
+    whole_sums = jax.ShapeDtypeStruct((5, rows, cells), F32)
+    edge_sums = jax.ShapeDtypeStruct((5, 2, cells), F32)
+
+    def first_in(*args):
         return pl.pallas_call(
-            functools.partial(edge_kernel, relax, rows, line),
+            first_in_kernel,
+            in_specs=[vmem] * 6,
+            out_specs=[vmem] * 2,
+            out_shape=[slab(2), edge_sums],
+            compiler_params=limits(LIMIT_MIB),
+            name="first_in",
+        )(*args, middle, coef, weights)
+
+    def first_cross(*args):
+        return pl.pallas_call(
+            functools.partial(first_cross_kernel, line),
+            in_specs=[vmem] * 8,
+            out_specs=[vmem] * 2,
+            out_shape=[slab(2), whole_sums],
+            compiler_params=limits(LIMIT_MIB),
+            name="first_cross",
+        )(*args)
+
+    def edge(halos, params, state, edges, sums):
+        args = (*halos, *params, table, factor, *state, *edges, coef, weights, sums)
+        return pl.pallas_call(
+            functools.partial(edge_kernel, rows, line),
             in_specs=[vmem] * len(args),
             out_specs=[vmem] * 3,
-            out_shape=[slab(2), slab(2), jax.ShapeDtypeStruct((5, rows, cells), F32)],
-            scratch_shapes=scratch,
+            out_shape=[slab(2), slab(2), whole_sums],
+            scratch_shapes=feature_scratch(4) + [slab_scratch(2)] * 2,
             compiler_params=limits(LIMIT_MIB),
-            name="edge_relax" if relax else "edge_first",
+            name="edge_relax",
         )(*args)
 
     def cell_params(parts, *sizes):
@@ -599,16 +647,16 @@
     cross, inside, codes, table, factor, weights, coef = load()
     halos = exchange(cross, inside)
     middle, m_mid, e_cross, e_in, sums = inner(False, (cross, inside, in_hbm(distribution)), None)
-    m_cross, m_in, sums = edge(
-        False, halos, None, (cross, middle, inside), (e_cross, e_in), sums
-    )
+    m_in, in_sums = first_in(halos[1], inside, e_in)
+    m_cross, sums = first_cross(halos[0], cross, e_cross, middle, coef, weights, sums, in_sums)
+    m_cross, m_in, sums = lax.optimization_barrier((m_cross, m_in, sums))
     for _ in range(1, STEPS):
         halos = exchange(m_cross, m_in)
         params, p_cross, p_in = cell_params(gather(sums), rows, 2, 2)
         p_halos = exchange(p_cross, p_in)
         moved = (m_cross, m_mid, m_in)
         *state, m_mid, e_cross, e_in, sums = inner(True, moved, params)
-        m_cross, m_in, sums = edge(True, halos, p_halos, state, (e_cross, e_in), sums)
+        m_cross, m_in, sums = edge(halos, p_halos, state, (e_cross, e_in), sums)
     (params,) = cell_params(gather(sums), rows)
     return final((m_cross, m_mid, m_in), params)
 

time: 73.1 us -> 72.3 us (0.989)
  waiting for transfers between devices: 15.9 us -> 14.6 us
    ppermute x5, waiting for transfers between devices: 6.46 us -> 5.19 us  [exchange(): lax.ppermute(cross, ('groups', 'gx'), across)]
    pallas_call x3 -> x4, Pallas kernels: 8.05 us -> 8.52 us  [the longest x2 5.81 us: edge(): pl.pallas_call(functools.partial(edge_kernel, rows, line), in_specs=[vmem...]
  transfers between devices with their start and end apart: 19 -> 19, of which waited for: 8 -> 8; matrix products, arithmetic and copies ran while one was open for 0% -> 0% of each run, Pallas kernels for 28% -> 30%
where the time goes in v8:
time: 72.3 us; the launch traced here: 72.2 us
  Pallas kernels  34.7 us (48%)
  starting transfers between devices  22.1 us (31%)
  waiting for transfers between devices  14.6 us (20%)
  between operations  0.77 us (1%)
    pallas_call x3, Pallas kernels, inner(): pl.pallas_call(functools.partial(inner_kernel, relax, rows), in_specs=[vm...  19.3 us
    ppermute x9, starting transfers between devices, gather(): parts.append(lax.ppermute(part, 'vert', pairs))  13.3 us
    ppermute x9, waiting for transfers between devices, gather(): parts.append(lax.ppermute(part, 'vert', pairs))  9.4 us
    ppermute x5, starting transfers between devices, exchange(): lax.ppermute(cross, ('groups', 'gx'), across)  7.8 us
    pallas_call x2, Pallas kernels, edge(): pl.pallas_call(functools.partial(edge_kernel, rows, line), in_specs=[vmem...  5.81 us
    ppermute x5, waiting for transfers between devices, exchange(): lax.ppermute(cross, ('groups', 'gx'), across)  5.19 us
    pallas_call x1, Pallas kernels, final(): pl.pallas_call(functools.partial(final_kernel, rows), in_specs=[vmem] * 6...  2.8 us
    pallas_call x1, Pallas kernels, load(): pl.pallas_call(load_kernel, in_specs=[hbm] * 3, out_specs=[vmem] * 7, out...  2.11 us
  transfers between devices with their start and end apart: 19, of which 8 were waited for; matrix products, arithmetic and copies ran while one was open for 0% of the time, Pallas kernels for 30%

profile of v8, /device:TPU:0, one launch (start us, length us, event | category | flops | bytes accessed | tf_op | source)
XLA Modules:
  0.0 72.2 jit_solution(4107329610002898042)
XLA Ops:
  0.0 2.1 %load_edges.1 = (f32[2,16,2,8,512]{4,3,2,1,0:T(8,128)S(1)}, f32[2,16,2,8,512]{4,3,2,1,0:T(8,128)S(1)}, s32[8,256]{1,0:T(8,128)S(1)}, bf16[32,512]{1,0:T(8,128)(2...) custom-call(s32[1,512]{1,0:T(1,128)} %bitcast.1, ...), custom_call_target="tpu_custom_call" | custom-call | tf_op jit(solution)/shard_map/load_edges/pallas_call | solution.py:517
  2.1 0.5 collective-permute-start.1
  2.6 2.6 %collective-permute-start = (f32[2,16,2,8,512]{4,3,2,1,0:T(8,128)S(1)}, f32[2,16,2,8,512]{4,3,2,1,0:T(8,128)S(1)}, u32[]{:S(2)}, u32[]{:S(2)}) collective-permute-start(f32[2,16,2,8,512]{4,3,2,1,0:T(8,128)S(1)} %get-tuple-element.50.refs_0_.cross), channel_id=1, source_target_pairs={{0,16},{12,28},{4,8},{8,4},{16,0},{28,12},{20,24},{24,20},{1,17},{... | collective-permute-start | bytes 3145736 | tf_op jit(solution)/shard_map/ppermute | solution.py:636
  5.2 6.3 %inner_first.1 = (f32[4,16,2,8,512]{4,3,2,1,0:T(8,128)S(1)}, f32[4,16,2,8,512]{4,3,2,1,0:T(8,128)S(1)}, f32[2,16,2,8,512]{4,3,2,1,0:T(8,128)S(1)}, f32[2,16,2,8,512]{4,3,2,1,0:T(8,128)S(1)}, f32[5,4,256]{2,1,0:T(4,128)S(1)}) custom-call(f32[2,16,2,8,512]{4,3,2,1,0:T(8,128)S(1)} %get-tuple-element.50.refs_0_.cross, ...), custom_call_target="tpu_custom_call" | custom-call | tf_op jit(solution)/shard_map/inner_first/pallas_call | solution.py:556
  11.5 0.0 collective-permute-done.1.high
  11.5 1.3 %first_in.1 = (f32[2,16,2,8,512]{4,3,2,1,0:T(8,128)S(1)}, f32[5,2,256]{2,1,0:T(2,128)S(1)}) custom-call(f32[2,16,2,8,512]{4,3,2,1,0:T(8,128)S(1)} %collective-permute-done.1.high, f32[2,16,2,8,512]{4,3,2,1,0:T(8,128)S(1)} %get-tuple-element.51.refs_1_.inside, f32[2,16,2,8,512]{4,3,2,1,0:T(8,128)S(1)} %get-tuple-element.57.e_in, ...), custom_call_target="tpu_custom_call" | custom-call | tf_op jit(solution)/shard_map/first_in/pallas_call | solution.py:570
  12.8 5.2 %collective-permute-done.low = f32[2,16,2,8,512]{4,3,2,1,0:T(8,128)S(1)} collective-permute-done((f32[2,16,2,8,512]{4,3,2,1,0:T(8,128)S(1)}, f32[2,16,2,8,512]{4,3,2,1,0:T(8,128)S(1)}, u32[]{:S(2)}, u32[]{:S(2)}) %collective-permute-start) | collective-permute-done | bytes 1048608 | tf_op jit(solution)/shard_map/ppermute | solution.py:636
  18.0 1.4 %first_cross.1 = (f32[2,16,2,8,512]{4,3,2,1,0:T(8,128)S(1)}, f32[5,8,256]{2,1,0:T(8,128)S(1)}) custom-call(f32[2,16,2,8,512]{4,3,2,1,0:T(8,128)S(1)} %collective-permute-done.low, f32[2,16,2,8,512]{4,3,2,1,0:T(8,128)S(1)} %get-tuple-element.50.refs_0_.cross, f32[2,16,2,8,512]{4,3,2,1,0:T(8,128)S(1)} %get-tuple-element.54.e_cross, ...), custom_call_target="tpu_custom_call" | custom-call | tf_op jit(solution)/shard_map/first_cross/pallas_call | solution.py:580
  19.4 2.0 %collective-permute-start.2 = (f32[2,16,2,8,512]{4,3,2,1,0:T(8,128)S(1)}, f32[2,16,2,8,512]{4,3,2,1,0:T(8,128)S(1)}, u32[]{:S(2)}, u32[]{:S(2)}) collective-permute-start(f32[2,16,2,8,512]{4,3,2,1,0:T(8,128)S(1)} %get-tuple-element.62.refs_0_), channel_id=1, source_target_pairs={{0,16},{12,28},{4,8},{8,4},{16,0},{28,12},{20,24},{24,20},{1,17},{... | collective-permute-start | bytes 3145736 | tf_op jit(solution)/shard_map/ppermute | solution.py:636
  21.4 0.0 collective-permute-start.3
  21.4 1.6 %collective-permute-start.4 = (f32[5,8,256]{2,1,0:T(8,128)S(1)}, f32[5,8,256]{2,1,0:T(8,128)S(1)}, u32[]{:S(2)}, u32[]{:S(2)}) collective-permute-start(f32[5,8,256]{2,1,0:T(8,128)S(1)} %get-tuple-element.64.refs_0_), channel_id=1, source_target_pairs={{0,1},{1,2},{2,3},{3,0},{4,5},{5,6},{6,7},{7,4},{8,9},{9,10},{10,1... | collective-permute-start | bytes 122888 | tf_op jit(solution)/shard_map/ppermute | solution.py:644
  23.0 2.6 %collective-permute-start.5 = (f32[5,8,256]{2,1,0:T(8,128)S(1)}, f32[5,8,256]{2,1,0:T(8,128)S(1)}, u32[]{:S(2)}, u32[]{:S(2)}) collective-permute-start(f32[5,8,256]{2,1,0:T(8,128)S(1)} %get-tuple-element.64.refs_0_), channel_id=1, source_target_pairs={{0,2},{1,3},{2,0},{3,1},{4,6},{5,7},{6,4},{7,5},{8,10},{9,11},{10,... | collective-permute-start | bytes 122888 | tf_op jit(solution)/shard_map/ppermute | solution.py:644
  25.6 1.3 %collective-permute-start.6 = (f32[5,8,256]{2,1,0:T(8,128)S(1)}, f32[5,8,256]{2,1,0:T(8,128)S(1)}, u32[]{:S(2)}, u32[]{:S(2)}) collective-permute-start(f32[5,8,256]{2,1,0:T(8,128)S(1)} %get-tuple-element.64.refs_0_), channel_id=1, source_target_pairs={{0,3},{1,0},{2,1},{3,2},{4,7},{5,4},{6,5},{7,6},{8,11},{9,8},{10,9... | collective-permute-start | bytes 122888 | tf_op jit(solution)/shard_map/ppermute | solution.py:644
  27.6 0.0 collective-permute-done.4.refs_1_
  27.6 1.6 %collective-permute-done.5.refs_2_ = f32[5,8,256]{2,1,0:T(8,128)S(1)} collective-permute-done((f32[5,8,256]{2,1,0:T(8,128)S(1)}, f32[5,8,256]{2,1,0:T(8,128)S(1)}, u32[]{:S(2)}, u32[]{:S(2)}) %collective-permute-start.5) | collective-permute-done | bytes 40992 | tf_op jit(solution)/shard_map/ppermute | solution.py:644
  29.2 0.4 collective-permute-done.6.refs_3_
  29.6 0.6 cell_params.3
  30.3 1.1 %collective-permute-start.7 = (f32[6,2,256]{2,1,0:T(2,128)S(1)}, f32[6,2,256]{2,1,0:T(2,128)S(1)}, u32[]{:S(2)}, u32[]{:S(2)}) collective-permute-start(f32[6,2,256]{2,1,0:T(2,128)S(1)} %get-tuple-element.66), channel_id=1, source_target_pairs={{0,16},{12,28},{4,8},{8,4},{16,0},{28,12},{20,24},{24,20},{1,17},{... | collective-permute-start | bytes 36872 | tf_op jit(solution)/shard_map/ppermute | solution.py:636
  31.3 0.0 collective-permute-start.8
  31.3 6.5 %inner_relax.2 = (f32[2,16,2,8,512]{4,3,2,1,0:T(8,128)S(1)}, f32[4,16,2,8,512]{4,3,2,1,0:T(8,128)S(1)}, f32[2,16,2,8,512]{4,3,2,1,0:T(8,128)S(1)}, f32[4,16,2,8,...) custom-call(f32[2,16,2,8,512]{4,3,2,1,0:T(8,128)S(1)} %get-tuple-ele, ...), custom_call_target="tpu_custom_call" | custom-call | tf_op jit(solution)/shard_map/inner_relax/pallas_call | solution.py:556
  37.9 0.0 collective-permute-done.7.p_cross
  37.9 0.0 collective-permute-done.8.p_in
  37.9 0.0 collective-permute-done.2.h_cross
  37.9 0.0 collective-permute-done.3.h_in
  37.9 2.9 %edge_relax.2 = (f32[2,16,2,8,512]{4,3,2,1,0:T(8,128)S(1)}, f32[2,16,2,8,512]{4,3,2,1,0:T(8,128)S(1)}, f32[5,8,256]{2,1,0:T(8,128)S(1)}) custom-call(f32[2,16,2,8,512]{4,3,2,1,0:T(8,128)S(1)} %collective-permute-done.2.h_cross, f32[2,16,2,8,512]{4,3,2,1,0:T(8,128)S(1)} %collective-permute-done.3.h_in, f32[6,2,256]{2,1,0:T(2,128)S(1)} %collective-permute-done.7.p_cross, ...), custom_call_target="tpu_custom_call" | custom-call | tf_op jit(solution)/shard_map/edge_relax/pallas_call | solution.py:591
  40.8 0.5 collective-permute-start.10
  41.3 1.0 %collective-permute-start.9 = (f32[2,16,2,8,512]{4,3,2,1,0:T(8,128)S(1)}, f32[2,16,2,8,512]{4,3,2,1,0:T(8,128)S(1)}, u32[]{:S(2)}, u32[]{:S(2)}) collective-permute-start(f32[2,16,2,8,512]{4,3,2,1,0:T(8,128)S(1)} %get-tuple-element.78.refs_0_), channel_id=1, source_target_pairs={{0,16},{12,28},{4,8},{8,4},{16,0},{28,12},{20,24},{24,20},{1,17},{... | collective-permute-start | bytes 3145736 | tf_op jit(solution)/shard_map/ppermute | solution.py:636
  42.4 0.8 %collective-permute-start.11 = (f32[5,8,256]{2,1,0:T(8,128)S(1)}, f32[5,8,256]{2,1,0:T(8,128)S(1)}, u32[]{:S(2)}, u32[]{:S(2)}) collective-permute-start(f32[5,8,256]{2,1,0:T(8,128)S(1)} %get-tuple-element.80.refs_0_), channel_id=1, source_target_pairs={{0,1},{1,2},{2,3},{3,0},{4,5},{5,6},{6,7},{7,4},{8,9},{9,10},{10,1... | collective-permute-start | bytes 122888 | tf_op jit(solution)/shard_map/ppermute | solution.py:644
  43.2 2.8 %collective-permute-start.12 = (f32[5,8,256]{2,1,0:T(8,128)S(1)}, f32[5,8,256]{2,1,0:T(8,128)S(1)}, u32[]{:S(2)}, u32[]{:S(2)}) collective-permute-start(f32[5,8,256]{2,1,0:T(8,128)S(1)} %get-tuple-element.80.refs_0_), channel_id=1, source_target_pairs={{0,2},{1,3},{2,0},{3,1},{4,6},{5,7},{6,4},{7,5},{8,10},{9,11},{10,... | collective-permute-start | bytes 122888 | tf_op jit(solution)/shard_map/ppermute | solution.py:644
  46.1 0.2 collective-permute-start.13
  46.3 2.0 %collective-permute-done.11.refs_1_ = f32[5,8,256]{2,1,0:T(8,128)S(1)} collective-permute-done((f32[5,8,256]{2,1,0:T(8,128)S(1)}, f32[5,8,256]{2,1,0:T(8,128)S(1)}, u32[]{:S(2)}, u32[]{:S(2)}) %collective-permute-start.11) | collective-permute-done | bytes 40992 | tf_op jit(solution)/shard_map/ppermute | solution.py:644
  48.3 0.8 %collective-permute-done.12.refs_2_ = f32[5,8,256]{2,1,0:T(8,128)S(1)} collective-permute-done((f32[5,8,256]{2,1,0:T(8,128)S(1)}, f32[5,8,256]{2,1,0:T(8,128)S(1)}, u32[]{:S(2)}, u32[]{:S(2)}) %collective-permute-start.12) | collective-permute-done | bytes 40992 | tf_op jit(solution)/shard_map/ppermute | solution.py:644
  49.1 1.0 %collective-permute-done.13.refs_3_ = f32[5,8,256]{2,1,0:T(8,128)S(1)} collective-permute-done((f32[5,8,256]{2,1,0:T(8,128)S(1)}, f32[5,8,256]{2,1,0:T(8,128)S(1)}, u32[]{:S(2)}, u32[]{:S(2)}) %collective-permute-start.13) | collective-permute-done | bytes 40992 | tf_op jit(solution)/shard_map/ppermute | solution.py:644
  50.1 0.6 cell_params.4
  50.7 1.1 %collective-permute-start.14 = (f32[6,2,256]{2,1,0:T(2,128)S(1)}, f32[6,2,256]{2,1,0:T(2,128)S(1)}, u32[]{:S(2)}, u32[]{:S(2)}) collective-permute-start(f32[6,2,256]{2,1,0:T(2,128)S(1)} %get-tuple-element.81), channel_id=1, source_target_pairs={{0,16},{12,28},{4,8},{8,4},{16,0},{28,12},{20,24},{24,20},{1,17},{... | collective-permute-start | bytes 36872 | tf_op jit(solution)/shard_map/ppermute | solution.py:636
  51.8 0.0 collective-permute-start.15
  51.8 6.5 %inner_relax.3 = (f32[2,16,2,8,512]{4,3,2,1,0:T(8,128)S(1)}, f32[4,16,2,8,512]{4,3,2,1,0:T(8,128)S(1)}, f32[2,16,2,8,512]{4,3,2,1,0:T(8,128)S(1)}, f32[4,16,2,8,...) custom-call(f32[2,16,2,8,512]{4,3,2,1,0:T(8,128)S(1)} %get-tuple-ele, ...), custom_call_target="tpu_custom_call" | custom-call | tf_op jit(solution)/shard_map/inner_relax/pallas_call | solution.py:556
  58.3 0.0 collective-permute-done.14.p_cross
  58.4 0.0 collective-permute-done.15.p_in
  58.4 0.0 collective-permute-done.9.h_cross
  58.4 2.9 %edge_relax.3 = (f32[2,16,2,8,512]{4,3,2,1,0:T(8,128)S(1)}, f32[2,16,2,8,512]{4,3,2,1,0:T(8,128)S(1)}, f32[5,8,256]{2,1,0:T(8,128)S(1)}) custom-call(f32[2,16,2,8,512]{4,3,2,1,0:T(8,128)S(1)} %collective-permute-done.9.h_cross, f32[2,16,2,8,512]{4,3,2,1,0:T(8,128)S(1)} %collective-permute-done.10.h_in, f32[6,2,256]{2,1,0:T(2,128)S(1)} %collective-permute-done.14.p_cross, ...), custom_call_target="tpu_custom_call" | custom-call | tf_op jit(solution)/shard_map/edge_relax/pallas_call | solution.py:591
  61.3 0.7 collective-permute-start.16
  62.0 2.1 %collective-permute-start.17 = (f32[5,8,256]{2,1,0:T(8,128)S(1)}, f32[5,8,256]{2,1,0:T(8,128)S(1)}, u32[]{:S(2)}, u32[]{:S(2)}) collective-permute-start(f32[5,8,256]{2,1,0:T(8,128)S(1)} %get-tuple-element.94.refs_0_), channel_id=1, source_target_pairs={{0,2},{1,3},{2,0},{3,1},{4,6},{5,7},{6,4},{7,5},{8,10},{9,11},{10,... | collective-permute-start | bytes 122888 | tf_op jit(solution)/shard_map/ppermute | solution.py:644
  64.1 1.0 %collective-permute-start.18 = (f32[5,8,256]{2,1,0:T(8,128)S(1)}, f32[5,8,256]{2,1,0:T(8,128)S(1)}, u32[]{:S(2)}, u32[]{:S(2)}) collective-permute-start(f32[5,8,256]{2,1,0:T(8,128)S(1)} %get-tuple-element.94.refs_0_), channel_id=1, source_target_pairs={{0,3},{1,0},{2,1},{3,2},{4,7},{5,4},{6,5},{7,6},{8,11},{9,8},{10,9... | collective-permute-start | bytes 122888 | tf_op jit(solution)/shard_map/ppermute | solution.py:644
  65.1 2.4 %collective-permute-done.16.refs_1_ = f32[5,8,256]{2,1,0:T(8,128)S(1)} collective-permute-done((f32[5,8,256]{2,1,0:T(8,128)S(1)}, f32[5,8,256]{2,1,0:T(8,128)S(1)}, u32[]{:S(2)}, u32[]{:S(2)}) %collective-permute-start.16) | collective-permute-done | bytes 40992 | tf_op jit(solution)/shard_map/ppermute | solution.py:644
  67.6 1.2 %collective-permute-done.17.refs_2_ = f32[5,8,256]{2,1,0:T(8,128)S(1)} collective-permute-done((f32[5,8,256]{2,1,0:T(8,128)S(1)}, f32[5,8,256]{2,1,0:T(8,128)S(1)}, u32[]{:S(2)}, u32[]{:S(2)}) %collective-permute-start.17) | collective-permute-done | bytes 40992 | tf_op jit(solution)/shard_map/ppermute | solution.py:644
  68.7 0.6 cell_params.5.params
  69.4 2.8 %final_relax.1 = f32[8,16,16,512]{3,2,1,0:T(8,128)} custom-call(f32[2,16,2,8,512]{4,3,2,1,0:T(8,128)S(1)} %get-tuple-element.91.m_cross, f32[4,16,2,8,512]{4,3,2,1,0:T(8,128)S(1)} %get-tuple-element.92.m_mid, f32[2,16,2,8,512]{4,3,2,1,0:T(8,128)S(1)} %get-tuple-element.93.m_in, f32[6,8,256]{2,1,0:T(8,128)S(1)} %cell_params.5.params, ...), custom_call_target="tpu_custom_call" | custom-call | tf_op jit(solution)/shard_map/final_relax/pallas_call | solution.py:612
  (4 shorter events, 0.0 us)
Async XLA Ops:
  2.1 9.4 %collective-permute-start.1 = (f32[2,16,2,8,512]{4,3,2,1,0:T(8,128)S(1)}, f32[2,16,2,8,512]{4,3,2,1,0:T(8,128)S(1)}, u32[]{:S(2)}, u32[]{:S(2)}) collective-permute-start(f32[2,16,2,8,512]{4,3,2,1,0:T(8,128)S(1)} %get-tuple-element.51.refs_1_.inside), channel_id=1, source_target_pairs={{0,4},{4,0},{8,12},{12,8},{1,5},{5,1},{9,13},{13,9},{2,6},{6,2},{1... | collective-permute-start | bytes 3145736 | tf_op jit(solution)/shard_map/ppermute | solution.py:637
  2.6 15.4 %collective-permute-start = (f32[2,16,2,8,512]{4,3,2,1,0:T(8,128)S(1)}, f32[2,16,2,8,512]{4,3,2,1,0:T(8,128)S(1)}, u32[]{:S(2)}, u32[]{:S(2)}) collective-permute-start(f32[2,16,2,8,512]{4,3,2,1,0:T(8,128)S(1)} %get-tuple-element.50.refs_0_.cross), channel_id=1, source_target_pairs={{0,16},{12,28},{4,8},{8,4},{16,0},{28,12},{20,24},{24,20},{1,17},{... | collective-permute-start | bytes 3145736 | tf_op jit(solution)/shard_map/ppermute | solution.py:636
  18.0 11.6 %copy-start = (f32[4]{0:T(128)S(1)}, f32[4]{0:T(128)}, u32[]{:S(2)}) copy-start(f32[4]{0:T(128)} %refs_6_.5) | copy-start | bytes 52
  19.4 18.5 %collective-permute-start.2 = (f32[2,16,2,8,512]{4,3,2,1,0:T(8,128)S(1)}, f32[2,16,2,8,512]{4,3,2,1,0:T(8,128)S(1)}, u32[]{:S(2)}, u32[]{:S(2)}) collective-permute-start(f32[2,16,2,8,512]{4,3,2,1,0:T(8,128)S(1)} %get-tuple-element.62.refs_0_), channel_id=1, source_target_pairs={{0,16},{12,28},{4,8},{8,4},{16,0},{28,12},{20,24},{24,20},{1,17},{... | collective-permute-start | bytes 3145736 | tf_op jit(solution)/shard_map/ppermute | solution.py:636
  21.4 16.5 %collective-permute-start.3 = (f32[2,16,2,8,512]{4,3,2,1,0:T(8,128)S(1)}, f32[2,16,2,8,512]{4,3,2,1,0:T(8,128)S(1)}, u32[]{:S(2)}, u32[]{:S(2)}) collective-permute-start(f32[2,16,2,8,512]{4,3,2,1,0:T(8,128)S(1)} %get-tuple-element.63.refs_2_), channel_id=1, source_target_pairs={{0,4},{4,0},{8,12},{12,8},{1,5},{5,1},{9,13},{13,9},{2,6},{6,2},{1... | collective-permute-start | bytes 3145736 | tf_op jit(solution)/shard_map/ppermute | solution.py:637
  21.4 6.2 %collective-permute-start.4 = (f32[5,8,256]{2,1,0:T(8,128)S(1)}, f32[5,8,256]{2,1,0:T(8,128)S(1)}, u32[]{:S(2)}, u32[]{:S(2)}) collective-permute-start(f32[5,8,256]{2,1,0:T(8,128)S(1)} %get-tuple-element.64.refs_0_), channel_id=1, source_target_pairs={{0,1},{1,2},{2,3},{3,0},{4,5},{5,6},{6,7},{7,4},{8,9},{9,10},{10,1... | collective-permute-start | bytes 122888 | tf_op jit(solution)/shard_map/ppermute | solution.py:644
  23.0 6.2 %collective-permute-start.5 = (f32[5,8,256]{2,1,0:T(8,128)S(1)}, f32[5,8,256]{2,1,0:T(8,128)S(1)}, u32[]{:S(2)}, u32[]{:S(2)}) collective-permute-start(f32[5,8,256]{2,1,0:T(8,128)S(1)} %get-tuple-element.64.refs_0_), channel_id=1, source_target_pairs={{0,2},{1,3},{2,0},{3,1},{4,6},{5,7},{6,4},{7,5},{8,10},{9,11},{10,... | collective-permute-start | bytes 122888 | tf_op jit(solution)/shard_map/ppermute | solution.py:644
  25.6 4.0 %collective-permute-start.6 = (f32[5,8,256]{2,1,0:T(8,128)S(1)}, f32[5,8,256]{2,1,0:T(8,128)S(1)}, u32[]{:S(2)}, u32[]{:S(2)}) collective-permute-start(f32[5,8,256]{2,1,0:T(8,128)S(1)} %get-tuple-element.64.refs_0_), channel_id=1, source_target_pairs={{0,3},{1,0},{2,1},{3,2},{4,7},{5,4},{6,5},{7,6},{8,11},{9,8},{10,9... | collective-permute-start | bytes 122888 | tf_op jit(solution)/shard_map/ppermute | solution.py:644
  30.3 7.6 %collective-permute-start.7 = (f32[6,2,256]{2,1,0:T(2,128)S(1)}, f32[6,2,256]{2,1,0:T(2,128)S(1)}, u32[]{:S(2)}, u32[]{:S(2)}) collective-permute-start(f32[6,2,256]{2,1,0:T(2,128)S(1)} %get-tuple-element.66), channel_id=1, source_target_pairs={{0,16},{12,28},{4,8},{8,4},{16,0},{28,12},{20,24},{24,20},{1,17},{... | collective-permute-start | bytes 36872 | tf_op jit(solution)/shard_map/ppermute | solution.py:636
  31.3 6.6 %collective-permute-start.8 = (f32[6,2,256]{2,1,0:T(2,128)S(1)}, f32[6,2,256]{2,1,0:T(2,128)S(1)}, u32[]{:S(2)}, u32[]{:S(2)}) collective-permute-start(f32[6,2,256]{2,1,0:T(2,128)S(1)} %get-tuple-element.67), channel_id=1, source_target_pairs={{0,4},{4,0},{8,12},{12,8},{1,5},{5,1},{9,13},{13,9},{2,6},{6,2},{1... | collective-permute-start | bytes 36872 | tf_op jit(solution)/shard_map/ppermute | solution.py:637
  40.8 17.5 %collective-permute-start.10 = (f32[2,16,2,8,512]{4,3,2,1,0:T(8,128)S(1)}, f32[2,16,2,8,512]{4,3,2,1,0:T(8,128)S(1)}, u32[]{:S(2)}, u32[]{:S(2)}) collective-permute-start(f32[2,16,2,8,512]{4,3,2,1,0:T(8,128)S(1)} %get-tuple-element.79.refs_2_), channel_id=1, source_target_pairs={{0,4},{4,0},{8,12},{12,8},{1,5},{5,1},{9,13},{13,9},{2,6},{6,2},{1... | collective-permute-start | bytes 3145736 | tf_op jit(solution)/shard_map/ppermute | solution.py:637
  41.3 17.0 %collective-permute-start.9 = (f32[2,16,2,8,512]{4,3,2,1,0:T(8,128)S(1)}, f32[2,16,2,8,512]{4,3,2,1,0:T(8,128)S(1)}, u32[]{:S(2)}, u32[]{:S(2)}) collective-permute-start(f32[2,16,2,8,512]{4,3,2,1,0:T(8,128)S(1)} %get-tuple-element.78.refs_0_), channel_id=1, source_target_pairs={{0,16},{12,28},{4,8},{8,4},{16,0},{28,12},{20,24},{24,20},{1,17},{... | collective-permute-start | bytes 3145736 | tf_op jit(solution)/shard_map/ppermute | solution.py:636
  42.4 5.9 %collective-permute-start.11 = (f32[5,8,256]{2,1,0:T(8,128)S(1)}, f32[5,8,256]{2,1,0:T(8,128)S(1)}, u32[]{:S(2)}, u32[]{:S(2)}) collective-permute-start(f32[5,8,256]{2,1,0:T(8,128)S(1)} %get-tuple-element.80.refs_0_), channel_id=1, source_target_pairs={{0,1},{1,2},{2,3},{3,0},{4,5},{5,6},{6,7},{7,4},{8,9},{9,10},{10,1... | collective-permute-start | bytes 122888 | tf_op jit(solution)/shard_map/ppermute | solution.py:644
  43.2 5.9 %collective-permute-start.12 = (f32[5,8,256]{2,1,0:T(8,128)S(1)}, f32[5,8,256]{2,1,0:T(8,128)S(1)}, u32[]{:S(2)}, u32[]{:S(2)}) collective-permute-start(f32[5,8,256]{2,1,0:T(8,128)S(1)} %get-tuple-element.80.refs_0_), channel_id=1, source_target_pairs={{0,2},{1,3},{2,0},{3,1},{4,6},{5,7},{6,4},{7,5},{8,10},{9,11},{10,... | collective-permute-start | bytes 122888 | tf_op jit(solution)/shard_map/ppermute | solution.py:644
  46.1 4.0 %collective-permute-start.13 = (f32[5,8,256]{2,1,0:T(8,128)S(1)}, f32[5,8,256]{2,1,0:T(8,128)S(1)}, u32[]{:S(2)}, u32[]{:S(2)}) collective-permute-start(f32[5,8,256]{2,1,0:T(8,128)S(1)} %get-tuple-element.80.refs_0_), channel_id=1, source_target_pairs={{0,3},{1,0},{2,1},{3,2},{4,7},{5,4},{6,5},{7,6},{8,11},{9,8},{10,9... | collective-permute-start | bytes 122888 | tf_op jit(solution)/shard_map/ppermute | solution.py:644
  50.7 7.7 %collective-permute-start.14 = (f32[6,2,256]{2,1,0:T(2,128)S(1)}, f32[6,2,256]{2,1,0:T(2,128)S(1)}, u32[]{:S(2)}, u32[]{:S(2)}) collective-permute-start(f32[6,2,256]{2,1,0:T(2,128)S(1)} %get-tuple-element.81), channel_id=1, source_target_pairs={{0,16},{12,28},{4,8},{8,4},{16,0},{28,12},{20,24},{24,20},{1,17},{... | collective-permute-start | bytes 36872 | tf_op jit(solution)/shard_map/ppermute | solution.py:636
  51.8 6.6 %collective-permute-start.15 = (f32[6,2,256]{2,1,0:T(2,128)S(1)}, f32[6,2,256]{2,1,0:T(2,128)S(1)}, u32[]{:S(2)}, u32[]{:S(2)}) collective-permute-start(f32[6,2,256]{2,1,0:T(2,128)S(1)} %get-tuple-element.82), channel_id=1, source_target_pairs={{0,4},{4,0},{8,12},{12,8},{1,5},{5,1},{9,13},{13,9},{2,6},{6,2},{1... | collective-permute-start | bytes 36872 | tf_op jit(solution)/shard_map/ppermute | solution.py:637
  61.3 6.3 %collective-permute-start.16 = (f32[5,8,256]{2,1,0:T(8,128)S(1)}, f32[5,8,256]{2,1,0:T(8,128)S(1)}, u32[]{:S(2)}, u32[]{:S(2)}) collective-permute-start(f32[5,8,256]{2,1,0:T(8,128)S(1)} %get-tuple-element.94.refs_0_), channel_id=1, source_target_pairs={{0,1},{1,2},{2,3},{3,0},{4,5},{5,6},{6,7},{7,4},{8,9},{9,10},{10,1... | collective-permute-start | bytes 122888 | tf_op jit(solution)/shard_map/ppermute | solution.py:644
  62.0 6.8 %collective-permute-start.17 = (f32[5,8,256]{2,1,0:T(8,128)S(1)}, f32[5,8,256]{2,1,0:T(8,128)S(1)}, u32[]{:S(2)}, u32[]{:S(2)}) collective-permute-start(f32[5,8,256]{2,1,0:T(8,128)S(1)} %get-tuple-element.94.refs_0_), channel_id=1, source_target_pairs={{0,2},{1,3},{2,0},{3,1},{4,6},{5,7},{6,4},{7,5},{8,10},{9,11},{10,... | collective-permute-start | bytes 122888 | tf_op jit(solution)/shard_map/ppermute | solution.py:644
  64.1 4.6 %collective-permute-start.18 = (f32[5,8,256]{2,1,0:T(8,128)S(1)}, f32[5,8,256]{2,1,0:T(8,128)S(1)}, u32[]{:S(2)}, u32[]{:S(2)}) collective-permute-start(f32[5,8,256]{2,1,0:T(8,128)S(1)} %get-tuple-element.94.refs_0_), channel_id=1, source_target_pairs={{0,3},{1,0},{2,1},{3,2},{4,7},{5,4},{6,5},{7,6},{8,11},{9,8},{10,9... | collective-permute-start | bytes 122888 | tf_op jit(solution)/shard_map/ppermute | solution.py:644

commit v9 on v8

--- a/solution.py
+++ b/solution.py
@@ -36,18 +36,18 @@
     return [coef_ref[k, :, lanes] for k in range(9)]
 
 
-def x_row(cells, rows, store, coef, change=False):
+def x_row(cells, rows, store, coef, change=False, known=None):
     reach, lean, ahead = coef[0], coef[1], coef[2] > 0.0
-    first, last = rows[0], rows[-1]
-    steps = {n: cells[n + 1] - cells[n] for n in range(first - 2, last + 2)}
-    faces = {
-        n: cells[n] + lean * minmod(steps[n - 1], steps[n])
-        for n in range(first - 1, last + 2)
-    }
+    steps = {n: cells[n + 1] - cells[n] for n in cells if n + 1 in cells}
+    faces = dict(known or {})
+    for n in range(rows[0] - 1, rows[-1] + 2):
+        if n not in faces:
+            faces[n] = cells[n] + lean * minmod(steps[n - 1], steps[n])
     for n in rows:
         source = jnp.where(ahead, faces[n - 1], faces[n + 1])
         v = reach * (faces[n] - source)
         store(n, v if change else cells[n] - v)
+    return faces
 
 
 def yz_row(source, out, fresh, row, lanes, coef):
@@ -240,8 +240,8 @@
     lax.fori_loop(0, staged.shape[0] * count, one, 0, unroll=4)
 
 
-def load_kernel(order_in, codes_in, state, cross, inside, codes, table, factor, weights, coef,
-                order, raw, flat, near_cross, near_inside, cross_sems, inside_sems, more_sems):
+def load_kernel(order_in, codes_in, state, cross, near_inside, codes, table, factor, weights, coef,
+                order, raw, flat, near_cross, cross_sems, inside_sems, more_sems):
     rows, width = state.shape[0], order.shape[-1]
     mirrored = lax.axis_index("gx") % 2
     more = [
@@ -308,13 +308,13 @@
     unstage(near_cross, cross)
     for copy in copies[half:]:
         copy.wait()
-    unstage(near_inside, inside)
 
 
 def inner_kernel(relax, rows, *refs):
     if relax:
         (m_cross, m_mid, m_in, params, table, factor, coef_ref, weights,
-         cross, middle, inside, out, e_cross, e_in, sums, wide, tall, kept) = refs
+         cross, middle, inside, out, e_cross, e_in, f_cross, f_in, sums,
+         wide, tall, kept) = refs
         spread_features([params[k] for k in range(6)], wide, tall, rows)
         group = [(r, m_cross.at[r], into(cross.at[r])) for r in range(2)]
         group += [(rows - 2 + r, m_in.at[r], into(inside.at[r])) for r in range(2)]
@@ -326,13 +326,15 @@
             ]
             relax_group(group, tall, table, factor, kept)
     else:
-        (cross, inside, state, coef_ref, weights, middle, out, e_cross, e_in, sums,
-         near, sems) = refs
+        (cross, near_inside, state, coef_ref, weights, middle, inside, out, e_cross, e_in,
+         f_cross, f_in, sums, near, sems) = refs
         mirrored = lax.axis_index("gx") % 2
         copies = row_copies(mirrored, state, near, 2, sems)
         for copy in copies:
             copy.start()
     yz_rows(cross, e_cross, True, 2, coef_ref)
+    if not relax:
+        unstage(near_inside, inside)
     yz_rows(inside, e_in, True, 2, coef_ref)
     if not relax:
         for copy in copies:
@@ -358,7 +360,10 @@
             def store(n, v, t=t):
                 out[n - 2, y, t, :, lanes] = v
 
-            x_row(cells, list(range(2, rows - 2)), store, coef)
+            faces = x_row(cells, list(range(2, rows - 2)), store, coef)
+            for n in range(2):
+                f_cross[n, y, t, :, lanes] = faces[1 + n]
+                f_in[n, y, t, :, lanes] = faces[rows - 3 + n]
         return carry
 
     lax.fori_loop(0, chunks * 16, along_x, 0, unroll=4)
@@ -371,34 +376,31 @@
     return jnp.where((place == 0) | (place == line - 1), 0.0, 1.0)
 
 
-def cross_x(low, cross, middle, before, out, y, t, lanes, coef, present):
+def cross_x(low, cross, known, before, out, y, t, lanes, coef, present):
     cells = {}
     for n in range(2):
         cells[-1 - n] = low[n, y, t, :, lanes] * present
         cells[n] = cross[n, y, t, :, lanes]
-        cells[2 + n] = middle[n, y, t, :, lanes]
 
     def store(n, v):
         out[n, y, t, :, lanes] = before[n, y, t, :, lanes] - v
 
-    x_row(cells, [0, 1], store, coef, True)
-
-
-def in_x(high, inside, middle, before, out, y, t, lanes, coef):
-    last = middle.shape[0]
+    x_row(cells, [0, 1], store, coef, True, {1 + n: known[n, y, t, :, lanes] for n in range(2)})
+
+
+def in_x(high, inside, known, before, out, y, t, lanes, coef):
     cells = {}
     for n in range(2):
-        cells[n] = middle[last - 2 + n, y, t, :, lanes]
-        cells[2 + n] = inside[n, y, t, :, lanes]
-        cells[4 + n] = high[1 - n, y, t, :, lanes]
+        cells[n] = inside[n, y, t, :, lanes]
+        cells[2 + n] = high[1 - n, y, t, :, lanes]
 
     def store(n, v):
-        out[n - 2, y, t, :, lanes] = before[n - 2, y, t, :, lanes] - v
-
-    x_row(cells, [2, 3], store, coef, True)
-
-
-def each_place(middle, coef_ref, work):
+        out[n, y, t, :, lanes] = before[n, y, t, :, lanes] - v
+
+    x_row(cells, [0, 1], store, coef, True, {n - 1: known[n, y, t, :, lanes] for n in range(2)})
+
+
+def each_place(width, coef_ref, work):
     def one(i, carry):
         lanes = lanes_of(i // 16)
         coef = coefs_of(coef_ref, lanes)
@@ -406,19 +408,24 @@
             work(i % 16, t, lanes, coef)
         return carry
 
-    lax.fori_loop(0, middle.shape[-1] // LANES * 16, one, 0, unroll=4)
-
-
-def first_in_kernel(high, inside, e_in, middle, coef_ref, weights, out, sums):
-    each_place(middle, coef_ref, lambda *at: in_x(high, inside, middle, e_in, out, *at))
+    lax.fori_loop(0, width // LANES * 16, one, 0, unroll=4)
+
+
+def first_in_kernel(near_high, inside, e_in, f_in, coef_ref, weights, out, sums, high):
+    unstage(near_high, high)
+    each_place(
+        out.shape[-1], coef_ref, lambda *at: in_x(high, inside, f_in, e_in, out, *at)
+    )
     row_moments([(out.at[r], r) for r in range(2)], weights, sums)
 
 
-def first_cross_kernel(line, low, cross, e_cross, middle, coef_ref, weights, inner_sums, in_sums,
+def first_cross_kernel(line, low, cross, e_cross, f_cross, coef_ref, weights, inner_sums, in_sums,
                        out, sums):
     present = presence(line)
     each_place(
-        middle, coef_ref, lambda *at: cross_x(low, cross, middle, e_cross, out, *at, present)
+        out.shape[-1],
+        coef_ref,
+        lambda *at: cross_x(low, cross, f_cross, e_cross, out, *at, present),
     )
     rows = sums.shape[1]
     for m in range(5):
@@ -427,8 +434,8 @@
     row_moments([(out.at[r], r) for r in range(2)], weights, sums)
 
 
-def edge_kernel(rows, line, h_cross, h_in, p_cross, p_in, table, factor, cross, middle, inside,
-                e_cross, e_in, coef_ref, weights, inner_sums, out_cross, out_in, sums,
+def edge_kernel(rows, line, h_cross, h_in, p_cross, p_in, table, factor, cross, inside,
+                e_cross, e_in, f_cross, f_in, coef_ref, weights, inner_sums, out_cross, out_in, sums,
                 wide, tall, kept, low, high):
     params = [jnp.concatenate([p_cross[k], p_in[k]], axis=0) for k in range(6)]
     spread_features(params, wide, tall, 4)
@@ -438,10 +445,10 @@
     present = presence(line)
 
     def work(*at):
-        cross_x(low, cross, middle, e_cross, out_cross, *at, present)
-        in_x(high, inside, middle, e_in, out_in, *at)
-
-    each_place(middle, coef_ref, work)
+        cross_x(low, cross, f_cross, e_cross, out_cross, *at, present)
+        in_x(high, inside, f_in, e_in, out_in, *at)
+
+    each_place(out_in.shape[-1], coef_ref, work)
     for m in range(5):
         sums[m, 2 : rows - 2, :] = inner_sums[m]
     edges = [(out_cross.at[r], r) for r in range(2)]
@@ -520,7 +527,7 @@
             out_specs=[vmem] * 7,
             out_shape=[
                 slab(2),
-                slab(2),
+                jax.ShapeDtypeStruct((2, count_y, chunks, count_z, LANES), F32),
                 jax.ShapeDtypeStruct((rows, cells), jnp.int32),
                 jax.ShapeDtypeStruct((FEATURES, width), BF16),
                 jax.ShapeDtypeStruct((FEATURES, LANES), BF16),
@@ -532,7 +539,6 @@
                 pltpu.VMEM((rows, count_y, count_z), jnp.int32),
                 pltpu.VMEM((rows, cells), jnp.int32),
                 staging(2)[0],
-                staging(2)[0],
                 staging(2)[1],
                 staging(2)[1],
                 pltpu.SemaphoreType.DMA((2,)),
@@ -543,14 +549,14 @@
 
     def inner(relax, state, params):
         sums = jax.ShapeDtypeStruct((5, rows - 4, cells), F32)
-        out_shape = [slab(rows - 4), slab(2), slab(2), sums]
+        out_shape = [slab(rows - 4)] + [slab(2)] * 4 + [sums]
         scratch = []
         if relax:
             out_shape = [slab(2), slab(rows - 4), slab(2)] + out_shape
             scratch = feature_scratch(rows)
             args = (*state, params, table, factor, coef, weights)
         else:
-            out_shape = [slab(rows - 4)] + out_shape
+            out_shape = [slab(rows - 4), slab(2)] + out_shape
             scratch = staging(rows - 4)
             args = (*state, coef, weights)
         return pl.pallas_call(
@@ -572,9 +578,10 @@
             in_specs=[vmem] * 6,
             out_specs=[vmem] * 2,
             out_shape=[slab(2), edge_sums],
+            scratch_shapes=[slab_scratch(2)],
             compiler_params=limits(LIMIT_MIB),
             name="first_in",
-        )(*args, middle, coef, weights)
+        )(*args, coef, weights)
 
     def first_cross(*args):
         return pl.pallas_call(
@@ -586,8 +593,8 @@
             name="first_cross",
         )(*args)
 
-    def edge(halos, params, state, edges, sums):
-        args = (*halos, *params, table, factor, *state, *edges, coef, weights, sums)
+    def edge(halos, params, edges, sums):
+        args = (*halos, *params, table, factor, *edges, coef, weights, sums)
         return pl.pallas_call(
             functools.partial(edge_kernel, rows, line),
             in_specs=[vmem] * len(args),
@@ -644,19 +651,22 @@
             parts.append(lax.ppermute(part, "vert", pairs))
         return parts
 
-    cross, inside, codes, table, factor, weights, coef = load()
-    halos = exchange(cross, inside)
-    middle, m_mid, e_cross, e_in, sums = inner(False, (cross, inside, in_hbm(distribution)), None)
-    m_in, in_sums = first_in(halos[1], inside, e_in)
-    m_cross, sums = first_cross(halos[0], cross, e_cross, middle, coef, weights, sums, in_sums)
+    cross, near_inside, codes, table, factor, weights, coef = load()
+    low, near_high = exchange(cross, near_inside)
+    _, inside, m_mid, e_cross, e_in, f_cross, f_in, sums = inner(
+        False, (cross, near_inside, in_hbm(distribution)), None
+    )
+    m_in, in_sums = first_in(near_high, inside, e_in, f_in)
+    m_cross, sums = first_cross(low, cross, e_cross, f_cross, coef, weights, sums, in_sums)
     m_cross, m_in, sums = lax.optimization_barrier((m_cross, m_in, sums))
     for _ in range(1, STEPS):
         halos = exchange(m_cross, m_in)
         params, p_cross, p_in = cell_params(gather(sums), rows, 2, 2)
         p_halos = exchange(p_cross, p_in)
         moved = (m_cross, m_mid, m_in)
-        *state, m_mid, e_cross, e_in, sums = inner(True, moved, params)
-        m_cross, m_in, sums = edge(halos, p_halos, state, (e_cross, e_in), sums)
+        cross, _, inside, m_mid, e_cross, e_in, f_cross, f_in, sums = inner(True, moved, params)
+        edges = (cross, inside, e_cross, e_in, f_cross, f_in)
+        m_cross, m_in, sums = edge(halos, p_halos, edges, sums)
     (params,) = cell_params(gather(sums), rows)
     return final((m_cross, m_mid, m_in), params)
 

time: 72.3 us -> 72.8 us (level)
  Pallas kernels: 34.7 us -> 36.4 us
  waiting for transfers between devices: 14.6 us -> 13.4 us
    pallas_call x3, Pallas kernels: 19.3 us -> 21.7 us  [inner(): pl.pallas_call(functools.partial(inner_kernel, relax, rows), in_specs=[vm...]
    ppermute x5, waiting for transfers between devices: 5.19 us -> 3.99 us  [exchange(): lax.ppermute(cross, ('groups', 'gx'), across)]
  transfers between devices with their start and end apart: 19 -> 19, of which waited for: 8 -> 8; matrix products, arithmetic and copies ran while one was open for 0% -> 0% of each run, Pallas kernels for 30% -> 34%
where the time goes in v9:
time: 72.8 us; the launch traced here: 72.7 us
  Pallas kernels  36.4 us (50%)
  starting transfers between devices  22.1 us (30%)
  waiting for transfers between devices  13.4 us (18%)
  between operations  0.73 us (1%)
    pallas_call x3, Pallas kernels, inner(): pl.pallas_call(functools.partial(inner_kernel, relax, rows), in_specs=[vm...  21.7 us
    ppermute x9, starting transfers between devices, gather(): parts.append(lax.ppermute(part, 'vert', pairs))  13.3 us
    ppermute x9, waiting for transfers between devices, gather(): parts.append(lax.ppermute(part, 'vert', pairs))  9.4 us
    ppermute x5, starting transfers between devices, exchange(): lax.ppermute(cross, ('groups', 'gx'), across)  7.81 us
    pallas_call x2, Pallas kernels, edge(): pl.pallas_call(functools.partial(edge_kernel, rows, line), in_specs=[vmem...  5.42 us
    ppermute x5, waiting for transfers between devices, exchange(): lax.ppermute(cross, ('groups', 'gx'), across)  3.99 us
    pallas_call x1, Pallas kernels, final(): pl.pallas_call(functools.partial(final_kernel, rows), in_specs=[vmem] * 6...  2.8 us
    pallas_call x3, Pallas kernels, cell_params(): pl.pallas_call(functools.partial(param_kernel, total, len(parts)), in_spe...  1.92 us
  transfers between devices with their start and end apart: 19, of which 8 were waited for; matrix products, arithmetic and copies ran while one was open for 0% of the time, Pallas kernels for 34%

profile of v9, /device:TPU:0, one launch (start us, length us, event | category | flops | bytes accessed | tf_op | source)
XLA Modules:
  0.0 72.7 jit_solution(9643776104255134089)
XLA Ops:
  0.0 1.8 %load_edges.1 = (f32[2,16,2,8,512]{4,3,2,1,0:T(8,128)S(1)}, f32[2,16,4,16,128]{4,3,2,1,0:T(8,128)S(1)}, s32[8,256]{1,0:T(8,128)S(1)}, bf16[32,512]{1,0:T(8,128)(...) custom-call(s32[1,512]{1,0:T(1,128)} %bitcast.1, ...), custom_call_target="tpu_custom_call" | custom-call | tf_op jit(solution)/shard_map/load_edges/pallas_call | solution.py:524
  1.8 0.5 collective-permute-start.1
  2.4 2.6 %collective-permute-start = (f32[2,16,2,8,512]{4,3,2,1,0:T(8,128)S(1)}, f32[2,16,2,8,512]{4,3,2,1,0:T(8,128)S(1)}, u32[]{:S(2)}, u32[]{:S(2)}) collective-permute-start(f32[2,16,2,8,512]{4,3,2,1,0:T(8,128)S(1)} %get-tuple-element.54.refs_0_.cross), channel_id=1, source_target_pairs={{0,16},{12,28},{4,8},{8,4},{16,0},{28,12},{20,24},{24,20},{1,17},{... | collective-permute-start | bytes 3145736 | tf_op jit(solution)/shard_map/ppermute | solution.py:643
  5.0 7.2 %inner_first.1 = (f32[4,16,2,8,512]{4,3,2,1,0:T(8,128)}, f32[2,16,2,8,512]{4,3,2,1,0:T(8,128)S(1)}, f32[4,16,2,8,512]{4,3,2,1,0:T(8,128)S(1)}, f32[2,16,2,8,512]...) custom-call(f32[2,16,2,8,512]{4,3,2,1,0:T(8,128)S(1)} %get-tuple-ele, ...), custom_call_target="tpu_custom_call" | custom-call | tf_op jit(solution)/shard_map/inner_first/pallas_call | solution.py:562
  12.2 0.0 collective-permute-done.1.near_high
  12.2 1.5 %first_in.1 = (f32[2,16,2,8,512]{4,3,2,1,0:T(8,128)S(1)}, f32[5,2,256]{2,1,0:T(2,128)S(1)}) custom-call(f32[2,16,4,16,128]{4,3,2,1,0:T(8,128)S(1)} %collective-permute-done.1.near_high, f32[2,16,2,8,512]{4,3,2,1,0:T(8,128)S(1)} %get-tuple-element.61.inside, f32[2,16,2,8,512]{4,3,2,1,0:T(8,128)S(1)} %get-tuple-element.62.e_in, ...), custom_call_target="tpu_custom_call" | custom-call | tf_op jit(solution)/shard_map/first_in/pallas_call | solution.py:576
  13.8 4.0 %collective-permute-done.low = f32[2,16,2,8,512]{4,3,2,1,0:T(8,128)S(1)} collective-permute-done((f32[2,16,2,8,512]{4,3,2,1,0:T(8,128)S(1)}, f32[2,16,2,8,512]{4,3,2,1,0:T(8,128)S(1)}, u32[]{:S(2)}, u32[]{:S(2)}) %collective-permute-start) | collective-permute-done | bytes 1048608 | tf_op jit(solution)/shard_map/ppermute | solution.py:643
  17.7 1.2 %first_cross.1 = (f32[2,16,2,8,512]{4,3,2,1,0:T(8,128)S(1)}, f32[5,8,256]{2,1,0:T(8,128)S(1)}) custom-call(f32[2,16,2,8,512]{4,3,2,1,0:T(8,128)S(1)} %collective-permute-done.low, f32[2,16,2,8,512]{4,3,2,1,0:T(8,128)S(1)} %get-tuple-element.54.refs_0_.cross, f32[2,16,2,8,512]{4,3,2,1,0:T(8,128)S(1)} %get-tuple-element.58.e_cross, ...), custom_call_target="tpu_custom_call" | custom-call | tf_op jit(solution)/shard_map/first_cross/pallas_call | solution.py:587
  19.0 2.0 %collective-permute-start.2 = (f32[2,16,2,8,512]{4,3,2,1,0:T(8,128)S(1)}, f32[2,16,2,8,512]{4,3,2,1,0:T(8,128)S(1)}, u32[]{:S(2)}, u32[]{:S(2)}) collective-permute-start(f32[2,16,2,8,512]{4,3,2,1,0:T(8,128)S(1)} %get-tuple-element.68.refs_0_), channel_id=1, source_target_pairs={{0,16},{12,28},{4,8},{8,4},{16,0},{28,12},{20,24},{24,20},{1,17},{... | collective-permute-start | bytes 3145736 | tf_op jit(solution)/shard_map/ppermute | solution.py:643
  21.0 0.0 collective-permute-start.3
  21.0 1.6 %collective-permute-start.4 = (f32[5,8,256]{2,1,0:T(8,128)S(1)}, f32[5,8,256]{2,1,0:T(8,128)S(1)}, u32[]{:S(2)}, u32[]{:S(2)}) collective-permute-start(f32[5,8,256]{2,1,0:T(8,128)S(1)} %get-tuple-element.70.refs_0_), channel_id=1, source_target_pairs={{0,1},{1,2},{2,3},{3,0},{4,5},{5,6},{6,7},{7,4},{8,9},{9,10},{10,1... | collective-permute-start | bytes 122888 | tf_op jit(solution)/shard_map/ppermute | solution.py:651
  22.6 2.6 %collective-permute-start.5 = (f32[5,8,256]{2,1,0:T(8,128)S(1)}, f32[5,8,256]{2,1,0:T(8,128)S(1)}, u32[]{:S(2)}, u32[]{:S(2)}) collective-permute-start(f32[5,8,256]{2,1,0:T(8,128)S(1)} %get-tuple-element.70.refs_0_), channel_id=1, source_target_pairs={{0,2},{1,3},{2,0},{3,1},{4,6},{5,7},{6,4},{7,5},{8,10},{9,11},{10,... | collective-permute-start | bytes 122888 | tf_op jit(solution)/shard_map/ppermute | solution.py:651
  25.2 1.3 %collective-permute-start.6 = (f32[5,8,256]{2,1,0:T(8,128)S(1)}, f32[5,8,256]{2,1,0:T(8,128)S(1)}, u32[]{:S(2)}, u32[]{:S(2)}) collective-permute-start(f32[5,8,256]{2,1,0:T(8,128)S(1)} %get-tuple-element.70.refs_0_), channel_id=1, source_target_pairs={{0,3},{1,0},{2,1},{3,2},{4,7},{5,4},{6,5},{7,6},{8,11},{9,8},{10,9... | collective-permute-start | bytes 122888 | tf_op jit(solution)/shard_map/ppermute | solution.py:651
  27.2 0.0 collective-permute-done.4.refs_1_
  27.2 1.6 %collective-permute-done.5.refs_2_ = f32[5,8,256]{2,1,0:T(8,128)S(1)} collective-permute-done((f32[5,8,256]{2,1,0:T(8,128)S(1)}, f32[5,8,256]{2,1,0:T(8,128)S(1)}, u32[]{:S(2)}, u32[]{:S(2)}) %collective-permute-start.5) | collective-permute-done | bytes 40992 | tf_op jit(solution)/shard_map/ppermute | solution.py:651
  28.8 0.4 collective-permute-done.6.refs_3_
  29.2 0.6 cell_params.3
  29.9 1.1 %collective-permute-start.7 = (f32[6,2,256]{2,1,0:T(2,128)S(1)}, f32[6,2,256]{2,1,0:T(2,128)S(1)}, u32[]{:S(2)}, u32[]{:S(2)}) collective-permute-start(f32[6,2,256]{2,1,0:T(2,128)S(1)} %get-tuple-element.72), channel_id=1, source_target_pairs={{0,16},{12,28},{4,8},{8,4},{16,0},{28,12},{20,24},{24,20},{1,17},{... | collective-permute-start | bytes 36872 | tf_op jit(solution)/shard_map/ppermute | solution.py:643
  30.9 0.0 collective-permute-start.8
  30.9 7.2 %inner_relax.2 = (f32[2,16,2,8,512]{4,3,2,1,0:T(8,128)S(1)}, f32[4,16,2,8,512]{4,3,2,1,0:T(8,128)}, f32[2,16,2,8,512]{4,3,2,1,0:T(8,128)S(1)}, f32[4,16,2,8,512]...) custom-call(f32[2,16,2,8,512]{4,3,2,1,0:T(8,128)S(1)} %get-tuple-ele, ...), custom_call_target="tpu_custom_call" | custom-call | tf_op jit(solution)/shard_map/inner_relax/pallas_call | solution.py:562
  38.1 0.0 collective-permute-done.7.p_cross
  38.1 0.0 collective-permute-done.8.p_in
  38.1 0.0 collective-permute-done.2.h_cross
  38.1 0.0 collective-permute-done.3.h_in
  38.1 2.7 %edge_relax.2 = (f32[2,16,2,8,512]{4,3,2,1,0:T(8,128)S(1)}, f32[2,16,2,8,512]{4,3,2,1,0:T(8,128)S(1)}, f32[5,8,256]{2,1,0:T(8,128)S(1)}) custom-call(f32[2,16,2,8,512]{4,3,2,1,0:T(8,128)S(1)} %collective-permute-done.2.h_cross, f32[2,16,2,8,512]{4,3,2,1,0:T(8,128)S(1)} %collective-permute-done.3.h_in, f32[6,2,256]{2,1,0:T(2,128)S(1)} %collective-permute-done.7.p_cross, ...), custom_call_target="tpu_custom_call" | custom-call | tf_op jit(solution)/shard_map/edge_relax/pallas_call | solution.py:598
  40.9 0.5 collective-permute-start.10
  41.4 1.0 %collective-permute-start.9 = (f32[2,16,2,8,512]{4,3,2,1,0:T(8,128)S(1)}, f32[2,16,2,8,512]{4,3,2,1,0:T(8,128)S(1)}, u32[]{:S(2)}, u32[]{:S(2)}) collective-permute-start(f32[2,16,2,8,512]{4,3,2,1,0:T(8,128)S(1)} %get-tuple-element.85.refs_0_), channel_id=1, source_target_pairs={{0,16},{12,28},{4,8},{8,4},{16,0},{28,12},{20,24},{24,20},{1,17},{... | collective-permute-start | bytes 3145736 | tf_op jit(solution)/shard_map/ppermute | solution.py:643
  42.4 0.8 %collective-permute-start.11 = (f32[5,8,256]{2,1,0:T(8,128)S(1)}, f32[5,8,256]{2,1,0:T(8,128)S(1)}, u32[]{:S(2)}, u32[]{:S(2)}) collective-permute-start(f32[5,8,256]{2,1,0:T(8,128)S(1)} %get-tuple-element.87.refs_0_), channel_id=1, source_target_pairs={{0,1},{1,2},{2,3},{3,0},{4,5},{5,6},{6,7},{7,4},{8,9},{9,10},{10,1... | collective-permute-start | bytes 122888 | tf_op jit(solution)/shard_map/ppermute | solution.py:651
  43.2 2.8 %collective-permute-start.12 = (f32[5,8,256]{2,1,0:T(8,128)S(1)}, f32[5,8,256]{2,1,0:T(8,128)S(1)}, u32[]{:S(2)}, u32[]{:S(2)}) collective-permute-start(f32[5,8,256]{2,1,0:T(8,128)S(1)} %get-tuple-element.87.refs_0_), channel_id=1, source_target_pairs={{0,2},{1,3},{2,0},{3,1},{4,6},{5,7},{6,4},{7,5},{8,10},{9,11},{10,... | collective-permute-start | bytes 122888 | tf_op jit(solution)/shard_map/ppermute | solution.py:651
  46.1 0.2 collective-permute-start.13
  46.3 2.0 %collective-permute-done.11.refs_1_ = f32[5,8,256]{2,1,0:T(8,128)S(1)} collective-permute-done((f32[5,8,256]{2,1,0:T(8,128)S(1)}, f32[5,8,256]{2,1,0:T(8,128)S(1)}, u32[]{:S(2)}, u32[]{:S(2)}) %collective-permute-start.11) | collective-permute-done | bytes 40992 | tf_op jit(solution)/shard_map/ppermute | solution.py:651
  48.3 0.8 %collective-permute-done.12.refs_2_ = f32[5,8,256]{2,1,0:T(8,128)S(1)} collective-permute-done((f32[5,8,256]{2,1,0:T(8,128)S(1)}, f32[5,8,256]{2,1,0:T(8,128)S(1)}, u32[]{:S(2)}, u32[]{:S(2)}) %collective-permute-start.12) | collective-permute-done | bytes 40992 | tf_op jit(solution)/shard_map/ppermute | solution.py:651
  49.1 1.0 %collective-permute-done.13.refs_3_ = f32[5,8,256]{2,1,0:T(8,128)S(1)} collective-permute-done((f32[5,8,256]{2,1,0:T(8,128)S(1)}, f32[5,8,256]{2,1,0:T(8,128)S(1)}, u32[]{:S(2)}, u32[]{:S(2)}) %collective-permute-start.13) | collective-permute-done | bytes 40992 | tf_op jit(solution)/shard_map/ppermute | solution.py:651
  50.1 0.6 cell_params.4
  50.7 1.1 %collective-permute-start.14 = (f32[6,2,256]{2,1,0:T(2,128)S(1)}, f32[6,2,256]{2,1,0:T(2,128)S(1)}, u32[]{:S(2)}, u32[]{:S(2)}) collective-permute-start(f32[6,2,256]{2,1,0:T(2,128)S(1)} %get-tuple-element.88), channel_id=1, source_target_pairs={{0,16},{12,28},{4,8},{8,4},{16,0},{28,12},{20,24},{24,20},{1,17},{... | collective-permute-start | bytes 36872 | tf_op jit(solution)/shard_map/ppermute | solution.py:643
  51.8 0.0 collective-permute-start.15
  51.8 7.2 %inner_relax.3 = (f32[2,16,2,8,512]{4,3,2,1,0:T(8,128)S(1)}, f32[4,16,2,8,512]{4,3,2,1,0:T(8,128)}, f32[2,16,2,8,512]{4,3,2,1,0:T(8,128)S(1)}, f32[4,16,2,8,512]...) custom-call(f32[2,16,2,8,512]{4,3,2,1,0:T(8,128)S(1)} %get-tuple-ele, ...), custom_call_target="tpu_custom_call" | custom-call | tf_op jit(solution)/shard_map/inner_relax/pallas_call | solution.py:562
  59.0 0.0 collective-permute-done.14.p_cross
  59.0 0.0 collective-permute-done.15.p_in
  59.0 0.0 collective-permute-done.10.h_in
  59.1 2.7 %edge_relax.3 = (f32[2,16,2,8,512]{4,3,2,1,0:T(8,128)S(1)}, f32[2,16,2,8,512]{4,3,2,1,0:T(8,128)S(1)}, f32[5,8,256]{2,1,0:T(8,128)S(1)}) custom-call(f32[2,16,2,8,512]{4,3,2,1,0:T(8,128)S(1)} %collective-permute-done.9.h_cross, f32[2,16,2,8,512]{4,3,2,1,0:T(8,128)S(1)} %collective-permute-done.10.h_in, f32[6,2,256]{2,1,0:T(2,128)S(1)} %collective-permute-done.14.p_cross, ...), custom_call_target="tpu_custom_call" | custom-call | tf_op jit(solution)/shard_map/edge_relax/pallas_call | solution.py:598
  61.8 0.7 collective-permute-start.16
  62.5 2.1 %collective-permute-start.17 = (f32[5,8,256]{2,1,0:T(8,128)S(1)}, f32[5,8,256]{2,1,0:T(8,128)S(1)}, u32[]{:S(2)}, u32[]{:S(2)}) collective-permute-start(f32[5,8,256]{2,1,0:T(8,128)S(1)} %get-tuple-element.102.refs_0_), channel_id=1, source_target_pairs={{0,2},{1,3},{2,0},{3,1},{4,6},{5,7},{6,4},{7,5},{8,10},{9,11},{10,... | collective-permute-start | bytes 122888 | tf_op jit(solution)/shard_map/ppermute | solution.py:651
  64.6 1.0 %collective-permute-start.18 = (f32[5,8,256]{2,1,0:T(8,128)S(1)}, f32[5,8,256]{2,1,0:T(8,128)S(1)}, u32[]{:S(2)}, u32[]{:S(2)}) collective-permute-start(f32[5,8,256]{2,1,0:T(8,128)S(1)} %get-tuple-element.102.refs_0_), channel_id=1, source_target_pairs={{0,3},{1,0},{2,1},{3,2},{4,7},{5,4},{6,5},{7,6},{8,11},{9,8},{10,9... | collective-permute-start | bytes 122888 | tf_op jit(solution)/shard_map/ppermute | solution.py:651
  65.6 2.4 %collective-permute-done.16.refs_1_ = f32[5,8,256]{2,1,0:T(8,128)S(1)} collective-permute-done((f32[5,8,256]{2,1,0:T(8,128)S(1)}, f32[5,8,256]{2,1,0:T(8,128)S(1)}, u32[]{:S(2)}, u32[]{:S(2)}) %collective-permute-start.16) | collective-permute-done | bytes 40992 | tf_op jit(solution)/shard_map/ppermute | solution.py:651
  68.0 1.2 %collective-permute-done.17.refs_2_ = f32[5,8,256]{2,1,0:T(8,128)S(1)} collective-permute-done((f32[5,8,256]{2,1,0:T(8,128)S(1)}, f32[5,8,256]{2,1,0:T(8,128)S(1)}, u32[]{:S(2)}, u32[]{:S(2)}) %collective-permute-start.17) | collective-permute-done | bytes 40992 | tf_op jit(solution)/shard_map/ppermute | solution.py:651
  69.2 0.6 cell_params.5.params
  69.9 2.8 %final_relax.1 = f32[8,16,16,512]{3,2,1,0:T(8,128)} custom-call(f32[2,16,2,8,512]{4,3,2,1,0:T(8,128)S(1)} %get-tuple-element.99.m_cross, f32[4,16,2,8,512]{4,3,2,1,0:T(8,128)S(1)} %get-tuple-element.100.m_mid, f32[2,16,2,8,512]{4,3,2,1,0:T(8,128)S(1)} %get-tuple-element.101.m_in, f32[6,8,256]{2,1,0:T(8,128)S(1)} %cell_params.5.params, ...), custom_call_target="tpu_custom_call" | custom-call | tf_op jit(solution)/shard_map/final_relax/pallas_call | solution.py:619
  (4 shorter events, 0.0 us)
Async XLA Ops:
  1.8 10.4 %collective-permute-start.1 = (f32[2,16,4,16,128]{4,3,2,1,0:T(8,128)S(1)}, f32[2,16,4,16,128]{4,3,2,1,0:T(8,128)S(1)}, u32[]{:S(2)}, u32[]{:S(2)}) collective-permute-start(f32[2,16,4,16,128]{4,3,2,1,0:T(8,128)S(1)} %get-tuple-element.55.refs_1_), channel_id=1, source_target_pairs={{0,4},{4,0},{8,12},{12,8},{1,5},{5,1},{9,13},{13,9},{2,6},{6,2},{1... | collective-permute-start | bytes 3145736 | tf_op jit(solution)/shard_map/ppermute | solution.py:644
  2.4 15.4 %collective-permute-start = (f32[2,16,2,8,512]{4,3,2,1,0:T(8,128)S(1)}, f32[2,16,2,8,512]{4,3,2,1,0:T(8,128)S(1)}, u32[]{:S(2)}, u32[]{:S(2)}) collective-permute-start(f32[2,16,2,8,512]{4,3,2,1,0:T(8,128)S(1)} %get-tuple-element.54.refs_0_.cross), channel_id=1, source_target_pairs={{0,16},{12,28},{4,8},{8,4},{16,0},{28,12},{20,24},{24,20},{1,17},{... | collective-permute-start | bytes 3145736 | tf_op jit(solution)/shard_map/ppermute | solution.py:643
  17.7 11.5 %copy-start = (f32[4]{0:T(128)S(1)}, f32[4]{0:T(128)}, u32[]{:S(2)}) copy-start(f32[4]{0:T(128)} %refs_6_.5) | copy-start | bytes 52
  19.0 19.2 %collective-permute-start.2 = (f32[2,16,2,8,512]{4,3,2,1,0:T(8,128)S(1)}, f32[2,16,2,8,512]{4,3,2,1,0:T(8,128)S(1)}, u32[]{:S(2)}, u32[]{:S(2)}) collective-permute-start(f32[2,16,2,8,512]{4,3,2,1,0:T(8,128)S(1)} %get-tuple-element.68.refs_0_), channel_id=1, source_target_pairs={{0,16},{12,28},{4,8},{8,4},{16,0},{28,12},{20,24},{24,20},{1,17},{... | collective-permute-start | bytes 3145736 | tf_op jit(solution)/shard_map/ppermute | solution.py:643
  21.0 17.1 %collective-permute-start.3 = (f32[2,16,2,8,512]{4,3,2,1,0:T(8,128)S(1)}, f32[2,16,2,8,512]{4,3,2,1,0:T(8,128)S(1)}, u32[]{:S(2)}, u32[]{:S(2)}) collective-permute-start(f32[2,16,2,8,512]{4,3,2,1,0:T(8,128)S(1)} %get-tuple-element.69.refs_2_), channel_id=1, source_target_pairs={{0,4},{4,0},{8,12},{12,8},{1,5},{5,1},{9,13},{13,9},{2,6},{6,2},{1... | collective-permute-start | bytes 3145736 | tf_op jit(solution)/shard_map/ppermute | solution.py:644
  21.0 6.2 %collective-permute-start.4 = (f32[5,8,256]{2,1,0:T(8,128)S(1)}, f32[5,8,256]{2,1,0:T(8,128)S(1)}, u32[]{:S(2)}, u32[]{:S(2)}) collective-permute-start(f32[5,8,256]{2,1,0:T(8,128)S(1)} %get-tuple-element.70.refs_0_), channel_id=1, source_target_pairs={{0,1},{1,2},{2,3},{3,0},{4,5},{5,6},{6,7},{7,4},{8,9},{9,10},{10,1... | collective-permute-start | bytes 122888 | tf_op jit(solution)/shard_map/ppermute | solution.py:651
  22.6 6.2 %collective-permute-start.5 = (f32[5,8,256]{2,1,0:T(8,128)S(1)}, f32[5,8,256]{2,1,0:T(8,128)S(1)}, u32[]{:S(2)}, u32[]{:S(2)}) collective-permute-start(f32[5,8,256]{2,1,0:T(8,128)S(1)} %get-tuple-element.70.refs_0_), channel_id=1, source_target_pairs={{0,2},{1,3},{2,0},{3,1},{4,6},{5,7},{6,4},{7,5},{8,10},{9,11},{10,... | collective-permute-start | bytes 122888 | tf_op jit(solution)/shard_map/ppermute | solution.py:651
  25.2 4.0 %collective-permute-start.6 = (f32[5,8,256]{2,1,0:T(8,128)S(1)}, f32[5,8,256]{2,1,0:T(8,128)S(1)}, u32[]{:S(2)}, u32[]{:S(2)}) collective-permute-start(f32[5,8,256]{2,1,0:T(8,128)S(1)} %get-tuple-element.70.refs_0_), channel_id=1, source_target_pairs={{0,3},{1,0},{2,1},{3,2},{4,7},{5,4},{6,5},{7,6},{8,11},{9,8},{10,9... | collective-permute-start | bytes 122888 | tf_op jit(solution)/shard_map/ppermute | solution.py:651
  29.9 8.3 %collective-permute-start.7 = (f32[6,2,256]{2,1,0:T(2,128)S(1)}, f32[6,2,256]{2,1,0:T(2,128)S(1)}, u32[]{:S(2)}, u32[]{:S(2)}) collective-permute-start(f32[6,2,256]{2,1,0:T(2,128)S(1)} %get-tuple-element.72), channel_id=1, source_target_pairs={{0,16},{12,28},{4,8},{8,4},{16,0},{28,12},{20,24},{24,20},{1,17},{... | collective-permute-start | bytes 36872 | tf_op jit(solution)/shard_map/ppermute | solution.py:643
  30.9 7.2 %collective-permute-start.8 = (f32[6,2,256]{2,1,0:T(2,128)S(1)}, f32[6,2,256]{2,1,0:T(2,128)S(1)}, u32[]{:S(2)}, u32[]{:S(2)}) collective-permute-start(f32[6,2,256]{2,1,0:T(2,128)S(1)} %get-tuple-element.73), channel_id=1, source_target_pairs={{0,4},{4,0},{8,12},{12,8},{1,5},{5,1},{9,13},{13,9},{2,6},{6,2},{1... | collective-permute-start | bytes 36872 | tf_op jit(solution)/shard_map/ppermute | solution.py:644
  40.9 18.2 %collective-permute-start.10 = (f32[2,16,2,8,512]{4,3,2,1,0:T(8,128)S(1)}, f32[2,16,2,8,512]{4,3,2,1,0:T(8,128)S(1)}, u32[]{:S(2)}, u32[]{:S(2)}) collective-permute-start(f32[2,16,2,8,512]{4,3,2,1,0:T(8,128)S(1)} %get-tuple-element.86.refs_2_), channel_id=1, source_target_pairs={{0,4},{4,0},{8,12},{12,8},{1,5},{5,1},{9,13},{13,9},{2,6},{6,2},{1... | collective-permute-start | bytes 3145736 | tf_op jit(solution)/shard_map/ppermute | solution.py:644
  41.4 17.7 %collective-permute-start.9 = (f32[2,16,2,8,512]{4,3,2,1,0:T(8,128)S(1)}, f32[2,16,2,8,512]{4,3,2,1,0:T(8,128)S(1)}, u32[]{:S(2)}, u32[]{:S(2)}) collective-permute-start(f32[2,16,2,8,512]{4,3,2,1,0:T(8,128)S(1)} %get-tuple-element.85.refs_0_), channel_id=1, source_target_pairs={{0,16},{12,28},{4,8},{8,4},{16,0},{28,12},{20,24},{24,20},{1,17},{... | collective-permute-start | bytes 3145736 | tf_op jit(solution)/shard_map/ppermute | solution.py:643
  42.4 5.9 %collective-permute-start.11 = (f32[5,8,256]{2,1,0:T(8,128)S(1)}, f32[5,8,256]{2,1,0:T(8,128)S(1)}, u32[]{:S(2)}, u32[]{:S(2)}) collective-permute-start(f32[5,8,256]{2,1,0:T(8,128)S(1)} %get-tuple-element.87.refs_0_), channel_id=1, source_target_pairs={{0,1},{1,2},{2,3},{3,0},{4,5},{5,6},{6,7},{7,4},{8,9},{9,10},{10,1... | collective-permute-start | bytes 122888 | tf_op jit(solution)/shard_map/ppermute | solution.py:651
  43.2 5.9 %collective-permute-start.12 = (f32[5,8,256]{2,1,0:T(8,128)S(1)}, f32[5,8,256]{2,1,0:T(8,128)S(1)}, u32[]{:S(2)}, u32[]{:S(2)}) collective-permute-start(f32[5,8,256]{2,1,0:T(8,128)S(1)} %get-tuple-element.87.refs_0_), channel_id=1, source_target_pairs={{0,2},{1,3},{2,0},{3,1},{4,6},{5,7},{6,4},{7,5},{8,10},{9,11},{10,... | collective-permute-start | bytes 122888 | tf_op jit(solution)/shard_map/ppermute | solution.py:651
  46.1 4.0 %collective-permute-start.13 = (f32[5,8,256]{2,1,0:T(8,128)S(1)}, f32[5,8,256]{2,1,0:T(8,128)S(1)}, u32[]{:S(2)}, u32[]{:S(2)}) collective-permute-start(f32[5,8,256]{2,1,0:T(8,128)S(1)} %get-tuple-element.87.refs_0_), channel_id=1, source_target_pairs={{0,3},{1,0},{2,1},{3,2},{4,7},{5,4},{6,5},{7,6},{8,11},{9,8},{10,9... | collective-permute-start | bytes 122888 | tf_op jit(solution)/shard_map/ppermute | solution.py:651
  50.7 8.3 %collective-permute-start.14 = (f32[6,2,256]{2,1,0:T(2,128)S(1)}, f32[6,2,256]{2,1,0:T(2,128)S(1)}, u32[]{:S(2)}, u32[]{:S(2)}) collective-permute-start(f32[6,2,256]{2,1,0:T(2,128)S(1)} %get-tuple-element.88), channel_id=1, source_target_pairs={{0,16},{12,28},{4,8},{8,4},{16,0},{28,12},{20,24},{24,20},{1,17},{... | collective-permute-start | bytes 36872 | tf_op jit(solution)/shard_map/ppermute | solution.py:643
  51.8 7.2 %collective-permute-start.15 = (f32[6,2,256]{2,1,0:T(2,128)S(1)}, f32[6,2,256]{2,1,0:T(2,128)S(1)}, u32[]{:S(2)}, u32[]{:S(2)}) collective-permute-start(f32[6,2,256]{2,1,0:T(2,128)S(1)} %get-tuple-element.89), channel_id=1, source_target_pairs={{0,4},{4,0},{8,12},{12,8},{1,5},{5,1},{9,13},{13,9},{2,6},{6,2},{1... | collective-permute-start | bytes 36872 | tf_op jit(solution)/shard_map/ppermute | solution.py:644
  61.8 6.3 %collective-permute-start.16 = (f32[5,8,256]{2,1,0:T(8,128)S(1)}, f32[5,8,256]{2,1,0:T(8,128)S(1)}, u32[]{:S(2)}, u32[]{:S(2)}) collective-permute-start(f32[5,8,256]{2,1,0:T(8,128)S(1)} %get-tuple-element.102.refs_0_), channel_id=1, source_target_pairs={{0,1},{1,2},{2,3},{3,0},{4,5},{5,6},{6,7},{7,4},{8,9},{9,10},{10,1... | collective-permute-start | bytes 122888 | tf_op jit(solution)/shard_map/ppermute | solution.py:651
  62.5 6.8 %collective-permute-start.17 = (f32[5,8,256]{2,1,0:T(8,128)S(1)}, f32[5,8,256]{2,1,0:T(8,128)S(1)}, u32[]{:S(2)}, u32[]{:S(2)}) collective-permute-start(f32[5,8,256]{2,1,0:T(8,128)S(1)} %get-tuple-element.102.refs_0_), channel_id=1, source_target_pairs={{0,2},{1,3},{2,0},{3,1},{4,6},{5,7},{6,4},{7,5},{8,10},{9,11},{10,... | collective-permute-start | bytes 122888 | tf_op jit(solution)/shard_map/ppermute | solution.py:651
  64.6 4.6 %collective-permute-start.18 = (f32[5,8,256]{2,1,0:T(8,128)S(1)}, f32[5,8,256]{2,1,0:T(8,128)S(1)}, u32[]{:S(2)}, u32[]{:S(2)}) collective-permute-start(f32[5,8,256]{2,1,0:T(8,128)S(1)} %get-tuple-element.102.refs_0_), channel_id=1, source_target_pairs={{0,3},{1,0},{2,1},{3,2},{4,7},{5,4},{6,5},{7,6},{8,11},{9,8},{10,9... | collective-permute-start | bytes 122888 | tf_op jit(solution)/shard_map/ppermute | solution.py:651

commit v10 on v8

--- a/solution.py
+++ b/solution.py
@@ -131,7 +131,7 @@
     return high, middle, low
 
 
-def spread_features(params, wide, tall, rows):
+def spread_features(params, wide, tall, rows, first=0):
     alpha, beta_x, beta_y, beta_z, gamma, keep = params
     alpha = jnp.where(gamma == 0.0, -10000.0, alpha)
     zero = jnp.zeros_like(alpha)
@@ -140,10 +140,13 @@
         columns.extend(three_parts(value))
     columns.extend([zero] * (FEATURES - len(columns)))
     for k, value in enumerate(columns):
-        for r in range(rows):
-            wide[r, k : k + 1, :] = value[r : r + 1]
+        for half in range(2):
+            part = value[:, half * LANES : (half + 1) * LANES]
+            wide[half, pl.ds(k, rows, stride=FEATURES), :] = part
     for r in range(rows):
-        tall[r] = wide[r].T.astype(BF16)
+        for half in range(2):
+            block = wide[half, r * FEATURES : (r + 1) * FEATURES, :]
+            tall[first + r, half * LANES : (half + 1) * LANES, :] = block.T.astype(BF16)
 
 
 def relax_group(group, tall, table, factor, kept):
@@ -240,8 +243,8 @@
     lax.fori_loop(0, staged.shape[0] * count, one, 0, unroll=4)
 
 
-def load_kernel(order_in, codes_in, state, cross, inside, codes, table, factor, weights, coef,
-                order, raw, flat, near_cross, near_inside, cross_sems, inside_sems, more_sems):
+def load_kernel(order_in, codes_in, state, cross, near_inside, codes, table, factor, weights, coef,
+                order, raw, flat, near_cross, cross_sems, inside_sems, more_sems):
     rows, width = state.shape[0], order.shape[-1]
     mirrored = lax.axis_index("gx") % 2
     more = [
@@ -308,7 +311,6 @@
     unstage(near_cross, cross)
     for copy in copies[half:]:
         copy.wait()
-    unstage(near_inside, inside)
 
 
 def inner_kernel(relax, rows, *refs):
@@ -326,13 +328,15 @@
             ]
             relax_group(group, tall, table, factor, kept)
     else:
-        (cross, inside, state, coef_ref, weights, middle, out, e_cross, e_in, sums,
+        (cross, near_inside, state, coef_ref, weights, middle, inside, out, e_cross, e_in, sums,
          near, sems) = refs
         mirrored = lax.axis_index("gx") % 2
         copies = row_copies(mirrored, state, near, 2, sems)
         for copy in copies:
             copy.start()
     yz_rows(cross, e_cross, True, 2, coef_ref)
+    if not relax:
+        unstage(near_inside, inside)
     yz_rows(inside, e_in, True, 2, coef_ref)
     if not relax:
         for copy in copies:
@@ -409,7 +413,8 @@
     lax.fori_loop(0, middle.shape[-1] // LANES * 16, one, 0, unroll=4)
 
 
-def first_in_kernel(high, inside, e_in, middle, coef_ref, weights, out, sums):
+def first_in_kernel(near_high, inside, e_in, middle, coef_ref, weights, out, sums, high):
+    unstage(near_high, high)
     each_place(middle, coef_ref, lambda *at: in_x(high, inside, middle, e_in, out, *at))
     row_moments([(out.at[r], r) for r in range(2)], weights, sums)
 
@@ -452,12 +457,12 @@
 def final_kernel(rows, m_cross, m_mid, m_in, params, table, factor, out,
                  wide, tall, kept, staged, sems):
     mirrored = lax.axis_index("gx") % 2
-    spread_features([params[k] for k in range(6)], wide, tall, rows)
     moved = [m_cross.at[r] for r in range(2)] + [m_mid.at[r] for r in range(rows - 4)]
     moved += [m_in.at[r] for r in range(2)]
     copies = []
     for first in range(0, rows, 2):
         near = staged.at[pl.ds(first, 2)]
+        spread_features([params[k, first : first + 2] for k in range(6)], wide, tall, 2, first)
         group = []
         for r in range(2):
 
@@ -496,7 +501,7 @@
 
     def feature_scratch(n):
         return [
-            pltpu.VMEM((n, FEATURES, cells), F32),
+            pltpu.VMEM((2, n * FEATURES, LANES), F32),
             pltpu.VMEM((n, cells, FEATURES), BF16),
             pltpu.VMEM((4, count_y, 2, SUB, LANES), F32),
         ]
@@ -520,7 +525,7 @@
             out_specs=[vmem] * 7,
             out_shape=[
                 slab(2),
-                slab(2),
+                jax.ShapeDtypeStruct((2, count_y, chunks, count_z, LANES), F32),
                 jax.ShapeDtypeStruct((rows, cells), jnp.int32),
                 jax.ShapeDtypeStruct((FEATURES, width), BF16),
                 jax.ShapeDtypeStruct((FEATURES, LANES), BF16),
@@ -532,7 +537,6 @@
                 pltpu.VMEM((rows, count_y, count_z), jnp.int32),
                 pltpu.VMEM((rows, cells), jnp.int32),
                 staging(2)[0],
-                staging(2)[0],
                 staging(2)[1],
                 staging(2)[1],
                 pltpu.SemaphoreType.DMA((2,)),
@@ -550,7 +554,7 @@
             scratch = feature_scratch(rows)
             args = (*state, params, table, factor, coef, weights)
         else:
-            out_shape = [slab(rows - 4)] + out_shape
+            out_shape = [slab(rows - 4), slab(2)] + out_shape
             scratch = staging(rows - 4)
             args = (*state, coef, weights)
         return pl.pallas_call(
@@ -572,6 +576,7 @@
             in_specs=[vmem] * 6,
             out_specs=[vmem] * 2,
             out_shape=[slab(2), edge_sums],
+            scratch_shapes=[slab_scratch(2)],
             compiler_params=limits(LIMIT_MIB),
             name="first_in",
         )(*args, middle, coef, weights)
@@ -644,9 +649,11 @@
             parts.append(lax.ppermute(part, "vert", pairs))
         return parts
 
-    cross, inside, codes, table, factor, weights, coef = load()
-    halos = exchange(cross, inside)
-    middle, m_mid, e_cross, e_in, sums = inner(False, (cross, inside, in_hbm(distribution)), None)
+    cross, near_inside, codes, table, factor, weights, coef = load()
+    halos = exchange(cross, near_inside)
+    middle, inside, m_mid, e_cross, e_in, sums = inner(
+        False, (cross, near_inside, in_hbm(distribution)), None
+    )
     m_in, in_sums = first_in(halos[1], inside, e_in)
     m_cross, sums = first_cross(halos[0], cross, e_cross, middle, coef, weights, sums, in_sums)
     m_cross, m_in, sums = lax.optimization_barrier((m_cross, m_in, sums))

time: 72.3 us -> 72.5 us (level)
  Pallas kernels: 34.7 us -> 35.5 us
  transfers between devices with their start and end apart: 19 -> 19, of which waited for: 8 -> 8; matrix products, arithmetic and copies ran while one was open for 0% -> 0% of each run, Pallas kernels for 30% -> 31%
where the time goes in v10:
time: 72.5 us; the launch traced here: 72.4 us
  Pallas kernels  35.5 us (49%)
  starting transfers between devices  22.1 us (30%)
  waiting for transfers between devices  14 us (19%)
  between operations  0.77 us (1%)
    pallas_call x3, Pallas kernels, inner(): pl.pallas_call(functools.partial(inner_kernel, relax, rows), in_specs=[vm...  19.8 us
    ppermute x9, starting transfers between devices, gather(): parts.append(lax.ppermute(part, 'vert', pairs))  13.3 us
    ppermute x9, waiting for transfers between devices, gather(): parts.append(lax.ppermute(part, 'vert', pairs))  9.4 us
    ppermute x5, starting transfers between devices, exchange(): lax.ppermute(cross, ('groups', 'gx'), across)  7.81 us
    pallas_call x2, Pallas kernels, edge(): pl.pallas_call(functools.partial(edge_kernel, rows, line), in_specs=[vmem...  5.84 us
    ppermute x5, waiting for transfers between devices, exchange(): lax.ppermute(cross, ('groups', 'gx'), across)  4.58 us
    pallas_call x1, Pallas kernels, final(): pl.pallas_call(functools.partial(final_kernel, rows), in_specs=[vmem] * 6...  3.12 us
    pallas_call x3, Pallas kernels, cell_params(): pl.pallas_call(functools.partial(param_kernel, total, len(parts)), in_spe...  1.92 us
  transfers between devices with their start and end apart: 19, of which 8 were waited for; matrix products, arithmetic and copies ran while one was open for 0% of the time, Pallas kernels for 31%

profile of v10, /device:TPU:0, one launch (start us, length us, event | category | flops | bytes accessed | tf_op | source)
XLA Modules:
  0.0 72.4 jit_solution(16047156697201637695)
XLA Ops:
  0.0 1.8 %load_edges.1 = (f32[2,16,2,8,512]{4,3,2,1,0:T(8,128)S(1)}, f32[2,16,4,16,128]{4,3,2,1,0:T(8,128)S(1)}, s32[8,256]{1,0:T(8,128)S(1)}, bf16[32,512]{1,0:T(8,128)(...) custom-call(s32[1,512]{1,0:T(1,128)} %bitcast.1, ...), custom_call_target="tpu_custom_call" | custom-call | tf_op jit(solution)/shard_map/load_edges/pallas_call | solution.py:522
  1.8 0.5 collective-permute-start.1
  2.4 2.6 %collective-permute-start = (f32[2,16,2,8,512]{4,3,2,1,0:T(8,128)S(1)}, f32[2,16,2,8,512]{4,3,2,1,0:T(8,128)S(1)}, u32[]{:S(2)}, u32[]{:S(2)}) collective-permute-start(f32[2,16,2,8,512]{4,3,2,1,0:T(8,128)S(1)} %get-tuple-element.51.refs_0_.cross), channel_id=1, source_target_pairs={{0,16},{12,28},{4,8},{8,4},{16,0},{28,12},{20,24},{24,20},{1,17},{... | collective-permute-start | bytes 3145736 | tf_op jit(solution)/shard_map/ppermute | solution.py:641
  5.0 6.6 %inner_first.1 = (f32[4,16,2,8,512]{4,3,2,1,0:T(8,128)S(1)}, f32[2,16,2,8,512]{4,3,2,1,0:T(8,128)S(1)}, f32[4,16,2,8,512]{4,3,2,1,0:T(8,128)S(1)}, f32[2,16,2,8,...) custom-call(f32[2,16,2,8,512]{4,3,2,1,0:T(8,128)S(1)} %get-tuple-element.51.refs_0_.cross, ...), custom_call_target="tpu_custom_call" | custom-call | tf_op jit(solution)/shard_map/inner_first/pallas_call | solution.py:560
  11.5 0.0 collective-permute-done.1.near_high
  11.5 1.6 %first_in.1 = (f32[2,16,2,8,512]{4,3,2,1,0:T(8,128)S(1)}, f32[5,2,256]{2,1,0:T(2,128)S(1)}) custom-call(f32[2,16,4,16,128]{4,3,2,1,0:T(8,128)S(1)} %collective-permute-done.1.near_high, f32[2,16,2,8,512]{4,3,2,1,0:T(8,128)S(1)} %get-tuple-element.58.inside, f32[2,16,2,8,512]{4,3,2,1,0:T(8,128)S(1)} %get-tuple-element.59.e_in, ...), custom_call_target="tpu_custom_call" | custom-call | tf_op jit(solution)/shard_map/first_in/pallas_call | solution.py:574
  13.2 4.6 %collective-permute-done.low = f32[2,16,2,8,512]{4,3,2,1,0:T(8,128)S(1)} collective-permute-done((f32[2,16,2,8,512]{4,3,2,1,0:T(8,128)S(1)}, f32[2,16,2,8,512]{4,3,2,1,0:T(8,128)S(1)}, u32[]{:S(2)}, u32[]{:S(2)}) %collective-permute-start) | collective-permute-done | bytes 1048608 | tf_op jit(solution)/shard_map/ppermute | solution.py:641
  17.7 1.3 %first_cross.1 = (f32[2,16,2,8,512]{4,3,2,1,0:T(8,128)S(1)}, f32[5,8,256]{2,1,0:T(8,128)S(1)}) custom-call(f32[2,16,2,8,512]{4,3,2,1,0:T(8,128)S(1)} %collective-permute-done.low, f32[2,16,2,8,512]{4,3,2,1,0:T(8,128)S(1)} %get-tuple-element.51.refs_0_.cross, f32[2,16,2,8,512]{4,3,2,1,0:T(8,128)S(1)} %get-tuple-element.55.e_cross, ...), custom_call_target="tpu_custom_call" | custom-call | tf_op jit(solution)/shard_map/first_cross/pallas_call | solution.py:585
  19.1 2.0 %collective-permute-start.2 = (f32[2,16,2,8,512]{4,3,2,1,0:T(8,128)S(1)}, f32[2,16,2,8,512]{4,3,2,1,0:T(8,128)S(1)}, u32[]{:S(2)}, u32[]{:S(2)}) collective-permute-start(f32[2,16,2,8,512]{4,3,2,1,0:T(8,128)S(1)} %get-tuple-element.64.refs_0_), channel_id=1, source_target_pairs={{0,16},{12,28},{4,8},{8,4},{16,0},{28,12},{20,24},{24,20},{1,17},{... | collective-permute-start | bytes 3145736 | tf_op jit(solution)/shard_map/ppermute | solution.py:641
  21.1 0.0 collective-permute-start.3
  21.1 1.6 %collective-permute-start.4 = (f32[5,8,256]{2,1,0:T(8,128)S(1)}, f32[5,8,256]{2,1,0:T(8,128)S(1)}, u32[]{:S(2)}, u32[]{:S(2)}) collective-permute-start(f32[5,8,256]{2,1,0:T(8,128)S(1)} %get-tuple-element.66.refs_0_), channel_id=1, source_target_pairs={{0,1},{1,2},{2,3},{3,0},{4,5},{5,6},{6,7},{7,4},{8,9},{9,10},{10,1... | collective-permute-start | bytes 122888 | tf_op jit(solution)/shard_map/ppermute | solution.py:649
  22.7 2.6 %collective-permute-start.5 = (f32[5,8,256]{2,1,0:T(8,128)S(1)}, f32[5,8,256]{2,1,0:T(8,128)S(1)}, u32[]{:S(2)}, u32[]{:S(2)}) collective-permute-start(f32[5,8,256]{2,1,0:T(8,128)S(1)} %get-tuple-element.66.refs_0_), channel_id=1, source_target_pairs={{0,2},{1,3},{2,0},{3,1},{4,6},{5,7},{6,4},{7,5},{8,10},{9,11},{10,... | collective-permute-start | bytes 122888 | tf_op jit(solution)/shard_map/ppermute | solution.py:649
  25.3 1.3 %collective-permute-start.6 = (f32[5,8,256]{2,1,0:T(8,128)S(1)}, f32[5,8,256]{2,1,0:T(8,128)S(1)}, u32[]{:S(2)}, u32[]{:S(2)}) collective-permute-start(f32[5,8,256]{2,1,0:T(8,128)S(1)} %get-tuple-element.66.refs_0_), channel_id=1, source_target_pairs={{0,3},{1,0},{2,1},{3,2},{4,7},{5,4},{6,5},{7,6},{8,11},{9,8},{10,9... | collective-permute-start | bytes 122888 | tf_op jit(solution)/shard_map/ppermute | solution.py:649
  27.3 0.0 collective-permute-done.4.refs_1_
  27.3 1.6 %collective-permute-done.5.refs_2_ = f32[5,8,256]{2,1,0:T(8,128)S(1)} collective-permute-done((f32[5,8,256]{2,1,0:T(8,128)S(1)}, f32[5,8,256]{2,1,0:T(8,128)S(1)}, u32[]{:S(2)}, u32[]{:S(2)}) %collective-permute-start.5) | collective-permute-done | bytes 40992 | tf_op jit(solution)/shard_map/ppermute | solution.py:649
  28.9 0.4 collective-permute-done.6.refs_3_
  29.3 0.6 cell_params.3
  30.0 1.1 %collective-permute-start.7 = (f32[6,2,256]{2,1,0:T(2,128)S(1)}, f32[6,2,256]{2,1,0:T(2,128)S(1)}, u32[]{:S(2)}, u32[]{:S(2)}) collective-permute-start(f32[6,2,256]{2,1,0:T(2,128)S(1)} %get-tuple-element.68), channel_id=1, source_target_pairs={{0,16},{12,28},{4,8},{8,4},{16,0},{28,12},{20,24},{24,20},{1,17},{... | collective-permute-start | bytes 36872 | tf_op jit(solution)/shard_map/ppermute | solution.py:641
  31.0 0.0 collective-permute-start.8
  31.0 6.6 %inner_relax.2 = (f32[2,16,2,8,512]{4,3,2,1,0:T(8,128)S(1)}, f32[4,16,2,8,512]{4,3,2,1,0:T(8,128)S(1)}, f32[2,16,2,8,512]{4,3,2,1,0:T(8,128)S(1)}, f32[4,16,2,8,...) custom-call(f32[2,16,2,8,512]{4,3,2,1,0:T(8,128)S(1)} %get-tuple-ele, ...), custom_call_target="tpu_custom_call" | custom-call | tf_op jit(solution)/shard_map/inner_relax/pallas_call | solution.py:560
  37.6 0.0 collective-permute-done.7.p_cross
  37.7 0.0 collective-permute-done.8.p_in
  37.7 0.0 collective-permute-done.2.h_cross
  37.7 0.0 collective-permute-done.3.h_in
  37.7 2.9 %edge_relax.2 = (f32[2,16,2,8,512]{4,3,2,1,0:T(8,128)S(1)}, f32[2,16,2,8,512]{4,3,2,1,0:T(8,128)S(1)}, f32[5,8,256]{2,1,0:T(8,128)S(1)}) custom-call(f32[2,16,2,8,512]{4,3,2,1,0:T(8,128)S(1)} %collective-permute-done.2.h_cross, f32[2,16,2,8,512]{4,3,2,1,0:T(8,128)S(1)} %collective-permute-done.3.h_in, f32[6,2,256]{2,1,0:T(2,128)S(1)} %collective-permute-done.7.p_cross, ...), custom_call_target="tpu_custom_call" | custom-call | tf_op jit(solution)/shard_map/edge_relax/pallas_call | solution.py:596
  40.6 0.5 collective-permute-start.10
  41.1 1.0 %collective-permute-start.9 = (f32[2,16,2,8,512]{4,3,2,1,0:T(8,128)S(1)}, f32[2,16,2,8,512]{4,3,2,1,0:T(8,128)S(1)}, u32[]{:S(2)}, u32[]{:S(2)}) collective-permute-start(f32[2,16,2,8,512]{4,3,2,1,0:T(8,128)S(1)} %get-tuple-element.80.refs_0_), channel_id=1, source_target_pairs={{0,16},{12,28},{4,8},{8,4},{16,0},{28,12},{20,24},{24,20},{1,17},{... | collective-permute-start | bytes 3145736 | tf_op jit(solution)/shard_map/ppermute | solution.py:641
  42.2 0.8 %collective-permute-start.11 = (f32[5,8,256]{2,1,0:T(8,128)S(1)}, f32[5,8,256]{2,1,0:T(8,128)S(1)}, u32[]{:S(2)}, u32[]{:S(2)}) collective-permute-start(f32[5,8,256]{2,1,0:T(8,128)S(1)} %get-tuple-element.82.refs_0_), channel_id=1, source_target_pairs={{0,1},{1,2},{2,3},{3,0},{4,5},{5,6},{6,7},{7,4},{8,9},{9,10},{10,1... | collective-permute-start | bytes 122888 | tf_op jit(solution)/shard_map/ppermute | solution.py:649
  43.0 2.8 %collective-permute-start.12 = (f32[5,8,256]{2,1,0:T(8,128)S(1)}, f32[5,8,256]{2,1,0:T(8,128)S(1)}, u32[]{:S(2)}, u32[]{:S(2)}) collective-permute-start(f32[5,8,256]{2,1,0:T(8,128)S(1)} %get-tuple-element.82.refs_0_), channel_id=1, source_target_pairs={{0,2},{1,3},{2,0},{3,1},{4,6},{5,7},{6,4},{7,5},{8,10},{9,11},{10,... | collective-permute-start | bytes 122888 | tf_op jit(solution)/shard_map/ppermute | solution.py:649
  45.8 0.2 collective-permute-start.13
  46.1 2.0 %collective-permute-done.11.refs_1_ = f32[5,8,256]{2,1,0:T(8,128)S(1)} collective-permute-done((f32[5,8,256]{2,1,0:T(8,128)S(1)}, f32[5,8,256]{2,1,0:T(8,128)S(1)}, u32[]{:S(2)}, u32[]{:S(2)}) %collective-permute-start.11) | collective-permute-done | bytes 40992 | tf_op jit(solution)/shard_map/ppermute | solution.py:649
  48.1 0.8 %collective-permute-done.12.refs_2_ = f32[5,8,256]{2,1,0:T(8,128)S(1)} collective-permute-done((f32[5,8,256]{2,1,0:T(8,128)S(1)}, f32[5,8,256]{2,1,0:T(8,128)S(1)}, u32[]{:S(2)}, u32[]{:S(2)}) %collective-permute-start.12) | collective-permute-done | bytes 40992 | tf_op jit(solution)/shard_map/ppermute | solution.py:649
  48.9 1.0 %collective-permute-done.13.refs_3_ = f32[5,8,256]{2,1,0:T(8,128)S(1)} collective-permute-done((f32[5,8,256]{2,1,0:T(8,128)S(1)}, f32[5,8,256]{2,1,0:T(8,128)S(1)}, u32[]{:S(2)}, u32[]{:S(2)}) %collective-permute-start.13) | collective-permute-done | bytes 40992 | tf_op jit(solution)/shard_map/ppermute | solution.py:649
  49.8 0.6 cell_params.4
  50.5 1.1 %collective-permute-start.14 = (f32[6,2,256]{2,1,0:T(2,128)S(1)}, f32[6,2,256]{2,1,0:T(2,128)S(1)}, u32[]{:S(2)}, u32[]{:S(2)}) collective-permute-start(f32[6,2,256]{2,1,0:T(2,128)S(1)} %get-tuple-element.83), channel_id=1, source_target_pairs={{0,16},{12,28},{4,8},{8,4},{16,0},{28,12},{20,24},{24,20},{1,17},{... | collective-permute-start | bytes 36872 | tf_op jit(solution)/shard_map/ppermute | solution.py:641
  51.6 0.0 collective-permute-start.15
  51.6 6.6 %inner_relax.3 = (f32[2,16,2,8,512]{4,3,2,1,0:T(8,128)S(1)}, f32[4,16,2,8,512]{4,3,2,1,0:T(8,128)S(1)}, f32[2,16,2,8,512]{4,3,2,1,0:T(8,128)S(1)}, f32[4,16,2,8,...) custom-call(f32[2,16,2,8,512]{4,3,2,1,0:T(8,128)S(1)} %get-tuple-ele, ...), custom_call_target="tpu_custom_call" | custom-call | tf_op jit(solution)/shard_map/inner_relax/pallas_call | solution.py:560
  58.2 0.0 collective-permute-done.14.p_cross
  58.2 0.0 collective-permute-done.15.p_in
  58.2 0.0 collective-permute-done.9.h_cross
  58.2 2.9 %edge_relax.3 = (f32[2,16,2,8,512]{4,3,2,1,0:T(8,128)S(1)}, f32[2,16,2,8,512]{4,3,2,1,0:T(8,128)S(1)}, f32[5,8,256]{2,1,0:T(8,128)S(1)}) custom-call(f32[2,16,2,8,512]{4,3,2,1,0:T(8,128)S(1)} %collective-permute-done.9.h_cross, f32[2,16,2,8,512]{4,3,2,1,0:T(8,128)S(1)} %collective-permute-done.10.h_in, f32[6,2,256]{2,1,0:T(2,128)S(1)} %collective-permute-done.14.p_cross, ...), custom_call_target="tpu_custom_call" | custom-call | tf_op jit(solution)/shard_map/edge_relax/pallas_call | solution.py:596
  61.2 0.7 collective-permute-start.16
  61.9 2.1 %collective-permute-start.17 = (f32[5,8,256]{2,1,0:T(8,128)S(1)}, f32[5,8,256]{2,1,0:T(8,128)S(1)}, u32[]{:S(2)}, u32[]{:S(2)}) collective-permute-start(f32[5,8,256]{2,1,0:T(8,128)S(1)} %get-tuple-element.96.refs_0_), channel_id=1, source_target_pairs={{0,2},{1,3},{2,0},{3,1},{4,6},{5,7},{6,4},{7,5},{8,10},{9,11},{10,... | collective-permute-start | bytes 122888 | tf_op jit(solution)/shard_map/ppermute | solution.py:649
  64.0 1.0 %collective-permute-start.18 = (f32[5,8,256]{2,1,0:T(8,128)S(1)}, f32[5,8,256]{2,1,0:T(8,128)S(1)}, u32[]{:S(2)}, u32[]{:S(2)}) collective-permute-start(f32[5,8,256]{2,1,0:T(8,128)S(1)} %get-tuple-element.96.refs_0_), channel_id=1, source_target_pairs={{0,3},{1,0},{2,1},{3,2},{4,7},{5,4},{6,5},{7,6},{8,11},{9,8},{10,9... | collective-permute-start | bytes 122888 | tf_op jit(solution)/shard_map/ppermute | solution.py:649
  65.0 2.4 %collective-permute-done.16.refs_1_ = f32[5,8,256]{2,1,0:T(8,128)S(1)} collective-permute-done((f32[5,8,256]{2,1,0:T(8,128)S(1)}, f32[5,8,256]{2,1,0:T(8,128)S(1)}, u32[]{:S(2)}, u32[]{:S(2)}) %collective-permute-start.16) | collective-permute-done | bytes 40992 | tf_op jit(solution)/shard_map/ppermute | solution.py:649
  67.4 1.2 %collective-permute-done.17.refs_2_ = f32[5,8,256]{2,1,0:T(8,128)S(1)} collective-permute-done((f32[5,8,256]{2,1,0:T(8,128)S(1)}, f32[5,8,256]{2,1,0:T(8,128)S(1)}, u32[]{:S(2)}, u32[]{:S(2)}) %collective-permute-start.17) | collective-permute-done | bytes 40992 | tf_op jit(solution)/shard_map/ppermute | solution.py:649
  68.6 0.6 cell_params.5.params
  69.3 3.1 %final_relax.1 = f32[8,16,16,512]{3,2,1,0:T(8,128)} custom-call(f32[2,16,2,8,512]{4,3,2,1,0:T(8,128)S(1)} %get-tuple-element.93.m_cross, f32[4,16,2,8,512]{4,3,2,1,0:T(8,128)S(1)} %get-tuple-element.94.m_mid, f32[2,16,2,8,512]{4,3,2,1,0:T(8,128)S(1)} %get-tuple-element.95.m_in, f32[6,8,256]{2,1,0:T(8,128)S(1)} %cell_params.5.params, ...), custom_call_target="tpu_custom_call" | custom-call | tf_op jit(solution)/shard_map/final_relax/pallas_call | solution.py:617
  (4 shorter events, 0.0 us)
Async XLA Ops:
  1.8 9.7 %collective-permute-start.1 = (f32[2,16,4,16,128]{4,3,2,1,0:T(8,128)S(1)}, f32[2,16,4,16,128]{4,3,2,1,0:T(8,128)S(1)}, u32[]{:S(2)}, u32[]{:S(2)}) collective-permute-start(f32[2,16,4,16,128]{4,3,2,1,0:T(8,128)S(1)} %get-tuple-element.52.refs_1_), channel_id=1, source_target_pairs={{0,4},{4,0},{8,12},{12,8},{1,5},{5,1},{9,13},{13,9},{2,6},{6,2},{1... | collective-permute-start | bytes 3145736 | tf_op jit(solution)/shard_map/ppermute | solution.py:642
  2.4 15.4 %collective-permute-start = (f32[2,16,2,8,512]{4,3,2,1,0:T(8,128)S(1)}, f32[2,16,2,8,512]{4,3,2,1,0:T(8,128)S(1)}, u32[]{:S(2)}, u32[]{:S(2)}) collective-permute-start(f32[2,16,2,8,512]{4,3,2,1,0:T(8,128)S(1)} %get-tuple-element.51.refs_0_.cross), channel_id=1, source_target_pairs={{0,16},{12,28},{4,8},{8,4},{16,0},{28,12},{20,24},{24,20},{1,17},{... | collective-permute-start | bytes 3145736 | tf_op jit(solution)/shard_map/ppermute | solution.py:641
  17.7 11.6 %copy-start = (f32[4]{0:T(128)S(1)}, f32[4]{0:T(128)}, u32[]{:S(2)}) copy-start(f32[4]{0:T(128)} %refs_6_.5) | copy-start | bytes 52
  19.1 18.6 %collective-permute-start.2 = (f32[2,16,2,8,512]{4,3,2,1,0:T(8,128)S(1)}, f32[2,16,2,8,512]{4,3,2,1,0:T(8,128)S(1)}, u32[]{:S(2)}, u32[]{:S(2)}) collective-permute-start(f32[2,16,2,8,512]{4,3,2,1,0:T(8,128)S(1)} %get-tuple-element.64.refs_0_), channel_id=1, source_target_pairs={{0,16},{12,28},{4,8},{8,4},{16,0},{28,12},{20,24},{24,20},{1,17},{... | collective-permute-start | bytes 3145736 | tf_op jit(solution)/shard_map/ppermute | solution.py:641
  21.1 16.6 %collective-permute-start.3 = (f32[2,16,2,8,512]{4,3,2,1,0:T(8,128)S(1)}, f32[2,16,2,8,512]{4,3,2,1,0:T(8,128)S(1)}, u32[]{:S(2)}, u32[]{:S(2)}) collective-permute-start(f32[2,16,2,8,512]{4,3,2,1,0:T(8,128)S(1)} %get-tuple-element.65.refs_2_), channel_id=1, source_target_pairs={{0,4},{4,0},{8,12},{12,8},{1,5},{5,1},{9,13},{13,9},{2,6},{6,2},{1... | collective-permute-start | bytes 3145736 | tf_op jit(solution)/shard_map/ppermute | solution.py:642
  21.1 6.2 %collective-permute-start.4 = (f32[5,8,256]{2,1,0:T(8,128)S(1)}, f32[5,8,256]{2,1,0:T(8,128)S(1)}, u32[]{:S(2)}, u32[]{:S(2)}) collective-permute-start(f32[5,8,256]{2,1,0:T(8,128)S(1)} %get-tuple-element.66.refs_0_), channel_id=1, source_target_pairs={{0,1},{1,2},{2,3},{3,0},{4,5},{5,6},{6,7},{7,4},{8,9},{9,10},{10,1... | collective-permute-start | bytes 122888 | tf_op jit(solution)/shard_map/ppermute | solution.py:649
  22.7 6.2 %collective-permute-start.5 = (f32[5,8,256]{2,1,0:T(8,128)S(1)}, f32[5,8,256]{2,1,0:T(8,128)S(1)}, u32[]{:S(2)}, u32[]{:S(2)}) collective-permute-start(f32[5,8,256]{2,1,0:T(8,128)S(1)} %get-tuple-element.66.refs_0_), channel_id=1, source_target_pairs={{0,2},{1,3},{2,0},{3,1},{4,6},{5,7},{6,4},{7,5},{8,10},{9,11},{10,... | collective-permute-start | bytes 122888 | tf_op jit(solution)/shard_map/ppermute | solution.py:649
  25.3 4.0 %collective-permute-start.6 = (f32[5,8,256]{2,1,0:T(8,128)S(1)}, f32[5,8,256]{2,1,0:T(8,128)S(1)}, u32[]{:S(2)}, u32[]{:S(2)}) collective-permute-start(f32[5,8,256]{2,1,0:T(8,128)S(1)} %get-tuple-element.66.refs_0_), channel_id=1, source_target_pairs={{0,3},{1,0},{2,1},{3,2},{4,7},{5,4},{6,5},{7,6},{8,11},{9,8},{10,9... | collective-permute-start | bytes 122888 | tf_op jit(solution)/shard_map/ppermute | solution.py:649
  30.0 7.7 %collective-permute-start.7 = (f32[6,2,256]{2,1,0:T(2,128)S(1)}, f32[6,2,256]{2,1,0:T(2,128)S(1)}, u32[]{:S(2)}, u32[]{:S(2)}) collective-permute-start(f32[6,2,256]{2,1,0:T(2,128)S(1)} %get-tuple-element.68), channel_id=1, source_target_pairs={{0,16},{12,28},{4,8},{8,4},{16,0},{28,12},{20,24},{24,20},{1,17},{... | collective-permute-start | bytes 36872 | tf_op jit(solution)/shard_map/ppermute | solution.py:641
  31.0 6.6 %collective-permute-start.8 = (f32[6,2,256]{2,1,0:T(2,128)S(1)}, f32[6,2,256]{2,1,0:T(2,128)S(1)}, u32[]{:S(2)}, u32[]{:S(2)}) collective-permute-start(f32[6,2,256]{2,1,0:T(2,128)S(1)} %get-tuple-element.69), channel_id=1, source_target_pairs={{0,4},{4,0},{8,12},{12,8},{1,5},{5,1},{9,13},{13,9},{2,6},{6,2},{1... | collective-permute-start | bytes 36872 | tf_op jit(solution)/shard_map/ppermute | solution.py:642
  40.6 17.6 %collective-permute-start.10 = (f32[2,16,2,8,512]{4,3,2,1,0:T(8,128)S(1)}, f32[2,16,2,8,512]{4,3,2,1,0:T(8,128)S(1)}, u32[]{:S(2)}, u32[]{:S(2)}) collective-permute-start(f32[2,16,2,8,512]{4,3,2,1,0:T(8,128)S(1)} %get-tuple-element.81.refs_2_), channel_id=1, source_target_pairs={{0,4},{4,0},{8,12},{12,8},{1,5},{5,1},{9,13},{13,9},{2,6},{6,2},{1... | collective-permute-start | bytes 3145736 | tf_op jit(solution)/shard_map/ppermute | solution.py:642
  41.1 17.1 %collective-permute-start.9 = (f32[2,16,2,8,512]{4,3,2,1,0:T(8,128)S(1)}, f32[2,16,2,8,512]{4,3,2,1,0:T(8,128)S(1)}, u32[]{:S(2)}, u32[]{:S(2)}) collective-permute-start(f32[2,16,2,8,512]{4,3,2,1,0:T(8,128)S(1)} %get-tuple-element.80.refs_0_), channel_id=1, source_target_pairs={{0,16},{12,28},{4,8},{8,4},{16,0},{28,12},{20,24},{24,20},{1,17},{... | collective-permute-start | bytes 3145736 | tf_op jit(solution)/shard_map/ppermute | solution.py:641
  42.2 5.9 %collective-permute-start.11 = (f32[5,8,256]{2,1,0:T(8,128)S(1)}, f32[5,8,256]{2,1,0:T(8,128)S(1)}, u32[]{:S(2)}, u32[]{:S(2)}) collective-permute-start(f32[5,8,256]{2,1,0:T(8,128)S(1)} %get-tuple-element.82.refs_0_), channel_id=1, source_target_pairs={{0,1},{1,2},{2,3},{3,0},{4,5},{5,6},{6,7},{7,4},{8,9},{9,10},{10,1... | collective-permute-start | bytes 122888 | tf_op jit(solution)/shard_map/ppermute | solution.py:649
  43.0 5.9 %collective-permute-start.12 = (f32[5,8,256]{2,1,0:T(8,128)S(1)}, f32[5,8,256]{2,1,0:T(8,128)S(1)}, u32[]{:S(2)}, u32[]{:S(2)}) collective-permute-start(f32[5,8,256]{2,1,0:T(8,128)S(1)} %get-tuple-element.82.refs_0_), channel_id=1, source_target_pairs={{0,2},{1,3},{2,0},{3,1},{4,6},{5,7},{6,4},{7,5},{8,10},{9,11},{10,... | collective-permute-start | bytes 122888 | tf_op jit(solution)/shard_map/ppermute | solution.py:649
  45.8 4.0 %collective-permute-start.13 = (f32[5,8,256]{2,1,0:T(8,128)S(1)}, f32[5,8,256]{2,1,0:T(8,128)S(1)}, u32[]{:S(2)}, u32[]{:S(2)}) collective-permute-start(f32[5,8,256]{2,1,0:T(8,128)S(1)} %get-tuple-element.82.refs_0_), channel_id=1, source_target_pairs={{0,3},{1,0},{2,1},{3,2},{4,7},{5,4},{6,5},{7,6},{8,11},{9,8},{10,9... | collective-permute-start | bytes 122888 | tf_op jit(solution)/shard_map/ppermute | solution.py:649
  50.5 7.7 %collective-permute-start.14 = (f32[6,2,256]{2,1,0:T(2,128)S(1)}, f32[6,2,256]{2,1,0:T(2,128)S(1)}, u32[]{:S(2)}, u32[]{:S(2)}) collective-permute-start(f32[6,2,256]{2,1,0:T(2,128)S(1)} %get-tuple-element.83), channel_id=1, source_target_pairs={{0,16},{12,28},{4,8},{8,4},{16,0},{28,12},{20,24},{24,20},{1,17},{... | collective-permute-start | bytes 36872 | tf_op jit(solution)/shard_map/ppermute | solution.py:641
  51.6 6.6 %collective-permute-start.15 = (f32[6,2,256]{2,1,0:T(2,128)S(1)}, f32[6,2,256]{2,1,0:T(2,128)S(1)}, u32[]{:S(2)}, u32[]{:S(2)}) collective-permute-start(f32[6,2,256]{2,1,0:T(2,128)S(1)} %get-tuple-element.84), channel_id=1, source_target_pairs={{0,4},{4,0},{8,12},{12,8},{1,5},{5,1},{9,13},{13,9},{2,6},{6,2},{1... | collective-permute-start | bytes 36872 | tf_op jit(solution)/shard_map/ppermute | solution.py:642
  61.2 6.3 %collective-permute-start.16 = (f32[5,8,256]{2,1,0:T(8,128)S(1)}, f32[5,8,256]{2,1,0:T(8,128)S(1)}, u32[]{:S(2)}, u32[]{:S(2)}) collective-permute-start(f32[5,8,256]{2,1,0:T(8,128)S(1)} %get-tuple-element.96.refs_0_), channel_id=1, source_target_pairs={{0,1},{1,2},{2,3},{3,0},{4,5},{5,6},{6,7},{7,4},{8,9},{9,10},{10,1... | collective-permute-start | bytes 122888 | tf_op jit(solution)/shard_map/ppermute | solution.py:649
  61.9 6.8 %collective-permute-start.17 = (f32[5,8,256]{2,1,0:T(8,128)S(1)}, f32[5,8,256]{2,1,0:T(8,128)S(1)}, u32[]{:S(2)}, u32[]{:S(2)}) collective-permute-start(f32[5,8,256]{2,1,0:T(8,128)S(1)} %get-tuple-element.96.refs_0_), channel_id=1, source_target_pairs={{0,2},{1,3},{2,0},{3,1},{4,6},{5,7},{6,4},{7,5},{8,10},{9,11},{10,... | collective-permute-start | bytes 122888 | tf_op jit(solution)/shard_map/ppermute | solution.py:649
  64.0 4.6 %collective-permute-start.18 = (f32[5,8,256]{2,1,0:T(8,128)S(1)}, f32[5,8,256]{2,1,0:T(8,128)S(1)}, u32[]{:S(2)}, u32[]{:S(2)}) collective-permute-start(f32[5,8,256]{2,1,0:T(8,128)S(1)} %get-tuple-element.96.refs_0_), channel_id=1, source_target_pairs={{0,3},{1,0},{2,1},{3,2},{4,7},{5,4},{6,5},{7,6},{8,11},{9,8},{10,9... | collective-permute-start | bytes 122888 | tf_op jit(solution)/shard_map/ppermute | solution.py:649

commit v11 on v8

--- a/solution.py
+++ b/solution.py
@@ -107,7 +107,7 @@
         yz_row(source, out, fresh, row, lanes, coefs_of(coef_ref, lanes))
         return carry
 
-    lax.fori_loop(0, chunks * rows, one, 0, unroll=2)
+    lax.fori_loop(0, chunks * rows, one, 0, unroll=4)
 
 
 def row_moments(rows, weights, sums):
@@ -317,14 +317,9 @@
          cross, middle, inside, out, e_cross, e_in, sums, wide, tall, kept) = refs
         spread_features([params[k] for k in range(6)], wide, tall, rows)
         group = [(r, m_cross.at[r], into(cross.at[r])) for r in range(2)]
+        group += [(2 + r, m_mid.at[r], into(middle.at[r])) for r in range(rows - 4)]
         group += [(rows - 2 + r, m_in.at[r], into(inside.at[r])) for r in range(2)]
         relax_group(group, tall, table, factor, kept)
-        for first in range(0, rows - 4, 4):
-            group = [
-                (2 + r, m_mid.at[r], into(middle.at[r]))
-                for r in range(first, min(first + 4, rows - 4))
-            ]
-            relax_group(group, tall, table, factor, kept)
     else:
         (cross, inside, state, coef_ref, weights, middle, out, e_cross, e_in, sums,
          near, sems) = refs
@@ -361,7 +356,7 @@
             x_row(cells, list(range(2, rows - 2)), store, coef)
         return carry
 
-    lax.fori_loop(0, chunks * 16, along_x, 0, unroll=4)
+    lax.fori_loop(0, chunks * 16, along_x, 0, unroll=8)
     yz_rows(middle, out, False, inner, coef_ref)
     row_moments([(out.at[r], r) for r in range(inner)], weights, sums)
 
@@ -498,7 +493,7 @@
         return [
             pltpu.VMEM((n, FEATURES, cells), F32),
             pltpu.VMEM((n, cells, FEATURES), BF16),
-            pltpu.VMEM((4, count_y, 2, SUB, LANES), F32),
+            pltpu.VMEM((n, count_y, 2, SUB, LANES), F32),
         ]
 
     def staging(n):

time: 72.3 us -> 72.1 us (level)
  no operation moved by 1% of the time
where the time goes in v11:
time: 72.1 us; the launch traced here: 71.9 us
  Pallas kernels  34.1 us (47%)
  starting transfers between devices  22.1 us (31%)
  waiting for transfers between devices  14.8 us (21%)
  between operations  0.93 us (1%)
    pallas_call x3, Pallas kernels, inner(): pl.pallas_call(functools.partial(inner_kernel, relax, rows), in_specs=[vm...  18.8 us
    ppermute x9, starting transfers between devices, gather(): parts.append(lax.ppermute(part, 'vert', pairs))  13.3 us
    ppermute x9, waiting for transfers between devices, gather(): parts.append(lax.ppermute(part, 'vert', pairs))  9.41 us
    ppermute x5, starting transfers between devices, exchange(): lax.ppermute(cross, ('groups', 'gx'), across)  7.81 us
    pallas_call x2, Pallas kernels, edge(): pl.pallas_call(functools.partial(edge_kernel, rows, line), in_specs=[vmem...  5.81 us
    ppermute x5, waiting for transfers between devices, exchange(): lax.ppermute(cross, ('groups', 'gx'), across)  5.37 us
    pallas_call x1, Pallas kernels, final(): pl.pallas_call(functools.partial(final_kernel, rows), in_specs=[vmem] * 6...  2.81 us
    pallas_call x1, Pallas kernels, load(): pl.pallas_call(load_kernel, in_specs=[hbm] * 3, out_specs=[vmem] * 7, out...  2.11 us
  transfers between devices with their start and end apart: 19, of which 8 were waited for; matrix products, arithmetic and copies ran while one was open for 0% of the time, Pallas kernels for 30%

profile of v11, /device:TPU:0, one launch (start us, length us, event | category | flops | bytes accessed | tf_op | source)
XLA Modules:
  0.0 71.9 jit_solution(15075669227901084693)
XLA Ops:
  0.0 2.1 %load_edges.1 = (f32[2,16,2,8,512]{4,3,2,1,0:T(8,128)S(1)}, f32[2,16,2,8,512]{4,3,2,1,0:T(8,128)S(1)}, s32[8,256]{1,0:T(8,128)S(1)}, bf16[32,512]{1,0:T(8,128)(2...) custom-call(s32[1,512]{1,0:T(1,128)} %bitcast.1, ...), custom_call_target="tpu_custom_call" | custom-call | tf_op jit(solution)/shard_map/load_edges/pallas_call | solution.py:512
  2.1 0.5 collective-permute-start.1
  2.6 2.6 %collective-permute-start = (f32[2,16,2,8,512]{4,3,2,1,0:T(8,128)S(1)}, f32[2,16,2,8,512]{4,3,2,1,0:T(8,128)S(1)}, u32[]{:S(2)}, u32[]{:S(2)}) collective-permute-start(f32[2,16,2,8,512]{4,3,2,1,0:T(8,128)S(1)} %get-tuple-element.50.refs_0_.cross), channel_id=1, source_target_pairs={{0,16},{12,28},{4,8},{8,4},{16,0},{28,12},{20,24},{24,20},{1,17},{... | collective-permute-start | bytes 3145736 | tf_op jit(solution)/shard_map/ppermute | solution.py:631
  5.2 6.1 %inner_first.1 = (f32[4,16,2,8,512]{4,3,2,1,0:T(8,128)S(1)}, f32[4,16,2,8,512]{4,3,2,1,0:T(8,128)S(1)}, f32[2,16,2,8,512]{4,3,2,1,0:T(8,128)S(1)}, f32[2,16,2,8,512]{4,3,2,1,0:T(8,128)S(1)}, f32[5,4,256]{2,1,0:T(4,128)S(1)}) custom-call(f32[2,16,2,8,512]{4,3,2,1,0:T(8,128)S(1)} %get-tuple-element.50.refs_0_.cross, ...), custom_call_target="tpu_custom_call" | custom-call | tf_op jit(solution)/shard_map/inner_first/pallas_call | solution.py:551
  11.3 0.0 collective-permute-done.1.high
  11.3 1.3 %first_in.1 = (f32[2,16,2,8,512]{4,3,2,1,0:T(8,128)S(1)}, f32[5,2,256]{2,1,0:T(2,128)S(1)}) custom-call(f32[2,16,2,8,512]{4,3,2,1,0:T(8,128)S(1)} %collective-permute-done.1.high, f32[2,16,2,8,512]{4,3,2,1,0:T(8,128)S(1)} %get-tuple-element.51.refs_1_.inside, f32[2,16,2,8,512]{4,3,2,1,0:T(8,128)S(1)} %get-tuple-element.57.e_in, ...), custom_call_target="tpu_custom_call" | custom-call | tf_op jit(solution)/shard_map/first_in/pallas_call | solution.py:565
  12.7 5.3 %collective-permute-done.low = f32[2,16,2,8,512]{4,3,2,1,0:T(8,128)S(1)} collective-permute-done((f32[2,16,2,8,512]{4,3,2,1,0:T(8,128)S(1)}, f32[2,16,2,8,512]{4,3,2,1,0:T(8,128)S(1)}, u32[]{:S(2)}, u32[]{:S(2)}) %collective-permute-start) | collective-permute-done | bytes 1048608 | tf_op jit(solution)/shard_map/ppermute | solution.py:631
  18.0 1.4 %first_cross.1 = (f32[2,16,2,8,512]{4,3,2,1,0:T(8,128)S(1)}, f32[5,8,256]{2,1,0:T(8,128)S(1)}) custom-call(f32[2,16,2,8,512]{4,3,2,1,0:T(8,128)S(1)} %collective-permute-done.low, f32[2,16,2,8,512]{4,3,2,1,0:T(8,128)S(1)} %get-tuple-element.50.refs_0_.cross, f32[2,16,2,8,512]{4,3,2,1,0:T(8,128)S(1)} %get-tuple-element.54.e_cross, ...), custom_call_target="tpu_custom_call" | custom-call | tf_op jit(solution)/shard_map/first_cross/pallas_call | solution.py:575
  19.4 2.0 %collective-permute-start.2 = (f32[2,16,2,8,512]{4,3,2,1,0:T(8,128)S(1)}, f32[2,16,2,8,512]{4,3,2,1,0:T(8,128)S(1)}, u32[]{:S(2)}, u32[]{:S(2)}) collective-permute-start(f32[2,16,2,8,512]{4,3,2,1,0:T(8,128)S(1)} %get-tuple-element.62.refs_0_), channel_id=1, source_target_pairs={{0,16},{12,28},{4,8},{8,4},{16,0},{28,12},{20,24},{24,20},{1,17},{... | collective-permute-start | bytes 3145736 | tf_op jit(solution)/shard_map/ppermute | solution.py:631
  21.4 0.0 collective-permute-start.3
  21.4 1.6 %collective-permute-start.4 = (f32[5,8,256]{2,1,0:T(8,128)S(1)}, f32[5,8,256]{2,1,0:T(8,128)S(1)}, u32[]{:S(2)}, u32[]{:S(2)}) collective-permute-start(f32[5,8,256]{2,1,0:T(8,128)S(1)} %get-tuple-element.64.refs_0_), channel_id=1, source_target_pairs={{0,1},{1,2},{2,3},{3,0},{4,5},{5,6},{6,7},{7,4},{8,9},{9,10},{10,1... | collective-permute-start | bytes 122888 | tf_op jit(solution)/shard_map/ppermute | solution.py:639
  23.0 2.6 %collective-permute-start.5 = (f32[5,8,256]{2,1,0:T(8,128)S(1)}, f32[5,8,256]{2,1,0:T(8,128)S(1)}, u32[]{:S(2)}, u32[]{:S(2)}) collective-permute-start(f32[5,8,256]{2,1,0:T(8,128)S(1)} %get-tuple-element.64.refs_0_), channel_id=1, source_target_pairs={{0,2},{1,3},{2,0},{3,1},{4,6},{5,7},{6,4},{7,5},{8,10},{9,11},{10,... | collective-permute-start | bytes 122888 | tf_op jit(solution)/shard_map/ppermute | solution.py:639
  25.6 1.3 %collective-permute-start.6 = (f32[5,8,256]{2,1,0:T(8,128)S(1)}, f32[5,8,256]{2,1,0:T(8,128)S(1)}, u32[]{:S(2)}, u32[]{:S(2)}) collective-permute-start(f32[5,8,256]{2,1,0:T(8,128)S(1)} %get-tuple-element.64.refs_0_), channel_id=1, source_target_pairs={{0,3},{1,0},{2,1},{3,2},{4,7},{5,4},{6,5},{7,6},{8,11},{9,8},{10,9... | collective-permute-start | bytes 122888 | tf_op jit(solution)/shard_map/ppermute | solution.py:639
  27.6 0.0 collective-permute-done.4.refs_1_
  27.6 1.6 %collective-permute-done.5.refs_2_ = f32[5,8,256]{2,1,0:T(8,128)S(1)} collective-permute-done((f32[5,8,256]{2,1,0:T(8,128)S(1)}, f32[5,8,256]{2,1,0:T(8,128)S(1)}, u32[]{:S(2)}, u32[]{:S(2)}) %collective-permute-start.5) | collective-permute-done | bytes 40992 | tf_op jit(solution)/shard_map/ppermute | solution.py:639
  29.2 0.4 collective-permute-done.6.refs_3_
  29.6 0.6 cell_params.3
  30.3 1.1 %collective-permute-start.7 = (f32[6,2,256]{2,1,0:T(2,128)S(1)}, f32[6,2,256]{2,1,0:T(2,128)S(1)}, u32[]{:S(2)}, u32[]{:S(2)}) collective-permute-start(f32[6,2,256]{2,1,0:T(2,128)S(1)} %get-tuple-element.66), channel_id=1, source_target_pairs={{0,16},{12,28},{4,8},{8,4},{16,0},{28,12},{20,24},{24,20},{1,17},{... | collective-permute-start | bytes 36872 | tf_op jit(solution)/shard_map/ppermute | solution.py:631
  31.3 0.0 collective-permute-start.8
  31.3 6.3 %inner_relax.2 = (f32[2,16,2,8,512]{4,3,2,1,0:T(8,128)S(1)}, f32[4,16,2,8,512]{4,3,2,1,0:T(8,128)S(1)}, f32[2,16,2,8,512]{4,3,2,1,0:T(8,128)S(1)}, f32[4,16,2,8,...) custom-call(f32[2,16,2,8,512]{4,3,2,1,0:T(8,128)S(1)} %get-tuple-ele, ...), custom_call_target="tpu_custom_call" | custom-call | tf_op jit(solution)/shard_map/inner_relax/pallas_call | solution.py:551
  37.7 0.0 collective-permute-done.7.p_cross
  37.7 0.0 collective-permute-done.8.p_in
  37.7 0.0 collective-permute-done.2.h_cross
  37.7 0.0 collective-permute-done.3.h_in
  37.7 2.9 %edge_relax.2 = (f32[2,16,2,8,512]{4,3,2,1,0:T(8,128)S(1)}, f32[2,16,2,8,512]{4,3,2,1,0:T(8,128)S(1)}, f32[5,8,256]{2,1,0:T(8,128)S(1)}) custom-call(f32[2,16,2,8,512]{4,3,2,1,0:T(8,128)S(1)} %collective-permute-done.2.h_cross, f32[2,16,2,8,512]{4,3,2,1,0:T(8,128)S(1)} %collective-permute-done.3.h_in, f32[6,2,256]{2,1,0:T(2,128)S(1)} %collective-permute-done.7.p_cross, ...), custom_call_target="tpu_custom_call" | custom-call | tf_op jit(solution)/shard_map/edge_relax/pallas_call | solution.py:586
  40.6 0.5 collective-permute-start.10
  41.1 1.0 %collective-permute-start.9 = (f32[2,16,2,8,512]{4,3,2,1,0:T(8,128)S(1)}, f32[2,16,2,8,512]{4,3,2,1,0:T(8,128)S(1)}, u32[]{:S(2)}, u32[]{:S(2)}) collective-permute-start(f32[2,16,2,8,512]{4,3,2,1,0:T(8,128)S(1)} %get-tuple-element.78.refs_0_), channel_id=1, source_target_pairs={{0,16},{12,28},{4,8},{8,4},{16,0},{28,12},{20,24},{24,20},{1,17},{... | collective-permute-start | bytes 3145736 | tf_op jit(solution)/shard_map/ppermute | solution.py:631
  42.2 0.8 %collective-permute-start.11 = (f32[5,8,256]{2,1,0:T(8,128)S(1)}, f32[5,8,256]{2,1,0:T(8,128)S(1)}, u32[]{:S(2)}, u32[]{:S(2)}) collective-permute-start(f32[5,8,256]{2,1,0:T(8,128)S(1)} %get-tuple-element.80.refs_0_), channel_id=1, source_target_pairs={{0,1},{1,2},{2,3},{3,0},{4,5},{5,6},{6,7},{7,4},{8,9},{9,10},{10,1... | collective-permute-start | bytes 122888 | tf_op jit(solution)/shard_map/ppermute | solution.py:639
  43.0 2.8 %collective-permute-start.12 = (f32[5,8,256]{2,1,0:T(8,128)S(1)}, f32[5,8,256]{2,1,0:T(8,128)S(1)}, u32[]{:S(2)}, u32[]{:S(2)}) collective-permute-start(f32[5,8,256]{2,1,0:T(8,128)S(1)} %get-tuple-element.80.refs_0_), channel_id=1, source_target_pairs={{0,2},{1,3},{2,0},{3,1},{4,6},{5,7},{6,4},{7,5},{8,10},{9,11},{10,... | collective-permute-start | bytes 122888 | tf_op jit(solution)/shard_map/ppermute | solution.py:639
  45.8 0.2 collective-permute-start.13
  46.1 2.0 %collective-permute-done.11.refs_1_ = f32[5,8,256]{2,1,0:T(8,128)S(1)} collective-permute-done((f32[5,8,256]{2,1,0:T(8,128)S(1)}, f32[5,8,256]{2,1,0:T(8,128)S(1)}, u32[]{:S(2)}, u32[]{:S(2)}) %collective-permute-start.11) | collective-permute-done | bytes 40992 | tf_op jit(solution)/shard_map/ppermute | solution.py:639
  48.1 0.8 %collective-permute-done.12.refs_2_ = f32[5,8,256]{2,1,0:T(8,128)S(1)} collective-permute-done((f32[5,8,256]{2,1,0:T(8,128)S(1)}, f32[5,8,256]{2,1,0:T(8,128)S(1)}, u32[]{:S(2)}, u32[]{:S(2)}) %collective-permute-start.12) | collective-permute-done | bytes 40992 | tf_op jit(solution)/shard_map/ppermute | solution.py:639
  48.9 1.0 %collective-permute-done.13.refs_3_ = f32[5,8,256]{2,1,0:T(8,128)S(1)} collective-permute-done((f32[5,8,256]{2,1,0:T(8,128)S(1)}, f32[5,8,256]{2,1,0:T(8,128)S(1)}, u32[]{:S(2)}, u32[]{:S(2)}) %collective-permute-start.13) | collective-permute-done | bytes 40992 | tf_op jit(solution)/shard_map/ppermute | solution.py:639
  49.8 0.6 cell_params.4
  50.5 1.1 %collective-permute-start.14 = (f32[6,2,256]{2,1,0:T(2,128)S(1)}, f32[6,2,256]{2,1,0:T(2,128)S(1)}, u32[]{:S(2)}, u32[]{:S(2)}) collective-permute-start(f32[6,2,256]{2,1,0:T(2,128)S(1)} %get-tuple-element.81), channel_id=1, source_target_pairs={{0,16},{12,28},{4,8},{8,4},{16,0},{28,12},{20,24},{24,20},{1,17},{... | collective-permute-start | bytes 36872 | tf_op jit(solution)/shard_map/ppermute | solution.py:631
  51.6 6.3 %inner_relax.3 = (f32[2,16,2,8,512]{4,3,2,1,0:T(8,128)S(1)}, f32[4,16,2,8,512]{4,3,2,1,0:T(8,128)S(1)}, f32[2,16,2,8,512]{4,3,2,1,0:T(8,128)S(1)}, f32[4,16,2,8,...) custom-call(f32[2,16,2,8,512]{4,3,2,1,0:T(8,128)S(1)} %get-tuple-ele, ...), custom_call_target="tpu_custom_call" | custom-call | tf_op jit(solution)/shard_map/inner_relax/pallas_call | solution.py:551
  57.9 0.0 collective-permute-done.14.p_cross
  57.9 0.0 collective-permute-done.15.p_in
  58.0 0.0 collective-permute-done.9.h_cross
  58.0 2.9 %edge_relax.3 = (f32[2,16,2,8,512]{4,3,2,1,0:T(8,128)S(1)}, f32[2,16,2,8,512]{4,3,2,1,0:T(8,128)S(1)}, f32[5,8,256]{2,1,0:T(8,128)S(1)}) custom-call(f32[2,16,2,8,512]{4,3,2,1,0:T(8,128)S(1)} %collective-permute-done.9.h_cross, f32[2,16,2,8,512]{4,3,2,1,0:T(8,128)S(1)} %collective-permute-done.10.h_in, f32[6,2,256]{2,1,0:T(2,128)S(1)} %collective-permute-done.14.p_cross, ...), custom_call_target="tpu_custom_call" | custom-call | tf_op jit(solution)/shard_map/edge_relax/pallas_call | solution.py:586
  60.9 0.7 collective-permute-start.16
  61.6 2.1 %collective-permute-start.17 = (f32[5,8,256]{2,1,0:T(8,128)S(1)}, f32[5,8,256]{2,1,0:T(8,128)S(1)}, u32[]{:S(2)}, u32[]{:S(2)}) collective-permute-start(f32[5,8,256]{2,1,0:T(8,128)S(1)} %get-tuple-element.94.refs_0_), channel_id=1, source_target_pairs={{0,2},{1,3},{2,0},{3,1},{4,6},{5,7},{6,4},{7,5},{8,10},{9,11},{10,... | collective-permute-start | bytes 122888 | tf_op jit(solution)/shard_map/ppermute | solution.py:639
  63.7 1.0 %collective-permute-start.18 = (f32[5,8,256]{2,1,0:T(8,128)S(1)}, f32[5,8,256]{2,1,0:T(8,128)S(1)}, u32[]{:S(2)}, u32[]{:S(2)}) collective-permute-start(f32[5,8,256]{2,1,0:T(8,128)S(1)} %get-tuple-element.94.refs_0_), channel_id=1, source_target_pairs={{0,3},{1,0},{2,1},{3,2},{4,7},{5,4},{6,5},{7,6},{8,11},{9,8},{10,9... | collective-permute-start | bytes 122888 | tf_op jit(solution)/shard_map/ppermute | solution.py:639
  64.7 2.4 %collective-permute-done.16.refs_1_ = f32[5,8,256]{2,1,0:T(8,128)S(1)} collective-permute-done((f32[5,8,256]{2,1,0:T(8,128)S(1)}, f32[5,8,256]{2,1,0:T(8,128)S(1)}, u32[]{:S(2)}, u32[]{:S(2)}) %collective-permute-start.16) | collective-permute-done | bytes 40992 | tf_op jit(solution)/shard_map/ppermute | solution.py:639
  67.2 1.2 %collective-permute-done.17.refs_2_ = f32[5,8,256]{2,1,0:T(8,128)S(1)} collective-permute-done((f32[5,8,256]{2,1,0:T(8,128)S(1)}, f32[5,8,256]{2,1,0:T(8,128)S(1)}, u32[]{:S(2)}, u32[]{:S(2)}) %collective-permute-start.17) | collective-permute-done | bytes 40992 | tf_op jit(solution)/shard_map/ppermute | solution.py:639
  68.3 0.0 collective-permute-done.18.refs_3_
  68.3 0.6 cell_params.5.params
  69.0 2.8 %final_relax.1 = f32[8,16,16,512]{3,2,1,0:T(8,128)} custom-call(f32[2,16,2,8,512]{4,3,2,1,0:T(8,128)S(1)} %get-tuple-element.91.m_cross, f32[4,16,2,8,512]{4,3,2,1,0:T(8,128)S(1)} %get-tuple-element.92.m_mid, f32[2,16,2,8,512]{4,3,2,1,0:T(8,128)S(1)} %get-tuple-element.93.m_in, f32[6,8,256]{2,1,0:T(8,128)S(1)} %cell_params.5.params, ...), custom_call_target="tpu_custom_call" | custom-call | tf_op jit(solution)/shard_map/final_relax/pallas_call | solution.py:607
  (4 shorter events, 0.0 us)
Async XLA Ops:
  2.1 9.2 %collective-permute-start.1 = (f32[2,16,2,8,512]{4,3,2,1,0:T(8,128)S(1)}, f32[2,16,2,8,512]{4,3,2,1,0:T(8,128)S(1)}, u32[]{:S(2)}, u32[]{:S(2)}) collective-permute-start(f32[2,16,2,8,512]{4,3,2,1,0:T(8,128)S(1)} %get-tuple-element.51.refs_1_.inside), channel_id=1, source_target_pairs={{0,4},{4,0},{8,12},{12,8},{1,5},{5,1},{9,13},{13,9},{2,6},{6,2},{1... | collective-permute-start | bytes 3145736 | tf_op jit(solution)/shard_map/ppermute | solution.py:632
  2.6 15.4 %collective-permute-start = (f32[2,16,2,8,512]{4,3,2,1,0:T(8,128)S(1)}, f32[2,16,2,8,512]{4,3,2,1,0:T(8,128)S(1)}, u32[]{:S(2)}, u32[]{:S(2)}) collective-permute-start(f32[2,16,2,8,512]{4,3,2,1,0:T(8,128)S(1)} %get-tuple-element.50.refs_0_.cross), channel_id=1, source_target_pairs={{0,16},{12,28},{4,8},{8,4},{16,0},{28,12},{20,24},{24,20},{1,17},{... | collective-permute-start | bytes 3145736 | tf_op jit(solution)/shard_map/ppermute | solution.py:631
  18.0 11.6 %copy-start = (f32[4]{0:T(128)S(1)}, f32[4]{0:T(128)}, u32[]{:S(2)}) copy-start(f32[4]{0:T(128)} %refs_6_.5) | copy-start | bytes 52
  19.4 18.3 %collective-permute-start.2 = (f32[2,16,2,8,512]{4,3,2,1,0:T(8,128)S(1)}, f32[2,16,2,8,512]{4,3,2,1,0:T(8,128)S(1)}, u32[]{:S(2)}, u32[]{:S(2)}) collective-permute-start(f32[2,16,2,8,512]{4,3,2,1,0:T(8,128)S(1)} %get-tuple-element.62.refs_0_), channel_id=1, source_target_pairs={{0,16},{12,28},{4,8},{8,4},{16,0},{28,12},{20,24},{24,20},{1,17},{... | collective-permute-start | bytes 3145736 | tf_op jit(solution)/shard_map/ppermute | solution.py:631
  21.4 16.3 %collective-permute-start.3 = (f32[2,16,2,8,512]{4,3,2,1,0:T(8,128)S(1)}, f32[2,16,2,8,512]{4,3,2,1,0:T(8,128)S(1)}, u32[]{:S(2)}, u32[]{:S(2)}) collective-permute-start(f32[2,16,2,8,512]{4,3,2,1,0:T(8,128)S(1)} %get-tuple-element.63.refs_2_), channel_id=1, source_target_pairs={{0,4},{4,0},{8,12},{12,8},{1,5},{5,1},{9,13},{13,9},{2,6},{6,2},{1... | collective-permute-start | bytes 3145736 | tf_op jit(solution)/shard_map/ppermute | solution.py:632
  21.4 6.2 %collective-permute-start.4 = (f32[5,8,256]{2,1,0:T(8,128)S(1)}, f32[5,8,256]{2,1,0:T(8,128)S(1)}, u32[]{:S(2)}, u32[]{:S(2)}) collective-permute-start(f32[5,8,256]{2,1,0:T(8,128)S(1)} %get-tuple-element.64.refs_0_), channel_id=1, source_target_pairs={{0,1},{1,2},{2,3},{3,0},{4,5},{5,6},{6,7},{7,4},{8,9},{9,10},{10,1... | collective-permute-start | bytes 122888 | tf_op jit(solution)/shard_map/ppermute | solution.py:639
  23.0 6.2 %collective-permute-start.5 = (f32[5,8,256]{2,1,0:T(8,128)S(1)}, f32[5,8,256]{2,1,0:T(8,128)S(1)}, u32[]{:S(2)}, u32[]{:S(2)}) collective-permute-start(f32[5,8,256]{2,1,0:T(8,128)S(1)} %get-tuple-element.64.refs_0_), channel_id=1, source_target_pairs={{0,2},{1,3},{2,0},{3,1},{4,6},{5,7},{6,4},{7,5},{8,10},{9,11},{10,... | collective-permute-start | bytes 122888 | tf_op jit(solution)/shard_map/ppermute | solution.py:639
  25.6 4.0 %collective-permute-start.6 = (f32[5,8,256]{2,1,0:T(8,128)S(1)}, f32[5,8,256]{2,1,0:T(8,128)S(1)}, u32[]{:S(2)}, u32[]{:S(2)}) collective-permute-start(f32[5,8,256]{2,1,0:T(8,128)S(1)} %get-tuple-element.64.refs_0_), channel_id=1, source_target_pairs={{0,3},{1,0},{2,1},{3,2},{4,7},{5,4},{6,5},{7,6},{8,11},{9,8},{10,9... | collective-permute-start | bytes 122888 | tf_op jit(solution)/shard_map/ppermute | solution.py:639
  30.3 7.4 %collective-permute-start.7 = (f32[6,2,256]{2,1,0:T(2,128)S(1)}, f32[6,2,256]{2,1,0:T(2,128)S(1)}, u32[]{:S(2)}, u32[]{:S(2)}) collective-permute-start(f32[6,2,256]{2,1,0:T(2,128)S(1)} %get-tuple-element.66), channel_id=1, source_target_pairs={{0,16},{12,28},{4,8},{8,4},{16,0},{28,12},{20,24},{24,20},{1,17},{... | collective-permute-start | bytes 36872 | tf_op jit(solution)/shard_map/ppermute | solution.py:631
  31.3 6.4 %collective-permute-start.8 = (f32[6,2,256]{2,1,0:T(2,128)S(1)}, f32[6,2,256]{2,1,0:T(2,128)S(1)}, u32[]{:S(2)}, u32[]{:S(2)}) collective-permute-start(f32[6,2,256]{2,1,0:T(2,128)S(1)} %get-tuple-element.67), channel_id=1, source_target_pairs={{0,4},{4,0},{8,12},{12,8},{1,5},{5,1},{9,13},{13,9},{2,6},{6,2},{1... | collective-permute-start | bytes 36872 | tf_op jit(solution)/shard_map/ppermute | solution.py:632
  40.6 17.3 %collective-permute-start.10 = (f32[2,16,2,8,512]{4,3,2,1,0:T(8,128)S(1)}, f32[2,16,2,8,512]{4,3,2,1,0:T(8,128)S(1)}, u32[]{:S(2)}, u32[]{:S(2)}) collective-permute-start(f32[2,16,2,8,512]{4,3,2,1,0:T(8,128)S(1)} %get-tuple-element.79.refs_2_), channel_id=1, source_target_pairs={{0,4},{4,0},{8,12},{12,8},{1,5},{5,1},{9,13},{13,9},{2,6},{6,2},{1... | collective-permute-start | bytes 3145736 | tf_op jit(solution)/shard_map/ppermute | solution.py:632
  41.1 16.8 %collective-permute-start.9 = (f32[2,16,2,8,512]{4,3,2,1,0:T(8,128)S(1)}, f32[2,16,2,8,512]{4,3,2,1,0:T(8,128)S(1)}, u32[]{:S(2)}, u32[]{:S(2)}) collective-permute-start(f32[2,16,2,8,512]{4,3,2,1,0:T(8,128)S(1)} %get-tuple-element.78.refs_0_), channel_id=1, source_target_pairs={{0,16},{12,28},{4,8},{8,4},{16,0},{28,12},{20,24},{24,20},{1,17},{... | collective-permute-start | bytes 3145736 | tf_op jit(solution)/shard_map/ppermute | solution.py:631
  42.2 5.9 %collective-permute-start.11 = (f32[5,8,256]{2,1,0:T(8,128)S(1)}, f32[5,8,256]{2,1,0:T(8,128)S(1)}, u32[]{:S(2)}, u32[]{:S(2)}) collective-permute-start(f32[5,8,256]{2,1,0:T(8,128)S(1)} %get-tuple-element.80.refs_0_), channel_id=1, source_target_pairs={{0,1},{1,2},{2,3},{3,0},{4,5},{5,6},{6,7},{7,4},{8,9},{9,10},{10,1... | collective-permute-start | bytes 122888 | tf_op jit(solution)/shard_map/ppermute | solution.py:639
  43.0 5.9 %collective-permute-start.12 = (f32[5,8,256]{2,1,0:T(8,128)S(1)}, f32[5,8,256]{2,1,0:T(8,128)S(1)}, u32[]{:S(2)}, u32[]{:S(2)}) collective-permute-start(f32[5,8,256]{2,1,0:T(8,128)S(1)} %get-tuple-element.80.refs_0_), channel_id=1, source_target_pairs={{0,2},{1,3},{2,0},{3,1},{4,6},{5,7},{6,4},{7,5},{8,10},{9,11},{10,... | collective-permute-start | bytes 122888 | tf_op jit(solution)/shard_map/ppermute | solution.py:639
  45.8 4.0 %collective-permute-start.13 = (f32[5,8,256]{2,1,0:T(8,128)S(1)}, f32[5,8,256]{2,1,0:T(8,128)S(1)}, u32[]{:S(2)}, u32[]{:S(2)}) collective-permute-start(f32[5,8,256]{2,1,0:T(8,128)S(1)} %get-tuple-element.80.refs_0_), channel_id=1, source_target_pairs={{0,3},{1,0},{2,1},{3,2},{4,7},{5,4},{6,5},{7,6},{8,11},{9,8},{10,9... | collective-permute-start | bytes 122888 | tf_op jit(solution)/shard_map/ppermute | solution.py:639
  50.5 7.4 %collective-permute-start.14 = (f32[6,2,256]{2,1,0:T(2,128)S(1)}, f32[6,2,256]{2,1,0:T(2,128)S(1)}, u32[]{:S(2)}, u32[]{:S(2)}) collective-permute-start(f32[6,2,256]{2,1,0:T(2,128)S(1)} %get-tuple-element.81), channel_id=1, source_target_pairs={{0,16},{12,28},{4,8},{8,4},{16,0},{28,12},{20,24},{24,20},{1,17},{... | collective-permute-start | bytes 36872 | tf_op jit(solution)/shard_map/ppermute | solution.py:631
  51.6 6.4 %collective-permute-start.15 = (f32[6,2,256]{2,1,0:T(2,128)S(1)}, f32[6,2,256]{2,1,0:T(2,128)S(1)}, u32[]{:S(2)}, u32[]{:S(2)}) collective-permute-start(f32[6,2,256]{2,1,0:T(2,128)S(1)} %get-tuple-element.82), channel_id=1, source_target_pairs={{0,4},{4,0},{8,12},{12,8},{1,5},{5,1},{9,13},{13,9},{2,6},{6,2},{1... | collective-permute-start | bytes 36872 | tf_op jit(solution)/shard_map/ppermute | solution.py:632
  60.9 6.3 %collective-permute-start.16 = (f32[5,8,256]{2,1,0:T(8,128)S(1)}, f32[5,8,256]{2,1,0:T(8,128)S(1)}, u32[]{:S(2)}, u32[]{:S(2)}) collective-permute-start(f32[5,8,256]{2,1,0:T(8,128)S(1)} %get-tuple-element.94.refs_0_), channel_id=1, source_target_pairs={{0,1},{1,2},{2,3},{3,0},{4,5},{5,6},{6,7},{7,4},{8,9},{9,10},{10,1... | collective-permute-start | bytes 122888 | tf_op jit(solution)/shard_map/ppermute | solution.py:639
  61.6 6.8 %collective-permute-start.17 = (f32[5,8,256]{2,1,0:T(8,128)S(1)}, f32[5,8,256]{2,1,0:T(8,128)S(1)}, u32[]{:S(2)}, u32[]{:S(2)}) collective-permute-start(f32[5,8,256]{2,1,0:T(8,128)S(1)} %get-tuple-element.94.refs_0_), channel_id=1, source_target_pairs={{0,2},{1,3},{2,0},{3,1},{4,6},{5,7},{6,4},{7,5},{8,10},{9,11},{10,... | collective-permute-start | bytes 122888 | tf_op jit(solution)/shard_map/ppermute | solution.py:639
  63.7 4.6 %collective-permute-start.18 = (f32[5,8,256]{2,1,0:T(8,128)S(1)}, f32[5,8,256]{2,1,0:T(8,128)S(1)}, u32[]{:S(2)}, u32[]{:S(2)}) collective-permute-start(f32[5,8,256]{2,1,0:T(8,128)S(1)} %get-tuple-element.94.refs_0_), channel_id=1, source_target_pairs={{0,3},{1,0},{2,1},{3,2},{4,7},{5,4},{6,5},{7,6},{8,11},{9,8},{10,9... | collective-permute-start | bytes 122888 | tf_op jit(solution)/shard_map/ppermute | solution.py:639

commit v12 on v11

--- a/solution.py
+++ b/solution.py
@@ -401,7 +401,7 @@
             work(i % 16, t, lanes, coef)
         return carry
 
-    lax.fori_loop(0, middle.shape[-1] // LANES * 16, one, 0, unroll=4)
+    lax.fori_loop(0, middle.shape[-1] // LANES * 16, one, 0, unroll=8)
 
 
 def first_in_kernel(high, inside, e_in, middle, coef_ref, weights, out, sums):

time: 72.1 us -> 71.7 us (level)
  no operation moved by 1% of the time
where the time goes in v12:
time: 71.7 us; the launch traced here: 71.5 us
  Pallas kernels  33.5 us (47%)
  starting transfers between devices  22.1 us (31%)
  waiting for transfers between devices  15 us (21%)
  between operations  0.93 us (1%)
    pallas_call x3, Pallas kernels, inner(): pl.pallas_call(functools.partial(inner_kernel, relax, rows), in_specs=[vm...  18.8 us
    ppermute x9, starting transfers between devices, gather(): parts.append(lax.ppermute(part, 'vert', pairs))  13.3 us
    ppermute x9, waiting for transfers between devices, gather(): parts.append(lax.ppermute(part, 'vert', pairs))  9.41 us
    ppermute x5, starting transfers between devices, exchange(): lax.ppermute(cross, ('groups', 'gx'), across)  7.81 us
    pallas_call x2, Pallas kernels, edge(): pl.pallas_call(functools.partial(edge_kernel, rows, line), in_specs=[vmem...  5.57 us
    ppermute x5, waiting for transfers between devices, exchange(): lax.ppermute(cross, ('groups', 'gx'), across)  5.55 us
    pallas_call x1, Pallas kernels, final(): pl.pallas_call(functools.partial(final_kernel, rows), in_specs=[vmem] * 6...  2.81 us
    pallas_call x1, Pallas kernels, load(): pl.pallas_call(load_kernel, in_specs=[hbm] * 3, out_specs=[vmem] * 7, out...  2.11 us
  transfers between devices with their start and end apart: 19, of which 8 were waited for; matrix products, arithmetic and copies ran while one was open for 0% of the time, Pallas kernels for 30%

profile of v12, /device:TPU:0, one launch (start us, length us, event | category | flops | bytes accessed | tf_op | source)
XLA Modules:
  0.0 71.5 jit_solution(16950955355835980945)
XLA Ops:
  0.0 2.1 %load_edges.1 = (f32[2,16,2,8,512]{4,3,2,1,0:T(8,128)S(1)}, f32[2,16,2,8,512]{4,3,2,1,0:T(8,128)S(1)}, s32[8,256]{1,0:T(8,128)S(1)}, bf16[32,512]{1,0:T(8,128)(2...) custom-call(s32[1,512]{1,0:T(1,128)} %bitcast.1, ...), custom_call_target="tpu_custom_call" | custom-call | tf_op jit(solution)/shard_map/load_edges/pallas_call | solution.py:512
  2.1 0.5 collective-permute-start.1
  2.6 2.6 %collective-permute-start = (f32[2,16,2,8,512]{4,3,2,1,0:T(8,128)S(1)}, f32[2,16,2,8,512]{4,3,2,1,0:T(8,128)S(1)}, u32[]{:S(2)}, u32[]{:S(2)}) collective-permute-start(f32[2,16,2,8,512]{4,3,2,1,0:T(8,128)S(1)} %get-tuple-element.50.refs_0_.cross), channel_id=1, source_target_pairs={{0,16},{12,28},{4,8},{8,4},{16,0},{28,12},{20,24},{24,20},{1,17},{... | collective-permute-start | bytes 3145736 | tf_op jit(solution)/shard_map/ppermute | solution.py:631
  5.2 6.1 %inner_first.1 = (f32[4,16,2,8,512]{4,3,2,1,0:T(8,128)S(1)}, f32[4,16,2,8,512]{4,3,2,1,0:T(8,128)S(1)}, f32[2,16,2,8,512]{4,3,2,1,0:T(8,128)S(1)}, f32[2,16,2,8,512]{4,3,2,1,0:T(8,128)S(1)}, f32[5,4,256]{2,1,0:T(4,128)S(1)}) custom-call(f32[2,16,2,8,512]{4,3,2,1,0:T(8,128)S(1)} %get-tuple-element.50.refs_0_.cross, ...), custom_call_target="tpu_custom_call" | custom-call | tf_op jit(solution)/shard_map/inner_first/pallas_call | solution.py:551
  11.3 0.0 collective-permute-done.1.high
  11.3 1.2 %first_in.1 = (f32[2,16,2,8,512]{4,3,2,1,0:T(8,128)S(1)}, f32[5,2,256]{2,1,0:T(2,128)S(1)}) custom-call(f32[2,16,2,8,512]{4,3,2,1,0:T(8,128)S(1)} %collective-permute-done.1.high, f32[2,16,2,8,512]{4,3,2,1,0:T(8,128)S(1)} %get-tuple-element.51.refs_1_.inside, f32[2,16,2,8,512]{4,3,2,1,0:T(8,128)S(1)} %get-tuple-element.57.e_in, ...), custom_call_target="tpu_custom_call" | custom-call | tf_op jit(solution)/shard_map/first_in/pallas_call | solution.py:565
  12.5 5.5 %collective-permute-done.low = f32[2,16,2,8,512]{4,3,2,1,0:T(8,128)S(1)} collective-permute-done((f32[2,16,2,8,512]{4,3,2,1,0:T(8,128)S(1)}, f32[2,16,2,8,512]{4,3,2,1,0:T(8,128)S(1)}, u32[]{:S(2)}, u32[]{:S(2)}) %collective-permute-start) | collective-permute-done | bytes 1048608 | tf_op jit(solution)/shard_map/ppermute | solution.py:631
  18.0 1.2 %first_cross.1 = (f32[2,16,2,8,512]{4,3,2,1,0:T(8,128)S(1)}, f32[5,8,256]{2,1,0:T(8,128)S(1)}) custom-call(f32[2,16,2,8,512]{4,3,2,1,0:T(8,128)S(1)} %collective-permute-done.low, f32[2,16,2,8,512]{4,3,2,1,0:T(8,128)S(1)} %get-tuple-element.50.refs_0_.cross, f32[2,16,2,8,512]{4,3,2,1,0:T(8,128)S(1)} %get-tuple-element.54.e_cross, ...), custom_call_target="tpu_custom_call" | custom-call | tf_op jit(solution)/shard_map/first_cross/pallas_call | solution.py:575
  19.2 2.0 %collective-permute-start.2 = (f32[2,16,2,8,512]{4,3,2,1,0:T(8,128)S(1)}, f32[2,16,2,8,512]{4,3,2,1,0:T(8,128)S(1)}, u32[]{:S(2)}, u32[]{:S(2)}) collective-permute-start(f32[2,16,2,8,512]{4,3,2,1,0:T(8,128)S(1)} %get-tuple-element.62.refs_0_), channel_id=1, source_target_pairs={{0,16},{12,28},{4,8},{8,4},{16,0},{28,12},{20,24},{24,20},{1,17},{... | collective-permute-start | bytes 3145736 | tf_op jit(solution)/shard_map/ppermute | solution.py:631
  21.3 0.0 collective-permute-start.3
  21.3 1.6 %collective-permute-start.4 = (f32[5,8,256]{2,1,0:T(8,128)S(1)}, f32[5,8,256]{2,1,0:T(8,128)S(1)}, u32[]{:S(2)}, u32[]{:S(2)}) collective-permute-start(f32[5,8,256]{2,1,0:T(8,128)S(1)} %get-tuple-element.64.refs_0_), channel_id=1, source_target_pairs={{0,1},{1,2},{2,3},{3,0},{4,5},{5,6},{6,7},{7,4},{8,9},{9,10},{10,1... | collective-permute-start | bytes 122888 | tf_op jit(solution)/shard_map/ppermute | solution.py:639
  22.8 2.6 %collective-permute-start.5 = (f32[5,8,256]{2,1,0:T(8,128)S(1)}, f32[5,8,256]{2,1,0:T(8,128)S(1)}, u32[]{:S(2)}, u32[]{:S(2)}) collective-permute-start(f32[5,8,256]{2,1,0:T(8,128)S(1)} %get-tuple-element.64.refs_0_), channel_id=1, source_target_pairs={{0,2},{1,3},{2,0},{3,1},{4,6},{5,7},{6,4},{7,5},{8,10},{9,11},{10,... | collective-permute-start | bytes 122888 | tf_op jit(solution)/shard_map/ppermute | solution.py:639
  25.4 1.3 %collective-permute-start.6 = (f32[5,8,256]{2,1,0:T(8,128)S(1)}, f32[5,8,256]{2,1,0:T(8,128)S(1)}, u32[]{:S(2)}, u32[]{:S(2)}) collective-permute-start(f32[5,8,256]{2,1,0:T(8,128)S(1)} %get-tuple-element.64.refs_0_), channel_id=1, source_target_pairs={{0,3},{1,0},{2,1},{3,2},{4,7},{5,4},{6,5},{7,6},{8,11},{9,8},{10,9... | collective-permute-start | bytes 122888 | tf_op jit(solution)/shard_map/ppermute | solution.py:639
  27.4 0.0 collective-permute-done.4.refs_1_
  27.4 1.6 %collective-permute-done.5.refs_2_ = f32[5,8,256]{2,1,0:T(8,128)S(1)} collective-permute-done((f32[5,8,256]{2,1,0:T(8,128)S(1)}, f32[5,8,256]{2,1,0:T(8,128)S(1)}, u32[]{:S(2)}, u32[]{:S(2)}) %collective-permute-start.5) | collective-permute-done | bytes 40992 | tf_op jit(solution)/shard_map/ppermute | solution.py:639
  29.1 0.4 collective-permute-done.6.refs_3_
  29.5 0.6 cell_params.3
  30.1 1.1 %collective-permute-start.7 = (f32[6,2,256]{2,1,0:T(2,128)S(1)}, f32[6,2,256]{2,1,0:T(2,128)S(1)}, u32[]{:S(2)}, u32[]{:S(2)}) collective-permute-start(f32[6,2,256]{2,1,0:T(2,128)S(1)} %get-tuple-element.66), channel_id=1, source_target_pairs={{0,16},{12,28},{4,8},{8,4},{16,0},{28,12},{20,24},{24,20},{1,17},{... | collective-permute-start | bytes 36872 | tf_op jit(solution)/shard_map/ppermute | solution.py:631
  31.2 0.0 collective-permute-start.8
  31.2 6.3 %inner_relax.2 = (f32[2,16,2,8,512]{4,3,2,1,0:T(8,128)S(1)}, f32[4,16,2,8,512]{4,3,2,1,0:T(8,128)S(1)}, f32[2,16,2,8,512]{4,3,2,1,0:T(8,128)S(1)}, f32[4,16,2,8,...) custom-call(f32[2,16,2,8,512]{4,3,2,1,0:T(8,128)S(1)} %get-tuple-ele, ...), custom_call_target="tpu_custom_call" | custom-call | tf_op jit(solution)/shard_map/inner_relax/pallas_call | solution.py:551
  37.5 0.0 collective-permute-done.7.p_cross
  37.5 0.0 collective-permute-done.2.h_cross
  37.6 0.0 collective-permute-done.3.h_in
  37.6 2.8 %edge_relax.2 = (f32[2,16,2,8,512]{4,3,2,1,0:T(8,128)S(1)}, f32[2,16,2,8,512]{4,3,2,1,0:T(8,128)S(1)}, f32[5,8,256]{2,1,0:T(8,128)S(1)}) custom-call(f32[2,16,2,8,512]{4,3,2,1,0:T(8,128)S(1)} %collective-permute-done.2.h_cross, f32[2,16,2,8,512]{4,3,2,1,0:T(8,128)S(1)} %collective-permute-done.3.h_in, f32[6,2,256]{2,1,0:T(2,128)S(1)} %collective-permute-done.7.p_cross, ...), custom_call_target="tpu_custom_call" | custom-call | tf_op jit(solution)/shard_map/edge_relax/pallas_call | solution.py:586
  40.3 0.5 collective-permute-start.10
  40.9 1.0 %collective-permute-start.9 = (f32[2,16,2,8,512]{4,3,2,1,0:T(8,128)S(1)}, f32[2,16,2,8,512]{4,3,2,1,0:T(8,128)S(1)}, u32[]{:S(2)}, u32[]{:S(2)}) collective-permute-start(f32[2,16,2,8,512]{4,3,2,1,0:T(8,128)S(1)} %get-tuple-element.78.refs_0_), channel_id=1, source_target_pairs={{0,16},{12,28},{4,8},{8,4},{16,0},{28,12},{20,24},{24,20},{1,17},{... | collective-permute-start | bytes 3145736 | tf_op jit(solution)/shard_map/ppermute | solution.py:631
  41.9 0.8 %collective-permute-start.11 = (f32[5,8,256]{2,1,0:T(8,128)S(1)}, f32[5,8,256]{2,1,0:T(8,128)S(1)}, u32[]{:S(2)}, u32[]{:S(2)}) collective-permute-start(f32[5,8,256]{2,1,0:T(8,128)S(1)} %get-tuple-element.80.refs_0_), channel_id=1, source_target_pairs={{0,1},{1,2},{2,3},{3,0},{4,5},{5,6},{6,7},{7,4},{8,9},{9,10},{10,1... | collective-permute-start | bytes 122888 | tf_op jit(solution)/shard_map/ppermute | solution.py:639
  42.7 2.8 %collective-permute-start.12 = (f32[5,8,256]{2,1,0:T(8,128)S(1)}, f32[5,8,256]{2,1,0:T(8,128)S(1)}, u32[]{:S(2)}, u32[]{:S(2)}) collective-permute-start(f32[5,8,256]{2,1,0:T(8,128)S(1)} %get-tuple-element.80.refs_0_), channel_id=1, source_target_pairs={{0,2},{1,3},{2,0},{3,1},{4,6},{5,7},{6,4},{7,5},{8,10},{9,11},{10,... | collective-permute-start | bytes 122888 | tf_op jit(solution)/shard_map/ppermute | solution.py:639
  45.6 0.2 collective-permute-start.13
  45.8 2.0 %collective-permute-done.11.refs_1_ = f32[5,8,256]{2,1,0:T(8,128)S(1)} collective-permute-done((f32[5,8,256]{2,1,0:T(8,128)S(1)}, f32[5,8,256]{2,1,0:T(8,128)S(1)}, u32[]{:S(2)}, u32[]{:S(2)}) %collective-permute-start.11) | collective-permute-done | bytes 40992 | tf_op jit(solution)/shard_map/ppermute | solution.py:639
  47.8 0.8 %collective-permute-done.12.refs_2_ = f32[5,8,256]{2,1,0:T(8,128)S(1)} collective-permute-done((f32[5,8,256]{2,1,0:T(8,128)S(1)}, f32[5,8,256]{2,1,0:T(8,128)S(1)}, u32[]{:S(2)}, u32[]{:S(2)}) %collective-permute-start.12) | collective-permute-done | bytes 40992 | tf_op jit(solution)/shard_map/ppermute | solution.py:639
  48.6 1.0 %collective-permute-done.13.refs_3_ = f32[5,8,256]{2,1,0:T(8,128)S(1)} collective-permute-done((f32[5,8,256]{2,1,0:T(8,128)S(1)}, f32[5,8,256]{2,1,0:T(8,128)S(1)}, u32[]{:S(2)}, u32[]{:S(2)}) %collective-permute-start.13) | collective-permute-done | bytes 40992 | tf_op jit(solution)/shard_map/ppermute | solution.py:639
  49.6 0.6 cell_params.4
  50.2 1.1 %collective-permute-start.14 = (f32[6,2,256]{2,1,0:T(2,128)S(1)}, f32[6,2,256]{2,1,0:T(2,128)S(1)}, u32[]{:S(2)}, u32[]{:S(2)}) collective-permute-start(f32[6,2,256]{2,1,0:T(2,128)S(1)} %get-tuple-element.81), channel_id=1, source_target_pairs={{0,16},{12,28},{4,8},{8,4},{16,0},{28,12},{20,24},{24,20},{1,17},{... | collective-permute-start | bytes 36872 | tf_op jit(solution)/shard_map/ppermute | solution.py:631
  51.3 0.0 collective-permute-start.15
  51.3 6.3 %inner_relax.3 = (f32[2,16,2,8,512]{4,3,2,1,0:T(8,128)S(1)}, f32[4,16,2,8,512]{4,3,2,1,0:T(8,128)S(1)}, f32[2,16,2,8,512]{4,3,2,1,0:T(8,128)S(1)}, f32[4,16,2,8,...) custom-call(f32[2,16,2,8,512]{4,3,2,1,0:T(8,128)S(1)} %get-tuple-ele, ...), custom_call_target="tpu_custom_call" | custom-call | tf_op jit(solution)/shard_map/inner_relax/pallas_call | solution.py:551
  57.7 0.0 collective-permute-done.14.p_cross
  57.7 0.0 collective-permute-done.10.h_in
  57.7 0.0 collective-permute-done.9.h_cross
  57.7 2.8 %edge_relax.3 = (f32[2,16,2,8,512]{4,3,2,1,0:T(8,128)S(1)}, f32[2,16,2,8,512]{4,3,2,1,0:T(8,128)S(1)}, f32[5,8,256]{2,1,0:T(8,128)S(1)}) custom-call(f32[2,16,2,8,512]{4,3,2,1,0:T(8,128)S(1)} %collective-permute-done.9.h_cross, f32[2,16,2,8,512]{4,3,2,1,0:T(8,128)S(1)} %collective-permute-done.10.h_in, f32[6,2,256]{2,1,0:T(2,128)S(1)} %collective-permute-done.14.p_cross, ...), custom_call_target="tpu_custom_call" | custom-call | tf_op jit(solution)/shard_map/edge_relax/pallas_call | solution.py:586
  60.5 0.7 collective-permute-start.16
  61.2 2.1 %collective-permute-start.17 = (f32[5,8,256]{2,1,0:T(8,128)S(1)}, f32[5,8,256]{2,1,0:T(8,128)S(1)}, u32[]{:S(2)}, u32[]{:S(2)}) collective-permute-start(f32[5,8,256]{2,1,0:T(8,128)S(1)} %get-tuple-element.94.refs_0_), channel_id=1, source_target_pairs={{0,2},{1,3},{2,0},{3,1},{4,6},{5,7},{6,4},{7,5},{8,10},{9,11},{10,... | collective-permute-start | bytes 122888 | tf_op jit(solution)/shard_map/ppermute | solution.py:639
  63.3 1.0 %collective-permute-start.18 = (f32[5,8,256]{2,1,0:T(8,128)S(1)}, f32[5,8,256]{2,1,0:T(8,128)S(1)}, u32[]{:S(2)}, u32[]{:S(2)}) collective-permute-start(f32[5,8,256]{2,1,0:T(8,128)S(1)} %get-tuple-element.94.refs_0_), channel_id=1, source_target_pairs={{0,3},{1,0},{2,1},{3,2},{4,7},{5,4},{6,5},{7,6},{8,11},{9,8},{10,9... | collective-permute-start | bytes 122888 | tf_op jit(solution)/shard_map/ppermute | solution.py:639
  64.3 2.4 %collective-permute-done.16.refs_1_ = f32[5,8,256]{2,1,0:T(8,128)S(1)} collective-permute-done((f32[5,8,256]{2,1,0:T(8,128)S(1)}, f32[5,8,256]{2,1,0:T(8,128)S(1)}, u32[]{:S(2)}, u32[]{:S(2)}) %collective-permute-start.16) | collective-permute-done | bytes 40992 | tf_op jit(solution)/shard_map/ppermute | solution.py:639
  66.8 1.2 %collective-permute-done.17.refs_2_ = f32[5,8,256]{2,1,0:T(8,128)S(1)} collective-permute-done((f32[5,8,256]{2,1,0:T(8,128)S(1)}, f32[5,8,256]{2,1,0:T(8,128)S(1)}, u32[]{:S(2)}, u32[]{:S(2)}) %collective-permute-start.17) | collective-permute-done | bytes 40992 | tf_op jit(solution)/shard_map/ppermute | solution.py:639
  67.9 0.0 collective-permute-done.18.refs_3_
  67.9 0.6 cell_params.5.params
  68.6 2.8 %final_relax.1 = f32[8,16,16,512]{3,2,1,0:T(8,128)} custom-call(f32[2,16,2,8,512]{4,3,2,1,0:T(8,128)S(1)} %get-tuple-element.91.m_cross, f32[4,16,2,8,512]{4,3,2,1,0:T(8,128)S(1)} %get-tuple-element.92.m_mid, f32[2,16,2,8,512]{4,3,2,1,0:T(8,128)S(1)} %get-tuple-element.93.m_in, f32[6,8,256]{2,1,0:T(8,128)S(1)} %cell_params.5.params, ...), custom_call_target="tpu_custom_call" | custom-call | tf_op jit(solution)/shard_map/final_relax/pallas_call | solution.py:607
  (4 shorter events, 0.0 us)
Async XLA Ops:
  2.1 9.2 %collective-permute-start.1 = (f32[2,16,2,8,512]{4,3,2,1,0:T(8,128)S(1)}, f32[2,16,2,8,512]{4,3,2,1,0:T(8,128)S(1)}, u32[]{:S(2)}, u32[]{:S(2)}) collective-permute-start(f32[2,16,2,8,512]{4,3,2,1,0:T(8,128)S(1)} %get-tuple-element.51.refs_1_.inside), channel_id=1, source_target_pairs={{0,4},{4,0},{8,12},{12,8},{1,5},{5,1},{9,13},{13,9},{2,6},{6,2},{1... | collective-permute-start | bytes 3145736 | tf_op jit(solution)/shard_map/ppermute | solution.py:632
  2.6 15.4 %collective-permute-start = (f32[2,16,2,8,512]{4,3,2,1,0:T(8,128)S(1)}, f32[2,16,2,8,512]{4,3,2,1,0:T(8,128)S(1)}, u32[]{:S(2)}, u32[]{:S(2)}) collective-permute-start(f32[2,16,2,8,512]{4,3,2,1,0:T(8,128)S(1)} %get-tuple-element.50.refs_0_.cross), channel_id=1, source_target_pairs={{0,16},{12,28},{4,8},{8,4},{16,0},{28,12},{20,24},{24,20},{1,17},{... | collective-permute-start | bytes 3145736 | tf_op jit(solution)/shard_map/ppermute | solution.py:631
  18.0 11.5 %copy-start = (f32[4]{0:T(128)S(1)}, f32[4]{0:T(128)}, u32[]{:S(2)}) copy-start(f32[4]{0:T(128)} %refs_6_.5) | copy-start | bytes 52
  19.2 18.3 %collective-permute-start.2 = (f32[2,16,2,8,512]{4,3,2,1,0:T(8,128)S(1)}, f32[2,16,2,8,512]{4,3,2,1,0:T(8,128)S(1)}, u32[]{:S(2)}, u32[]{:S(2)}) collective-permute-start(f32[2,16,2,8,512]{4,3,2,1,0:T(8,128)S(1)} %get-tuple-element.62.refs_0_), channel_id=1, source_target_pairs={{0,16},{12,28},{4,8},{8,4},{16,0},{28,12},{20,24},{24,20},{1,17},{... | collective-permute-start | bytes 3145736 | tf_op jit(solution)/shard_map/ppermute | solution.py:631
  21.3 16.3 %collective-permute-start.3 = (f32[2,16,2,8,512]{4,3,2,1,0:T(8,128)S(1)}, f32[2,16,2,8,512]{4,3,2,1,0:T(8,128)S(1)}, u32[]{:S(2)}, u32[]{:S(2)}) collective-permute-start(f32[2,16,2,8,512]{4,3,2,1,0:T(8,128)S(1)} %get-tuple-element.63.refs_2_), channel_id=1, source_target_pairs={{0,4},{4,0},{8,12},{12,8},{1,5},{5,1},{9,13},{13,9},{2,6},{6,2},{1... | collective-permute-start | bytes 3145736 | tf_op jit(solution)/shard_map/ppermute | solution.py:632
  21.3 6.2 %collective-permute-start.4 = (f32[5,8,256]{2,1,0:T(8,128)S(1)}, f32[5,8,256]{2,1,0:T(8,128)S(1)}, u32[]{:S(2)}, u32[]{:S(2)}) collective-permute-start(f32[5,8,256]{2,1,0:T(8,128)S(1)} %get-tuple-element.64.refs_0_), channel_id=1, source_target_pairs={{0,1},{1,2},{2,3},{3,0},{4,5},{5,6},{6,7},{7,4},{8,9},{9,10},{10,1... | collective-permute-start | bytes 122888 | tf_op jit(solution)/shard_map/ppermute | solution.py:639
  22.8 6.2 %collective-permute-start.5 = (f32[5,8,256]{2,1,0:T(8,128)S(1)}, f32[5,8,256]{2,1,0:T(8,128)S(1)}, u32[]{:S(2)}, u32[]{:S(2)}) collective-permute-start(f32[5,8,256]{2,1,0:T(8,128)S(1)} %get-tuple-element.64.refs_0_), channel_id=1, source_target_pairs={{0,2},{1,3},{2,0},{3,1},{4,6},{5,7},{6,4},{7,5},{8,10},{9,11},{10,... | collective-permute-start | bytes 122888 | tf_op jit(solution)/shard_map/ppermute | solution.py:639
  25.4 4.0 %collective-permute-start.6 = (f32[5,8,256]{2,1,0:T(8,128)S(1)}, f32[5,8,256]{2,1,0:T(8,128)S(1)}, u32[]{:S(2)}, u32[]{:S(2)}) collective-permute-start(f32[5,8,256]{2,1,0:T(8,128)S(1)} %get-tuple-element.64.refs_0_), channel_id=1, source_target_pairs={{0,3},{1,0},{2,1},{3,2},{4,7},{5,4},{6,5},{7,6},{8,11},{9,8},{10,9... | collective-permute-start | bytes 122888 | tf_op jit(solution)/shard_map/ppermute | solution.py:639
  30.1 7.4 %collective-permute-start.7 = (f32[6,2,256]{2,1,0:T(2,128)S(1)}, f32[6,2,256]{2,1,0:T(2,128)S(1)}, u32[]{:S(2)}, u32[]{:S(2)}) collective-permute-start(f32[6,2,256]{2,1,0:T(2,128)S(1)} %get-tuple-element.66), channel_id=1, source_target_pairs={{0,16},{12,28},{4,8},{8,4},{16,0},{28,12},{20,24},{24,20},{1,17},{... | collective-permute-start | bytes 36872 | tf_op jit(solution)/shard_map/ppermute | solution.py:631
  31.2 6.4 %collective-permute-start.8 = (f32[6,2,256]{2,1,0:T(2,128)S(1)}, f32[6,2,256]{2,1,0:T(2,128)S(1)}, u32[]{:S(2)}, u32[]{:S(2)}) collective-permute-start(f32[6,2,256]{2,1,0:T(2,128)S(1)} %get-tuple-element.67), channel_id=1, source_target_pairs={{0,4},{4,0},{8,12},{12,8},{1,5},{5,1},{9,13},{13,9},{2,6},{6,2},{1... | collective-permute-start | bytes 36872 | tf_op jit(solution)/shard_map/ppermute | solution.py:632
  40.3 17.3 %collective-permute-start.10 = (f32[2,16,2,8,512]{4,3,2,1,0:T(8,128)S(1)}, f32[2,16,2,8,512]{4,3,2,1,0:T(8,128)S(1)}, u32[]{:S(2)}, u32[]{:S(2)}) collective-permute-start(f32[2,16,2,8,512]{4,3,2,1,0:T(8,128)S(1)} %get-tuple-element.79.refs_2_), channel_id=1, source_target_pairs={{0,4},{4,0},{8,12},{12,8},{1,5},{5,1},{9,13},{13,9},{2,6},{6,2},{1... | collective-permute-start | bytes 3145736 | tf_op jit(solution)/shard_map/ppermute | solution.py:632
  40.9 16.8 %collective-permute-start.9 = (f32[2,16,2,8,512]{4,3,2,1,0:T(8,128)S(1)}, f32[2,16,2,8,512]{4,3,2,1,0:T(8,128)S(1)}, u32[]{:S(2)}, u32[]{:S(2)}) collective-permute-start(f32[2,16,2,8,512]{4,3,2,1,0:T(8,128)S(1)} %get-tuple-element.78.refs_0_), channel_id=1, source_target_pairs={{0,16},{12,28},{4,8},{8,4},{16,0},{28,12},{20,24},{24,20},{1,17},{... | collective-permute-start | bytes 3145736 | tf_op jit(solution)/shard_map/ppermute | solution.py:631
  41.9 5.9 %collective-permute-start.11 = (f32[5,8,256]{2,1,0:T(8,128)S(1)}, f32[5,8,256]{2,1,0:T(8,128)S(1)}, u32[]{:S(2)}, u32[]{:S(2)}) collective-permute-start(f32[5,8,256]{2,1,0:T(8,128)S(1)} %get-tuple-element.80.refs_0_), channel_id=1, source_target_pairs={{0,1},{1,2},{2,3},{3,0},{4,5},{5,6},{6,7},{7,4},{8,9},{9,10},{10,1... | collective-permute-start | bytes 122888 | tf_op jit(solution)/shard_map/ppermute | solution.py:639
  42.7 5.9 %collective-permute-start.12 = (f32[5,8,256]{2,1,0:T(8,128)S(1)}, f32[5,8,256]{2,1,0:T(8,128)S(1)}, u32[]{:S(2)}, u32[]{:S(2)}) collective-permute-start(f32[5,8,256]{2,1,0:T(8,128)S(1)} %get-tuple-element.80.refs_0_), channel_id=1, source_target_pairs={{0,2},{1,3},{2,0},{3,1},{4,6},{5,7},{6,4},{7,5},{8,10},{9,11},{10,... | collective-permute-start | bytes 122888 | tf_op jit(solution)/shard_map/ppermute | solution.py:639
  45.6 4.0 %collective-permute-start.13 = (f32[5,8,256]{2,1,0:T(8,128)S(1)}, f32[5,8,256]{2,1,0:T(8,128)S(1)}, u32[]{:S(2)}, u32[]{:S(2)}) collective-permute-start(f32[5,8,256]{2,1,0:T(8,128)S(1)} %get-tuple-element.80.refs_0_), channel_id=1, source_target_pairs={{0,3},{1,0},{2,1},{3,2},{4,7},{5,4},{6,5},{7,6},{8,11},{9,8},{10,9... | collective-permute-start | bytes 122888 | tf_op jit(solution)/shard_map/ppermute | solution.py:639
  50.2 7.4 %collective-permute-start.14 = (f32[6,2,256]{2,1,0:T(2,128)S(1)}, f32[6,2,256]{2,1,0:T(2,128)S(1)}, u32[]{:S(2)}, u32[]{:S(2)}) collective-permute-start(f32[6,2,256]{2,1,0:T(2,128)S(1)} %get-tuple-element.81), channel_id=1, source_target_pairs={{0,16},{12,28},{4,8},{8,4},{16,0},{28,12},{20,24},{24,20},{1,17},{... | collective-permute-start | bytes 36872 | tf_op jit(solution)/shard_map/ppermute | solution.py:631
  51.3 6.4 %collective-permute-start.15 = (f32[6,2,256]{2,1,0:T(2,128)S(1)}, f32[6,2,256]{2,1,0:T(2,128)S(1)}, u32[]{:S(2)}, u32[]{:S(2)}) collective-permute-start(f32[6,2,256]{2,1,0:T(2,128)S(1)} %get-tuple-element.82), channel_id=1, source_target_pairs={{0,4},{4,0},{8,12},{12,8},{1,5},{5,1},{9,13},{13,9},{2,6},{6,2},{1... | collective-permute-start | bytes 36872 | tf_op jit(solution)/shard_map/ppermute | solution.py:632
  60.5 6.3 %collective-permute-start.16 = (f32[5,8,256]{2,1,0:T(8,128)S(1)}, f32[5,8,256]{2,1,0:T(8,128)S(1)}, u32[]{:S(2)}, u32[]{:S(2)}) collective-permute-start(f32[5,8,256]{2,1,0:T(8,128)S(1)} %get-tuple-element.94.refs_0_), channel_id=1, source_target_pairs={{0,1},{1,2},{2,3},{3,0},{4,5},{5,6},{6,7},{7,4},{8,9},{9,10},{10,1... | collective-permute-start | bytes 122888 | tf_op jit(solution)/shard_map/ppermute | solution.py:639
  61.2 6.8 %collective-permute-start.17 = (f32[5,8,256]{2,1,0:T(8,128)S(1)}, f32[5,8,256]{2,1,0:T(8,128)S(1)}, u32[]{:S(2)}, u32[]{:S(2)}) collective-permute-start(f32[5,8,256]{2,1,0:T(8,128)S(1)} %get-tuple-element.94.refs_0_), channel_id=1, source_target_pairs={{0,2},{1,3},{2,0},{3,1},{4,6},{5,7},{6,4},{7,5},{8,10},{9,11},{10,... | collective-permute-start | bytes 122888 | tf_op jit(solution)/shard_map/ppermute | solution.py:639
  63.3 4.6 %collective-permute-start.18 = (f32[5,8,256]{2,1,0:T(8,128)S(1)}, f32[5,8,256]{2,1,0:T(8,128)S(1)}, u32[]{:S(2)}, u32[]{:S(2)}) collective-permute-start(f32[5,8,256]{2,1,0:T(8,128)S(1)} %get-tuple-element.94.refs_0_), channel_id=1, source_target_pairs={{0,3},{1,0},{2,1},{3,2},{4,7},{5,4},{6,5},{7,6},{8,11},{9,8},{10,9... | collective-permute-start | bytes 122888 | tf_op jit(solution)/shard_map/ppermute | solution.py:639
